TPU v7x, 32 devices: a whole 2x2x4 slice. The times are simulated.
32 devices in a mesh: dp: 4 (over y, x), expert: 8 (over z, core).
Axes of the slice: x: 2, y: 2, z: 4, core: 2. Of those that a mesh axis runs over, the one named last changes fastest.
Arguments:
- tokens: bfloat16 [8192, 1280], P(('dp', 'expert')), may hold values from -6 to 6
- query_weight: bfloat16 [1280, 1280], P('dp'), may hold values from -0.15625 to 0.15625
- key_weight: bfloat16 [1280, 1280], P('dp'), may hold values from -0.15625 to 0.15625
- value_weight: bfloat16 [1280, 1280], P('dp'), may hold values from -0.15625 to 0.15625
- output_weight: bfloat16 [1280, 1280], P('dp'), may hold values from -0.625 to 0.625
- attn_gain: bfloat16 [1280], P('dp'), may hold values from 0.5 to 1.5
- ffn_gain: bfloat16 [1280], P('dp'), may hold values from 0.5 to 1.5
- router_weight: bfloat16 [1280, 16], P('dp'), may hold values from -0.078125 to 0.078125
- shared_gate: bfloat16 [1280, 896], P('dp'), may hold values from -0.15625 to 0.15625
- shared_up: bfloat16 [1280, 896], P('dp'), may hold values from -0.15625 to 0.15625
- shared_down: bfloat16 [896, 1280], P('dp'), may hold values from -0.25 to 0.25
- expert_gate: bfloat16 [16, 1280, 896], P('expert'), may hold values from -0.15625 to 0.15625
- expert_up: bfloat16 [16, 1280, 896], P('expert'), may hold values from -0.15625 to 0.15625
- expert_down: bfloat16 [16, 896, 1280], P('expert'), may hold values from -2 to 2
- expert_ids: int32 [8192, 7], P(('dp', 'expert')), may hold values from 0 to 15, all different within a row; in each aligned block of 256 rows (0 to 255, 256 to 511, ...) at most 128 rows name the same one
- piece_starts: int32 [32], P(('dp', 'expert')), may hold values from 0 to 128
- out_grad: bfloat16 [8192, 1280], P(('dp', 'expert')), may hold values from -6 to 6
Outputs:
- layer_out: bfloat16 [8192, 1280], P(('dp', 'expert'))
- tokens_grad: bfloat16 [8192, 1280], P(('dp', 'expert'))
- query_weight_grad: float32 [1280, 1280], P('dp')
- key_weight_grad: float32 [1280, 1280], P('dp')
- value_weight_grad: float32 [1280, 1280], P('dp')
- output_weight_grad: float32 [1280, 1280], P('dp')
- attn_gain_grad: float32 [1280], P('dp')
- ffn_gain_grad: float32 [1280], P('dp')
- router_weight_grad: float32 [1280, 16], P('dp')
- shared_gate_grad: float32 [1280, 896], P('dp')
- shared_up_grad: float32 [1280, 896], P('dp')
- shared_down_grad: float32 [896, 1280], P('dp')
- expert_gate_grad: float32 [16, 1280, 896], P('expert', 'dp')
- expert_up_grad: float32 [16, 1280, 896], P('expert', 'dp')
- expert_down_grad: float32 [16, 896, 1280], P('expert', 'dp')
- stat_rms: float32 [32, 3], P(('dp', 'expert'))
Inputs may be any that keep to these rules, and one draw needn't show every extreme that they name: `expert_ids`: within each sequence (aligned blocks of 256 rows) no expert is named by more than 128 rows; each row names 7 different experts. The picture piece of sequence s is tokens piece_starts[s] to piece_starts[s] + 127 of it.
All inputs are finite; a program needn't handle non-finite values.
Results may differ from a plain program's by a relative error of at most 0.023.
Values may be sent and summed in bfloat16 or wider, within the bound.
No kernel may reach another device: no remote copies, remote signals or barrier semaphores. Data moves between devices by JAX's collectives and lax.ppermute only.
A program may use at most 320 MiB of HBM per device.

v0:
```python
import jax
import jax.numpy as jnp
from jax import lax
from jax.sharding import PartitionSpec as P

HEAD_DIM = 128
TOP = 7
EXP_DEV = 2


def product(first_arg, second_arg):
    return jnp.dot(first_arg, second_arg, preferred_element_type=jnp.float32)


def product_high(first_arg, second_arg):
    return jnp.dot(
        first_arg, second_arg, precision=lax.Precision.HIGHEST, preferred_element_type=jnp.float32
    )


def rotary_tables(length, head_size):
    half_dim = head_size // 2
    frequency = 10000.0 ** (-jnp.arange(half_dim, dtype=jnp.float32) * 2.0 / head_size)
    angles = jnp.arange(length, dtype=jnp.float32)[:, None] * frequency[None, :]
    return (jnp.cos(angles), jnp.sin(angles))


def rotate(tensor, cosine, sine_part):
    half_dim = tensor.shape[-1] // 2
    first_half = tensor[..., :half_dim]
    second_half = tensor[..., half_dim:]
    cos_rows = cosine[:, None, :]
    sin_rows = sine_part[:, None, :]
    return jnp.concatenate(
        [
            first_half * cos_rows - second_half * sin_rows,
            first_half * sin_rows + second_half * cos_rows,
        ],
        axis=-1,
    )


def unrotate(tensor, cosine, sine_part):
    half_dim = tensor.shape[-1] // 2
    first_half = tensor[..., :half_dim]
    second_half = tensor[..., half_dim:]
    cos_rows = cosine[:, None, :]
    sin_rows = sine_part[:, None, :]
    return jnp.concatenate(
        [
            first_half * cos_rows + second_half * sin_rows,
            second_half * cos_rows - first_half * sin_rows,
        ],
        axis=-1,
    )


def allowed_mask(length, piece_start, piece_len):
    row_index = jnp.arange(length, dtype=jnp.int32)[:, None]
    col_index = jnp.arange(length, dtype=jnp.int32)[None, :]
    row_inside = (row_index >= piece_start) & (row_index < piece_start + piece_len)
    col_inside = (col_index >= piece_start) & (col_index < piece_start + piece_len)
    return (col_index <= row_index) | row_inside & col_inside


def silu_grad(inputs):
    sigmoid_part = jax.nn.sigmoid(inputs)
    return sigmoid_part * (1.0 + inputs * (1.0 - sigmoid_part))


def body(
    tokens,
    query_weight,
    key_weight,
    value_weight,
    output_weight,
    attn_gain,
    ffn_gain,
    router_weight,
    shared_gate,
    shared_up,
    shared_down,
    expert_gate,
    expert_up,
    expert_down,
    expert_ids,
    piece_starts,
    out_grad,
):
    (
        query_full,
        key_full,
        value_full,
        output_full,
        gain_one,
        gain_two,
        router_full,
        shared_gate_full,
        shared_up_full,
        shared_down_full,
    ) = (
        lax.all_gather(query_weight, "dp", axis=0, tiled=True),
        lax.all_gather(key_weight, "dp", axis=0, tiled=True),
        lax.all_gather(value_weight, "dp", axis=0, tiled=True),
        lax.all_gather(output_weight, "dp", axis=0, tiled=True),
        lax.all_gather(attn_gain, "dp", axis=0, tiled=True),
        lax.all_gather(ffn_gain, "dp", axis=0, tiled=True),
        lax.all_gather(router_weight, "dp", axis=0, tiled=True),
        lax.all_gather(shared_gate, "dp", axis=0, tiled=True),
        lax.all_gather(shared_up, "dp", axis=0, tiled=True),
        lax.all_gather(shared_down, "dp", axis=0, tiled=True),
    )
    length = tokens.shape[0]
    model_width = tokens.shape[1]
    head_count = model_width // HEAD_DIM
    score_scale = HEAD_DIM ** (-0.5)
    piece_len = min(256, length // 2)
    owners = lax.axis_size("expert")
    experts = EXP_DEV * owners
    capacity = 8 * length // experts
    token_f = tokens.astype(jnp.float32)
    gain_one_f = gain_one.astype(jnp.float32)
    gain_two_f = gain_two.astype(jnp.float32)
    norm_one = lax.rsqrt(jnp.mean(token_f * token_f, axis=-1, keepdims=True) + 1e-06)
    attn_in = (token_f * norm_one * gain_one_f).astype(jnp.bfloat16)
    cosine, sine_part = rotary_tables(length, HEAD_DIM)
    query_pre = product(attn_in, query_full).reshape(length, head_count, HEAD_DIM)
    key_pre = product(attn_in, key_full).reshape(length, head_count, HEAD_DIM)
    query_rot = rotate(query_pre, cosine, sine_part).astype(jnp.bfloat16)
    key_rot = rotate(key_pre, cosine, sine_part).astype(jnp.bfloat16)
    values = product(attn_in, value_full).astype(jnp.bfloat16).reshape(length, head_count, HEAD_DIM)
    allowed = allowed_mask(length, piece_starts[0], piece_len)

    def score_block():
        raw_scores = (
            jnp.einsum("qhd,khd->hqk", query_rot, key_rot, preferred_element_type=jnp.float32)
            * score_scale
        )
        return jnp.where(allowed[None], raw_scores, -1e30)

    scores = score_block()
    row_max = jnp.max(scores, axis=-1, keepdims=True)
    log_total = row_max + jnp.log(jnp.sum(jnp.exp(scores - row_max), axis=-1, keepdims=True))
    probs_low = jnp.exp(scores - log_total).astype(jnp.bfloat16)
    context = jnp.einsum("hqk,khd->qhd", probs_low, values, preferred_element_type=jnp.float32)
    context = context.astype(jnp.bfloat16).reshape(length, model_width)
    attn_out = product(context, output_full)
    residual = token_f + attn_out
    norm_two = lax.rsqrt(jnp.mean(residual * residual, axis=-1, keepdims=True) + 1e-06)
    ffn_in = (residual * norm_two * gain_two_f).astype(jnp.bfloat16)
    router_probs = jax.nn.softmax(product(ffn_in, router_full), axis=-1)
    gate_values = jnp.take_along_axis(router_probs, expert_ids, axis=1)
    shared_gate_act = product(ffn_in, shared_gate_full)
    shared_up_act = product(ffn_in, shared_up_full)
    shared_hidden = (jax.nn.silu(shared_gate_act) * shared_up_act).astype(jnp.bfloat16)
    shared_out = product(shared_hidden, shared_down_full)
    flat_ids = expert_ids.reshape(-1)
    onehot = (flat_ids[:, None] == jnp.arange(experts, dtype=jnp.int32)[None, :]).astype(jnp.int32)
    before = jnp.cumsum(onehot, axis=0) - onehot
    slot_index = jnp.sum(before * onehot, axis=1)
    position = (
        flat_ids % EXP_DEV * (owners * capacity) + flat_ids // EXP_DEV * capacity + slot_index
    )
    token_index = jnp.arange(length * TOP, dtype=jnp.int32) // TOP
    send_rows = (
        jnp.zeros((experts * capacity, model_width), jnp.bfloat16)
        .at[position]
        .set(ffn_in[token_index])
    )
    send_rows = send_rows.reshape(EXP_DEV, owners * capacity, model_width)
    expert_in = lax.all_to_all(send_rows, "expert", split_axis=1, concat_axis=1, tiled=True)
    routed_gate = jnp.einsum(
        "erd,edf->erf", expert_in, expert_gate, preferred_element_type=jnp.float32
    )
    routed_up = jnp.einsum("erd,edf->erf", expert_in, expert_up, preferred_element_type=jnp.float32)
    routed_hidden = (jax.nn.silu(routed_gate) * routed_up).astype(jnp.bfloat16)
    routed_res = jnp.einsum(
        "erf,efd->erd", routed_hidden, expert_down, preferred_element_type=jnp.float32
    ).astype(jnp.bfloat16)
    returned = lax.all_to_all(
        routed_res, "expert", split_axis=1, concat_axis=1, tiled=True
    ).reshape(experts * capacity, model_width)
    picked = returned[position].reshape(length, TOP, model_width)
    routed_out = jnp.sum(gate_values[:, :, None] * picked, axis=1)
    moe_out = shared_out + routed_out
    stream_out = residual + moe_out
    stat_rms = jnp.stack(
        [
            jnp.sqrt(jnp.mean(attn_out * attn_out)),
            jnp.sqrt(jnp.mean(moe_out * moe_out)),
            jnp.sqrt(jnp.mean(stream_out * stream_out)),
        ]
    )[None, :]
    grad_f = out_grad.astype(jnp.float32)
    gate_grad = jnp.sum(picked * grad_f[:, None, :], axis=-1)
    slot_grad = (
        (gate_values[:, :, None] * grad_f[:, None, :])
        .astype(jnp.bfloat16)
        .reshape(length * TOP, model_width)
    )
    send_grad = (
        jnp.zeros((experts * capacity, model_width), jnp.bfloat16).at[position].set(slot_grad)
    )
    send_grad = send_grad.reshape(EXP_DEV, owners * capacity, model_width)
    res_grad = lax.all_to_all(send_grad, "expert", split_axis=1, concat_axis=1, tiled=True)
    hidden_grad = jnp.einsum(
        "erd,efd->erf", res_grad, expert_down, preferred_element_type=jnp.float32
    )
    expert_down_part = jnp.einsum(
        "erf,erd->efd", routed_hidden, res_grad, preferred_element_type=jnp.float32
    )
    routed_gate_grad = (hidden_grad * routed_up * silu_grad(routed_gate)).astype(jnp.bfloat16)
    routed_up_grad = (hidden_grad * jax.nn.silu(routed_gate)).astype(jnp.bfloat16)
    expert_gate_part = jnp.einsum(
        "erd,erf->edf", expert_in, routed_gate_grad, preferred_element_type=jnp.float32
    )
    expert_up_part = jnp.einsum(
        "erd,erf->edf", expert_in, routed_up_grad, preferred_element_type=jnp.float32
    )
    expert_in_grad = jnp.einsum(
        "erf,edf->erd", routed_gate_grad, expert_gate, preferred_element_type=jnp.float32
    ) + jnp.einsum("erf,edf->erd", routed_up_grad, expert_up, preferred_element_type=jnp.float32)
    expert_in_grad = expert_in_grad.astype(jnp.bfloat16)
    returned_grad = lax.all_to_all(
        expert_in_grad, "expert", split_axis=1, concat_axis=1, tiled=True
    ).reshape(experts * capacity, model_width)
    routed_in_grad = jnp.sum(
        returned_grad[position].reshape(length, TOP, model_width), axis=1, dtype=jnp.float32
    )
    chosen = (expert_ids[:, :, None] == jnp.arange(experts, dtype=jnp.int32)[None, None, :]).astype(
        jnp.float32
    )
    probs_grad = jnp.sum(chosen * gate_grad[:, :, None], axis=1)
    logits_grad = router_probs * (
        probs_grad - jnp.sum(router_probs * probs_grad, axis=-1, keepdims=True)
    )
    router_grad = product_high(ffn_in.astype(jnp.float32).T, logits_grad)
    router_in_grad = product_high(logits_grad, router_full.astype(jnp.float32).T)
    shared_out_grad = grad_f.astype(jnp.bfloat16)
    shared_hidden_grad = product(shared_out_grad, shared_down_full.T)
    shared_down_grad = product(shared_hidden.T, shared_out_grad)
    shared_gate_act_grad = (shared_hidden_grad * shared_up_act * silu_grad(shared_gate_act)).astype(
        jnp.bfloat16
    )
    shared_up_act_grad = (shared_hidden_grad * jax.nn.silu(shared_gate_act)).astype(jnp.bfloat16)
    shared_gate_grad = product(ffn_in.T, shared_gate_act_grad)
    shared_up_grad = product(ffn_in.T, shared_up_act_grad)
    ffn_in_grad = (
        product(shared_gate_act_grad, shared_gate_full.T)
        + product(shared_up_act_grad, shared_up_full.T)
        + routed_in_grad
        + router_in_grad
    )
    ffn_gain_grad = jnp.sum(ffn_in_grad * residual * norm_two, axis=0)
    upstream_two = ffn_in_grad * gain_two_f
    residual_grad = (
        grad_f
        + norm_two * upstream_two
        - residual * norm_two**3 * jnp.mean(upstream_two * residual, axis=-1, keepdims=True)
    )
    attn_out_grad = residual_grad.astype(jnp.bfloat16)
    output_grad = product(context.T, attn_out_grad)
    context_grad = (
        product(attn_out_grad, output_full.T)
        .astype(jnp.bfloat16)
        .reshape(length, head_count, HEAD_DIM)
    )
    attn_probs = jnp.exp(score_block() - log_total)
    probs_again = attn_probs.astype(jnp.bfloat16)
    value_grad = jnp.einsum(
        "hqk,qhd->khd", probs_again, context_grad, preferred_element_type=jnp.float32
    )
    value_grad = value_grad.astype(jnp.bfloat16).reshape(length, model_width)
    probs_grad_att = jnp.einsum(
        "qhd,khd->hqk", context_grad, values, preferred_element_type=jnp.float32
    )
    row_delta = jnp.sum(attn_probs * probs_grad_att, axis=-1, keepdims=True)
    scores_grad = (attn_probs * (probs_grad_att - row_delta)).astype(jnp.bfloat16)
    query_grad = (
        jnp.einsum("hqk,khd->qhd", scores_grad, key_rot, preferred_element_type=jnp.float32)
        * score_scale
    )
    key_grad = (
        jnp.einsum("hqk,qhd->khd", scores_grad, query_rot, preferred_element_type=jnp.float32)
        * score_scale
    )
    query_pre_grad = (
        unrotate(query_grad, cosine, sine_part).astype(jnp.bfloat16).reshape(length, model_width)
    )
    key_pre_grad = (
        unrotate(key_grad, cosine, sine_part).astype(jnp.bfloat16).reshape(length, model_width)
    )
    query_wgrad = product(attn_in.T, query_pre_grad)
    key_wgrad = product(attn_in.T, key_pre_grad)
    value_wgrad = product(attn_in.T, value_grad)
    attn_in_grad = (
        product(query_pre_grad, query_full.T)
        + product(key_pre_grad, key_full.T)
        + product(value_grad, value_full.T)
    )
    attn_gain_grad = jnp.sum(attn_in_grad * token_f * norm_one, axis=0)
    upstream_one = attn_in_grad * gain_one_f
    tokens_grad = (
        residual_grad
        + norm_one * upstream_one
        - token_f * norm_one**3 * jnp.mean(upstream_one * token_f, axis=-1, keepdims=True)
    )
    dense_grads = (
        query_wgrad,
        key_wgrad,
        value_wgrad,
        output_grad,
        attn_gain_grad,
        ffn_gain_grad,
        router_grad,
        shared_gate_grad,
        shared_up_grad,
        shared_down_grad,
    )
    partial_shares = (
        lax.psum_scatter(
            dense_grads[0].astype(jnp.bfloat16), "dp", scatter_dimension=0, tiled=True
        ).astype(jnp.float32),
        lax.psum_scatter(
            dense_grads[1].astype(jnp.bfloat16), "dp", scatter_dimension=0, tiled=True
        ).astype(jnp.float32),
        lax.psum_scatter(
            dense_grads[2].astype(jnp.bfloat16), "dp", scatter_dimension=0, tiled=True
        ).astype(jnp.float32),
        lax.psum_scatter(
            dense_grads[3].astype(jnp.bfloat16), "dp", scatter_dimension=0, tiled=True
        ).astype(jnp.float32),
        lax.psum_scatter(
            dense_grads[4].astype(jnp.bfloat16), "dp", scatter_dimension=0, tiled=True
        ).astype(jnp.float32),
        lax.psum_scatter(
            dense_grads[5].astype(jnp.bfloat16), "dp", scatter_dimension=0, tiled=True
        ).astype(jnp.float32),
        lax.psum_scatter(
            dense_grads[6].astype(jnp.bfloat16), "dp", scatter_dimension=0, tiled=True
        ).astype(jnp.float32),
        lax.psum_scatter(
            dense_grads[7].astype(jnp.bfloat16), "dp", scatter_dimension=0, tiled=True
        ).astype(jnp.float32),
        lax.psum_scatter(
            dense_grads[8].astype(jnp.bfloat16), "dp", scatter_dimension=0, tiled=True
        ).astype(jnp.float32),
        lax.psum_scatter(
            dense_grads[9].astype(jnp.bfloat16), "dp", scatter_dimension=0, tiled=True
        ).astype(jnp.float32),
    )
    shares = (
        lax.psum(partial_shares[0].astype(jnp.bfloat16), "expert").astype(jnp.float32),
        lax.psum(partial_shares[1].astype(jnp.bfloat16), "expert").astype(jnp.float32),
        lax.psum(partial_shares[2].astype(jnp.bfloat16), "expert").astype(jnp.float32),
        lax.psum(partial_shares[3].astype(jnp.bfloat16), "expert").astype(jnp.float32),
        lax.psum(partial_shares[4].astype(jnp.bfloat16), "expert").astype(jnp.float32),
        lax.psum(partial_shares[5].astype(jnp.bfloat16), "expert").astype(jnp.float32),
        lax.psum(partial_shares[6].astype(jnp.bfloat16), "expert").astype(jnp.float32),
        lax.psum(partial_shares[7].astype(jnp.bfloat16), "expert").astype(jnp.float32),
        lax.psum(partial_shares[8].astype(jnp.bfloat16), "expert").astype(jnp.float32),
        lax.psum(partial_shares[9].astype(jnp.bfloat16), "expert").astype(jnp.float32),
    )
    expert_shares = (
        lax.psum_scatter(
            expert_gate_part.astype(jnp.bfloat16), "dp", scatter_dimension=1, tiled=True
        ).astype(jnp.float32),
        lax.psum_scatter(
            expert_up_part.astype(jnp.bfloat16), "dp", scatter_dimension=1, tiled=True
        ).astype(jnp.float32),
        lax.psum_scatter(
            expert_down_part.astype(jnp.bfloat16), "dp", scatter_dimension=1, tiled=True
        ).astype(jnp.float32),
    )
    return (
        stream_out.astype(jnp.bfloat16),
        tokens_grad.astype(jnp.bfloat16),
        shares[0],
        shares[1],
        shares[2],
        shares[3],
        shares[4],
        shares[5],
        shares[6],
        shares[7],
        shares[8],
        shares[9],
        expert_shares[0],
        expert_shares[1],
        expert_shares[2],
        stat_rms,
    )


def solution(mesh):
    in_specs = (
        P(("dp", "expert"), None),
        P("dp", None),
        P("dp", None),
        P("dp", None),
        P("dp", None),
        P("dp"),
        P("dp"),
        P("dp", None),
        P("dp", None),
        P("dp", None),
        P("dp", None),
        P("expert", None, None),
        P("expert", None, None),
        P("expert", None, None),
        P(("dp", "expert"), None),
        P(("dp", "expert")),
        P(("dp", "expert"), None),
    )
    out_specs = (
        P(("dp", "expert"), None),
        P(("dp", "expert"), None),
        P("dp", None),
        P("dp", None),
        P("dp", None),
        P("dp", None),
        P("dp"),
        P("dp"),
        P("dp", None),
        P("dp", None),
        P("dp", None),
        P("dp", None),
        P("expert", "dp", None),
        P("expert", "dp", None),
        P("expert", "dp", None),
        P(("dp", "expert"), None),
    )
    return jax.shard_map(body, mesh=mesh, in_specs=in_specs, out_specs=out_specs, check_vma=False)
```

profile of v0, /device:TPU:0, one launch (start us, length us, event | category | flops | bytes accessed | tf_op | source)
XLA Modules:
  0.0 1338.6 jit_solution(12538028427813180450)
XLA Ops:
  12.6 11.6 all-reduce.7
  32.5 25.0 %all-gather.11.cloned.1.call-done = bf16[1280,1280]{1,0:T(8,128)(2,1)} async-done(((bf16[320,1280]{1,0:T(8,128)(2,1)}), bf16[1280,1280]{1,0:T(8,128)(2,1)}) %all-gather.11.cloned.1.call-update) | async-done | bytes 3276816 | tf_op jit(solution)/shard_map/all_gather | solution.py:102
  63.8 40.6 %all-gather.13.cloned.1.call-done = bf16[1280,1280]{1,0:T(8,128)(2,1)} async-done(((bf16[320,1280]{1,0:T(8,128)(2,1)}), bf16[1280,1280]{1,0:T(8,128)(2,1)}) %all-gather.13.cloned.1.call-update) | async-done | bytes 3276816 | tf_op jit(solution)/shard_map/all_gather | solution.py:103
  114.0 37.2 %all-gather.9.cloned.1.call-done = bf16[1280,1280]{1,0:T(8,128)(2,1)} async-done(((bf16[320,1280]{1,0:T(8,128)(2,1)}), bf16[1280,1280]{1,0:T(8,128)(2,1)}) %all-gather.9.cloned.1.call-update) | async-done | bytes 3276816 | tf_op jit(solution)/shard_map/all_gather | solution.py:104
  163.6 34.3 %all-gather.15.cloned.1.call-done = bf16[1280,1280]{1,0:T(8,128)(2,1)} async-done(((bf16[320,1280]{1,0:T(8,128)(2,1)}), bf16[1280,1280]{1,0:T(8,128)(2,1)}) %all-gather.15.cloned.1.call-update) | async-done | bytes 3276816 | tf_op jit(solution)/shard_map/all_gather | solution.py:105
  203.1 32.3 %scatter_custom_fusion = bf16[2048,1280]{1,0:T(8,128)(2,1)} fusion(s32[1792]{0:T(1024)S(1)} %fusion.37, bf16[256,1280]{1,0:T(8,128)(2,1)S(1)} %multiply_convert_fusion.6, s32[2048]{0:T(1024)S(1)} %pad_clamp_fusion.1, bf16[]{:T(256)} %constant.95.clone.1), kind=kCustom, calls=%fused_computation.27 | custom fusion | bytes 5242882 | tf_op jit(solution)/shard_map/scatter | solution.py:168
  275.5 14.1 %gather_fusion.2 = f32[1792]{0:T(1024)S(1)} fusion(f32[256,16]{0,1:T(8,128)S(1)} %fusion.35, s32[1792]{0:T(1024)S(1)} %reshape.479), kind=kCustom, calls=%fused_computation.3 | custom fusion | bytes 28672 | tf_op jit(solution)/shard_map/jit(take_along_axis)/gather | solution.py:152
  290.2 22.3 %scatter_custom_fusion.1 = bf16[2048,1280]{1,0:T(8,128)(2,1)} fusion(s32[1792]{0:T(1024)S(1)} %fusion.37, f32[1792,1280]{1,0:T(8,128)} %mul.558, f32[1792]{0:T(1024)S(1)} %mul.555, bf16[]{:T(256)} %constant.95.clone.1), kind=kCustom, calls=%fused_computation.26 | custom fusion | flops 4587520 | bytes 14426114 | tf_op jit(solution)/shard_map/scatter | solution.py:202
  322.7 44.1 %all-to-all-done = bf16[2,1024,1280]{2,0,1:T(2,128)(2,1)} async-done(((bf16[2,1024,1280]{2,0,1:T(2,128)(2,1)}), bf16[2,1024,1280]{2,0,1:T(2,128)(2,1)}, u32[]{:S(2)}, u32[]{:S(2)}) %all-to-all-start) | async-done | bytes 5242912 | tf_op jit(solution)/shard_map/all_to_all | solution.py:171
  372.7 13.7 %copy.294 = bf16[2,1024,1280]{1,2,0:T(8,128)(2,1)} copy(bf16[2,1024,1280]{2,0,1:T(2,128)(2,1)} %all-to-all-done) | data formatting | bytes 10485760 | tf_op jit(solution)/shard_map/all_to_all | solution.py:171
  386.4 10.9 fusion.61
  407.3 80.6 %all-to-all-done.2 = bf16[2,1024,1280]{2,0,1:T(2,128)(2,1)} async-done(((bf16[2,1024,1280]{2,0,1:T(2,128)(2,1)}), bf16[2,1024,1280]{2,0,1:T(2,128)(2,1)}, u32[]{:S(2)}, u32[]{:S(2)}) %all-to-all-start.2) | async-done | bytes 5242912 | tf_op jit(solution)/shard_map/all_to_all | solution.py:205
  488.0 16.1 %multiply_convert_fusion.1 = (bf16[2,1024,896]{2,1,0:T(8,128)(2,1)}, bf16[2,1024,896]{2,1,0:T(8,128)(2,1)}, bf16[2,1024,896]{2,1,0:T(8,128)(2,1)}) fusion(f32[2,1024,896]{2,1,0:T(8,128)} %fusion.61, f32[2,1024,896]{2,1,0:T(8,128)} %fusion.62, bf16[2,896,1280]{2,1,0:T(8,128)(2,1)} %param.30, bf16[2,1024,1280]{2,0,1:T(2,128)(2,1)} %all-to-all-done.2), kind=kOutput, calls=%fused_computation.14 | convolution fusion | flops 4725145600 | bytes 35520512 | tf_op jit(solution)/shard_map/erd,efd->erf/dot_general | solution.py:206
  504.0 10.6 convolution_convert_fusion.4
  514.7 10.3 copy.274
  537.2 32.2 %all-gather.21.cloned.1.call-done = bf16[896,1280]{1,0:T(8,128)(2,1)} async-done(((bf16[224,1280]{1,0:T(8,128)(2,1)}), bf16[896,1280]{1,0:T(8,128)(2,1)}) %all-gather.21.cloned.1.call-update) | async-done | bytes 2293776 | tf_op jit(solution)/shard_map/all_gather | solution.py:111
  593.3 10.3 copy.279
  603.6 42.4 %all-to-all-done.1 = bf16[2,1024,1280]{2,0,1:T(2,128)(2,1)} async-done(((bf16[2,1024,1280]{2,0,1:T(2,128)(2,1)}), bf16[2,1024,1280]{2,0,1:T(2,128)(2,1)}, u32[]{:S(2)}, u32[]{:S(2)}) %all-to-all-start.1) | async-done | bytes 5242912 | tf_op jit(solution)/shard_map/all_to_all | solution.py:180
  666.2 13.6 %gather_fusion = bf16[1792,1280]{1,0:T(8,128)(2,1)} fusion(bf16[2048,1280]{1,0:T(8,128)(2,1)} %bitcast.117, s32[2048]{0:T(1024)S(1)} %pad_clamp_fusion), kind=kCustom, calls=%fused_computation.1 | custom fusion | bytes 9182208 | tf_op jit(solution)/shard_map/gather | solution.py:183
  688.1 14.8 %multiply_reduce_fusion = (f32[256,7]{1,0:T(8,128)S(1)}, f32[256,1280]{1,0:T(8,128)S(1)}) fusion(f32[256,7,1280]{2,1,0:T(8,128)} %reshape.453, f32[256,1280]{1,0:T(8,128)} %convert_element_type.235, f32[256,7]{1,0:T(8,128)S(1)} %copy.267), kind=kLoop, calls=%fused_computation.6 | loop fusion | flops 8845568 | bytes 11810816 | tf_op jit(solution)/shard_map/reduce_sum | solution.py:195
  703.0 64.1 %all-to-all-done.3 = bf16[2,1024,1280]{2,0,1:T(2,128)(2,1)} async-done(((bf16[2,1024,1280]{2,0,1:T(2,128)(2,1)}), bf16[2,1024,1280]{2,0,1:T(2,128)(2,1)}, u32[]{:S(2)}, u32[]{:S(2)}) %all-to-all-start.3) | async-done | bytes 5242912 | tf_op jit(solution)/shard_map/all_to_all | solution.py:224
  772.6 13.4 %gather_fusion.1 = bf16[1792,1280]{1,0:T(8,128)(2,1)} fusion(bf16[2048,1280]{1,0:T(8,128)(2,1)} %bitcast.116, s32[2048]{0:T(1024)S(1)} %pad_clamp_fusion), kind=kCustom, calls=%fused_computation.2 | custom fusion | bytes 9182208 | tf_op jit(solution)/shard_map/gather | solution.py:228
  841.3 10.7 convolution_convert_fusion.5
  875.1 30.4 %reduce-scatter.18.cloned.1.call-done = bf16[320,1280]{1,0:T(8,128)(2,1)} async-done(((bf16[1280,1280]{1,0:T(8,128)(2,1)}), bf16[320,1280]{1,0:T(8,128)(2,1)}) %reduce-scatter.18.cloned.1.call-update) | async-done | bytes 819216 | tf_op jit(solution)/shard_map/reduce_scatter | solution.py:327
  905.5 48.0 %reduce-scatter.14.cloned.1.call-done = bf16[320,1280]{1,0:T(8,128)(2,1)} async-done(((bf16[1280,1280]{1,0:T(8,128)(2,1)}), bf16[320,1280]{1,0:T(8,128)(2,1)}) %reduce-scatter.14.cloned.1.call-update) | async-done | bytes 819216 | tf_op jit(solution)/shard_map/reduce_scatter | solution.py:321
  953.5 47.9 %reduce-scatter.16.cloned.1.call-done = bf16[320,1280]{1,0:T(8,128)(2,1)} async-done(((bf16[1280,1280]{1,0:T(8,128)(2,1)}), bf16[320,1280]{1,0:T(8,128)(2,1)}) %reduce-scatter.16.cloned.1.call-update) | async-done | bytes 819216 | tf_op jit(solution)/shard_map/reduce_scatter | solution.py:324
  1020.8 39.9 %reduce-scatter.32.cloned.1.call-done = bf16[2,224,1280]{2,1,0:T(8,128)(2,1)} async-done(((bf16[2,896,1280]{2,1,0:T(8,128)(2,1)}), bf16[2,224,1280]{2,1,0:T(8,128)(2,1)}) %reduce-scatter.32.cloned.1.call-update) | async-done | bytes 1146896 | tf_op jit(solution)/shard_map/reduce_scatter | solution.py:371
  1063.6 56.0 %reduce-scatter.28.cloned.1.call-done = bf16[2,320,896]{2,1,0:T(8,128)(2,1)} async-done(((bf16[2,1280,896]{2,1,0:T(8,128)(2,1)}), bf16[2,320,896]{2,1,0:T(8,128)(2,1)}) %reduce-scatter.28.cloned.1.call-update) | async-done | bytes 1146896 | tf_op jit(solution)/shard_map/reduce_scatter | solution.py:365
  1122.4 56.0 %reduce-scatter.30.cloned.1.call-done = bf16[2,320,896]{2,1,0:T(8,128)(2,1)} async-done(((bf16[2,1280,896]{2,1,0:T(8,128)(2,1)}), bf16[2,320,896]{2,1,0:T(8,128)(2,1)}) %reduce-scatter.30.cloned.1.call-update) | async-done | bytes 1146896 | tf_op jit(solution)/shard_map/reduce_scatter | solution.py:368
  1183.1 23.1 %reduce-scatter.34.cloned.1.call-done = bf16[320,16]{1,0:T(8,128)(2,1)} async-done(((bf16[1280,16]{1,0:T(8,128)(2,1)}), bf16[320,16]{1,0:T(8,128)(2,1)}) %reduce-scatter.34.cloned.1.call-update) | async-done | bytes 10256
  1207.1 29.3 %all-reduce.4 = (bf16[320]{0:T(512)(128)(2,1)S(1)}, bf16[320]{0:T(512)(128)(2,1)S(1)}, bf16[320,16]{0,1:T(8,128)(2,1)S(1)}) all-reduce(bf16[320]{0:T(512)(128)(2,1)S(1)} %dynamic-slice.3, bf16[320]{0:T(512)(128)(2,1)S(1)} %dynamic-slice.5, bf16[320,16]{0,1:T(8,128)(2,1)S(1)} %copy.312), channel_id=1, replica_groups=mesh['dp'=4,'expert'=8] {'expert'}, use_global_device_ids=true, to_apply=%region_29.30 | all-reduce | flops 5760 | bytes 23040 | tf_op jit(solution)/shard_map/psum | solution.py:357
  1238.2 83.8 %all-reduce.10.cloned.1.call-done = (bf16[320,1280]{1,0:T(8,128)(2,1)}, bf16[320,1280]{1,0:T(8,128)(2,1)}, bf16[320,1280]{1,0:T(8,128)(2,1)}, bf16[320,1280]{1,0...) async-done(((bf16[320,1280]{1,0:T(8,128)(2,1)}, bf16[320,1280]{1,0:T(8,128)(2,1)}, bf16[320,1280]{1,0:T(8,128)(2,1)}, ...) | async-done | bytes 4997136 | tf_op jit(solution)/shard_map/psum | solution.py:353
  (317 shorter events, 299.1 us)
Async XLA Ops:
  7.2 50.3 %all-gather.11.cloned.1.call-start = ((), (), s32[]{:S(2)}) async-start(), calls=%async_computation.16 | async-start | bytes 4096000 | tf_op jit(solution)/shard_map/all_gather | solution.py:102
  8.0 96.4 %all-gather.13.cloned.1.call-start = ((), (), s32[]{:S(2)}) async-start(), calls=%async_computation.17 | async-start | bytes 4096000 | tf_op jit(solution)/shard_map/all_gather | solution.py:103
  8.7 142.5 %all-gather.9.cloned.1.call-start = ((), (), s32[]{:S(2)}) async-start(), calls=%async_computation.15 | async-start | bytes 4096000 | tf_op jit(solution)/shard_map/all_gather | solution.py:104
  9.5 188.4 %all-gather.15.cloned.1.call-start = ((), (), s32[]{:S(2)}) async-start(), calls=%async_computation.18 | async-start | bytes 4096000 | tf_op jit(solution)/shard_map/all_gather | solution.py:105
  24.3 126.9 %copy-start.46 = (f32[1280]{0:T(1024)}, f32[1280]{0:T(1024)S(1)}, u32[]{:S(2)}) copy-start(f32[1280]{0:T(1024)S(1)} %convert_element_type.219) | copy-start | bytes 15364
  24.9 177.4 %copy-start.50 = (f32[1280]{0:T(1024)}, f32[1280]{0:T(1024)S(1)}, u32[]{:S(2)}) copy-start(f32[1280]{0:T(1024)S(1)} %convert_element_type.225) | copy-start | bytes 15364
  31.3 119.9 %copy-start.54 = (f32[256]{0:T(256)}, f32[256]{0:T(256)S(1)}, u32[]{:S(2)}) copy-start(f32[256]{0:T(256)S(1)} %get-tuple-element.67) | copy-start | bytes 3076
  31.4 130.4 %copy-start.29 = (pred[256,256]{0,1:T(8,128)(4,1)}, pred[256,256]{0,1:T(8,128)(4,1)S(1)}, u32[]{:S(2)}) copy-start(pred[256,256]{0,1:T(8,128)(4,1)S(1)} %fusion.27) | copy-start | bytes 196612
  32.5 124.7 %copy-start.31 = (f32[256,64]{1,0:T(8,128)}, f32[256,64]{1,0:T(8,128)S(1)}, u32[]{:S(2)}) copy-start(f32[256,64]{1,0:T(8,128)S(1)} %get-tuple-element.72) | copy-start | bytes 196612
  203.1 447.6 %copy-start.6 = (bf16[256,1280]{1,0:T(8,128)(2,1)}, bf16[256,1280]{1,0:T(8,128)(2,1)S(1)}, u32[]{:S(2)}) copy-start(bf16[256,1280]{1,0:T(8,128)(2,1)S(1)} %multiply_convert_fusion.6) | copy-start | bytes 1966084
  245.6 121.3 %all-to-all-start = ((bf16[2,1024,1280]{2,0,1:T(2,128)(2,1)}), bf16[2,1024,1280]{2,0,1:T(2,128)(2,1)}, u32[]{:S(2)}, u32[]{:S(2)}) async-start(bf16[2,1024,1280]{2,0,1:T(2,128)(2,1)} %copy.271), calls=%async_computation | async-start | bytes 10485760 | tf_op jit(solution)/shard_map/all_to_all | solution.py:171
  366.9 121.1 %all-to-all-start.2 = ((bf16[2,1024,1280]{2,0,1:T(2,128)(2,1)}), bf16[2,1024,1280]{2,0,1:T(2,128)(2,1)}, u32[]{:S(2)}, u32[]{:S(2)}) async-start(bf16[2,1024,1280]{2,0,1:T(2,128)(2,1)} %copy.277), calls=%async_computation.2 | async-start | bytes 10485760 | tf_op jit(solution)/shard_map/all_to_all | solution.py:205
  371.5 158.9 %all-gather.17.cloned.1.call-start = ((), (), s32[]{:S(2)}) async-start(), calls=%async_computation.19 | async-start | bytes 2867200 | tf_op jit(solution)/shard_map/all_gather | solution.py:109
  372.1 161.7 %all-gather.19.cloned.1.call-start = ((), (), s32[]{:S(2)}) async-start(), calls=%async_computation.20 | async-start | bytes 2867200 | tf_op jit(solution)/shard_map/all_gather | solution.py:110
  524.9 121.1 %all-to-all-start.1 = ((bf16[2,1024,1280]{2,0,1:T(2,128)(2,1)}), bf16[2,1024,1280]{2,0,1:T(2,128)(2,1)}, u32[]{:S(2)}, u32[]{:S(2)}) async-start(bf16[2,1024,1280]{2,0,1:T(2,128)(2,1)} %copy.274), calls=%async_computation.1 | async-start | bytes 10485760 | tf_op jit(solution)/shard_map/all_to_all | solution.py:180
  529.6 39.9 %all-gather.21.cloned.1.call-start = ((), (), s32[]{:S(2)}) async-start(), calls=%async_computation.21 | async-start | bytes 2867200 | tf_op jit(solution)/shard_map/all_gather | solution.py:111
  530.3 344.7 %reduce-scatter.22.cloned.1.call-start = ((), (), s32[]{:S(2)}) async-start(), calls=%async_computation.26 | async-start | bytes 2867200 | tf_op jit(solution)/shard_map/reduce_scatter | solution.py:342
  572.7 80.4 %copy-start.27 = (bf16[256,896]{1,0:T(8,128)(2,1)}, bf16[256,896]{1,0:T(8,128)(2,1)S(1)}, u32[]{:S(2)}) copy-start(bf16[256,896]{1,0:T(8,128)(2,1)S(1)} %get-tuple-element.52) | copy-start | bytes 1376260
  646.0 121.1 %all-to-all-start.3 = ((bf16[2,1024,1280]{2,0,1:T(2,128)(2,1)}), bf16[2,1024,1280]{2,0,1:T(2,128)(2,1)}, u32[]{:S(2)}, u32[]{:S(2)}) async-start(bf16[2,1024,1280]{2,0,1:T(2,128)(2,1)} %copy.279), calls=%async_computation.3 | async-start | bytes 10485760 | tf_op jit(solution)/shard_map/all_to_all | solution.py:224
  650.6 224.4 %reduce-scatter.24.cloned.1.call-start = ((), (), s32[]{:S(2)}) async-start(), calls=%async_computation.27 | async-start | bytes 2867200 | tf_op jit(solution)/shard_map/reduce_scatter | solution.py:345
  653.0 222.1 %reduce-scatter.26.cloned.1.call-start = ((), (), s32[]{:S(2)}) async-start(), calls=%async_computation.28 | async-start | bytes 2867200 | tf_op jit(solution)/shard_map/reduce_scatter | solution.py:348
  655.3 219.8 %reduce-scatter.20.cloned.1.call-start = ((), (), s32[]{:S(2)}) async-start(), calls=%async_computation.25 | async-start | bytes 4096000 | tf_op jit(solution)/shard_map/reduce_scatter | solution.py:330
  814.5 91.0 %reduce-scatter.18.cloned.1.call-start = ((), (), s32[]{:S(2)}) async-start(), calls=%async_computation.24 | async-start | bytes 4096000 | tf_op jit(solution)/shard_map/reduce_scatter | solution.py:327
  826.9 126.7 %reduce-scatter.14.cloned.1.call-start = ((), (), s32[]{:S(2)}) async-start(), calls=%async_computation.22 | async-start | bytes 4096000 | tf_op jit(solution)/shard_map/reduce_scatter | solution.py:321
  837.8 163.6 %reduce-scatter.16.cloned.1.call-start = ((), (), s32[]{:S(2)}) async-start(), calls=%async_computation.23 | async-start | bytes 4096000 | tf_op jit(solution)/shard_map/reduce_scatter | solution.py:324
  841.0 219.8 %reduce-scatter.32.cloned.1.call-start = ((), (), s32[]{:S(2)}) async-start(), calls=%async_computation.31 | async-start | bytes 5734400 | tf_op jit(solution)/shard_map/reduce_scatter | solution.py:371
  852.0 267.6 %reduce-scatter.28.cloned.1.call-start = ((), (), s32[]{:S(2)}) async-start(), calls=%async_computation.29 | async-start | bytes 5734400 | tf_op jit(solution)/shard_map/reduce_scatter | solution.py:365
  862.2 316.3 %reduce-scatter.30.cloned.1.call-start = ((), (), s32[]{:S(2)}) async-start(), calls=%async_computation.30 | async-start | bytes 5734400 | tf_op jit(solution)/shard_map/reduce_scatter | solution.py:368
  872.3 333.9 %reduce-scatter.34.cloned.1.call-start = ((), (), s32[]{:S(2)}) async-start(), calls=%async_computation.32 | async-start | bytes 409600
  874.7 447.3 %all-reduce.10.cloned.1.call-start = ((), (), s32[]{:S(2)}) async-start(), calls=%async_computation.33 | async-start | bytes 9994240 | tf_op jit(solution)/shard_map/psum | solution.py:353
  1063.6 118.3 %copy-start.11 = (f32[256,1280]{1,0:T(8,128)S(1)}, f32[256,1280]{1,0:T(8,128)}, u32[]{:S(2)}) copy-start(f32[256,1280]{1,0:T(8,128)} %copy-done.10) | copy-start | bytes 3932164
  1063.6 118.3 %copy-start.64 = (f32[256]{0:T(256)S(1)}, f32[256]{0:T(256)}, u32[]{:S(2)}) copy-start(f32[256]{0:T(256)} %get-tuple-element.66) | copy-start | bytes 3076
  (61 other events, 279.5 us)
Sparse Core Ops, SparseCore 0:
  9.9 47.6 all-gather.10
  59.4 44.9 all-gather.12
  106.2 44.9 all-gather.8
  152.9 44.9 all-gather.14
  373.9 37.1 all-gather.16
  412.8 36.7 all-gather.18
  532.2 37.1 all-gather.20
  575.1 36.8 reduce-scatter.21
  655.1 37.2 reduce-scatter.23
  695.8 36.8 reduce-scatter.25
  814.6 42.9 reduce-scatter.19
  860.5 44.9 reduce-scatter.17
  908.5 44.9 reduce-scatter.13
  956.4 44.9 reduce-scatter.15
  1004.3 56.4 reduce-scatter.31
  1063.7 55.8 reduce-scatter.27
  1122.5 55.8 reduce-scatter.29
  1181.6 24.4 reduce-scatter.33
  1209.1 112.8 all-reduce.9
where the time goes:
time: 1350 us; the launch traced here: 1340 us
  waiting for transfers between devices  790 us (59%)
  local copies, waits for them, and re-layouts  200 us (15%)
  matrix products  168 us (12%)
  other arithmetic  81.8 us (6%)
  blocking collectives  59.2 us (4%)
  starting transfers between devices  20.6 us (2%)
  between operations  19.5 us (1%)
    psum x1, waiting for transfers between devices, body(): lax.psum(partial_shares[0].astype(jnp.bfloat16), 'expert')  83.8 us
    all_to_all x1, waiting for transfers between devices, body(): lax.all_to_all(send_grad, 'expert', split_axis=1, concat_axis=1, tiled=True)  80.6 us
    all_to_all x1, waiting for transfers between devices, body(): lax.all_to_all(expert_in_grad, 'expert', split_axis=1, concat_axis=1, til...  64.1 us
    dot_general x22, matrix products, product(): return jnp.dot(first_arg, second_arg, preferred_element_type=jnp.float32)  62.4 us
    reduce_scatter x1, waiting for transfers between devices, body(): lax.psum_scatter(expert_gate_part.astype(jnp.bfloat16), 'dp', scatter_dim...  56 us
    reduce_scatter x1, waiting for transfers between devices, body(): lax.psum_scatter(expert_up_part.astype(jnp.bfloat16), 'dp', scatter_dimen...  56 us
    reduce_scatter x1, waiting for transfers between devices, body(): lax.psum_scatter(dense_grads[0].astype(jnp.bfloat16), 'dp', scatter_dimen...  48 us
    reduce_scatter x1, waiting for transfers between devices, body(): lax.psum_scatter(dense_grads[1].astype(jnp.bfloat16), 'dp', scatter_dimen...  47.9 us
  transfers between devices with their start and end apart: 23, of which 17 were waited for; matrix products, arithmetic and copies ran while one was open for 29% of the time, Pallas kernels for 0%

commit v1 on v0

v1 whole, which is shorter than its diff:
```python
import jax
import jax.numpy as jnp
from jax import lax
from jax.sharding import PartitionSpec as P

HEAD_DIM = 128
TOP = 7
EXP_DEV = 2
BF = jnp.bfloat16


def product(first_arg, second_arg):
    return jnp.dot(first_arg, second_arg, preferred_element_type=jnp.float32)


def product_high(first_arg, second_arg):
    return jnp.dot(
        first_arg, second_arg, precision=lax.Precision.HIGHEST, preferred_element_type=jnp.float32
    )


def rotary_tables(length, head_size):
    half_dim = head_size // 2
    frequency = 10000.0 ** (-jnp.arange(half_dim, dtype=jnp.float32) * 2.0 / head_size)
    angles = jnp.arange(length, dtype=jnp.float32)[:, None] * frequency[None, :]
    return (jnp.cos(angles), jnp.sin(angles))


def rotate(tensor, cosine, sine_part):
    half_dim = tensor.shape[-1] // 2
    first_half = tensor[..., :half_dim]
    second_half = tensor[..., half_dim:]
    cos_rows = cosine[:, None, :]
    sin_rows = sine_part[:, None, :]
    return jnp.concatenate(
        [
            first_half * cos_rows - second_half * sin_rows,
            first_half * sin_rows + second_half * cos_rows,
        ],
        axis=-1,
    )


def allowed_mask(length, piece_start, piece_len):
    row_index = jnp.arange(length, dtype=jnp.int32)[:, None]
    col_index = jnp.arange(length, dtype=jnp.int32)[None, :]
    row_inside = (row_index >= piece_start) & (row_index < piece_start + piece_len)
    col_inside = (col_index >= piece_start) & (col_index < piece_start + piece_len)
    return (col_index <= row_index) | row_inside & col_inside


def silu_grad(inputs):
    sigmoid_part = jax.nn.sigmoid(inputs)
    return sigmoid_part * (1.0 + inputs * (1.0 - sigmoid_part))


def high_low(values):
    high = values.astype(BF)
    low = (values - high.astype(jnp.float32)).astype(BF)
    return high, low


def body(
    tokens,
    query_weight,
    key_weight,
    value_weight,
    output_weight,
    attn_gain,
    ffn_gain,
    router_weight,
    shared_gate,
    shared_up,
    shared_down,
    expert_gate,
    expert_up,
    expert_down,
    expert_ids,
    piece_starts,
    out_grad,
):
    dp = lax.axis_size("dp")
    owners = lax.axis_size("expert")
    me = lax.axis_index("expert")
    experts = EXP_DEV * owners
    length, width = tokens.shape
    rows = query_weight.shape[0]
    hidden = shared_gate.shape[1]
    head_count = width // HEAD_DIM
    score_scale = HEAD_DIM ** (-0.5)
    piece_len = min(256, length // 2)
    capacity = 8 * length // experts

    chosen = (expert_ids[:, :, None] == jnp.arange(experts, dtype=jnp.int32)).any(axis=1)
    chosen_low = jnp.pad(chosen.astype(BF), ((0, 0), (0, 128 - experts)))
    grads_all = lax.all_gather(
        jnp.concatenate([out_grad, chosen_low], axis=1), "expert", axis=0, tiled=True
    ).reshape(owners, length, width + 128)

    small = jnp.concatenate(
        [router_weight, attn_gain[:, None], ffn_gain[:, None]], axis=1
    )
    small = jnp.pad(small, ((0, 0), (0, 128 - small.shape[1])))
    first_full = lax.all_gather(
        jnp.concatenate([query_weight, key_weight, value_weight, small], axis=1),
        "dp", axis=0, tiled=True,
    )
    second_full = lax.all_gather(
        jnp.concatenate(
            [output_weight, shared_gate, shared_up, shared_down.reshape(rows, -1)], axis=1
        ),
        "dp", axis=0, tiled=True,
    )
    query_full = first_full[:, :width]
    key_full = first_full[:, width : 2 * width]
    value_full = first_full[:, 2 * width : 3 * width]
    small_full = first_full[:, 3 * width :]
    router_full = small_full[:, :experts]
    gain_one_f = small_full[:, experts].astype(jnp.float32)
    gain_two_f = small_full[:, experts + 1].astype(jnp.float32)
    output_full = second_full[:, :width]
    shared_gate_full = second_full[:, width : width + hidden]
    shared_up_full = second_full[:, width + hidden : width + 2 * hidden]
    shared_down_full = second_full[:, width + 2 * hidden :].reshape(hidden, width)

    token_f = tokens.astype(jnp.float32)
    norm_one = lax.rsqrt(jnp.mean(token_f * token_f, axis=-1, keepdims=True) + 1e-06)
    attn_in = (token_f * norm_one * gain_one_f).astype(BF)
    cosine, sine_part = rotary_tables(length, HEAD_DIM)
    query_pre = product(attn_in, query_full).reshape(length, head_count, HEAD_DIM)
    key_pre = product(attn_in, key_full).reshape(length, head_count, HEAD_DIM)
    query_rot = rotate(query_pre, cosine, sine_part).astype(BF)
    key_rot = rotate(key_pre, cosine, sine_part).astype(BF)
    values = product(attn_in, value_full).astype(BF).reshape(length, head_count, HEAD_DIM)
    allowed = allowed_mask(length, piece_starts[0], piece_len)
    scores = (
        jnp.einsum("qhd,khd->hqk", query_rot, key_rot, preferred_element_type=jnp.float32)
        * score_scale
    )
    scores = jnp.where(allowed[None], scores, -1e30)
    row_max = jnp.max(scores, axis=-1, keepdims=True)
    exps = jnp.exp(scores - row_max)
    attn_probs = exps / jnp.sum(exps, axis=-1, keepdims=True)
    probs_low = attn_probs.astype(BF)
    context = jnp.einsum("hqk,khd->qhd", probs_low, values, preferred_element_type=jnp.float32)
    context = context.astype(BF).reshape(length, width)
    attn_out = product(context, output_full)
    residual = token_f + attn_out
    norm_two = lax.rsqrt(jnp.mean(residual * residual, axis=-1, keepdims=True) + 1e-06)
    ffn_in = (residual * norm_two * gain_two_f).astype(BF)
    router_probs = jax.nn.softmax(product(ffn_in, router_full), axis=-1)
    gates = jnp.where(chosen, router_probs, 0.0)
    gates_high, gates_low = high_low(gates)
    sent = jnp.concatenate(
        [ffn_in, gates_high, gates_low, jnp.zeros((length, 128 - 2 * experts), BF)], axis=1
    )
    rows_all = lax.all_gather(sent, "expert", axis=0, tiled=True).reshape(
        owners, length, width + 128
    )

    grad_f = out_grad.astype(jnp.float32)
    shared_gate_act = product(ffn_in, shared_gate_full)
    shared_up_act = product(ffn_in, shared_up_full)
    shared_hidden = (jax.nn.silu(shared_gate_act) * shared_up_act).astype(BF)
    shared_out = product(shared_hidden, shared_down_full)
    shared_hidden_grad = product(out_grad, shared_down_full.T)
    shared_down_grad = product(shared_hidden.T, out_grad)
    shared_gate_act_grad = (shared_hidden_grad * shared_up_act * silu_grad(shared_gate_act)).astype(
        BF
    )
    shared_up_act_grad = (shared_hidden_grad * jax.nn.silu(shared_gate_act)).astype(BF)
    shared_gate_grad = product(ffn_in.T, shared_gate_act_grad)
    shared_up_grad = product(ffn_in.T, shared_up_act_grad)
    shared_in_grad = product(shared_gate_act_grad, shared_gate_full.T) + product(
        shared_up_act_grad, shared_up_full.T
    )
    shared_parts = jnp.concatenate(
        [
            shared_gate_grad.astype(BF),
            shared_up_grad.astype(BF),
            shared_down_grad.astype(BF).reshape(dp * rows, -1),
        ],
        axis=1,
    )
    shared_share = lax.psum_scatter(shared_parts, "dp", scatter_dimension=0, tiled=True)

    own = me * EXP_DEV + jnp.arange(EXP_DEV)
    own_hot = (own[:, None] == jnp.arange(experts)[None, :]).astype(jnp.float32)
    mask = jnp.einsum("ste,oe->ost", grads_all[:, :, width : width + experts].astype(jnp.float32), own_hot)
    slot = jnp.cumsum(mask, axis=2) - 1.0
    spread = (
        (slot[:, :, None, :] == jnp.arange(capacity, dtype=jnp.float32)[None, None, :, None])
        & (mask[:, :, None, :] > 0)
    ).astype(BF)
    gates_pair = (
        rows_all[:, :, width : width + experts].astype(jnp.float32)
        + rows_all[:, :, width + experts : width + 2 * experts].astype(jnp.float32)
    )
    gates_own = jnp.einsum("ste,oe->ost", gates_pair, own_hot, precision=lax.Precision.HIGHEST)
    slot_gates = jnp.einsum(
        "osct,ost->osc", spread.astype(jnp.float32), gates_own, precision=lax.Precision.HIGHEST
    )
    take = lambda source: jnp.einsum(
        "osct,std->oscd", spread, source, preferred_element_type=jnp.float32
    ).astype(BF)
    expert_in = take(rows_all[:, :, :width]).reshape(EXP_DEV, owners * capacity, width)
    slot_out_grad = take(grads_all[:, :, :width])
    res_grad = (slot_gates[..., None] * slot_out_grad.astype(jnp.float32)).astype(BF)
    res_grad = res_grad.reshape(EXP_DEV, owners * capacity, width)
    mm = lambda spec, a, b: jnp.einsum(spec, a, b, preferred_element_type=jnp.float32)
    routed_gate = mm("erd,edf->erf", expert_in, expert_gate)
    routed_up = mm("erd,edf->erf", expert_in, expert_up)
    routed_hidden = (jax.nn.silu(routed_gate) * routed_up).astype(BF)
    hidden_grad = mm("erd,efd->erf", res_grad, expert_down)
    routed_gate_grad = (hidden_grad * routed_up * silu_grad(routed_gate)).astype(BF)
    routed_up_grad = (hidden_grad * jax.nn.silu(routed_gate)).astype(BF)
    expert_in_grad = (
        mm("erf,edf->erd", routed_gate_grad, expert_gate)
        + mm("erf,edf->erd", routed_up_grad, expert_up)
    ).astype(BF).reshape(EXP_DEV, owners, capacity, width)
    routed_res = mm("erf,efd->erd", routed_hidden, expert_down).astype(BF)
    routed_res = routed_res.reshape(EXP_DEV, owners, capacity, width)
    slot_gate_grad = jnp.sum(
        routed_res.astype(jnp.float32) * slot_out_grad.astype(jnp.float32), axis=-1
    )
    token_gate_grad = jnp.einsum(
        "osct,osc,oe->ste", spread.astype(jnp.float32), slot_gate_grad, own_hot,
        precision=lax.Precision.HIGHEST,
    )
    gg_high, gg_low = high_low(token_gate_grad)
    in_grad_part = mm("osct,oscd->std", spread, expert_in_grad).astype(BF)
    back = jnp.concatenate(
        [in_grad_part, gg_high, gg_low, jnp.zeros((owners, length, 128 - 2 * experts), BF)], axis=2
    ).reshape(owners * length, width + 128)
    back = lax.psum_scatter(back, "expert", scatter_dimension=0, tiled=True)
    out_part = mm(
        "osct,oscd->std", (spread.astype(jnp.float32) * slot_gates[..., None]).astype(BF), routed_res
    ).astype(BF)
    expert_down_part = mm("erf,erd->efd", routed_hidden, res_grad).astype(BF)
    expert_gate_part = mm("erd,erf->edf", expert_in, routed_gate_grad).astype(BF)
    expert_up_part = mm("erd,erf->edf", expert_in, routed_up_grad).astype(BF)
    expert_parts = jnp.concatenate(
        [
            expert_gate_part.reshape(EXP_DEV, dp, rows, hidden),
            expert_up_part.reshape(EXP_DEV, dp, rows, hidden),
            expert_down_part.reshape(EXP_DEV, dp, rows, hidden),
        ],
        axis=0,
    ).transpose(1, 0, 2, 3)
    expert_share = lax.psum_scatter(expert_parts, "dp", scatter_dimension=0, tiled=True)[0]
    expert_share = expert_share.astype(jnp.float32)
    out_sum = lax.psum_scatter(
        out_part.reshape(owners * length, width), "expert", scatter_dimension=0, tiled=True
    )

    routed_in_grad = back[:, :width].astype(jnp.float32)
    probs_grad = back[:, width : width + experts].astype(jnp.float32) + back[
        :, width + experts : width + 2 * experts
    ].astype(jnp.float32)
    logits_grad = router_probs * (
        probs_grad - jnp.sum(router_probs * probs_grad, axis=-1, keepdims=True)
    )
    router_grad = product_high(ffn_in.astype(jnp.float32).T, logits_grad)
    router_in_grad = product_high(logits_grad, router_full.astype(jnp.float32).T)
    ffn_in_grad = shared_in_grad + routed_in_grad + router_in_grad
    ffn_gain_grad = jnp.sum(ffn_in_grad * residual * norm_two, axis=0)
    upstream_two = ffn_in_grad * gain_two_f
    residual_grad = (
        grad_f
        + norm_two * upstream_two
        - residual * norm_two**3 * jnp.mean(upstream_two * residual, axis=-1, keepdims=True)
    )
    attn_out_grad = residual_grad.astype(BF)
    output_grad = product(context.T, attn_out_grad)
    context_grad = (
        product(attn_out_grad, output_full.T).astype(BF).reshape(length, head_count, HEAD_DIM)
    )
    value_grad = mm("hqk,qhd->khd", probs_low, context_grad).astype(BF).reshape(length, width)
    probs_grad_att = mm("qhd,khd->hqk", context_grad, values)
    row_delta = jnp.sum(attn_probs * probs_grad_att, axis=-1, keepdims=True)
    scores_grad = (attn_probs * (probs_grad_att - row_delta)).astype(BF)
    query_grad = mm("hqk,khd->qhd", scores_grad, key_rot) * score_scale
    key_grad = mm("hqk,qhd->khd", scores_grad, query_rot) * score_scale
    query_pre_grad = rotate(query_grad, cosine, -sine_part).astype(BF).reshape(length, width)
    key_pre_grad = rotate(key_grad, cosine, -sine_part).astype(BF).reshape(length, width)
    query_wgrad = product(attn_in.T, query_pre_grad)
    key_wgrad = product(attn_in.T, key_pre_grad)
    value_wgrad = product(attn_in.T, value_grad)
    attn_in_grad = (
        product(query_pre_grad, query_full.T)
        + product(key_pre_grad, key_full.T)
        + product(value_grad, value_full.T)
    )
    attn_gain_grad = jnp.sum(attn_in_grad * token_f * norm_one, axis=0)
    upstream_one = attn_in_grad * gain_one_f
    tokens_grad = (
        residual_grad
        + norm_one * upstream_one
        - token_f * norm_one**3 * jnp.mean(upstream_one * token_f, axis=-1, keepdims=True)
    )
    small_grads = jnp.concatenate(
        [router_grad, attn_gain_grad[:, None], ffn_gain_grad[:, None]], axis=1
    ).astype(BF)
    small_grads = jnp.pad(small_grads, ((0, 0), (0, 128 - small_grads.shape[1])))
    attn_parts = jnp.concatenate(
        [
            query_wgrad.astype(BF),
            key_wgrad.astype(BF),
            value_wgrad.astype(BF),
            output_grad.astype(BF),
            small_grads,
        ],
        axis=1,
    )
    attn_share = lax.psum_scatter(attn_parts, "dp", scatter_dimension=0, tiled=True)
    shared_share = lax.psum(shared_share, "expert").astype(jnp.float32)
    attn_share = lax.psum(attn_share, "expert").astype(jnp.float32)

    moe_out = shared_out + out_sum.astype(jnp.float32)
    stream_out = residual + moe_out
    stat_rms = jnp.stack(
        [
            jnp.sqrt(jnp.mean(attn_out * attn_out)),
            jnp.sqrt(jnp.mean(moe_out * moe_out)),
            jnp.sqrt(jnp.mean(stream_out * stream_out)),
        ]
    )[None, :]
    return (
        stream_out.astype(BF),
        tokens_grad.astype(BF),
        attn_share[:, :width],
        attn_share[:, width : 2 * width],
        attn_share[:, 2 * width : 3 * width],
        attn_share[:, 3 * width : 4 * width],
        attn_share[:, 4 * width + experts],
        attn_share[:, 4 * width + experts + 1],
        attn_share[:, 4 * width : 4 * width + experts],
        shared_share[:, :hidden],
        shared_share[:, hidden : 2 * hidden],
        shared_share[:, 2 * hidden :].reshape(shared_down.shape),
        expert_share[0:2],
        expert_share[2:4],
        expert_share[4:6].reshape(EXP_DEV, shared_down.shape[0], width),
        stat_rms,
    )


def solution(mesh):
    in_specs = (
        P(("dp", "expert"), None),
        P("dp", None),
        P("dp", None),
        P("dp", None),
        P("dp", None),
        P("dp"),
        P("dp"),
        P("dp", None),
        P("dp", None),
        P("dp", None),
        P("dp", None),
        P("expert", None, None),
        P("expert", None, None),
        P("expert", None, None),
        P(("dp", "expert"), None),
        P(("dp", "expert")),
        P(("dp", "expert"), None),
    )
    out_specs = (
        P(("dp", "expert"), None),
        P(("dp", "expert"), None),
        P("dp", None),
        P("dp", None),
        P("dp", None),
        P("dp", None),
        P("dp"),
        P("dp"),
        P("dp", None),
        P("dp", None),
        P("dp", None),
        P("dp", None),
        P("expert", "dp", None),
        P("expert", "dp", None),
        P("expert", "dp", None),
        P(("dp", "expert"), None),
    )
    return jax.shard_map(body, mesh=mesh, in_specs=in_specs, out_specs=out_specs, check_vma=False)
```

time: 1350 us -> 1120 us (0.83)
  waiting for transfers between devices: 790 us -> 677 us
  blocking collectives: 59.2 us -> 0 us
  other arithmetic: 81.8 us -> 43.5 us
  local copies, waits for them, and re-layouts: 200 us -> 170 us
  matrix products: 168 us -> 195 us
  starting transfers between devices: 20.6 us -> 1.24 us
    all_to_all x4 -> x0, waiting for transfers between devices: 231 us -> none  [the longest x1 80.6 us: body(): lax.all_to_all(send_grad, 'expert', split_axis=1, concat_axis=1, tiled=True)]
    reduce_scatter x10 -> x2, waiting for transfers between devices: 278 us -> 59.7 us  [the longest x1 55.2 us: body(): lax.psum_scatter(out_part.reshape(owners * length, width), 'expert', scat...]
    unnamed x20 -> x13, waiting for transfers between devices: 27.4 us -> 213 us
    all_gather x7 -> x4, waiting for transfers between devices: 169 us -> 279 us  [the longest x1 96.2 us: body(): lax.all_gather(jnp.concatenate([query_weight, key_weight, value_weight, s...]
    unnamed x155 -> x161, local copies, waits for them, and re-layouts: 19.6 us -> 83.6 us
    psum x1, waiting for transfers between devices: 83.8 us -> 126 us  [body(): shared_share = lax.psum(shared_share, 'expert').astype(jnp.float32)]
    gather x7 -> x0, local copies, waits for them, and re-layouts: 41.8 us -> none  [the longest x5 14.7 us: body(): gate_values = jnp.take_along_axis(router_probs, expert_ids, axis=1)]
    convert_element_type x6, local copies, waits for them, and re-layouts: 41.8 us -> 7.26 us  [the longest x1 2.74 us: body(): (slot_gates[..., None] * slot_out_grad.astype(jnp.float32)).astype(BF)]
  transfers between devices with their start and end apart: 23 -> 10, of which waited for: 17 -> 9; matrix products, arithmetic and copies ran while one was open for 29% -> 22% of each run, Pallas kernels for 0% -> 0%
where the time goes in v1:
time: 1120 us; the launch traced here: 1110 us
  waiting for transfers between devices  677 us (60%)
  matrix products  195 us (17%)
  local copies, waits for them, and re-layouts  170 us (15%)
  other arithmetic  43.5 us (4%)
  between operations  18.3 us (2%)
    unnamed x13, waiting for transfers between devices  213 us
    psum x1, waiting for transfers between devices, body(): shared_share = lax.psum(shared_share, 'expert').astype(jnp.float32)  126 us
    dot_general x15, matrix products, body(): jnp.einsum(spec, a, b, preferred_element_type=jnp.float32)  106 us
    all_gather x1, waiting for transfers between devices, body(): lax.all_gather(jnp.concatenate([query_weight, key_weight, value_weight, s...  96.2 us
    unnamed x161, local copies, waits for them, and re-layouts  83.6 us
    all_gather x1, waiting for transfers between devices, body(): lax.all_gather(jnp.concatenate([output_weight, shared_gate, shared_up, sh...  69.7 us
    dot_general x22, matrix products, product(): return jnp.dot(first_arg, second_arg, preferred_element_type=jnp.float32)  64 us
    all_gather x1, waiting for transfers between devices, body(): lax.all_gather(sent, 'expert', axis=0, tiled=True)  58.7 us
  transfers between devices with their start and end apart: 10, of which 9 were waited for; matrix products, arithmetic and copies ran while one was open for 22% of the time, Pallas kernels for 0%

profile of v1, /device:TPU:0, one launch (start us, length us, event | category | flops | bytes accessed | tf_op | source)
XLA Modules:
  0.0 1105.5 jit_solution(541754291438317677)
XLA Ops:
  21.2 96.2 %all-gather.5.cloned.1.call-done = bf16[1280,3968]{1,0:T(8,128)(2,1)} async-done(((bf16[320,3968]{1,0:T(8,128)(2,1)}), bf16[1280,3968]{1,0:T(8,128)(2,1)}) %all-gather.5.cloned.1.call-update) | async-done | bytes 10158096 | tf_op jit(solution)/shard_map/all_gather | solution.py:104
  151.9 69.7 %all-gather.7.cloned.1.call-done = bf16[1280,3968]{1,0:T(8,128)(2,1)} async-done(((bf16[320,3968]{1,0:T(8,128)(2,1)}), bf16[1280,3968]{1,0:T(8,128)(2,1)}) %all-gather.7.cloned.1.call-update) | async-done | bytes 10158096 | tf_op jit(solution)/shard_map/all_gather | solution.py:108
  230.1 54.0 %all-gather.9.cloned.1.call-done = bf16[2048,1408]{1,0:T(8,128)(2,1)} async-done(((bf16[256,1408]{1,0:T(8,128)(2,1)}), bf16[2048,1408]{1,0:T(8,128)(2,1)}) %all-gather.9.cloned.1.call-update) | async-done | bytes 5767184 | tf_op jit(solution)/shard_map/all_gather | solution.py:96
  286.9 58.7 %all-gather.11.cloned.1.call-done = bf16[2048,1408]{0,1:T(8,128)(2,1)} async-done(((bf16[256,1408]{0,1:T(8,128)(2,1)}), bf16[2048,1408]{0,1:T(8,128)(2,1)}) %all-gather.11.cloned.1.call-update) | async-done | bytes 5767184 | tf_op jit(solution)/shard_map/all_gather | solution.py:157
  345.7 5.1 copy.343
  356.1 5.1 fusion.1
  364.0 8.6 copy.341
  377.7 11.8 %fusion.136 = f32[2,1024,896]{2,1,0:T(8,128)} fusion(bf16[2,1024,1280]{2,1,0:T(8,128)(2,1)S(1)} %bitcast.159, bf16[2,1280,896]{2,1,0:T(8,128)(2,1)} %param.28), kind=kOutput, calls=%fused_computation.225 | convolution fusion | flops 4697620480 | bytes 17170432 | tf_op jit(solution)/shard_map/erd,edf->erf/dot_general | solution.py:210
  389.6 7.6 fusion.137
  397.2 14.7 %multiply_convert_fusion = (bf16[2,1024,896]{2,1,0:T(8,128)(2,1)}, bf16[2,1024,896]{2,1,0:T(8,128)(2,1)}, bf16[2,1024,896]{2,1,0:T(8,128)(2,1)}) fusion(f32[2,1024,896]{2,1,0:T(8,128)} %fusion.136, f32[2,1024,896]{2,1,0:T(8,128)} %fusion.137, bf16[2,1024,1280]{2,1,0:T(8,128)(2,1)} %bitcast.163, bf16[2,896,1280]{2,1,0:T(8,128)(2,1)S(1)} %bitcast.194), kind=kOutput, calls=%fused_computation.18 | convolution fusion | flops 4725145600 | bytes 35520512 | tf_op jit(solution)/shard_map/erd,efd->erf/dot_general | solution.py:210
  412.0 7.5 convolution_convert_fusion.5
  425.1 11.4 %fusion.138 = f32[2,1024,1280]{2,1,0:T(8,128)} fusion(bf16[2,1024,896]{2,1,0:T(8,128)(2,1)} %get-tuple-element.115, bf16[2,1280,896]{2,1,0:T(8,128)(2,1)} %param.28), kind=kOutput, calls=%fused_computation.227 | convolution fusion | flops 4697620480 | bytes 18743296 | tf_op jit(solution)/shard_map/erf,edf->erd/dot_general | solution.py:210
  436.5 9.9 add_convert_fusion
  450.5 10.0 concatenate.54
  460.5 8.2 copy.328
  468.7 5.2 bitcast_convert_fusion.1
  473.9 7.9 copy.327
  506.9 5.6 pad_maximum_fusion.1
  512.6 10.0 copy.332
  537.1 55.2 %reduce-scatter.12.cloned.1.call-done = bf16[256,1280]{0,1:T(8,128)(2,1)} async-done(((bf16[2048,1280]{0,1:T(8,128)(2,1)}), bf16[256,1280]{0,1:T(8,128)(2,1)}) %reduce-scatter.12.cloned.1.call-update) | async-done | bytes 655376 | tf_op jit(solution)/shard_map/reduce_scatter | solution.py:252
  592.3 4.9 multiply_reduce_fusion.2
  638.7 18.6 %copy.330 = bf16[1280,5248]{1,0:T(8,128)(2,1)} copy(bf16[1280,5248]{0,1:T(8,128)(2,1)} %fusion.84) | data formatting | bytes 26869760
  657.3 10.8 convolution_convert_fusion.7
  668.1 9.1 reshape.335
  677.2 10.0 convolution_convert_fusion.9
  687.2 8.4 convolution_convert_fusion.8
  695.7 6.9 copy_bitcast_fusion
  707.0 92.5 %reduce-scatter.16.cloned.1.call-done = bf16[320,5248]{1,0:T(8,128)(2,1)} async-done(((bf16[1280,5248]{1,0:T(8,128)(2,1)}), bf16[320,5248]{1,0:T(8,128)(2,1)}) %reduce-scatter.16.cloned.1.call-update) | async-done | bytes 3358736
  799.5 6.1 copy.331
  812.3 120.6 %reduce-scatter.20.cloned.1.call-done = bf16[1,6,320,896]{3,2,1,0:T(8,128)(2,1)} async-done(((bf16[4,6,320,896]{3,2,1,0:T(8,128)(2,1)}), bf16[1,6,320,896]{3,2,1,0:T(8,128)(2,1)}) %reduce-scatter.20.cloned.1.call-update) | async-done | bytes 3440656
  941.7 125.9 %all-reduce.7.cloned.1.call-done = (bf16[320,2688]{0,1:T(8,128)(2,1)}, bf16[320,5248]{0,1:T(8,128)(2,1)}) async-done(((bf16[320,2688]{0,1:T(8,128)(2,1)}, bf16[320,5248]{0,1:T(8,128)(2,1)}), (bf16[320,2688]{0,1:T(8,128)(2,1)}, bf16[320,5248]{0,1:T(8,128)(2,1)})) %all-reduce.7.cloned.1.call-update) | async-done | bytes 5079056 | tf_op jit(solution)/shard_map/psum | solution.py:316
  1067.6 5.0 fusion.130
  (298 shorter events, 205.9 us)
Async XLA Ops:
  7.2 110.3 %all-gather.5.cloned.1.call-start = ((), (), s32[]{:S(2)}) async-start(), calls=%async_computation.5 | async-start | bytes 12697600 | tf_op jit(solution)/shard_map/all_gather | solution.py:104
  12.4 209.2 %all-gather.7.cloned.1.call-start = ((), (), s32[]{:S(2)}) async-start(), calls=%async_computation.6 | async-start | bytes 12697600 | tf_op jit(solution)/shard_map/all_gather | solution.py:108
  15.5 268.7 %all-gather.9.cloned.1.call-start = ((), (), s32[]{:S(2)}) async-start(), calls=%async_computation.7 | async-start | bytes 6488064 | tf_op jit(solution)/shard_map/all_gather | solution.py:96
  17.5 328.2 %all-gather.11.cloned.1.call-start = ((), (), s32[]{:S(2)}) async-start(), calls=%async_computation.8 | async-start | bytes 6488064 | tf_op jit(solution)/shard_map/all_gather | solution.py:157
  17.8 208.1 %copy-start.3 = (bf16[256,1280]{0,1:T(8,128)(2,1)}, bf16[256,1280]{0,1:T(8,128)(2,1)S(1)}, u32[]{:S(2)}) copy-start(bf16[256,1280]{0,1:T(8,128)(2,1)S(1)} %copy.227) | copy-start | bytes 1966084
  19.3 103.2 %copy-start.53 = (f32[256]{0:T(256)}, f32[256]{0:T(256)S(1)}, u32[]{:S(2)}) copy-start(f32[256]{0:T(256)S(1)} %get-tuple-element.151) | copy-start | bytes 3076
  21.2 120.9 %copy-start.24 = (f32[256,64]{1,0:T(8,128)}, f32[256,64]{1,0:T(8,128)S(1)}, u32[]{:S(2)}) copy-start(f32[256,64]{1,0:T(8,128)S(1)} %get-tuple-element.156) | copy-start | bytes 196612
  119.0 107.7 %copy-start.42 = (f32[1280]{0:T(1024)}, f32[1280]{0:T(1024)S(1)}, u32[]{:S(2)}) copy-start(f32[1280]{0:T(1024)S(1)} %get-tuple-element.96) | copy-start | bytes 15364
  229.9 301.9 %reduce-scatter.14.cloned.1.call-start = ((), (), s32[]{:S(2)}) async-start(), calls=%async_computation.10 | async-start | bytes 6488064 | tf_op jit(solution)/shard_map/reduce_scatter | solution.py:235
  377.2 12.4 %slice-start.12 = ((s8[4587520]{0:T(1024)(128)(4,1)}), s8[393216]{0:T(1024)(128)(4,1)S(1)}, s32[]{:S(2)}) async-start(s8[4587520]{0:T(1024)(128)(4,1)} %bitcast.195), calls=%async_computation.27 | async-start | bytes 786432
  377.7 11.9 %copy-start.12 = (bf16[2,8,128,1280]{3,2,1,0:T(8,128)(2,1)}, bf16[2,8,128,1280]{3,2,1,0:T(8,128)(2,1)S(1)}, u32[]{:S(2)}) copy-start(bf16[2,8,128,1280]{3,2,1,0:T(8,128)(2,1)S(1)} %copy.246) | copy-start | bytes 15728644
  377.7 11.9 %slice-start.13 = ((s8[4587520]{0:T(1024)(128)(4,1)}), s8[4194304]{0:T(1024)(128)(4,1)S(1)}, s32[]{:S(2)}) async-start(s8[4587520]{0:T(1024)(128)(4,1)} %bitcast.195), calls=%async_computation.28 | async-start | bytes 8388608
  377.7 19.5 %slice-start.10 = ((s8[4587520]{0:T(1024)(128)(4,1)}), s8[4194304]{0:T(1024)(128)(4,1)S(1)}, s32[]{:S(2)}) async-start(s8[4587520]{0:T(1024)(128)(4,1)} %bitcast.193), calls=%async_computation.25 | async-start | bytes 8388608
  389.6 7.7 slice-start.11
  412.0 7.5 slice-start.3
  412.0 7.5 slice-start.4
  425.1 11.4 %copy-start.55 = (bf16[2,1024,896]{2,1,0:T(8,128)(2,1)S(1)}, bf16[2,1024,896]{2,1,0:T(8,128)(2,1)}, u32[]{:S(2)}) copy-start(bf16[2,1024,896]{2,1,0:T(8,128)(2,1)} %get-tuple-element.114) | copy-start | bytes 11010052
  468.7 123.6 %reduce-scatter.12.cloned.1.call-start = ((), (), s32[]{:S(2)}) async-start(), calls=%async_computation.9 | async-start | bytes 5898240 | tf_op jit(solution)/shard_map/reduce_scatter | solution.py:252
  481.9 221.1 %reduce-scatter.18.cloned.1.call-start = ((), (), s32[]{:S(2)}) async-start(), calls=%async_computation.12 | async-start | bytes 8601600
  522.6 276.9 %reduce-scatter.16.cloned.1.call-start = ((), (), s32[]{:S(2)}) async-start(), calls=%async_computation.11 | async-start | bytes 16793600
  535.2 57.0 %copy-start.2 = (f32[256,1280]{0,1:T(8,128)S(1)}, f32[256,1280]{0,1:T(8,128)}, u32[]{:S(2)}) copy-start(f32[256,1280]{0,1:T(8,128)} %copy-done.1) | copy-start | bytes 3932164
  535.3 57.0 %copy-start.43 = (f32[1280]{0:T(1024)S(1)}, f32[1280]{0:T(1024)}, u32[]{:S(2)}) copy-start(f32[1280]{0:T(1024)} %copy-done.42) | copy-start | bytes 15364
  535.3 57.0 %copy-start.49 = (f32[256]{0:T(256)S(1)}, f32[256]{0:T(256)}, u32[]{:S(2)}) copy-start(f32[256]{0:T(256)} %copy-done.48) | copy-start | bytes 3076
  537.1 60.1 %copy-start.11 = (f32[256,1280]{0,1:T(8,128)}, f32[256,1280]{0,1:T(8,128)S(1)}, u32[]{:S(2)}) copy-start(f32[256,1280]{0,1:T(8,128)S(1)} %convolution_add_fusion) | copy-start | bytes 3932164
  537.1 60.1 %copy-start.51 = (f32[256]{0:T(256)S(1)}, f32[256]{0:T(256)}, u32[]{:S(2)}) copy-start(f32[256]{0:T(256)} %get-tuple-element.152) | copy-start | bytes 3076
  598.9 5.8 copy-start.28
  614.2 7.5 slice-start.5
  657.3 275.6 %reduce-scatter.20.cloned.1.call-start = ((), (), s32[]{:S(2)}) async-start(), calls=%async_computation.13 | async-start | bytes 17203200
  677.2 10.0 copy-start.56
  677.2 18.4 %slice-start = ((s8[4587520]{0:T(1024)(128)(4,1)}), s8[4194304]{0:T(1024)(128)(4,1)S(1)}, s32[]{:S(2)}) async-start(s8[4587520]{0:T(1024)(128)(4,1)} %bitcast.156), calls=%async_computation.15 | async-start | bytes 8388608
  687.2 8.5 slice-start.1
  702.7 364.9 %all-reduce.7.cloned.1.call-start = ((), (), s32[]{:S(2)}) async-start(), calls=%async_computation.14 | async-start | bytes 12189696 | tf_op jit(solution)/shard_map/psum | solution.py:316
  (49 other events, 130.3 us)
Sparse Core Ops, SparseCore 0:
  12.5 104.9 all-gather.4
  119.3 102.1 all-gather.6
  223.7 60.3 all-gather.8
  286.1 59.4 all-gather.10
  468.8 62.9 reduce-scatter.13
  534.0 58.2 reduce-scatter.11
  595.3 73.4 reduce-scatter.17
  672.0 127.5 reduce-scatter.15
  802.6 130.2 reduce-scatter.19
  935.2 132.3 all-reduce.6

commit v2 on v1

v2 whole, which is shorter than its diff:
```python
import math

import jax
import jax.numpy as jnp
from jax import lax
from jax.sharding import Mesh
from jax.sharding import PartitionSpec as P

HEAD_DIM = 128
TOP = 7
EXP_DEV = 2
BF = jnp.bfloat16
F32 = jnp.float32
DP = ("y", "x")
OWN = ("z", "c")


def product(first_arg, second_arg):
    return jnp.dot(first_arg, second_arg, preferred_element_type=F32)


def product_high(first_arg, second_arg):
    return jnp.dot(
        first_arg, second_arg, precision=lax.Precision.HIGHEST, preferred_element_type=F32
    )


def mm(spec, first_arg, second_arg):
    return jnp.einsum(spec, first_arg, second_arg, preferred_element_type=F32)


def mm_high(spec, *args):
    return jnp.einsum(spec, *args, precision=lax.Precision.HIGHEST, preferred_element_type=F32)


def rotary_tables(length, head_size):
    half_dim = head_size // 2
    frequency = 10000.0 ** (-jnp.arange(half_dim, dtype=F32) * 2.0 / head_size)
    angles = jnp.arange(length, dtype=F32)[:, None] * frequency[None, :]
    return (jnp.cos(angles), jnp.sin(angles))


def rotate(tensor, cosine, sine_part):
    half_dim = tensor.shape[-1] // 2
    first_half = tensor[..., :half_dim]
    second_half = tensor[..., half_dim:]
    cos_rows = cosine[:, None, :]
    sin_rows = sine_part[:, None, :]
    return jnp.concatenate(
        [
            first_half * cos_rows - second_half * sin_rows,
            first_half * sin_rows + second_half * cos_rows,
        ],
        axis=-1,
    )


def allowed_mask(length, piece_start, piece_len):
    row_index = jnp.arange(length, dtype=jnp.int32)[:, None]
    col_index = jnp.arange(length, dtype=jnp.int32)[None, :]
    row_inside = (row_index >= piece_start) & (row_index < piece_start + piece_len)
    col_inside = (col_index >= piece_start) & (col_index < piece_start + piece_len)
    return (col_index <= row_index) | row_inside & col_inside


def silu_grad(inputs):
    sigmoid_part = jax.nn.sigmoid(inputs)
    return sigmoid_part * (1.0 + inputs * (1.0 - sigmoid_part))


def high_low(values):
    high = values.astype(BF)
    low = (values - high.astype(F32)).astype(BF)
    return high, low


def swap(value):
    return lax.ppermute(value, "c", [(0, 1), (1, 0)])


def half(value, index, axis):
    size = value.shape[axis] // 2
    return lax.dynamic_slice_in_dim(value, index * size, size, axis)


def joined(mine, other, core, axis):
    return jnp.where(
        core == 0, jnp.concatenate([mine, other], axis), jnp.concatenate([other, mine], axis)
    )


def body(
    tokens,
    query_weight,
    key_weight,
    value_weight,
    output_weight,
    attn_gain,
    ffn_gain,
    router_weight,
    shared_gate,
    shared_up,
    shared_down,
    expert_gate,
    expert_up,
    expert_down,
    expert_ids,
    piece_starts,
    out_grad,
):
    dp = lax.axis_size(DP)
    owners = lax.axis_size(OWN)
    depth = lax.axis_size("z")
    core, level = lax.axis_index("c"), lax.axis_index("z")
    me = lax.axis_index(OWN)
    experts = EXP_DEV * owners
    length, width = tokens.shape
    rows = query_weight.shape[0]
    hidden = shared_gate.shape[1]
    part = hidden // (2 * dp)
    wide, narrow = width // 2, hidden // 2
    head_count = wide // HEAD_DIM
    score_scale = HEAD_DIM ** (-0.5)
    piece_len = min(256, length // 2)
    capacity = 8 * length // experts
    two = lambda mine: jnp.stack([mine, swap(mine)])

    small = jnp.concatenate([router_weight, attn_gain[:, None], ffn_gain[:, None]], axis=1)
    small = jnp.pad(small, ((0, 0), (0, 128 - small.shape[1])))
    first_full = lax.all_gather(
        jnp.concatenate(
            [half(query_weight, core, 1), half(key_weight, core, 1), half(value_weight, core, 1), small],
            axis=1,
        ),
        DP, axis=0, tiled=True,
    )
    units = lambda weight: lax.dynamic_index_in_dim(
        weight.reshape(rows, dp, 2, part), core, 2, False
    ).reshape(rows, narrow)
    second_full = lax.all_gather(
        jnp.concatenate(
            [
                half(output_weight, core, 1),
                units(shared_gate),
                units(shared_up),
                half(shared_down, core, 0).reshape(rows, narrow),
            ],
            axis=1,
        ),
        DP, axis=0, tiled=True,
    )
    tokens_two = two(tokens)
    starts_two = two(piece_starts[0])
    out_grad_two = two(out_grad)

    chosen = (expert_ids[:, :, None] == jnp.arange(experts, dtype=jnp.int32)).any(axis=1)
    chosen_low = jnp.pad(chosen.astype(BF), ((0, 0), (0, 128 - experts)))
    grads_all = lax.all_gather(
        jnp.concatenate([out_grad, chosen_low], axis=1), OWN, axis=0, tiled=True
    ).reshape(owners, length, width + 128)

    query_half = first_full[:, :wide]
    key_half = first_full[:, wide : 2 * wide]
    value_half = first_full[:, 2 * wide : 3 * wide]
    small_full = first_full[:, 3 * wide :]
    router_full = small_full[:, :experts]
    gain_one_f = small_full[:, experts].astype(F32)
    gain_two_f = small_full[:, experts + 1].astype(F32)
    output_cols = second_full[:, :wide]
    gate_half = second_full[:, wide : wide + narrow]
    up_half = second_full[:, wide + narrow : wide + 2 * narrow]
    down_half = second_full[:, wide + 2 * narrow :].reshape(narrow, width)
    output_half = joined(
        half(output_cols, core, 0), swap(half(output_cols, 1 - core, 0)), core, 1
    )

    token_f = tokens_two.astype(F32)
    norm_one = lax.rsqrt(jnp.mean(token_f * token_f, axis=-1, keepdims=True) + 1e-06)
    attn_in = (token_f * norm_one * gain_one_f).astype(BF).reshape(2 * length, width)
    cosine, sine_part = rotary_tables(length, HEAD_DIM)
    by_head = lambda value: value.reshape(2, length, head_count, HEAD_DIM)
    flat = lambda value: value.reshape(2 * length, wide)
    query_rot = rotate(by_head(product(attn_in, query_half)), cosine, sine_part).astype(BF)
    key_rot = rotate(by_head(product(attn_in, key_half)), cosine, sine_part).astype(BF)
    values = by_head(product(attn_in, value_half).astype(BF))
    allowed = jnp.stack([allowed_mask(length, starts_two[i], piece_len) for i in range(2)])
    scores = mm("sqhd,skhd->shqk", query_rot, key_rot) * score_scale
    scores = jnp.where(allowed[:, None], scores, -1e30)
    row_max = jnp.max(scores, axis=-1, keepdims=True)
    exps = jnp.exp(scores - row_max)
    attn_probs = exps / jnp.sum(exps, axis=-1, keepdims=True)
    probs_low = attn_probs.astype(BF)
    context = flat(mm("shqk,skhd->sqhd", probs_low, values).astype(BF))
    out_partial = product(context, output_half).reshape(2, length, width)
    attn_out = out_partial[0] + swap(out_partial[1].astype(BF)).astype(F32)
    residual = token_f[0] + attn_out
    norm_two = lax.rsqrt(jnp.mean(residual * residual, axis=-1, keepdims=True) + 1e-06)
    ffn_in = (residual * norm_two * gain_two_f).astype(BF)
    router_probs = jax.nn.softmax(product(ffn_in, router_full), axis=-1)
    gates = jnp.where(chosen, router_probs, 0.0)
    gates_high, gates_low = high_low(gates)
    sent = jnp.concatenate(
        [ffn_in, gates_high, gates_low, jnp.zeros((length, 128 - 2 * experts), BF)], axis=1
    )
    rows_all = lax.all_gather(sent, OWN, axis=0, tiled=True).reshape(owners, length, width + 128)

    ffn_two = two(ffn_in).reshape(2 * length, width)
    grad_two = out_grad_two.reshape(2 * length, width)
    shared_gate_act = product(ffn_two, gate_half)
    shared_up_act = product(ffn_two, up_half)
    shared_hidden = (jax.nn.silu(shared_gate_act) * shared_up_act).astype(BF)
    shared_out = product(shared_hidden, down_half).reshape(2, length, width)
    shared_hidden_grad = product(grad_two, down_half.T)
    shared_down_grad = product(shared_hidden.T, grad_two)
    shared_gate_act_grad = (shared_hidden_grad * shared_up_act * silu_grad(shared_gate_act)).astype(
        BF
    )
    shared_up_act_grad = (shared_hidden_grad * jax.nn.silu(shared_gate_act)).astype(BF)
    shared_gate_grad = product(ffn_two.T, shared_gate_act_grad)
    shared_up_grad = product(ffn_two.T, shared_up_act_grad)
    shared_in_grad = (
        product(shared_gate_act_grad, gate_half.T) + product(shared_up_act_grad, up_half.T)
    ).reshape(2, length, width)
    shared_parts = jnp.concatenate(
        [
            shared_gate_grad.astype(BF),
            shared_up_grad.astype(BF),
            shared_down_grad.astype(BF).reshape(dp * rows, narrow),
        ],
        axis=1,
    )
    shared_share = lax.psum_scatter(shared_parts, DP, scatter_dimension=0, tiled=True)

    own = me * EXP_DEV + jnp.arange(EXP_DEV)
    own_hot = (own[:, None] == jnp.arange(experts)[None, :]).astype(F32)
    mask = mm("ste,oe->ost", grads_all[:, :, width : width + experts].astype(F32), own_hot)
    slot = jnp.cumsum(mask, axis=2) - 1.0
    spread = (
        (slot[:, :, None, :] == jnp.arange(capacity, dtype=F32)[None, None, :, None])
        & (mask[:, :, None, :] > 0)
    ).astype(BF)
    gates_pair = rows_all[:, :, width : width + experts].astype(F32) + rows_all[
        :, :, width + experts : width + 2 * experts
    ].astype(F32)
    gates_own = mm_high("ste,oe->ost", gates_pair, own_hot)
    slot_gates = mm_high("osct,ost->osc", spread.astype(F32), gates_own)
    take = lambda source: mm("osct,std->oscd", spread, source).astype(BF)
    expert_in = take(rows_all[:, :, :width]).reshape(EXP_DEV, owners * capacity, width)
    slot_out_grad = take(grads_all[:, :, :width])
    res_grad = (slot_gates[..., None] * slot_out_grad.astype(F32)).astype(BF)
    res_grad = res_grad.reshape(EXP_DEV, owners * capacity, width)
    routed_gate = mm("erd,edf->erf", expert_in, expert_gate)
    routed_up = mm("erd,edf->erf", expert_in, expert_up)
    routed_hidden = (jax.nn.silu(routed_gate) * routed_up).astype(BF)
    hidden_grad = mm("erd,efd->erf", res_grad, expert_down)
    routed_gate_grad = (hidden_grad * routed_up * silu_grad(routed_gate)).astype(BF)
    routed_up_grad = (hidden_grad * jax.nn.silu(routed_gate)).astype(BF)
    expert_in_grad = (
        (
            mm("erf,edf->erd", routed_gate_grad, expert_gate)
            + mm("erf,edf->erd", routed_up_grad, expert_up)
        )
        .astype(BF)
        .reshape(EXP_DEV, owners, capacity, width)
    )
    routed_res = mm("erf,efd->erd", routed_hidden, expert_down).astype(BF)
    routed_res = routed_res.reshape(EXP_DEV, owners, capacity, width)
    slot_gate_grad = jnp.sum(routed_res.astype(F32) * slot_out_grad.astype(F32), axis=-1)
    token_gate_grad = mm_high(
        "osct,osc,oe->ste", spread.astype(F32), slot_gate_grad, own_hot
    )
    gg_high, gg_low = high_low(token_gate_grad)
    seat = jnp.arange(owners)[:, None, None]
    placed = lambda pair: jnp.where(
        seat == me, pair[0][None], jnp.where(seat == me + 1 - 2 * core, pair[1][None], 0.0)
    )
    in_grad_part = (mm("osct,oscd->std", spread, expert_in_grad) + placed(shared_in_grad)).astype(BF)
    back = jnp.concatenate(
        [in_grad_part, gg_high, gg_low, jnp.zeros((owners, length, 128 - 2 * experts), BF)], axis=2
    ).reshape(owners * length, width + 128)
    back = lax.psum_scatter(back, OWN, scatter_dimension=0, tiled=True)

    expert_down_part = mm("erf,erd->efd", routed_hidden, res_grad).astype(BF)
    expert_gate_part = mm("erd,erf->edf", expert_in, routed_gate_grad).astype(BF)
    expert_up_part = mm("erd,erf->edf", expert_in, routed_up_grad).astype(BF)
    expert_parts = jnp.concatenate(
        [
            expert_gate_part.reshape(EXP_DEV, dp, rows, hidden),
            expert_up_part.reshape(EXP_DEV, dp, rows, hidden),
            expert_down_part.reshape(EXP_DEV, dp, rows, hidden),
        ],
        axis=0,
    ).transpose(1, 0, 2, 3)
    expert_share = lax.psum_scatter(expert_parts, DP, scatter_dimension=0, tiled=True)[0]
    expert_share = expert_share.astype(F32)

    out_part = (
        mm(
            "osct,oscd->std", (spread.astype(F32) * slot_gates[..., None]).astype(BF), routed_res
        )
        + placed(shared_out)
    ).astype(BF)
    out_part = out_part.reshape(depth, 2, length, width)
    kept = lax.dynamic_index_in_dim(out_part, core, 1, False)
    given = swap(lax.dynamic_index_in_dim(out_part, 1 - core, 1, False))
    chip_part = (kept.astype(F32) + given.astype(F32)).astype(BF)
    moe_out = lax.dynamic_index_in_dim(chip_part, level, 0, False).astype(F32)
    for step in range(1, depth):
        block = lax.dynamic_index_in_dim(chip_part, (level + step) % depth, 0, False)
        moe_out += lax.ppermute(
            block, "z", [(i, (i + step) % depth) for i in range(depth)]
        ).astype(F32)

    routed_in_grad = back[:, :width].astype(F32)
    probs_grad = back[:, width : width + experts].astype(F32) + back[
        :, width + experts : width + 2 * experts
    ].astype(F32)
    logits_grad = router_probs * (
        probs_grad - jnp.sum(router_probs * probs_grad, axis=-1, keepdims=True)
    )
    router_grad = product_high(ffn_in.astype(F32).T, logits_grad)
    router_in_grad = product_high(logits_grad, router_full.astype(F32).T)
    ffn_in_grad = routed_in_grad + router_in_grad
    ffn_gain_grad = jnp.sum(ffn_in_grad * residual * norm_two, axis=0)
    upstream_two = ffn_in_grad * gain_two_f
    residual_grad = (
        out_grad.astype(F32)
        + norm_two * upstream_two
        - residual * norm_two**3 * jnp.mean(upstream_two * residual, axis=-1, keepdims=True)
    )
    attn_grad_two = two(residual_grad.astype(BF)).reshape(2 * length, width)
    output_grad = product(context.T, attn_grad_two).astype(BF)
    output_grad = joined(half(output_grad, core, 1), swap(half(output_grad, 1 - core, 1)), core, 0)
    context_grad = by_head(product(attn_grad_two, output_half.T).astype(BF))
    value_grad = flat(mm("shqk,sqhd->skhd", probs_low, context_grad).astype(BF))
    probs_grad_att = mm("sqhd,skhd->shqk", context_grad, values)
    row_delta = jnp.sum(attn_probs * probs_grad_att, axis=-1, keepdims=True)
    scores_grad = (attn_probs * (probs_grad_att - row_delta)).astype(BF)
    query_grad = mm("shqk,skhd->sqhd", scores_grad, key_rot) * score_scale
    key_grad = mm("shqk,sqhd->skhd", scores_grad, query_rot) * score_scale
    query_pre_grad = flat(rotate(query_grad, cosine, -sine_part).astype(BF))
    key_pre_grad = flat(rotate(key_grad, cosine, -sine_part).astype(BF))
    query_wgrad = product(attn_in.T, query_pre_grad)
    key_wgrad = product(attn_in.T, key_pre_grad)
    value_wgrad = product(attn_in.T, value_grad)
    in_partial = (
        product(query_pre_grad, query_half.T)
        + product(key_pre_grad, key_half.T)
        + product(value_grad, value_half.T)
    ).reshape(2, length, width)
    attn_in_grad = in_partial[0] + swap(in_partial[1].astype(BF)).astype(F32)
    token_mine, norm_mine = token_f[0], norm_one[0]
    attn_gain_grad = jnp.sum(attn_in_grad * token_mine * norm_mine, axis=0)
    upstream_one = attn_in_grad * gain_one_f
    tokens_grad = (
        residual_grad
        + norm_mine * upstream_one
        - token_mine * norm_mine**3 * jnp.mean(upstream_one * token_mine, axis=-1, keepdims=True)
    )
    small_grads = jnp.concatenate(
        [router_grad, attn_gain_grad[:, None], ffn_gain_grad[:, None]], axis=1
    ).astype(BF)
    small_grads = jnp.pad(small_grads, ((0, 0), (0, 128 - small_grads.shape[1])))
    attn_parts = jnp.concatenate(
        [
            query_wgrad.astype(BF),
            key_wgrad.astype(BF),
            value_wgrad.astype(BF),
            output_grad,
            small_grads,
        ],
        axis=1,
    )
    attn_share = lax.psum_scatter(attn_parts, DP, scatter_dimension=0, tiled=True)
    shared_share = lax.psum(shared_share, "z")
    attn_share = lax.psum(attn_share, "z")
    attn_other, shared_other = swap(attn_share), swap(shared_share)
    attn_col = lambda i: joined(
        attn_share[:, i * wide : (i + 1) * wide],
        attn_other[:, i * wide : (i + 1) * wide],
        core,
        1,
    ).astype(F32)
    small_sum = attn_share[:, 4 * wide :].astype(F32) + attn_other[:, 4 * wide :].astype(F32)
    unit_col = lambda i: joined(
        shared_share[:, i * narrow : (i + 1) * narrow].reshape(rows, dp, 1, part),
        shared_other[:, i * narrow : (i + 1) * narrow].reshape(rows, dp, 1, part),
        core,
        2,
    ).reshape(rows, hidden).astype(F32)
    down_rows = joined(
        shared_share[:, 2 * narrow :].reshape(part, width),
        shared_other[:, 2 * narrow :].reshape(part, width),
        core,
        0,
    ).astype(F32)

    stream_out = residual + moe_out
    stat_rms = jnp.stack(
        [
            jnp.sqrt(jnp.mean(attn_out * attn_out)),
            jnp.sqrt(jnp.mean(moe_out * moe_out)),
            jnp.sqrt(jnp.mean(stream_out * stream_out)),
        ]
    )[None, :]
    return (
        stream_out.astype(BF),
        tokens_grad.astype(BF),
        attn_col(0),
        attn_col(1),
        attn_col(2),
        attn_col(3),
        small_sum[:, experts],
        small_sum[:, experts + 1],
        small_sum[:, :experts],
        unit_col(0),
        unit_col(1),
        down_rows,
        expert_share[0:2],
        expert_share[2:4],
        expert_share[4:6].reshape(EXP_DEV, shared_down.shape[0], width),
        stat_rms,
    )


def solution(mesh):
    side = math.isqrt(mesh.shape["dp"])
    fine = Mesh(
        mesh.devices.reshape(side, side, mesh.shape["expert"] // 2, 2), ("y", "x", "z", "c")
    )
    whole = P(("y", "x", "z", "c"), None)
    dense = P(DP, None)
    routed = P(OWN, None, None)
    in_specs = (
        whole, dense, dense, dense, dense, P(DP), P(DP), dense, dense, dense, dense,
        routed, routed, routed, whole, P(("y", "x", "z", "c")), whole,
    )
    shares = P(OWN, DP, None)
    out_specs = (
        whole, whole, dense, dense, dense, dense, P(DP), P(DP), dense, dense, dense, dense,
        shares, shares, shares, whole,
    )
    return jax.shard_map(body, mesh=fine, in_specs=in_specs, out_specs=out_specs, check_vma=False)
```

time: 1120 us -> 990 us (0.88)
  waiting for transfers between devices: 677 us -> 507 us
  local copies, waits for them, and re-layouts: 170 us -> 205 us
  other arithmetic: 43.5 us -> 63.5 us
  matrix products: 195 us -> 177 us
    all_gather x4, waiting for transfers between devices: 279 us -> 171 us  [the longest x1 61 us: body(): lax.all_gather(jnp.concatenate([half(query_weight, core, 1), half(key_wei...]
    unnamed x13 -> x12, waiting for transfers between devices: 213 us -> 145 us
    ppermute x0 -> x15, waiting for transfers between devices: none -> 35.9 us  [the longest x3 31.5 us: body(): lax.ppermute(block, 'z', [(i, (i + step) % depth) for i in range(depth)])]
    reduce_scatter x2 -> x1, waiting for transfers between devices: 59.7 us -> 40.6 us  [body(): back = lax.psum_scatter(back, OWN, scatter_dimension=0, tiled=True)]
    convert_element_type x3 -> x16, other arithmetic: 5.71 us -> 23 us  [the longest x1 5.21 us: body(): expert_share = expert_share.astype(F32)]
    dot_general x45, matrix products: 189 us -> 172 us  [the longest x19 121 us: mm(): return jnp.einsum(spec, first_arg, second_arg, preferred_element_type=F32)]
    unnamed x161 -> x234, local copies, waits for them, and re-layouts: 83.6 us -> 69.1 us
    convert_element_type x5 -> x13, local copies, waits for them, and re-layouts: 6.99 us -> 20.8 us  [the longest x4 12 us: body(): unit_col = lambda i: joined(shared_share[:, i * narrow:(i + 1) * narrow]....]
  transfers between devices with their start and end apart: 10 -> 24, of which waited for: 9 -> 11; matrix products, arithmetic and copies ran while one was open for 22% -> 27% of each run, Pallas kernels for 0% -> 0%
where the time goes in v2:
time: 990 us; the launch traced here: 979 us
  waiting for transfers between devices  507 us (51%)
  local copies, waits for them, and re-layouts  205 us (21%)
  matrix products  177 us (18%)
  other arithmetic  63.5 us (6%)
  between operations  19.2 us (2%)
    unnamed x12, waiting for transfers between devices  145 us
    dot_general x19, matrix products, mm(): return jnp.einsum(spec, first_arg, second_arg, preferred_element_type=F32)  121 us
    psum x1, waiting for transfers between devices, body(): attn_share = lax.psum(attn_share, 'z')  114 us
    unnamed x234, local copies, waits for them, and re-layouts  69.1 us
    all_gather x1, waiting for transfers between devices, body(): lax.all_gather(jnp.concatenate([half(query_weight, core, 1), half(key_wei...  61 us
    all_gather x1, waiting for transfers between devices, body(): lax.all_gather(sent, OWN, axis=0, tiled=True)  58.7 us
    all_gather x1, waiting for transfers between devices, body(): lax.all_gather(jnp.concatenate([half(output_weight, core, 1), units(share...  49.5 us
    dot_general x22, matrix products, product(): return jnp.dot(first_arg, second_arg, preferred_element_type=F32)  45.7 us
  transfers between devices with their start and end apart: 24, of which 11 were waited for; matrix products, arithmetic and copies ran while one was open for 27% of the time, Pallas kernels for 0%

profile of v2, /device:TPU:0, one launch (start us, length us, event | category | flops | bytes accessed | tf_op | source)
XLA Modules:
  0.0 979.3 jit_solution(13413251181151024860)
XLA Ops:
  36.9 49.5 %all-gather.7.cloned.1.call-done = bf16[1280,1984]{1,0:T(8,128)(2,1)} async-done(((bf16[320,1984]{1,0:T(8,128)(2,1)}), bf16[1280,1984]{1,0:T(8,128)(2,1)}) %all-gather.7.cloned.1.call-update) | async-done | bytes 5079056 | tf_op jit(solution)/shard_map/all_gather | solution.py:140
  89.1 61.0 %all-gather.5.cloned.1.call-done = bf16[1280,2048]{1,0:T(8,128)(2,1)} async-done(((bf16[320,2048]{1,0:T(8,128)(2,1)}), bf16[1280,2048]{1,0:T(8,128)(2,1)}) %all-gather.5.cloned.1.call-update) | async-done | bytes 5242896 | tf_op jit(solution)/shard_map/all_gather | solution.py:130
  215.5 58.7 %all-gather.11.cloned.1.call-done = bf16[2048,1408]{0,1:T(8,128)(2,1)} async-done(((bf16[256,1408]{0,1:T(8,128)(2,1)}), bf16[2048,1408]{0,1:T(8,128)(2,1)}) %all-gather.11.cloned.1.call-update) | async-done | bytes 5767184 | tf_op jit(solution)/shard_map/all_gather | solution.py:205
  274.2 5.1 copy.478
  281.9 8.7 copy.464
  290.6 4.8 fusion.10
  298.1 6.3 fusion.2
  304.8 11.9 %fusion.137 = f32[2,1024,896]{2,1,0:T(8,128)} fusion(bf16[2,1024,1280]{2,1,0:T(8,128)(2,1)S(1)} %bitcast.262, bf16[2,1280,896]{2,1,0:T(8,128)(2,1)} %param.28), kind=kOutput, calls=%fused_computation.279 | convolution fusion | flops 4697620480 | bytes 17170432 | tf_op jit(solution)/shard_map/erd,edf->erf/dot_general | solution.py:29
  316.8 10.1 %fusion.139 = f32[2,1024,896]{2,1,0:T(8,128)} fusion(bf16[2,1024,1280]{2,1,0:T(8,128)(2,1)S(1)} %bitcast.266, bf16[2,896,1280]{2,1,0:T(8,128)(2,1)} %param.30), kind=kOutput, calls=%fused_computation.281 | convolution fusion | flops 4697620480 | bytes 17170432 | tf_op jit(solution)/shard_map/erd,efd->erf/dot_general | solution.py:29
  326.9 14.9 %multiply_convert_fusion.2 = (bf16[2,1024,896]{2,1,0:T(8,128)(2,1)}, bf16[2,1024,896]{2,1,0:T(8,128)(2,1)}, bf16[2,1024,896]{2,1,0:T(8,128)(2,1)}) fusion(f32[2,1024,896]{2,1,0:T(8,128)} %fusion.137, f32[2,1024,896]{2,1,0:T(8,128)} %fusion.139, bf16[2,1024,1280]{2,1,0:T(8,128)(2,1)S(1)} %bitcast.263, bf16[2,1280,896]{2,1,0:T(8,128)(2,1)} %param.29), kind=kOutput, calls=%fused_computation.14 | convolution fusion | flops 4725145600 | bytes 35520512 | tf_op jit(solution)/shard_map/erd,edf->erf/dot_general | solution.py:29
  341.8 9.8 %fusion.140 = f32[2,1024,1280]{2,1,0:T(8,128)} fusion(bf16[2,1024,896]{2,1,0:T(8,128)(2,1)} %get-tuple-element.132, bf16[2,1280,896]{2,1,0:T(8,128)(2,1)S(1)} %bitcast.321), kind=kOutput, calls=%fused_computation.282 | convolution fusion | flops 4697620480 | bytes 18743296 | tf_op jit(solution)/shard_map/erf,edf->erd/dot_general | solution.py:29
  351.6 8.6 convolution_convert_fusion.1
  365.8 10.3 %add_convert_fusion = bf16[2,1024,1280]{2,1,0:T(8,128)(2,1)S(1)} fusion(f32[2,1024,1280]{2,1,0:T(8,128)} %fusion.140, bf16[2,1024,896]{2,1,0:T(8,128)(2,1)} %get-tuple-element.133, bf16[2,1280,896]{2,1,0:T(8,128)(2,1)} %param.29), kind=kOutput, calls=%fused_computation.11 | convolution fusion | flops 4702863360 | bytes 23986176 | tf_op jit(solution)/shard_map/erf,edf->erd/dot_general | solution.py:29
  376.1 5.0 fusion.1
  381.2 9.8 %concatenate.113 = bf16[8,256,1408]{2,1,0:T(8,128)(2,1)} concatenate(bf16[8,256,1280]{2,1,0:T(8,128)(2,1)} %fusion.1, bf16[8,256,16]{2,1,0:T(8,128)(2,1)S(1)} %copy.368, bf16[8,256,16]{2,1,0:T(8,128)(2,1)S(1)} %copy.369, bf16[8,256,96]{2,1,0:T(8,128)(2,1)S(1)} %broadcast_in_dim.136), dimensions={2} | concatenate | bytes 11534336 | tf_op jit(solution)/shard_map/concatenate | solution.py:278
  391.0 8.2 copy.453
  407.8 4.4 copy.362
  442.4 40.6 %reduce-scatter.11.cloned.1.call-done = bf16[256,1408]{0,1:T(8,128)(2,1)} async-done(((bf16[2048,1408]{0,1:T(8,128)(2,1)}), bf16[256,1408]{0,1:T(8,128)(2,1)}) %reduce-scatter.11.cloned.1.call-update) | async-done | bytes 720912 | tf_op jit(solution)/shard_map/reduce_scatter | solution.py:281
  485.7 31.5 %collective-permute-done.7 = bf16[256,1280]{0,1:T(8,128)(2,1)} collective-permute-done((bf16[256,1280]{0,1:T(8,128)(2,1)}, bf16[256,1280]{0,1:T(8,128)(2,1)}, u32[]{:S(2)}, u32[]{:S(2)}) %collective-permute-start.7) | collective-permute-done | bytes 655392 | tf_op jit(solution)/shard_map/ppermute | solution.py:310
  517.2 4.2 multiply_reduce_fusion.3
  525.5 6.0 copy.457
  573.5 10.0 %copy.455 = bf16[1280,2688]{1,0:T(8,128)(2,1)} copy(bf16[1280,2688]{0,1:T(8,128)(2,1)} %fusion.80) | data formatting | bytes 13762560
  583.6 10.8 %convolution_convert_fusion.3 = bf16[2,896,1280]{2,1,0:T(8,128)(2,1)} fusion(bf16[2,1024,896]{2,1,0:T(8,128)(2,1)} %get-tuple-element.131, bf16[2,1024,1280]{2,1,0:T(8,128)(2,1)} %bitcast.267), kind=kOutput, calls=%fused_computation.25 | convolution fusion | flops 4699914240 | bytes 13500416 | tf_op jit(solution)/shard_map/erf,erd->efd/dot_general | solution.py:29
  594.3 9.3 reshape.768
  603.7 9.0 convolution_convert_fusion.4
  612.7 8.4 convolution_convert_fusion.5
  621.2 6.9 copy_bitcast_fusion
  630.9 26.0 %reduce-scatter.13.cloned.1.call-done = bf16[320,2688]{1,0:T(8,128)(2,1)} async-done(((bf16[1280,2688]{1,0:T(8,128)(2,1)}), bf16[320,2688]{1,0:T(8,128)(2,1)}) %reduce-scatter.13.cloned.1.call-update) | async-done | bytes 1720336
  671.6 118.7 %reduce-scatter.17.cloned.1.call-done = bf16[1,6,320,896]{3,2,1,0:T(8,128)(2,1)} async-done(((bf16[4,6,320,896]{3,2,1,0:T(8,128)(2,1)}), bf16[1,6,320,896]{3,2,1,0:T(8,128)(2,1)}) %reduce-scatter.17.cloned.1.call-update) | async-done | bytes 3440656
  793.3 5.2 convert_element_type.455
  798.6 114.4 %all-reduce.7.cloned.1.call-done = (bf16[320,2688]{0,1:T(8,128)(2,1)}, bf16[320,1344]{0,1:T(8,128)(2,1)}) async-done(((bf16[320,2688]{0,1:T(8,128)(2,1)}, bf16[320,1344]{0,1:T(8,128)(2,1)}), (bf16[320,2688]{0,1:T(8,128)(2,1)}, bf16[320,1344]{0,1:T(8,128)(2,1)})) %all-reduce.7.cloned.1.call-update) | async-done | bytes 2580496 | tf_op jit(solution)/shard_map/psum | solution.py:376
  919.4 4.8 slice_bitcast_fusion.2
  (466 shorter events, 267.3 us)
Async XLA Ops:
  7.2 79.1 %all-gather.7.cloned.1.call-start = ((), (), s32[]{:S(2)}) async-start(), calls=%async_computation.5 | async-start | bytes 6553600 | tf_op jit(solution)/shard_map/all_gather | solution.py:140
  22.2 127.9 %all-gather.5.cloned.1.call-start = ((), (), s32[]{:S(2)}) async-start(), calls=%async_computation.4 | async-start | bytes 6553600 | tf_op jit(solution)/shard_map/all_gather | solution.py:130
  24.9 187.8 %all-gather.9.cloned.1.call-start = ((), (), s32[]{:S(2)}) async-start(), calls=%async_computation.6 | async-start | bytes 6488064 | tf_op jit(solution)/shard_map/all_gather | solution.py:158
  26.0 248.2 %all-gather.11.cloned.1.call-start = ((), (), s32[]{:S(2)}) async-start(), calls=%async_computation.7 | async-start | bytes 6488064 | tf_op jit(solution)/shard_map/all_gather | solution.py:205
  26.3 4.5 collective-permute-start
  26.9 1.8 collective-permute-start.1
  28.6 139.5 %copy-start.59 = (f32[256,64]{0,1:T(8,128)}, f32[256,64]{0,1:T(8,128)S(1)}, u32[]{:S(2)}) copy-start(f32[256,64]{0,1:T(8,128)S(1)} %get-tuple-element.193) | copy-start | bytes 196612
  36.9 127.2 %copy-start.81 = (f32[2,256]{1,0:T(2,128)}, f32[2,256]{1,0:T(2,128)S(1)}, u32[]{:S(2)}) copy-start(f32[2,256]{1,0:T(2,128)S(1)} %get-tuple-element.187) | copy-start | bytes 6148
  89.1 87.6 %collective-permute-start.2 = (bf16[640,640]{1,0:T(8,128)(2,1)}, bf16[640,640]{1,0:T(8,128)(2,1)}, u32[]{:S(2)}, u32[]{:S(2)}) collective-permute-start(bf16[640,640]{1,0:T(8,128)(2,1)} %get-tuple-element.164), channel_id=1, source_target_pairs={{0,1},{1,0},{2,3},{3,2},{4,5},{5,4},{6,7},{7,6},{8,9},{9,8},{10,11... | collective-permute-start | bytes 2457608 | tf_op jit(solution)/shard_map/ppermute | solution.py:78
  179.9 2.3 collective-permute-start.3
  186.7 296.3 %reduce-scatter.11.cloned.1.call-start = ((), (), s32[]{:S(2)}) async-start(), calls=%async_computation.8 | async-start | bytes 6488064 | tf_op jit(solution)/shard_map/reduce_scatter | solution.py:281
  187.2 2.4 collective-permute-start.9
  195.7 3.8 collective-permute-start.4
  399.2 228.9 %reduce-scatter.15.cloned.1.call-start = ((), (), s32[]{:S(2)}) async-start(), calls=%async_computation.10 | async-start | bytes 4505600
  412.2 19.6 %collective-permute-start.5 = (bf16[4,256,1280]{1,2,0:T(8,128)(2,1)}, bf16[4,256,1280]{1,2,0:T(8,128)(2,1)}, u32[]{:S(2)}, u32[]{:S(2)}) collective-permute-start(bf16[4,256,1280]{1,2,0:T(8,128)(2,1)} %bitcast.281), channel_id=1, source_target_pairs={{0,1},{1,0},{2,3},{3,2},{4,5},{5,4},{6,7},{7,6},{8,9},{9,8},{10,11... | collective-permute-start | bytes 7864328 | tf_op jit(solution)/shard_map/ppermute | solution.py:78
  413.8 107.6 %copy-start.13 = (bf16[256,1280]{0,1:T(8,128)(2,1)}, bf16[256,1280]{0,1:T(8,128)(2,1)S(1)}, u32[]{:S(2)}) copy-start(bf16[256,1280]{0,1:T(8,128)(2,1)S(1)} %copy.363) | copy-start | bytes 1966084
  436.4 49.2 %collective-permute-start.8 = (bf16[256,1280]{0,1:T(8,128)(2,1)}, bf16[256,1280]{0,1:T(8,128)(2,1)}, u32[]{:S(2)}, u32[]{:S(2)}) collective-permute-start(bf16[256,1280]{0,1:T(8,128)(2,1)} %get-tuple-element.144), channel_id=1, source_target_pairs={{0,6},{2,0},{4,2},{6,4},{1,7},{3,1},{5,3},{7,5},{8,14},{10,8},{12,... | collective-permute-start | bytes 1966088 | tf_op jit(solution)/shard_map/ppermute | solution.py:310
  437.4 79.8 %collective-permute-start.7 = (bf16[256,1280]{0,1:T(8,128)(2,1)}, bf16[256,1280]{0,1:T(8,128)(2,1)}, u32[]{:S(2)}, u32[]{:S(2)}) collective-permute-start(bf16[256,1280]{0,1:T(8,128)(2,1)} %get-tuple-element.145), channel_id=1, source_target_pairs={{0,4},{2,6},{4,0},{6,2},{1,5},{3,7},{5,1},{7,3},{8,12},{10,14},{12... | collective-permute-start | bytes 1966088 | tf_op jit(solution)/shard_map/ppermute | solution.py:310
  438.6 44.5 %copy-start.76 = (f32[256]{0:T(256)S(1)}, f32[256]{0:T(256)}, u32[]{:S(2)}) copy-start(f32[256]{0:T(256)} %copy-done.75) | copy-start | bytes 3076
  438.6 44.5 %copy-start.78 = (f32[256]{0:T(256)S(1)}, f32[256]{0:T(256)}, u32[]{:S(2)}) copy-start(f32[256]{0:T(256)} %copy-done.77) | copy-start | bytes 3076
  438.6 78.6 %copy-start.67 = (f32[1280]{0:T(1024)S(1)}, f32[1280]{0:T(1024)}, u32[]{:S(2)}) copy-start(f32[1280]{0:T(1024)} %copy-done.66) | copy-start | bytes 15364
  438.6 78.6 %copy-start.74 = (f32[256]{0:T(256)S(1)}, f32[256]{0:T(256)}, u32[]{:S(2)}) copy-start(f32[256]{0:T(256)} %copy-done.73) | copy-start | bytes 3076
  438.6 78.6 %collective-permute-start.6 = (bf16[256,1280]{0,1:T(8,128)(2,1)}, bf16[256,1280]{0,1:T(8,128)(2,1)}, u32[]{:S(2)}, u32[]{:S(2)}) collective-permute-start(bf16[256,1280]{0,1:T(8,128)(2,1)} %get-tuple-element.143), channel_id=1, source_target_pairs={{0,2},{2,4},{4,6},{6,0},{1,3},{3,5},{5,7},{7,1},{8,10},{10,12},{12... | collective-permute-start | bytes 1966088 | tf_op jit(solution)/shard_map/ppermute | solution.py:310
  442.4 74.8 %copy-start.3 = (f32[256,1280]{0,1:T(8,128)S(1)}, f32[256,1280]{0,1:T(8,128)}, u32[]{:S(2)}) copy-start(f32[256,1280]{0,1:T(8,128)} %copy-done.2) | copy-start | bytes 3932164
  522.6 11.2 %collective-permute-start.10 = (bf16[256,1280]{0,1:T(8,128)(2,1)}, bf16[256,1280]{0,1:T(8,128)(2,1)}, u32[]{:S(2)}, u32[]{:S(2)}) collective-permute-start(bf16[256,1280]{0,1:T(8,128)(2,1)} %fusion.121), channel_id=1, source_target_pairs={{0,1},{1,0},{2,3},{3,2},{4,5},{5,4},{6,7},{7,6},{8,9},{9,8},{10,11... | collective-permute-start | bytes 1966088 | tf_op jit(solution)/shard_map/ppermute | solution.py:78
  531.5 125.4 %reduce-scatter.13.cloned.1.call-start = ((), (), s32[]{:S(2)}) async-start(), calls=%async_computation.9 | async-start | bytes 8601600
  561.1 9.3 collective-permute-start.11
  565.6 5.6 collective-permute-start.12
  583.5 206.7 %reduce-scatter.17.cloned.1.call-start = ((), (), s32[]{:S(2)}) async-start(), calls=%async_computation.11 | async-start | bytes 17203200
  628.1 284.9 %all-reduce.7.cloned.1.call-start = ((), (), s32[]{:S(2)}) async-start(), calls=%async_computation.12 | async-start | bytes 6193152 | tf_op jit(solution)/shard_map/psum | solution.py:376
  917.1 36.3 %collective-permute-start.13 = (bf16[320,2688]{1,0:T(8,128)(2,1)}, bf16[320,2688]{1,0:T(8,128)(2,1)}, u32[]{:S(2)}, u32[]{:S(2)}) collective-permute-start(bf16[320,2688]{1,0:T(8,128)(2,1)} %copy.388), channel_id=1, source_target_pairs={{0,1},{1,0},{2,3},{3,2},{4,5},{5,4},{6,7},{7,6},{8,9},{9,8},{10,11... | collective-permute-start | bytes 5160968 | tf_op jit(solution)/shard_map/ppermute | solution.py:78
  918.9 9.7 collective-permute-start.14
  (97 other events, 567.7 us)
Sparse Core Ops, SparseCore 0:
  22.3 64.0 all-gather.6
  88.7 61.2 all-gather.4
  152.3 60.3 all-gather.8
  214.7 59.4 all-gather.10
  399.3 83.6 reduce-scatter.10
  531.6 45.8 reduce-scatter.14
  583.7 73.1 reduce-scatter.12
  660.0 130.2 reduce-scatter.16
  793.3 119.6 all-reduce.6

commit v3 on v2

v3 whole, which is shorter than its diff:
```python
import functools
import math

import jax
import jax.numpy as jnp
from jax import lax
from jax.experimental import pallas as pl
from jax.experimental.pallas import tpu as pltpu
from jax.sharding import Mesh
from jax.sharding import PartitionSpec as P

HEAD_DIM = 128
TOP = 7
EXP_DEV = 2
BF = jnp.bfloat16
F32 = jnp.float32
DP = ("y", "x")
OWN = ("z", "c")
NT = (((1,), (1,)), ((), ()))
TN = (((0,), (0,)), ((), ()))


def dot(first, second, dims=(((1,), (0,)), ((), ()))):
    return lax.dot_general(first, second, dims, preferred_element_type=F32)


def expert_kernel(count, width, capacity, experts, chunk, me_ref, slots_ref, *refs):
    rows_refs = refs[:count]
    grads_refs = refs[count : 2 * count]
    gate_ref, up_ref, down_ref = refs[2 * count : 2 * count + 3]
    in_mine, in_other, res_mine, res_other, xin, rgrad, hid, ggrad, ugrad = refs[-14:-5]
    ograd, in_ext, res_low, in_acc, out_acc = refs[-5:]
    step = pl.program_id(0)
    expert = me_ref[0] * EXP_DEV + step
    lane = lax.broadcasted_iota(jnp.int32, (capacity, 128), 1)
    mine = (lane == expert) | (lane == expert + experts)

    def spread(piece):
        want = slots_ref[step, piece]
        place = lax.broadcasted_iota(jnp.int32, (capacity, want.shape[-1]), 0)
        return (want == place).astype(F32)

    for piece in range(count):
        hot = spread(piece).astype(BF)
        area = pl.ds(piece * capacity, capacity)
        rows = dot(hot, rows_refs[piece][...])
        xin[0, area, :] = rows[:, :width].astype(BF)
        gates = jnp.sum(jnp.where(mine, rows[:, width:], 0.0), axis=1, keepdims=True)
        grads = dot(hot, grads_refs[piece][:, :width])
        ograd[area, :] = grads.astype(BF)
        rgrad[0, area, :] = (grads * gates).astype(BF)

    def part(index, carry):
        area = pl.ds(pl.multiple_of(index * chunk, chunk), chunk)
        rows = xin[0, area, :]
        res_grad = rgrad[0, area, :]
        gate = dot(rows, gate_ref[0])
        up = dot(rows, up_ref[0])
        hidden_grad = dot(res_grad, down_ref[0], NT)
        sig = jax.nn.sigmoid(gate)
        silu = gate * sig
        hidden = (silu * up).astype(BF)
        hid[0, area, :] = hidden
        gate_grad = (hidden_grad * up * (sig * (1.0 + gate * (1.0 - sig)))).astype(BF)
        up_grad = (hidden_grad * silu).astype(BF)
        ggrad[0, area, :] = gate_grad
        ugrad[0, area, :] = up_grad
        in_ext[area, pl.ds(0, width)] = (
            dot(gate_grad, gate_ref[0], NT) + dot(up_grad, up_ref[0], NT)
        ).astype(BF)
        res = dot(hidden, down_ref[0]).astype(BF)
        res_low[area, :] = res
        slot_gate = jnp.sum(res.astype(F32) * ograd[area, :].astype(F32), axis=1, keepdims=True)
        high = slot_gate.astype(BF).astype(F32)
        lanes = lax.broadcasted_iota(jnp.int32, (chunk, 128), 1)
        in_ext[area, pl.ds(width, 128)] = jnp.where(
            lanes == expert, high, jnp.where(lanes == expert + experts, slot_gate - high, 0.0)
        ).astype(BF)
        return carry

    lax.fori_loop(0, count * capacity // chunk, part, 0)

    for piece in range(count):
        hot = spread(piece)
        area = pl.ds(piece * capacity, capacity)
        low = hot.astype(BF)
        gates = jnp.sum(
            jnp.where(mine, dot(low, rows_refs[piece][:, width:]), 0.0), axis=1, keepdims=True
        )
        back = dot(low, in_ext[area, :], TN)
        result = dot((hot * gates).astype(BF), res_low[area, :], TN)
        in_out, res_out = ((in_mine, res_mine), (in_other, res_other))[piece % 2]

        @pl.when(step == 0)
        def _():
            in_acc[piece] = back
            out_acc[piece] = result

        @pl.when(step == EXP_DEV - 1)
        def _():
            in_out[piece // 2] = (in_acc[piece] + back).astype(BF)
            res_out[piece // 2] = (out_acc[piece] + result).astype(BF)


def expert_call(me, slots, rows, grads, gate, up, down, owners, first, carried=None):
    count = len(rows)
    length, wide = rows[0].shape
    width, hidden = gate.shape[1:]
    experts = EXP_DEV * owners
    capacity = 8 * length // experts
    block = count * capacity
    total = owners * capacity
    still = lambda shape: pl.BlockSpec(
        shape, lambda e, m: (0,) * len(shape), pipeline_mode=pl.Buffered(1)
    )
    weight = lambda a, b: pl.BlockSpec((1, a, b), lambda e, m: (e, 0, 0))
    kept = lambda cols: pl.BlockSpec((1, block, cols), lambda e, m: (e, first, 0))
    kept_cols = (width, width, hidden, hidden, hidden)
    in_specs = (
        [still((EXP_DEV, count, 1, length))]
        + [still((length, wide))] * (2 * count)
        + [weight(width, hidden), weight(width, hidden), weight(hidden, width)]
    )
    args = [me, slots, *rows, *grads, gate, up, down]
    alias = {}
    if carried is not None:
        for i, value in enumerate(carried):
            alias[len(args)] = 4 + i
            args.append(value)
            in_specs.append(pl.BlockSpec(memory_space=pl.ANY))
    sums = [(count // 2, length, wide)] * 2 + [(count // 2, length, width)] * 2
    return pl.pallas_call(
        functools.partial(expert_kernel, count, width, capacity, experts, min(512, block)),
        out_shape=[jax.ShapeDtypeStruct(shape, BF) for shape in sums]
        + [jax.ShapeDtypeStruct((EXP_DEV, total, cols), BF) for cols in kept_cols],
        grid_spec=pltpu.PrefetchScalarGridSpec(
            num_scalar_prefetch=1,
            grid=(EXP_DEV,),
            in_specs=in_specs,
            out_specs=[still(shape) for shape in sums] + [kept(cols) for cols in kept_cols],
            scratch_shapes=[
                pltpu.VMEM((block, width), BF),
                pltpu.VMEM((block, wide), BF),
                pltpu.VMEM((block, width), BF),
                pltpu.VMEM((count, length, wide), F32),
                pltpu.VMEM((count, length, width), F32),
            ],
        ),
        input_output_aliases=alias,
        compiler_params=pltpu.CompilerParams(
            dimension_semantics=("arbitrary",), vmem_limit_bytes=60 * 1024 * 1024
        ),
        cost_estimate=pl.CostEstimate(
            flops=14 * EXP_DEV * block * width * hidden,
            transcendentals=EXP_DEV * block * hidden,
            bytes_accessed=60 * 1024 * 1024,
        ),
        name="experts",
    )(*args)


def place_kernel(count, offsets_ref, *refs):
    pieces, out = refs[:count], refs[count]
    for i in range(count):
        start = pl.multiple_of(offsets_ref[i], 16)
        out[pl.ds(start, pieces[i].shape[0]), :] = pieces[i][...]


def place(pieces, offsets, total):
    count, cols = len(pieces), pieces[0].shape[1]
    return pl.pallas_call(
        functools.partial(place_kernel, count),
        out_shape=jax.ShapeDtypeStruct((total, cols), pieces[0].dtype),
        in_specs=[pl.BlockSpec(memory_space=pltpu.SMEM)]
        + [pl.BlockSpec(memory_space=pltpu.VMEM)] * count,
        out_specs=pl.BlockSpec(memory_space=pltpu.VMEM),
        cost_estimate=pl.CostEstimate(
            flops=0, transcendentals=0, bytes_accessed=4 * total * cols
        ),
        name="place",
    )(jnp.stack(offsets).astype(jnp.int32), *pieces)


def product(first_arg, second_arg):
    return jnp.dot(first_arg, second_arg, preferred_element_type=F32)


def product_high(first_arg, second_arg):
    return jnp.dot(
        first_arg, second_arg, precision=lax.Precision.HIGHEST, preferred_element_type=F32
    )


def mm(spec, first_arg, second_arg):
    return jnp.einsum(spec, first_arg, second_arg, preferred_element_type=F32)


def rotary_tables(length, head_size):
    half_dim = head_size // 2
    frequency = 10000.0 ** (-jnp.arange(half_dim, dtype=F32) * 2.0 / head_size)
    angles = jnp.arange(length, dtype=F32)[:, None] * frequency[None, :]
    return (jnp.cos(angles), jnp.sin(angles))


def rotate(tensor, cosine, sine_part):
    half_dim = tensor.shape[-1] // 2
    first_half = tensor[..., :half_dim]
    second_half = tensor[..., half_dim:]
    cos_rows = cosine[:, None, :]
    sin_rows = sine_part[:, None, :]
    return jnp.concatenate(
        [
            first_half * cos_rows - second_half * sin_rows,
            first_half * sin_rows + second_half * cos_rows,
        ],
        axis=-1,
    )


def allowed_mask(length, piece_start, piece_len):
    row_index = jnp.arange(length, dtype=jnp.int32)[:, None]
    col_index = jnp.arange(length, dtype=jnp.int32)[None, :]
    row_inside = (row_index >= piece_start) & (row_index < piece_start + piece_len)
    col_inside = (col_index >= piece_start) & (col_index < piece_start + piece_len)
    return (col_index <= row_index) | row_inside & col_inside


def silu_grad(inputs):
    sigmoid_part = jax.nn.sigmoid(inputs)
    return sigmoid_part * (1.0 + inputs * (1.0 - sigmoid_part))


def high_low(values):
    high = values.astype(BF)
    low = (values - high.astype(F32)).astype(BF)
    return high, low


def shifted(value, axis, by):
    size = lax.axis_size(axis)
    return lax.ppermute(value, axis, [(i, (i + by) % size) for i in range(size)])


def swap(value):
    return shifted(value, "c", 1)


def half(value, index, axis):
    size = value.shape[axis] // 2
    return lax.dynamic_slice_in_dim(value, index * size, size, axis)


def joined(mine, other, core, axis):
    return jnp.where(
        core == 0, jnp.concatenate([mine, other], axis), jnp.concatenate([other, mine], axis)
    )


def pick(value, index, axis):
    return lax.dynamic_index_in_dim(value, index % value.shape[axis], axis, False)


def after(value, *first):
    return lax.optimization_barrier((value, *first))[0]


def ring_gather(value, axis):
    found = [value]
    for _ in range(lax.axis_size(axis) - 1):
        found.append(shifted(found[-1], axis, 1))
    return found


def gather_dp(value):
    rows = value.shape[0]
    cut = (rows // 2 + 15) // 16 * 16
    side = lax.axis_size("x")
    pieces, offsets = [], []
    for start, part, order in ((0, value[:cut], "xy"), (cut, value[cut:], "yx")):
        for first, kept in enumerate(ring_gather(part, order[0])):
            for second, piece in enumerate(ring_gather(kept, order[1])):
                back = dict(zip(order, (first, second)))
                pieces.append(piece)
                from_y = (lax.axis_index("y") - back["y"]) % side
                from_x = (lax.axis_index("x") - back["x"]) % side
                offsets.append((from_y * side + from_x) * rows + start)
    return place(pieces, offsets, rows * side * side)


def ring_reduce(value, axis, at):
    size, index = lax.axis_size(axis), lax.axis_index(axis)
    moving = pick(value, index - 1, at)
    for step in range(2, size + 1):
        other = shifted(moving, axis, 1)
        moving = (other.astype(F32) + pick(value, index - step, at).astype(F32)).astype(BF)
    return moving


def reduce_dp(value, order):
    dims = value.ndim
    if order == "yx":
        return ring_reduce(ring_reduce(value, "y", dims - 4), "x", dims - 4)
    return ring_reduce(ring_reduce(value, "x", dims - 3), "y", dims - 4)


def reduce_level(value):
    depth, level = lax.axis_size("z"), lax.axis_index("z")
    rows, cols = value.shape
    parts = value.reshape(depth, rows // depth, cols)
    total = pick(parts, level, 0).astype(F32)
    for step in range(1, depth):
        total += shifted(pick(parts, level + step, 0), "z", step).astype(F32)
    mine = total.astype(BF)
    found = [mine] + [shifted(mine, "z", step) for step in range(1, depth)]
    turned = jnp.stack(found[::-1] * 2)
    return lax.dynamic_slice_in_dim(turned, depth - 1 - level, depth, 0).reshape(rows, cols)


def body(
    tokens,
    query_weight,
    key_weight,
    value_weight,
    output_weight,
    attn_gain,
    ffn_gain,
    router_weight,
    shared_gate,
    shared_up,
    shared_down,
    expert_gate,
    expert_up,
    expert_down,
    expert_ids,
    piece_starts,
    out_grad,
):
    side = lax.axis_size("x")
    dp = side * side
    owners = lax.axis_size(OWN)
    depth = lax.axis_size("z")
    core = lax.axis_index("c")
    me = lax.axis_index(OWN)
    experts = EXP_DEV * owners
    length, width = tokens.shape
    rows = query_weight.shape[0]
    hidden = shared_gate.shape[1]
    part = hidden // (2 * dp)
    wide, narrow = width // 2, hidden // 2
    head_count = wide // HEAD_DIM
    score_scale = HEAD_DIM ** (-0.5)
    piece_len = min(256, length // 2)
    capacity = 8 * length // experts
    two = lambda mine: jnp.stack([mine, swap(mine)])

    small = jnp.concatenate([router_weight, attn_gain[:, None], ffn_gain[:, None]], axis=1)
    small = jnp.pad(small, ((0, 0), (0, 128 - small.shape[1])))
    first_full = gather_dp(
        jnp.concatenate(
            [half(query_weight, core, 1), half(key_weight, core, 1), half(value_weight, core, 1), small],
            axis=1,
        )
    )
    units = lambda weight: pick(weight.reshape(rows, dp, 2, part), core, 2).reshape(rows, narrow)
    second_shard = jnp.concatenate(
        [
            half(output_weight, core, 1),
            units(shared_gate),
            units(shared_up),
            half(shared_down, core, 0).reshape(rows, narrow),
        ],
        axis=1,
    )
    second_full = gather_dp(after(second_shard, first_full))
    tokens_two = two(tokens)
    starts_two = two(piece_starts[0])

    chosen = (expert_ids[:, :, None] == jnp.arange(experts, dtype=jnp.int32)).any(axis=1)
    chosen_low = jnp.pad(chosen.astype(BF), ((0, 0), (0, 128 - experts)))

    def spread_out(mine):
        found = []
        for step in range(depth):
            piece = shifted(mine, "z", step) if step else mine
            found += [piece, swap(piece)]
        return found

    grads_all = spread_out(jnp.concatenate([out_grad, chosen_low], axis=1))
    own = me * EXP_DEV + jnp.arange(EXP_DEV)
    own_hot = (own[:, None] == jnp.arange(experts)[None, :]).astype(F32)
    marks = jnp.stack([piece[:, width : width + experts] for piece in grads_all]).astype(F32)
    mask = mm("ste,oe->ost", marks, own_hot)
    slots = jnp.where(mask > 0, jnp.cumsum(mask, axis=2) - 1.0, -1.0).astype(jnp.int32)
    slots = slots[:, :, None, :]

    query_half = first_full[:, :wide]
    key_half = first_full[:, wide : 2 * wide]
    value_half = first_full[:, 2 * wide : 3 * wide]
    small_full = first_full[:, 3 * wide :]
    router_full = small_full[:, :experts]
    gain_one_f = small_full[:, experts].astype(F32)
    gain_two_f = small_full[:, experts + 1].astype(F32)
    output_cols = second_full[:, :wide]
    gate_half = second_full[:, wide : wide + narrow]
    up_half = second_full[:, wide + narrow : wide + 2 * narrow]
    down_half = second_full[:, wide + 2 * narrow :].reshape(narrow, width)
    output_half = joined(
        half(output_cols, core, 0), swap(half(output_cols, 1 - core, 0)), core, 1
    )

    token_f = tokens_two.astype(F32)
    norm_one = lax.rsqrt(jnp.mean(token_f * token_f, axis=-1, keepdims=True) + 1e-06)
    attn_in = (token_f * norm_one * gain_one_f).astype(BF).reshape(2 * length, width)
    cosine, sine_part = rotary_tables(length, HEAD_DIM)
    by_head = lambda value: value.reshape(2, length, head_count, HEAD_DIM)
    flat = lambda value: value.reshape(2 * length, wide)
    query_rot = rotate(by_head(product(attn_in, query_half)), cosine, sine_part).astype(BF)
    key_rot = rotate(by_head(product(attn_in, key_half)), cosine, sine_part).astype(BF)
    values = by_head(product(attn_in, value_half).astype(BF))
    allowed = jnp.stack([allowed_mask(length, starts_two[i], piece_len) for i in range(2)])
    scores = mm("sqhd,skhd->shqk", query_rot, key_rot) * score_scale
    scores = jnp.where(allowed[:, None], scores, -1e30)
    row_max = jnp.max(scores, axis=-1, keepdims=True)
    exps = jnp.exp(scores - row_max)
    attn_probs = exps / jnp.sum(exps, axis=-1, keepdims=True)
    probs_low = attn_probs.astype(BF)
    context = flat(mm("shqk,skhd->sqhd", probs_low, values).astype(BF))
    out_partial = product(context, output_half).reshape(2, length, width)
    attn_out = out_partial[0] + swap(out_partial[1].astype(BF)).astype(F32)
    residual = token_f[0] + attn_out
    norm_two = lax.rsqrt(jnp.mean(residual * residual, axis=-1, keepdims=True) + 1e-06)
    ffn_in = (residual * norm_two * gain_two_f).astype(BF)
    router_probs = jax.nn.softmax(product(ffn_in, router_full), axis=-1)
    gates = jnp.where(chosen, router_probs, 0.0)
    gates_high, gates_low = high_low(gates)
    sent = jnp.concatenate(
        [ffn_in, gates_high, gates_low, jnp.zeros((length, 128 - 2 * experts), BF)], axis=1
    )
    rows_all = spread_out(sent)

    ffn_two = jnp.stack([ffn_in, rows_all[1][:, :width]]).reshape(2 * length, width)
    grad_two = jnp.stack([out_grad, grads_all[1][:, :width]]).reshape(2 * length, width)
    shared_gate_act = product(ffn_two, gate_half)
    shared_up_act = product(ffn_two, up_half)
    shared_hidden = (jax.nn.silu(shared_gate_act) * shared_up_act).astype(BF)
    shared_out = product(shared_hidden, down_half).astype(BF).reshape(2, length, width)
    shared_hidden_grad = product(grad_two, down_half.T)
    shared_down_grad = product(shared_hidden.T, grad_two).astype(BF)
    shared_gate_act_grad = (shared_hidden_grad * shared_up_act * silu_grad(shared_gate_act)).astype(
        BF
    )
    shared_up_act_grad = (shared_hidden_grad * jax.nn.silu(shared_gate_act)).astype(BF)
    shared_gate_grad = product(ffn_two.T, shared_gate_act_grad).astype(BF)
    shared_up_grad = product(ffn_two.T, shared_up_act_grad).astype(BF)
    shared_in_grad = (
        (product(shared_gate_act_grad, gate_half.T) + product(shared_up_act_grad, up_half.T))
        .astype(BF)
        .reshape(2, length, width)
    )
    shares = lambda value: value.reshape(side, side, rows, -1)
    gate_share = reduce_dp(shares(shared_gate_grad), "yx")
    up_share = reduce_dp(shares(shared_up_grad), "xy")
    down_share = reduce_dp(shares(shared_down_grad), "yx")
    shared_share = reduce_level(jnp.concatenate([gate_share, up_share, down_share], axis=1))

    place_me = me.reshape(1).astype(jnp.int32)
    near = expert_call(
        place_me, slots[:, : owners // 2], rows_all[: owners // 2], grads_all[: owners // 2],
        expert_gate, expert_up, expert_down, owners, 0,
    )
    far = expert_call(
        place_me, slots[:, owners // 2 :], rows_all[owners // 2 :], grads_all[owners // 2 :],
        expert_gate, expert_up, expert_down, owners, 1, near[4:],
    )
    expert_in, res_grad, routed_hidden, routed_gate_grad, routed_up_grad = far[4:]

    def collected(mine, other, shared, barrier=None):
        chip = []
        for step in range(depth):
            own_part, far_part = mine[step], other[step]
            if step == 0:
                far_part = lax.dynamic_update_slice(
                    far_part, far_part[:, :width] + shared[1], (0, 0)
                )
            chip.append(own_part.astype(F32) + swap(far_part).astype(F32))
        total = chip[0]
        for step in range(1, depth):
            moving = chip[step].astype(BF)
            if barrier is not None:
                moving = after(moving, barrier)
            total += shifted(moving, "z", -step).astype(F32)
        return total

    unstack = lambda i: [call[i][k] for call in (near, far) for k in range(depth // 2)]
    back = collected(unstack(0), unstack(1), shared_in_grad)
    moe_out = collected(unstack(2), unstack(3), shared_out, back) + shared_out[0].astype(F32)

    down_grad = mm("erf,erd->efd", routed_hidden, res_grad).astype(BF)
    gate_grad = mm("erd,erf->edf", expert_in, routed_gate_grad).astype(BF)
    up_grad = mm("erd,erf->edf", expert_in, routed_up_grad).astype(BF)
    expert_shares = []
    for grad in (gate_grad, up_grad, down_grad):
        blocks = grad.reshape(EXP_DEV, side, side, grad.shape[1] // dp, grad.shape[2])
        expert_shares.append(
            jnp.stack([reduce_dp(blocks[0], "yx"), reduce_dp(blocks[1], "xy")]).astype(F32)
        )

    probs_grad = back[:, width : width + experts] + back[:, width + experts : width + 2 * experts]
    logits_grad = router_probs * (
        probs_grad - jnp.sum(router_probs * probs_grad, axis=-1, keepdims=True)
    )
    router_grad = product_high(ffn_in.astype(F32).T, logits_grad)
    router_in_grad = product_high(logits_grad, router_full.astype(F32).T)
    ffn_in_grad = back[:, :width] + shared_in_grad[0].astype(F32) + router_in_grad
    ffn_gain_grad = jnp.sum(ffn_in_grad * residual * norm_two, axis=0)
    upstream_two = ffn_in_grad * gain_two_f
    residual_grad = (
        out_grad.astype(F32)
        + norm_two * upstream_two
        - residual * norm_two**3 * jnp.mean(upstream_two * residual, axis=-1, keepdims=True)
    )
    attn_grad_two = two(residual_grad.astype(BF)).reshape(2 * length, width)
    output_grad = product(context.T, attn_grad_two).astype(BF)
    output_grad = joined(half(output_grad, core, 1), swap(half(output_grad, 1 - core, 1)), core, 0)
    context_grad = by_head(product(attn_grad_two, output_half.T).astype(BF))
    value_grad = flat(mm("shqk,sqhd->skhd", probs_low, context_grad).astype(BF))
    probs_grad_att = mm("sqhd,skhd->shqk", context_grad, values)
    row_delta = jnp.sum(attn_probs * probs_grad_att, axis=-1, keepdims=True)
    scores_grad = (attn_probs * (probs_grad_att - row_delta)).astype(BF)
    query_grad = mm("shqk,skhd->sqhd", scores_grad, key_rot) * score_scale
    key_grad = mm("shqk,sqhd->skhd", scores_grad, query_rot) * score_scale
    query_pre_grad = flat(rotate(query_grad, cosine, -sine_part).astype(BF))
    key_pre_grad = flat(rotate(key_grad, cosine, -sine_part).astype(BF))
    query_wgrad = product(attn_in.T, query_pre_grad).astype(BF)
    key_wgrad = product(attn_in.T, key_pre_grad).astype(BF)
    value_wgrad = product(attn_in.T, value_grad).astype(BF)
    in_partial = (
        product(query_pre_grad, query_half.T)
        + product(key_pre_grad, key_half.T)
        + product(value_grad, value_half.T)
    ).reshape(2, length, width)
    attn_in_grad = in_partial[0] + swap(in_partial[1].astype(BF)).astype(F32)
    token_mine, norm_mine = token_f[0], norm_one[0]
    attn_gain_grad = jnp.sum(attn_in_grad * token_mine * norm_mine, axis=0)
    upstream_one = attn_in_grad * gain_one_f
    tokens_grad = (
        residual_grad
        + norm_mine * upstream_one
        - token_mine * norm_mine**3 * jnp.mean(upstream_one * token_mine, axis=-1, keepdims=True)
    )
    small_grads = jnp.concatenate(
        [router_grad, attn_gain_grad[:, None], ffn_gain_grad[:, None]], axis=1
    ).astype(BF)
    small_grads = jnp.pad(small_grads, ((0, 0), (0, 128 - small_grads.shape[1])))
    output_share = reduce_dp(shares(output_grad), "yx")
    value_share = reduce_dp(shares(value_wgrad), "xy")
    early_share = reduce_level(jnp.concatenate([output_share, value_share], axis=1))
    query_share = reduce_dp(shares(query_wgrad), "yx")
    key_share = reduce_dp(shares(jnp.concatenate([key_wgrad, small_grads], axis=1)), "xy")
    late_share = reduce_level(jnp.concatenate([query_share, key_share], axis=1))

    early_other, late_other, shared_other = swap(early_share), swap(late_share), swap(shared_share)
    column = lambda mine, other, i: joined(
        mine[:, i * wide : (i + 1) * wide], other[:, i * wide : (i + 1) * wide], core, 1
    ).astype(F32)
    small_sum = late_share[:, 2 * wide :].astype(F32) + late_other[:, 2 * wide :].astype(F32)
    unit_col = lambda i: joined(
        shared_share[:, i * narrow : (i + 1) * narrow].reshape(rows, dp, 1, part),
        shared_other[:, i * narrow : (i + 1) * narrow].reshape(rows, dp, 1, part),
        core,
        2,
    ).reshape(rows, hidden).astype(F32)
    down_rows = joined(
        shared_share[:, 2 * narrow :].reshape(part, width),
        shared_other[:, 2 * narrow :].reshape(part, width),
        core,
        0,
    ).astype(F32)

    stream_out = residual + moe_out
    stat_rms = jnp.stack(
        [
            jnp.sqrt(jnp.mean(attn_out * attn_out)),
            jnp.sqrt(jnp.mean(moe_out * moe_out)),
            jnp.sqrt(jnp.mean(stream_out * stream_out)),
        ]
    )[None, :]
    return (
        stream_out.astype(BF),
        tokens_grad.astype(BF),
        column(late_share, late_other, 0),
        column(late_share, late_other, 1),
        column(early_share, early_other, 1),
        column(early_share, early_other, 0),
        small_sum[:, experts],
        small_sum[:, experts + 1],
        small_sum[:, :experts],
        unit_col(0),
        unit_col(1),
        down_rows,
        *expert_shares,
        stat_rms,
    )


def solution(mesh):
    side = math.isqrt(mesh.shape["dp"])
    fine = Mesh(
        mesh.devices.reshape(side, side, mesh.shape["expert"] // 2, 2), ("y", "x", "z", "c")
    )
    whole = P(("y", "x", "z", "c"), None)
    dense = P(DP, None)
    routed = P(OWN, None, None)
    in_specs = (
        whole, dense, dense, dense, dense, P(DP), P(DP), dense, dense, dense, dense,
        routed, routed, routed, whole, P(("y", "x", "z", "c")), whole,
    )
    shares = P(OWN, DP, None)
    out_specs = (
        whole, whole, dense, dense, dense, dense, P(DP), P(DP), dense, dense, dense, dense,
        shares, shares, shares, whole,
    )
    return jax.shard_map(body, mesh=fine, in_specs=in_specs, out_specs=out_specs, check_vma=False)
```

time: 990 us -> 887 us (0.90)
  waiting for transfers between devices: 507 us -> 396 us
  matrix products: 177 us -> 80.3 us
  Pallas kernels: 0 us -> 79.7 us
  starting transfers between devices: 7.42 us -> 83.8 us
  local copies, waits for them, and re-layouts: 205 us -> 148 us
  other arithmetic: 63.5 us -> 82.5 us
  between operations: 19.2 us -> 6.72 us
    ppermute x15 -> x94, waiting for transfers between devices: 35.9 us -> 396 us  [shifted(): lax.ppermute(value, axis, [(i, (i + by) % size) for i in range(size)])]
    all_gather x4 -> x0, waiting for transfers between devices: 171 us -> none  [the longest x1 61 us: body(): lax.all_gather(jnp.concatenate([half(query_weight, core, 1), half(key_wei...]
    unnamed x12 -> x0, waiting for transfers between devices: 145 us -> none
    psum x1 -> x0, waiting for transfers between devices: 114 us -> none  [body(): attn_share = lax.psum(attn_share, 'z')]
    dot_general x19 -> x9, matrix products: 121 us -> 28.4 us  [mm(): return jnp.einsum(spec, first_arg, second_arg, preferred_element_type=F32)]
    pallas_call x0 -> x4, Pallas kernels: none -> 79.7 us  [the longest x2 69.4 us: expert_call(): pl.pallas_call(functools.partial(expert_kernel, count, width, capacity, e...]
    ppermute x15 -> x94, starting transfers between devices: 6.64 us -> 83.8 us  [shifted(): lax.ppermute(value, axis, [(i, (i + by) % size) for i in range(size)])]
    unnamed x234 -> x305, local copies, waits for them, and re-layouts: 69.1 us -> 17.1 us
  transfers between devices with their start and end apart: 24 -> 94, of which waited for: 11 -> 33; matrix products, arithmetic and copies ran while one was open for 27% -> 30% of each run, Pallas kernels for 0% -> 9%
where the time goes in v3:
time: 887 us; the launch traced here: 877 us
  waiting for transfers between devices  396 us (45%)
  local copies, waits for them, and re-layouts  148 us (17%)
  starting transfers between devices  83.8 us (9%)
  other arithmetic  82.5 us (9%)
  matrix products  80.3 us (9%)
  Pallas kernels  79.7 us (9%)
    ppermute x94, waiting for transfers between devices, shifted(): lax.ppermute(value, axis, [(i, (i + by) % size) for i in range(size)])  396 us
    ppermute x94, starting transfers between devices, shifted(): lax.ppermute(value, axis, [(i, (i + by) % size) for i in range(size)])  83.8 us
    pallas_call x2, Pallas kernels, expert_call(): pl.pallas_call(functools.partial(expert_kernel, count, width, capacity, e...  69.4 us
    dot_general x22, matrix products, product(): return jnp.dot(first_arg, second_arg, preferred_element_type=F32)  47.3 us
    dot_general x9, matrix products, mm(): return jnp.einsum(spec, first_arg, second_arg, preferred_element_type=F32)  28.4 us
    squeeze x29, local copies, waits for them, and re-layouts, pick(): lax.dynamic_index_in_dim(value, index % value.shape[axis], axis, False)  23 us
  transfers between devices with their start and end apart: 94, of which 33 were waited for; matrix products, arithmetic and copies ran while one was open for 30% of the time, Pallas kernels for 9%

profile of v3, /device:TPU:0, one launch (start us, length us, event | category | flops | bytes accessed | tf_op | source)
XLA Modules:
  0.0 876.6 jit_solution(9736901500806646353)
XLA Ops:
  3.7 5.1 collective-permute-start.21
  48.6 22.2 %collective-permute-done.19.refs_4_ = bf16[256,1408]{1,0:T(8,128)(2,1)} collective-permute-done((bf16[256,1408]{1,0:T(8,128)(2,1)}, bf16[256,1408]{1,0:T(8,128)(2,1)}, u32[]{:S(2)}, u32[]{:S(2)}) %collective-permute-start.19) | collective-permute-done | bytes 720928 | tf_op jit(solution)/shard_map/ppermute | solution.py:241
  81.7 7.0 collective-permute-done.4.refs_5_
  91.7 9.0 %collective-permute-done.6.refs_7_ = bf16[160,2048]{1,0:T(8,128)(2,1)} collective-permute-done((bf16[160,2048]{1,0:T(8,128)(2,1)}, bf16[160,2048]{1,0:T(8,128)(2,1)}, u32[]{:S(2)}, u32[]{:S(2)}) %collective-permute-start.6) | collective-permute-done | bytes 655392 | tf_op jit(solution)/shard_map/ppermute | solution.py:241
  103.5 5.1 place.2
  150.2 11.2 %collective-permute-done.8.refs_1_ = bf16[160,1984]{1,0:T(8,128)(2,1)} collective-permute-done((bf16[160,1984]{1,0:T(8,128)(2,1)}, bf16[160,1984]{1,0:T(8,128)(2,1)}, u32[]{:S(2)}, u32[]{:S(2)}) %collective-permute-start.8) | collective-permute-done | bytes 634912 | tf_op jit(solution)/shard_map/ppermute | solution.py:241
  161.4 13.5 %collective-permute-done.10.refs_3_ = bf16[160,1984]{1,0:T(8,128)(2,1)} collective-permute-done((bf16[160,1984]{1,0:T(8,128)(2,1)}, bf16[160,1984]{1,0:T(8,128)(2,1)}, u32[]{:S(2)}, u32[]{:S(2)}) %collective-permute-start.10) | collective-permute-done | bytes 634912 | tf_op jit(solution)/shard_map/ppermute | solution.py:241
  174.9 5.2 place.3
  244.9 24.3 %collective-permute-done.31.refs_0_ = bf16[256,1408]{1,0:T(8,128)(2,1)} collective-permute-done((bf16[256,1408]{1,0:T(8,128)(2,1)}, bf16[256,1408]{1,0:T(8,128)(2,1)}, u32[]{:S(2)}, u32[]{:S(2)}) %collective-permute-start.31) | collective-permute-done | bytes 720928 | tf_op jit(solution)/shard_map/ppermute | solution.py:241
  278.3 34.5 %experts.2 = (bf16[2,256,1408]{2,1,0:T(8,128)(2,1)}, bf16[2,256,1408]{2,1,0:T(8,128)(2,1)}, bf16[2,256,1280]{2,1,0:T(8,128)(2,1)}, bf16[2,256,1280]{2,1,0:T(8,12...) custom-call(s32[1]{0:T(128)} %bitcast.23.me_ref, ...), custom_call_target="tpu_custom_call" | custom-call | flops 16441671680 | bytes 62914560 | tf_op jit(solution)/shard_map/experts/pallas_call | solution.py:132
  317.9 34.9 %experts.3 = (bf16[2,256,1408]{2,1,0:T(8,128)(2,1)}, bf16[2,256,1408]{2,1,0:T(8,128)(2,1)}, bf16[2,256,1280]{2,1,0:T(8,128)(2,1)}, bf16[2,256,1280]{2,1,0:T(8,12...) custom-call(s32[1]{0:T(128)} %bitcast.23.me_ref, ...), custom_call_target="tpu_custom_call", output_to_operand_aliasing={{4}: (13, {}), {5}: (14, {}), {6}: (15, {}), {7}: (16, {}),... | custom-call | flops 16441671680 | bytes 62914560 | tf_op jit(solution)/shard_map/experts/pallas_call | solution.py:132
  356.7 9.1 %convolution_convert_fusion.2 = bf16[2,1280,896]{2,1,0:T(8,128)(2,1)S(1)} fusion(bf16[2,1024,1280]{2,1,0:T(8,128)(2,1)} %get-tuple-element.55, bf16[2,1024,896]{2,1,0:T(8,128)(2,1)S(1)} %copy-done.128), kind=kOutput, calls=%fused_computation.3 | convolution fusion | flops 4699914240 | bytes 13500416 | tf_op jit(solution)/shard_map/erd,erf->edf/dot_general | solution.py:195
  365.8 6.0 convolution_convert_fusion.1
  376.9 7.6 convolution_convert_fusion
  412.2 9.6 %collective-permute-done.76 = bf16[80,1344]{1,0:T(8,128)(2,1)S(1)} collective-permute-done((bf16[80,1344]{1,0:T(8,128)(2,1)S(1)}, bf16[80,1344]{1,0:T(8,128)(2,1)S(1)}, u32[]{:S(2)}, u32[]{:S(2)}) %collective-permute-start.76) | collective-permute-done | bytes 215072 | tf_op jit(solution)/shard_map/ppermute | solution.py:241
  430.0 11.8 %collective-permute-done.79 = bf16[80,1344]{1,0:T(8,128)(2,1)S(1)} collective-permute-done((bf16[80,1344]{1,0:T(8,128)(2,1)S(1)}, bf16[80,1344]{1,0:T(8,128)(2,1)S(1)}, u32[]{:S(2)}, u32[]{:S(2)}) %collective-permute-start.79) | collective-permute-done | bytes 215072 | tf_op jit(solution)/shard_map/ppermute | solution.py:241
  441.8 9.2 %collective-permute-done.80 = bf16[80,1344]{1,0:T(8,128)(2,1)S(1)} collective-permute-done((bf16[80,1344]{1,0:T(8,128)(2,1)S(1)}, bf16[80,1344]{1,0:T(8,128)(2,1)S(1)}, u32[]{:S(2)}, u32[]{:S(2)}) %collective-permute-start.80) | collective-permute-done | bytes 215072 | tf_op jit(solution)/shard_map/ppermute | solution.py:241
  473.6 19.6 %collective-permute-done.86 = bf16[2,320,896]{2,1,0:T(8,128)(2,1)S(1)} collective-permute-done((bf16[2,320,896]{2,1,0:T(8,128)(2,1)}, bf16[2,320,896]{2,1,0:T(8,128)(2,1)S(1)}, u32[]{:S(2)}, u32[]{:S(2)}) %collective-permute-start.86) | collective-permute-done | bytes 1146912 | tf_op jit(solution)/shard_map/ppermute | solution.py:241
  498.0 19.7 %collective-permute-done.82 = bf16[2,320,896]{2,1,0:T(8,128)(2,1)S(1)} collective-permute-done((bf16[2,320,896]{2,1,0:T(8,128)(2,1)S(1)}, bf16[2,320,896]{2,1,0:T(8,128)(2,1)S(1)}, u32[]{:S(2)}, u32[]{:S(2)}) %collective-permute-start.82) | collective-permute-done | bytes 1146912 | tf_op jit(solution)/shard_map/ppermute | solution.py:241
  519.5 22.2 %collective-permute-done.90 = bf16[2,224,1280]{2,1,0:T(8,128)(2,1)S(1)} collective-permute-done((bf16[2,224,1280]{2,1,0:T(8,128)(2,1)S(1)}, bf16[2,224,1280]{2,1,0:T(8,128)(2,1)S(1)}, u32[]{:S(2)}, u32[]{:S(2)}) %collective-permute-start.90) | collective-permute-done | bytes 1146912 | tf_op jit(solution)/shard_map/ppermute | solution.py:241
  571.8 34.4 %collective-permute-done.36 = bf16[256,1408]{1,0:T(8,128)(2,1)} collective-permute-done((bf16[256,1408]{1,0:T(8,128)(2,1)}, bf16[256,1408]{1,0:T(8,128)(2,1)}, u32[]{:S(2)}, u32[]{:S(2)}) %collective-permute-start.36) | collective-permute-done | bytes 720928 | tf_op jit(solution)/shard_map/ppermute | solution.py:241
  613.2 20.0 %collective-permute-done.91 = bf16[224,1280]{1,0:T(8,128)(2,1)S(1)} collective-permute-done((bf16[224,1280]{1,0:T(8,128)(2,1)}, bf16[224,1280]{1,0:T(8,128)(2,1)S(1)}, u32[]{:S(2)}, u32[]{:S(2)}) %collective-permute-start.91) | collective-permute-done | bytes 573472 | tf_op jit(solution)/shard_map/ppermute | solution.py:241
  636.5 12.5 %collective-permute-done.85 = bf16[320,896]{1,0:T(8,128)(2,1)S(1)} collective-permute-done((bf16[320,896]{1,0:T(8,128)(2,1)S(1)}, bf16[320,896]{1,0:T(8,128)(2,1)S(1)}, u32[]{:S(2)}, u32[]{:S(2)}) %collective-permute-start.85) | collective-permute-done | bytes 573472 | tf_op jit(solution)/shard_map/ppermute | solution.py:241
  649.3 9.8 %collective-permute-done.93 = bf16[224,1280]{1,0:T(8,128)(2,1)S(1)} collective-permute-done((bf16[224,1280]{1,0:T(8,128)(2,1)S(1)}, bf16[224,1280]{1,0:T(8,128)(2,1)S(1)}, u32[]{:S(2)}, u32[]{:S(2)}) %collective-permute-start.93) | collective-permute-done | bytes 573472 | tf_op jit(solution)/shard_map/ppermute | solution.py:241
  659.3 31.2 %collective-permute-done.41 = bf16[256,1280]{1,0:T(8,128)(2,1)S(1)} collective-permute-done((bf16[256,1280]{1,0:T(8,128)(2,1)S(1)}, bf16[256,1280]{1,0:T(8,128)(2,1)S(1)}, u32[]{:S(2)}, u32[]{:S(2)}) %collective-permute-start.41) | collective-permute-done | bytes 655392 | tf_op jit(solution)/shard_map/ppermute | solution.py:241
  752.5 27.3 %collective-permute-done.47 = bf16[320,640]{1,0:T(8,128)(2,1)S(1)} collective-permute-done((bf16[320,640]{1,0:T(8,128)(2,1)S(1)}, bf16[320,640]{1,0:T(8,128)(2,1)S(1)}, u32[]{:S(2)}, u32[]{:S(2)}) %collective-permute-start.47) | collective-permute-done | bytes 409632 | tf_op jit(solution)/shard_map/ppermute | solution.py:241
  782.6 8.7 collective-permute-done.59
  801.3 9.9 %collective-permute-start.51 = (bf16[80,1408]{1,0:T(8,128)(2,1)S(1)}, bf16[80,1408]{1,0:T(8,128)(2,1)S(1)}, u32[]{:S(2)}, u32[]{:S(2)}) collective-permute-start(bf16[80,1408]{1,0:T(8,128)(2,1)S(1)} %get-tuple-element.227), channel_id=1, source_target_pairs={{0,4},{2,6},{4,0},{6,2},{1,5},{3,7},{5,1},{7,3},{8,12},{10,14},{12... | collective-permute-start | bytes 675848 | tf_op jit(solution)/shard_map/ppermute | solution.py:241
  811.2 15.9 %collective-permute-done.63 = bf16[80,1280]{1,0:T(8,128)(2,1)S(1)} collective-permute-done((bf16[80,1280]{1,0:T(8,128)(2,1)S(1)}, bf16[80,1280]{1,0:T(8,128)(2,1)S(1)}, u32[]{:S(2)}, u32[]{:S(2)}) %collective-permute-start.63) | collective-permute-done | bytes 204832 | tf_op jit(solution)/shard_map/ppermute | solution.py:241
  831.1 10.2 %collective-permute-done.51 = bf16[80,1408]{1,0:T(8,128)(2,1)S(1)} collective-permute-done((bf16[80,1408]{1,0:T(8,128)(2,1)S(1)}, bf16[80,1408]{1,0:T(8,128)(2,1)S(1)}, u32[]{:S(2)}, u32[]{:S(2)}) %collective-permute-start.51) | collective-permute-done | bytes 225312 | tf_op jit(solution)/shard_map/ppermute | solution.py:241
  848.9 6.5 collective-permute-done.66
  855.7 12.8 %collective-permute-done.53 = bf16[80,1408]{1,0:T(8,128)(2,1)S(1)} collective-permute-done((bf16[80,1408]{1,0:T(8,128)(2,1)S(1)}, bf16[80,1408]{1,0:T(8,128)(2,1)S(1)}, u32[]{:S(2)}, u32[]{:S(2)}) %collective-permute-start.53) | collective-permute-done | bytes 225312 | tf_op jit(solution)/shard_map/ppermute | solution.py:241
  (729 shorter events, 384.0 us)
Async XLA Ops:
  3.7 41.8 %collective-permute-start.21 = (bf16[256,1408]{1,0:T(8,128)(2,1)}, bf16[256,1408]{1,0:T(8,128)(2,1)}, u32[]{:S(2)}, u32[]{:S(2)}) collective-permute-start(bf16[256,1408]{1,0:T(8,128)(2,1)} %pad_maximum_fusion.6.refs_4_), channel_id=1, source_target_pairs={{0,6},{2,0},{4,2},{6,4},{1,7},{3,1},{5,3},{7,5},{8,14},{10,8},{12,... | collective-permute-start | bytes 2162696 | tf_op jit(solution)/shard_map/ppermute | solution.py:241
  8.8 61.9 %collective-permute-start.19 = (bf16[256,1408]{1,0:T(8,128)(2,1)}, bf16[256,1408]{1,0:T(8,128)(2,1)}, u32[]{:S(2)}, u32[]{:S(2)}) collective-permute-start(bf16[256,1408]{1,0:T(8,128)(2,1)} %pad_maximum_fusion.6.refs_4_), channel_id=1, source_target_pairs={{0,4},{2,6},{4,0},{6,2},{1,5},{3,7},{5,1},{7,3},{8,12},{10,14},{12... | collective-permute-start | bytes 2162696 | tf_op jit(solution)/shard_map/ppermute | solution.py:241
  8.8 67.0 %collective-permute-start.17 = (bf16[256,1408]{1,0:T(8,128)(2,1)}, bf16[256,1408]{1,0:T(8,128)(2,1)}, u32[]{:S(2)}, u32[]{:S(2)}) collective-permute-start(bf16[256,1408]{1,0:T(8,128)(2,1)} %pad_maximum_fusion.6.refs_4_), channel_id=1, source_target_pairs={{0,2},{2,4},{4,6},{6,0},{1,3},{3,5},{5,7},{7,1},{8,10},{10,12},{12... | collective-permute-start | bytes 2162696 | tf_op jit(solution)/shard_map/ppermute | solution.py:241
  79.4 63.9 %collective-permute-start.22 = (bf16[256,1408]{1,0:T(8,128)(2,1)}, bf16[256,1408]{1,0:T(8,128)(2,1)}, u32[]{:S(2)}, u32[]{:S(2)}) collective-permute-start(bf16[256,1408]{1,0:T(8,128)(2,1)} %collective-permute-done.21.refs_6_), channel_id=1, source_target_pairs={{0,1},{1,0},{2,3},{3,2},{4,5},{5,4},{6,7},{7,6},{8,9},{9,8},{10,11... | collective-permute-start | bytes 2162696 | tf_op jit(solution)/shard_map/ppermute | solution.py:241
  88.7 93.1 %collective-permute-start.20 = (bf16[256,1408]{1,0:T(8,128)(2,1)}, bf16[256,1408]{1,0:T(8,128)(2,1)}, u32[]{:S(2)}, u32[]{:S(2)}) collective-permute-start(bf16[256,1408]{1,0:T(8,128)(2,1)} %collective-permute-done.19.refs_4_), channel_id=1, source_target_pairs={{0,1},{1,0},{2,3},{3,2},{4,5},{5,4},{6,7},{7,6},{8,9},{9,8},{10,11... | collective-permute-start | bytes 2162696 | tf_op jit(solution)/shard_map/ppermute | solution.py:241
  143.3 39.6 %collective-permute-start.18 = (bf16[256,1408]{1,0:T(8,128)(2,1)}, bf16[256,1408]{1,0:T(8,128)(2,1)}, u32[]{:S(2)}, u32[]{:S(2)}) collective-permute-start(bf16[256,1408]{1,0:T(8,128)(2,1)} %collective-permute-done.17.refs_6_), channel_id=1, source_target_pairs={{0,1},{1,0},{2,3},{3,2},{4,5},{5,4},{6,7},{7,6},{8,9},{9,8},{10,11... | collective-permute-start | bytes 2162696 | tf_op jit(solution)/shard_map/ppermute | solution.py:241
  206.6 62.6 %collective-permute-start.31 = (bf16[256,1408]{1,0:T(8,128)(2,1)}, bf16[256,1408]{1,0:T(8,128)(2,1)}, u32[]{:S(2)}, u32[]{:S(2)}) collective-permute-start(bf16[256,1408]{1,0:T(8,128)(2,1)} %concatenate.112.refs_0_), channel_id=1, source_target_pairs={{0,4},{2,6},{4,0},{6,2},{1,5},{3,7},{5,1},{7,3},{8,12},{10,14},{12... | collective-permute-start | bytes 2162696 | tf_op jit(solution)/shard_map/ppermute | solution.py:241
  206.6 62.6 %collective-permute-start.24 = (bf16[256,1408]{1,0:T(8,128)(2,1)}, bf16[256,1408]{1,0:T(8,128)(2,1)}, u32[]{:S(2)}, u32[]{:S(2)}) collective-permute-start(bf16[256,1408]{1,0:T(8,128)(2,1)} %concatenate.112.refs_0_), channel_id=1, source_target_pairs={{0,2},{2,4},{4,6},{6,0},{1,3},{3,5},{5,7},{7,1},{8,10},{10,12},{12... | collective-permute-start | bytes 2162696 | tf_op jit(solution)/shard_map/ppermute | solution.py:241
  230.1 39.6 %collective-permute-start.73 = (bf16[2,320,448]{2,1,0:T(8,128)(2,1)}, bf16[2,320,448]{2,1,0:T(8,128)(2,1)}, u32[]{:S(2)}, u32[]{:S(2)}) collective-permute-start(bf16[2,320,448]{2,1,0:T(8,128)(2,1)} %dynamic-slice_bitcast_fusion.10), channel_id=1, source_target_pairs={{0,16},{16,0},{1,17},{17,1},{2,18},{18,2},{3,19},{19,3},{4,20},{20... | collective-permute-start | bytes 1720328 | tf_op jit(solution)/shard_map/ppermute | solution.py:241
  233.1 38.8 %collective-permute-start.71 = (bf16[2,320,448]{2,1,0:T(8,128)(2,1)}, bf16[2,320,448]{2,1,0:T(8,128)(2,1)}, u32[]{:S(2)}, u32[]{:S(2)}) collective-permute-start(bf16[2,320,448]{2,1,0:T(8,128)(2,1)} %dynamic-slice_bitcast_fusion.11), channel_id=1, source_target_pairs={{0,8},{8,0},{1,9},{9,1},{2,10},{10,2},{3,11},{11,3},{4,12},{12,4},... | collective-permute-start | bytes 1720328 | tf_op jit(solution)/shard_map/ppermute | solution.py:241
  269.2 48.2 %collective-permute-start.34 = (bf16[256,1408]{1,0:T(8,128)(2,1)}, bf16[256,1408]{1,0:T(8,128)(2,1)}, u32[]{:S(2)}, u32[]{:S(2)}) collective-permute-start(bf16[256,1408]{1,0:T(8,128)(2,1)} %collective-permute-done.33.refs_2_), channel_id=1, source_target_pairs={{0,1},{1,0},{2,3},{3,2},{4,5},{5,4},{6,7},{7,6},{8,9},{9,8},{10,11... | collective-permute-start | bytes 2162696 | tf_op jit(solution)/shard_map/ppermute | solution.py:241
  269.2 48.2 %collective-permute-start.32 = (bf16[256,1408]{1,0:T(8,128)(2,1)}, bf16[256,1408]{1,0:T(8,128)(2,1)}, u32[]{:S(2)}, u32[]{:S(2)}) collective-permute-start(bf16[256,1408]{1,0:T(8,128)(2,1)} %collective-permute-done.31.refs_0_), channel_id=1, source_target_pairs={{0,1},{1,0},{2,3},{3,2},{4,5},{5,4},{6,7},{7,6},{8,9},{9,8},{10,11... | collective-permute-start | bytes 2162696 | tf_op jit(solution)/shard_map/ppermute | solution.py:241
  271.9 120.5 %collective-permute-start.74 = (bf16[320,448]{1,0:T(8,128)(2,1)}, bf16[320,448]{1,0:T(8,128)(2,1)S(1)}, u32[]{:S(2)}, u32[]{:S(2)}) collective-permute-start(bf16[320,448]{1,0:T(8,128)(2,1)} %dynamic-slice_bitcast_fusion.23), channel_id=1, source_target_pairs={{0,8},{8,0},{1,9},{9,1},{2,10},{10,2},{3,11},{11,3},{4,12},{12,4},... | collective-permute-start | bytes 860168 | tf_op jit(solution)/shard_map/ppermute | solution.py:241
  274.5 118.1 %collective-permute-start.72 = (bf16[320,448]{1,0:T(8,128)(2,1)}, bf16[320,448]{1,0:T(8,128)(2,1)}, u32[]{:S(2)}, u32[]{:S(2)}) collective-permute-start(bf16[320,448]{1,0:T(8,128)(2,1)} %dynamic-slice_bitcast_fusion.24), channel_id=1, source_target_pairs={{0,16},{16,0},{1,17},{17,1},{2,18},{18,2},{3,19},{19,3},{4,20},{20... | collective-permute-start | bytes 860168 | tf_op jit(solution)/shard_map/ppermute | solution.py:241
  276.8 117.9 %collective-permute-start.70 = (bf16[320,448]{1,0:T(8,128)(2,1)}, bf16[320,448]{1,0:T(8,128)(2,1)}, u32[]{:S(2)}, u32[]{:S(2)}) collective-permute-start(bf16[320,448]{1,0:T(8,128)(2,1)} %dynamic-slice_bitcast_fusion.25), channel_id=1, source_target_pairs={{0,8},{8,0},{1,9},{9,1},{2,10},{10,2},{3,11},{11,3},{4,12},{12,4},... | collective-permute-start | bytes 860168 | tf_op jit(solution)/shard_map/ppermute | solution.py:241
  317.4 341.9 %collective-permute-start.26 = (bf16[256,1280]{1,0:T(8,128)(2,1)}, bf16[256,1280]{1,0:T(8,128)(2,1)}, u32[]{:S(2)}, u32[]{:S(2)}) collective-permute-start(bf16[256,1280]{1,0:T(8,128)(2,1)} %slice_add_fusion.4), channel_id=1, source_target_pairs={{0,1},{1,0},{2,3},{3,2},{4,5},{5,4},{6,7},{7,6},{8,9},{9,8},{10,11... | collective-permute-start | bytes 1966088 | tf_op jit(solution)/shard_map/ppermute | solution.py:241
  317.4 147.4 %collective-permute-start.27 = (bf16[256,1280]{1,0:T(8,128)(2,1)}, bf16[256,1280]{1,0:T(8,128)(2,1)}, u32[]{:S(2)}, u32[]{:S(2)}) collective-permute-start(bf16[256,1280]{1,0:T(8,128)(2,1)} %slice_bitcast_fusion.11), channel_id=1, source_target_pairs={{0,1},{1,0},{2,3},{3,2},{4,5},{5,4},{6,7},{7,6},{8,9},{9,8},{10,11... | collective-permute-start | bytes 1966088 | tf_op jit(solution)/shard_map/ppermute | solution.py:241
  408.3 62.4 %collective-permute-start.29 = (bf16[256,1408]{1,0:T(8,128)(2,1)}, bf16[256,1408]{1,0:T(8,128)(2,1)}, u32[]{:S(2)}, u32[]{:S(2)}) collective-permute-start(bf16[256,1408]{1,0:T(8,128)(2,1)} %get-tuple-element.194), channel_id=1, source_target_pairs={{0,1},{1,0},{2,3},{3,2},{4,5},{5,4},{6,7},{7,6},{8,9},{9,8},{10,11... | collective-permute-start | bytes 2162696 | tf_op jit(solution)/shard_map/ppermute | solution.py:241
  412.2 48.8 %collective-permute-start.40 = (bf16[256,1280]{1,0:T(8,128)(2,1)}, bf16[256,1280]{1,0:T(8,128)(2,1)}, u32[]{:S(2)}, u32[]{:S(2)}) collective-permute-start(bf16[256,1280]{1,0:T(8,128)(2,1)} %get-tuple-element.206), channel_id=1, source_target_pairs={{0,1},{1,0},{2,3},{3,2},{4,5},{5,4},{6,7},{7,6},{8,9},{9,8},{10,11... | collective-permute-start | bytes 1966088 | tf_op jit(solution)/shard_map/ppermute | solution.py:241
  468.5 102.4 %collective-permute-start.28 = (bf16[256,1408]{1,0:T(8,128)(2,1)}, bf16[256,1408]{1,0:T(8,128)(2,1)}, u32[]{:S(2)}, u32[]{:S(2)}) collective-permute-start(bf16[256,1408]{1,0:T(8,128)(2,1)} %fusion.83), channel_id=1, source_target_pairs={{0,1},{1,0},{2,3},{3,2},{4,5},{5,4},{6,7},{7,6},{8,9},{9,8},{10,11... | collective-permute-start | bytes 2162696 | tf_op jit(solution)/shard_map/ppermute | solution.py:241
  470.7 47.0 %collective-permute-start.82 = (bf16[2,320,896]{2,1,0:T(8,128)(2,1)S(1)}, bf16[2,320,896]{2,1,0:T(8,128)(2,1)S(1)}, u32[]{:S(2)}, u32[]{:S(2)}) collective-permute-start(bf16[2,320,896]{2,1,0:T(8,128)(2,1)S(1)} %copy-done.86), channel_id=1, source_target_pairs={{0,16},{16,0},{1,17},{17,1},{2,18},{18,2},{3,19},{19,3},{4,20},{20... | collective-permute-start | bytes 3440648 | tf_op jit(solution)/shard_map/ppermute | solution.py:241
  493.1 48.6 %collective-permute-start.90 = (bf16[2,224,1280]{2,1,0:T(8,128)(2,1)S(1)}, bf16[2,224,1280]{2,1,0:T(8,128)(2,1)S(1)}, u32[]{:S(2)}, u32[]{:S(2)}) collective-permute-start(bf16[2,224,1280]{2,1,0:T(8,128)(2,1)S(1)} %copy-done.89), channel_id=1, source_target_pairs={{0,16},{16,0},{1,17},{17,1},{2,18},{18,2},{3,19},{19,3},{4,20},{20... | collective-permute-start | bytes 3440648 | tf_op jit(solution)/shard_map/ppermute | solution.py:241
  496.2 46.8 %collective-permute-start.84 = (bf16[2,320,896]{2,1,0:T(8,128)(2,1)S(1)}, bf16[2,320,896]{2,1,0:T(8,128)(2,1)S(1)}, u32[]{:S(2)}, u32[]{:S(2)}) collective-permute-start(bf16[2,320,896]{2,1,0:T(8,128)(2,1)S(1)} %copy-done.85), channel_id=1, source_target_pairs={{0,8},{8,0},{1,9},{9,1},{2,10},{10,2},{3,11},{11,3},{4,12},{12,4},... | collective-permute-start | bytes 3440648 | tf_op jit(solution)/shard_map/ppermute | solution.py:241
  547.4 58.7 %collective-permute-start.36 = (bf16[256,1408]{1,0:T(8,128)(2,1)}, bf16[256,1408]{1,0:T(8,128)(2,1)}, u32[]{:S(2)}, u32[]{:S(2)}) collective-permute-start(bf16[256,1408]{1,0:T(8,128)(2,1)} %get-tuple-element.195), channel_id=1, source_target_pairs={{0,4},{2,6},{4,0},{6,2},{1,5},{3,7},{5,1},{7,3},{8,12},{10,14},{12... | collective-permute-start | bytes 2162696 | tf_op jit(solution)/shard_map/ppermute | solution.py:241
  548.7 58.0 %collective-permute-start.38 = (bf16[256,1408]{1,0:T(8,128)(2,1)}, bf16[256,1408]{1,0:T(8,128)(2,1)}, u32[]{:S(2)}, u32[]{:S(2)}) collective-permute-start(bf16[256,1408]{1,0:T(8,128)(2,1)} %get-tuple-element.196), channel_id=1, source_target_pairs={{0,2},{2,4},{4,6},{6,0},{1,3},{3,5},{5,7},{7,1},{8,10},{10,12},{12... | collective-permute-start | bytes 2162696 | tf_op jit(solution)/shard_map/ppermute | solution.py:241
  570.8 64.0 %collective-permute-start.87 = (bf16[320,896]{1,0:T(8,128)(2,1)}, bf16[320,896]{1,0:T(8,128)(2,1)S(1)}, u32[]{:S(2)}, u32[]{:S(2)}) collective-permute-start(bf16[320,896]{1,0:T(8,128)(2,1)} %dynamic-slice_bitcast_fusion.16), channel_id=1, source_target_pairs={{0,8},{8,0},{1,9},{9,1},{2,10},{10,2},{3,11},{11,3},{4,12},{12,4},... | collective-permute-start | bytes 1720328 | tf_op jit(solution)/shard_map/ppermute | solution.py:241
  571.4 64.2 %collective-permute-start.89 = (bf16[320,896]{1,0:T(8,128)(2,1)}, bf16[320,896]{1,0:T(8,128)(2,1)S(1)}, u32[]{:S(2)}, u32[]{:S(2)}) collective-permute-start(bf16[320,896]{1,0:T(8,128)(2,1)} %dynamic-slice_bitcast_fusion.15), channel_id=1, source_target_pairs={{0,16},{16,0},{1,17},{17,1},{2,18},{18,2},{3,19},{19,3},{4,20},{20... | collective-permute-start | bytes 1720328 | tf_op jit(solution)/shard_map/ppermute | solution.py:241
  635.9 54.6 %collective-permute-start.41 = (bf16[256,1280]{1,0:T(8,128)(2,1)S(1)}, bf16[256,1280]{1,0:T(8,128)(2,1)S(1)}, u32[]{:S(2)}, u32[]{:S(2)}) collective-permute-start(bf16[256,1280]{1,0:T(8,128)(2,1)S(1)} %copy-done.97), channel_id=1, source_target_pairs={{0,4},{2,6},{4,0},{6,2},{1,5},{3,7},{5,1},{7,3},{8,12},{10,14},{12... | collective-permute-start | bytes 1966088 | tf_op jit(solution)/shard_map/ppermute | solution.py:241
  649.0 41.5 %collective-permute-start.43 = (bf16[256,1280]{1,0:T(8,128)(2,1)S(1)}, bf16[256,1280]{1,0:T(8,128)(2,1)S(1)}, u32[]{:S(2)}, u32[]{:S(2)}) collective-permute-start(bf16[256,1280]{1,0:T(8,128)(2,1)S(1)} %copy-done.96), channel_id=1, source_target_pairs={{0,2},{2,4},{4,6},{6,0},{1,3},{3,5},{5,7},{7,1},{8,10},{10,12},{12... | collective-permute-start | bytes 1966088 | tf_op jit(solution)/shard_map/ppermute | solution.py:241
  738.5 42.4 %collective-permute-start.48 = (bf16[2,320,768]{2,1,0:T(8,128)(2,1)S(1)}, bf16[2,320,768]{2,1,0:T(8,128)(2,1)S(1)}, u32[]{:S(2)}, u32[]{:S(2)}) collective-permute-start(bf16[2,320,768]{2,1,0:T(8,128)(2,1)S(1)} %dynamic-slice_bitcast_fusion.6), channel_id=1, source_target_pairs={{0,8},{8,0},{1,9},{9,1},{2,10},{10,2},{3,11},{11,3},{4,12},{12,4},... | collective-permute-start | bytes 2949128 | tf_op jit(solution)/shard_map/ppermute | solution.py:241
  742.2 37.7 %collective-permute-start.58 = (bf16[2,320,640]{2,1,0:T(8,128)(2,1)S(1)}, bf16[2,320,640]{2,1,0:T(8,128)(2,1)S(1)}, u32[]{:S(2)}, u32[]{:S(2)}) collective-permute-start(bf16[2,320,640]{2,1,0:T(8,128)(2,1)S(1)} %dynamic-slice_bitcast_fusion.8), channel_id=1, source_target_pairs={{0,16},{16,0},{1,17},{17,1},{2,18},{18,2},{3,19},{19,3},{4,20},{20... | collective-permute-start | bytes 2457608 | tf_op jit(solution)/shard_map/ppermute | solution.py:241
  801.3 40.0 %collective-permute-start.51 = (bf16[80,1408]{1,0:T(8,128)(2,1)S(1)}, bf16[80,1408]{1,0:T(8,128)(2,1)S(1)}, u32[]{:S(2)}, u32[]{:S(2)}) collective-permute-start(bf16[80,1408]{1,0:T(8,128)(2,1)S(1)} %get-tuple-element.227), channel_id=1, source_target_pairs={{0,4},{2,6},{4,0},{6,2},{1,5},{3,7},{5,1},{7,3},{8,12},{10,14},{12... | collective-permute-start | bytes 675848 | tf_op jit(solution)/shard_map/ppermute | solution.py:241
  (200 other events, 2605.1 us)

commit v4 on v3

--- a/solution.py
+++ b/solution.py
@@ -28,7 +28,8 @@
     rows_refs = refs[:count]
     grads_refs = refs[count : 2 * count]
     gate_ref, up_ref, down_ref = refs[2 * count : 2 * count + 3]
-    in_mine, in_other, res_mine, res_other, xin, rgrad, hid, ggrad, ugrad = refs[-14:-5]
+    sums = refs[-10 - count : -10]
+    xin, rgrad, hid, ggrad, ugrad = refs[-10:-5]
     ograd, in_ext, res_low, in_acc, out_acc = refs[-5:]
     step = pl.program_id(0)
     expert = me_ref[0] * EXP_DEV + step
@@ -89,7 +90,6 @@
         )
         back = dot(low, in_ext[area, :], TN)
         result = dot((hot * gates).astype(BF), res_low[area, :], TN)
-        in_out, res_out = ((in_mine, res_mine), (in_other, res_other))[piece % 2]
 
         @pl.when(step == 0)
         def _():
@@ -98,8 +98,9 @@
 
         @pl.when(step == EXP_DEV - 1)
         def _():
-            in_out[piece // 2] = (in_acc[piece] + back).astype(BF)
-            res_out[piece // 2] = (out_acc[piece] + result).astype(BF)
+            wide = back.shape[1]
+            sums[piece][:, :wide] = (in_acc[piece] + back).astype(BF)
+            sums[piece][:, wide:] = (out_acc[piece] + result).astype(BF)
 
 
 def expert_call(me, slots, rows, grads, gate, up, down, owners, first, carried=None):
@@ -125,10 +126,10 @@
     alias = {}
     if carried is not None:
         for i, value in enumerate(carried):
-            alias[len(args)] = 4 + i
+            alias[len(args)] = count + i
             args.append(value)
             in_specs.append(pl.BlockSpec(memory_space=pl.ANY))
-    sums = [(count // 2, length, wide)] * 2 + [(count // 2, length, width)] * 2
+    sums = [(length, wide + width)] * count
     return pl.pallas_call(
         functools.partial(expert_kernel, count, width, capacity, experts, min(512, block)),
         out_shape=[jax.ShapeDtypeStruct(shape, BF) for shape in sums]
@@ -260,8 +261,10 @@
     return lax.dynamic_index_in_dim(value, index % value.shape[axis], axis, False)
 
 
-def after(value, *first):
-    return lax.optimization_barrier((value, *first))[0]
+def after(values, *first):
+    if not isinstance(values, (list, tuple)):
+        return lax.optimization_barrier((values, *first))[0]
+    return list(lax.optimization_barrier((*values, *first))[: len(values)])
 
 
 def ring_gather(value, axis):
@@ -276,31 +279,46 @@
     cut = (rows // 2 + 15) // 16 * 16
     side = lax.axis_size("x")
     pieces, offsets = [], []
-    for start, part, order in ((0, value[:cut], "xy"), (cut, value[cut:], "yx")):
-        for first, kept in enumerate(ring_gather(part, order[0])):
-            for second, piece in enumerate(ring_gather(kept, order[1])):
-                back = dict(zip(order, (first, second)))
-                pieces.append(piece)
-                from_y = (lax.axis_index("y") - back["y"]) % side
-                from_x = (lax.axis_index("x") - back["x"]) % side
-                offsets.append((from_y * side + from_x) * rows + start)
-    return place(pieces, offsets, rows * side * side)
-
-
-def ring_reduce(value, axis, at):
+
+    def add(piece, start, back):
+        from_y = (lax.axis_index("y") - back["y"]) % side
+        from_x = (lax.axis_index("x") - back["x"]) % side
+        pieces.append(piece)
+        offsets.append((from_y * side + from_x) * rows + start)
+
+    add(value, 0, {"x": 0, "y": 0})
+    along = {axis: ring_gather(value, axis) for axis in "xy"}
+    for axis, other in ("xy", "yx"):
+        for step in range(1, side):
+            add(along[axis][step], 0, {axis: step, other: 0})
+    near = len(pieces)
+    for start, stop, order in ((0, cut, "xy"), (cut, rows, "yx")):
+        for first in range(1, side):
+            kept = ring_gather(along[order[0]][first][start:stop], order[1])
+            for second in range(1, side):
+                add(kept[second], start, {order[0]: first, order[1]: second})
+    return place(pieces, offsets, rows * side * side), pieces[1:near], pieces[near:]
+
+
+def ring_reduce(value, axis, at, late):
     size, index = lax.axis_size(axis), lax.axis_index(axis)
     moving = pick(value, index - 1, at)
     for step in range(2, size + 1):
         other = shifted(moving, axis, 1)
+        if late:
+            other = after(other, *late)
         moving = (other.astype(F32) + pick(value, index - step, at).astype(F32)).astype(BF)
     return moving
 
 
-def reduce_dp(value, order):
-    dims = value.ndim
-    if order == "yx":
-        return ring_reduce(ring_reduce(value, "y", dims - 4), "x", dims - 4)
-    return ring_reduce(ring_reduce(value, "x", dims - 3), "y", dims - 4)
+def stage_one(values, orders, first=(), late=()):
+    values = after(values, *first) if first else values
+    return [ring_reduce(v, o[0], "yx".index(o[0]), late) for v, o in zip(values, orders)]
+
+
+def stage_two(values, orders, first=(), late=()):
+    values = after(values, *first) if first else values
+    return [ring_reduce(v, o[1], 0, late) for v, o in zip(values, orders)]
 
 
 def reduce_level(value):
@@ -345,7 +363,6 @@
     length, width = tokens.shape
     rows = query_weight.shape[0]
     hidden = shared_gate.shape[1]
-    part = hidden // (2 * dp)
     wide, narrow = width // 2, hidden // 2
     head_count = wide // HEAD_DIM
     score_scale = HEAD_DIM ** (-0.5)
@@ -355,37 +372,37 @@
 
     small = jnp.concatenate([router_weight, attn_gain[:, None], ffn_gain[:, None]], axis=1)
     small = jnp.pad(small, ((0, 0), (0, 128 - small.shape[1])))
-    first_full = gather_dp(
+    first_full, first_near, first_far = gather_dp(
         jnp.concatenate(
             [half(query_weight, core, 1), half(key_weight, core, 1), half(value_weight, core, 1), small],
             axis=1,
         )
     )
-    units = lambda weight: pick(weight.reshape(rows, dp, 2, part), core, 2).reshape(rows, narrow)
-    second_shard = jnp.concatenate(
-        [
-            half(output_weight, core, 1),
-            units(shared_gate),
-            units(shared_up),
-            half(shared_down, core, 0).reshape(rows, narrow),
-        ],
-        axis=1,
-    )
-    second_full = gather_dp(after(second_shard, first_full))
     tokens_two = two(tokens)
     starts_two = two(piece_starts[0])
+    later = after([output_weight, shared_gate, shared_up, shared_down, out_grad], *first_near)
+    second_shard = jnp.concatenate(
+        [half(later[0], core, 1), half(later[1], core, 1), half(later[2], core, 1)]
+        + [half(later[3], core, 1).reshape(rows, narrow)],
+        axis=1,
+    )
+    second_full, _, _ = gather_dp(after(second_shard, *first_far))
 
     chosen = (expert_ids[:, :, None] == jnp.arange(experts, dtype=jnp.int32)).any(axis=1)
     chosen_low = jnp.pad(chosen.astype(BF), ((0, 0), (0, 128 - experts)))
 
-    def spread_out(mine):
-        found = []
-        for step in range(depth):
-            piece = shifted(mine, "z", step) if step else mine
-            found += [piece, swap(piece)]
-        return found
-
-    grads_all = spread_out(jnp.concatenate([out_grad, chosen_low], axis=1))
+    levels = [0, depth // 2] + [step for step in range(1, depth) if step != depth // 2]
+
+    def spread_out(mine, paired, *filler):
+        found = {0: mine, levels[1]: shifted(mine, "z", levels[1])}
+        mine = after(mine, found[levels[1]], *filler)
+        for step in levels[2:]:
+            found[step] = shifted(mine, "z", step)
+        rest = [piece for step in levels[1:] for piece in (found[step], swap(found[step]))]
+        return [found[0], paired, *rest]
+
+    grads_sent = jnp.concatenate([later[4], chosen_low], axis=1)
+    grads_all = spread_out(grads_sent, swap(grads_sent))
     own = me * EXP_DEV + jnp.arange(EXP_DEV)
     own_hot = (own[:, None] == jnp.arange(experts)[None, :]).astype(F32)
     marks = jnp.stack([piece[:, width : width + experts] for piece in grads_all]).astype(F32)
@@ -403,10 +420,12 @@
     output_cols = second_full[:, :wide]
     gate_half = second_full[:, wide : wide + narrow]
     up_half = second_full[:, wide + narrow : wide + 2 * narrow]
-    down_half = second_full[:, wide + 2 * narrow :].reshape(narrow, width)
-    output_half = joined(
-        half(output_cols, core, 0), swap(half(output_cols, 1 - core, 0)), core, 1
-    )
+    down_cols = second_full[:, wide + 2 * narrow :].reshape(hidden, wide)
+    met = swap(
+        jnp.concatenate([half(output_cols, 1 - core, 0), half(down_cols, 1 - core, 0)], axis=0)
+    )
+    output_half = joined(half(output_cols, core, 0), met[:wide], core, 1)
+    down_half = joined(half(down_cols, core, 0), met[wide:], core, 1)
 
     token_f = tokens_two.astype(F32)
     norm_one = lax.rsqrt(jnp.mean(token_f * token_f, axis=-1, keepdims=True) + 1e-06)
@@ -436,9 +455,9 @@
     sent = jnp.concatenate(
         [ffn_in, gates_high, gates_low, jnp.zeros((length, 128 - 2 * experts), BF)], axis=1
     )
-    rows_all = spread_out(sent)
-
-    ffn_two = jnp.stack([ffn_in, rows_all[1][:, :width]]).reshape(2 * length, width)
+    sent_other = swap(sent)
+
+    ffn_two = jnp.stack([ffn_in, sent_other[:, :width]]).reshape(2 * length, width)
     grad_two = jnp.stack([out_grad, grads_all[1][:, :width]]).reshape(2 * length, width)
     shared_gate_act = product(ffn_two, gate_half)
     shared_up_act = product(ffn_two, up_half)
@@ -457,53 +476,56 @@
         .astype(BF)
         .reshape(2, length, width)
     )
-    shares = lambda value: value.reshape(side, side, rows, -1)
-    gate_share = reduce_dp(shares(shared_gate_grad), "yx")
-    up_share = reduce_dp(shares(shared_up_grad), "xy")
-    down_share = reduce_dp(shares(shared_down_grad), "yx")
-    shared_share = reduce_level(jnp.concatenate([gate_share, up_share, down_share], axis=1))
+    rows_all = spread_out(sent, sent_other, shared_gate_grad, shared_in_grad)
+    shared_both = jnp.concatenate(
+        [shared_in_grad, jnp.zeros((2, length, 128), BF), shared_out], axis=2
+    )
+    turn = lambda grad: joined(half(grad, core, 1), swap(half(grad, 1 - core, 1)), core, 0)
+    shares = lambda value: value.reshape(side, side, value.shape[0] // dp, -1)
+    shared_orders = ("yx", "xy", "yx")
+    shared_part = [shares(g) for g in (shared_gate_grad, shared_up_grad, turn(shared_down_grad))]
 
     place_me = me.reshape(1).astype(jnp.int32)
+    block = owners // 2
     near = expert_call(
-        place_me, slots[:, : owners // 2], rows_all[: owners // 2], grads_all[: owners // 2],
+        place_me, slots[:, :block], rows_all[:block], grads_all[:block],
         expert_gate, expert_up, expert_down, owners, 0,
     )
+    wider = width + 128
+    shared_part = stage_one(shared_part, shared_orders, late=(near[block],))
+    chips = [None] * depth
+    for place_at in range(1, depth // 2):
+        chips[place_at] = near[2 * place_at].astype(F32) + swap(near[2 * place_at + 1]).astype(F32)
+    sent_back = [None] + [chips[i][:, :wider].astype(BF) for i in range(1, depth // 2)]
+    far_slots = after(slots[:, block:], *sent_back[1:])
     far = expert_call(
-        place_me, slots[:, owners // 2 :], rows_all[owners // 2 :], grads_all[owners // 2 :],
-        expert_gate, expert_up, expert_down, owners, 1, near[4:],
-    )
-    expert_in, res_grad, routed_hidden, routed_gate_grad, routed_up_grad = far[4:]
-
-    def collected(mine, other, shared, barrier=None):
-        chip = []
-        for step in range(depth):
-            own_part, far_part = mine[step], other[step]
-            if step == 0:
-                far_part = lax.dynamic_update_slice(
-                    far_part, far_part[:, :width] + shared[1], (0, 0)
-                )
-            chip.append(own_part.astype(F32) + swap(far_part).astype(F32))
-        total = chip[0]
-        for step in range(1, depth):
-            moving = chip[step].astype(BF)
-            if barrier is not None:
-                moving = after(moving, barrier)
-            total += shifted(moving, "z", -step).astype(F32)
-        return total
-
-    unstack = lambda i: [call[i][k] for call in (near, far) for k in range(depth // 2)]
-    back = collected(unstack(0), unstack(1), shared_in_grad)
-    moe_out = collected(unstack(2), unstack(3), shared_out, back) + shared_out[0].astype(F32)
-
-    down_grad = mm("erf,erd->efd", routed_hidden, res_grad).astype(BF)
+        place_me, far_slots, rows_all[block:], grads_all[block:],
+        expert_gate, expert_up, expert_down, owners, 1, near[block:],
+    )
+    expert_in, res_grad, routed_hidden, routed_gate_grad, routed_up_grad = far[block:]
+    for place_at in range(depth // 2, depth):
+        mine, other = far[2 * place_at - block], far[2 * place_at - block + 1]
+        chips[place_at] = mine.astype(F32) + swap(other).astype(F32)
+        sent_back.append(chips[place_at][:, :wider].astype(BF))
+    back_in = [shifted(sent_back[i], "z", -levels[i]) for i in range(1, depth)]
+    shared_part = stage_two(shared_part, shared_orders, late=(far[block],))
+
     gate_grad = mm("erd,erf->edf", expert_in, routed_gate_grad).astype(BF)
     up_grad = mm("erd,erf->edf", expert_in, routed_up_grad).astype(BF)
-    expert_shares = []
-    for grad in (gate_grad, up_grad, down_grad):
-        blocks = grad.reshape(EXP_DEV, side, side, grad.shape[1] // dp, grad.shape[2])
-        expert_shares.append(
-            jnp.stack([reduce_dp(blocks[0], "yx"), reduce_dp(blocks[1], "xy")]).astype(F32)
-        )
+    down_grad = mm("erf,erd->efd", routed_hidden, res_grad).astype(BF)
+    both = ("yx", "xy")
+    blocks = [
+        [grad[e].reshape(side, side, grad.shape[1] // dp, grad.shape[2]) for e in range(EXP_DEV)]
+        for grad in (gate_grad, up_grad, down_grad)
+    ]
+    gate_one = stage_one(blocks[0], both)
+    back_in = after(back_in, *gate_one)
+    chips[0] = (near[0].astype(F32) + shared_both[0].astype(F32)) + swap(
+        near[1] + shared_both[1]
+    ).astype(F32)
+    back = chips[0][:, :wider]
+    for piece in back_in:
+        back += piece.astype(F32)
 
     probs_grad = back[:, width : width + experts] + back[:, width + experts : width + 2 * experts]
     logits_grad = router_probs * (
@@ -511,7 +533,7 @@
     )
     router_grad = product_high(ffn_in.astype(F32).T, logits_grad)
     router_in_grad = product_high(logits_grad, router_full.astype(F32).T)
-    ffn_in_grad = back[:, :width] + shared_in_grad[0].astype(F32) + router_in_grad
+    ffn_in_grad = back[:, :width] + router_in_grad
     ffn_gain_grad = jnp.sum(ffn_in_grad * residual * norm_two, axis=0)
     upstream_two = ffn_in_grad * gain_two_f
     residual_grad = (
@@ -519,14 +541,19 @@
         + norm_two * upstream_two
         - residual * norm_two**3 * jnp.mean(upstream_two * residual, axis=-1, keepdims=True)
     )
-    attn_grad_two = two(residual_grad.astype(BF)).reshape(2 * length, width)
+    residual_low = residual_grad.astype(BF)
+    up_one = stage_one(blocks[1], both, gate_one, (residual_low,))
+    gate_two = stage_two(gate_one, both, (back,), ())
+    attn_grad_two = two(residual_low).reshape(2 * length, width)
     output_grad = product(context.T, attn_grad_two).astype(BF)
-    output_grad = joined(half(output_grad, core, 1), swap(half(output_grad, 1 - core, 1)), core, 0)
+    output_grad = turn(output_grad)
     context_grad = by_head(product(attn_grad_two, output_half.T).astype(BF))
     value_grad = flat(mm("shqk,sqhd->skhd", probs_low, context_grad).astype(BF))
     probs_grad_att = mm("sqhd,skhd->shqk", context_grad, values)
     row_delta = jnp.sum(attn_probs * probs_grad_att, axis=-1, keepdims=True)
     scores_grad = (attn_probs * (probs_grad_att - row_delta)).astype(BF)
+    down_one = stage_one(blocks[2], both, up_one, (scores_grad,))
+    up_two = stage_two(up_one, both, gate_two, (scores_grad,))
     query_grad = mm("shqk,skhd->sqhd", scores_grad, key_rot) * score_scale
     key_grad = mm("shqk,sqhd->skhd", scores_grad, query_rot) * score_scale
     query_pre_grad = flat(rotate(query_grad, cosine, -sine_part).astype(BF))
@@ -552,29 +579,36 @@
         [router_grad, attn_gain_grad[:, None], ffn_gain_grad[:, None]], axis=1
     ).astype(BF)
     small_grads = jnp.pad(small_grads, ((0, 0), (0, 128 - small_grads.shape[1])))
-    output_share = reduce_dp(shares(output_grad), "yx")
-    value_share = reduce_dp(shares(value_wgrad), "xy")
-    early_share = reduce_level(jnp.concatenate([output_share, value_share], axis=1))
-    query_share = reduce_dp(shares(query_wgrad), "yx")
-    key_share = reduce_dp(shares(jnp.concatenate([key_wgrad, small_grads], axis=1)), "xy")
-    late_share = reduce_level(jnp.concatenate([query_share, key_share], axis=1))
+    early = stage_one([shares(output_grad), shares(value_wgrad)], both, (*down_one, *up_two))
+    down_two = stage_two(down_one, both)
+    early = stage_two(early, both)
+    late = [shares(query_wgrad), shares(jnp.concatenate([key_wgrad, small_grads], axis=1))]
+    late = stage_two(stage_one(late, both, early), both)
+    expert_shares = [jnp.stack(pair).astype(F32) for pair in (gate_two, up_two, down_two)]
+    shared_share = lax.psum(
+        jnp.concatenate([*shared_part[:2], shared_part[2].reshape(rows, narrow)], axis=1), "z"
+    )
+    early_share = reduce_level(jnp.concatenate(early, axis=1))
+    late_share = reduce_level(jnp.concatenate(late, axis=1))
+
+    moe_out = chips[0][:, wider:]
+    for i in range(1, depth):
+        moving = after(chips[i][:, wider:].astype(BF), back)
+        if i > 1:
+            moving = after(moving, piece)
+        piece = after(shifted(moving, "z", -levels[i]), (scores_grad, query_wgrad, early[0])[min(i - 1, 2)])
+        moe_out += piece.astype(F32)
 
     early_other, late_other, shared_other = swap(early_share), swap(late_share), swap(shared_share)
-    column = lambda mine, other, i: joined(
-        mine[:, i * wide : (i + 1) * wide], other[:, i * wide : (i + 1) * wide], core, 1
+    column = lambda mine, other, start, size: joined(
+        mine[:, start : start + size], other[:, start : start + size], core, 1
     ).astype(F32)
     small_sum = late_share[:, 2 * wide :].astype(F32) + late_other[:, 2 * wide :].astype(F32)
-    unit_col = lambda i: joined(
-        shared_share[:, i * narrow : (i + 1) * narrow].reshape(rows, dp, 1, part),
-        shared_other[:, i * narrow : (i + 1) * narrow].reshape(rows, dp, 1, part),
+    down_rows = joined(
+        shared_share[:, 2 * narrow :].reshape(-1, wide),
+        shared_other[:, 2 * narrow :].reshape(-1, wide),
         core,
-        2,
-    ).reshape(rows, hidden).astype(F32)
-    down_rows = joined(
-        shared_share[:, 2 * narrow :].reshape(part, width),
-        shared_other[:, 2 * narrow :].reshape(part, width),
-        core,
-        0,
+        1,
     ).astype(F32)
 
     stream_out = residual + moe_out
@@ -588,15 +622,15 @@
     return (
         stream_out.astype(BF),
         tokens_grad.astype(BF),
-        column(late_share, late_other, 0),
-        column(late_share, late_other, 1),
-        column(early_share, early_other, 1),
-        column(early_share, early_other, 0),
+        column(late_share, late_other, 0, wide),
+        column(late_share, late_other, wide, wide),
+        column(early_share, early_other, wide, wide),
+        column(early_share, early_other, 0, wide),
         small_sum[:, experts],
         small_sum[:, experts + 1],
         small_sum[:, :experts],
-        unit_col(0),
-        unit_col(1),
+        column(shared_share, shared_other, 0, narrow),
+        column(shared_share, shared_other, narrow, narrow),
         down_rows,
         *expert_shares,
         stat_rms,

time: 887 us -> 682 us (0.77)
  waiting for transfers between devices: 396 us -> 208 us
  local copies, waits for them, and re-layouts: 148 us -> 121 us
  between operations: 6.72 us -> 19.6 us
    ppermute x94 -> x81, waiting for transfers between devices: 396 us -> 200 us  [shifted(): lax.ppermute(value, axis, [(i, (i + by) % size) for i in range(size)])]
    reshape x15 -> x7, local copies, waits for them, and re-layouts: 30.7 us -> 10 us  [the longest x1 2.32 us: body(): down_cols = second_full[:, wide + 2 * narrow:].reshape(hidden, wide)]
    convert_element_type x15 -> x12, other arithmetic: 33 us -> 16.7 us  [the longest x6 9.53 us: body(): column = lambda mine, other, start, size: joined(mine[:, start:start + si...]
    slice x15 -> x25, local copies, waits for them, and re-layouts: 9.06 us -> 23.5 us  [the longest x4 6.23 us: gather_dp(): kept = ring_gather(along[order[0]][first][start:stop], order[1])]
    convert_element_type x20 -> x24, other arithmetic: 12.1 us -> 24 us  [ring_reduce(): (other.astype(F32) + pick(value, index - step, at).astype(F32)).astype(BF)]
    ppermute x94 -> x81, starting transfers between devices: 83.8 us -> 76.3 us  [shifted(): lax.ppermute(value, axis, [(i, (i + by) % size) for i in range(size)])]
    squeeze x29 -> x28, local copies, waits for them, and re-layouts: 23 us -> 16.4 us  [pick(): lax.dynamic_index_in_dim(value, index % value.shape[axis], axis, False)]
  transfers between devices with their start and end apart: 94 -> 82, of which waited for: 33 -> 28; matrix products, arithmetic and copies ran while one was open for 30% -> 38% of each run, Pallas kernels for 9% -> 12%
where the time goes in v4:
time: 682 us; the launch traced here: 676 us
  waiting for transfers between devices  208 us (30%)
  local copies, waits for them, and re-layouts  121 us (18%)
  other arithmetic  88.7 us (13%)
  matrix products  83.3 us (12%)
  Pallas kernels  79.5 us (12%)
  starting transfers between devices  76.3 us (11%)
  between operations  19.6 us (3%)
    ppermute x81, waiting for transfers between devices, shifted(): lax.ppermute(value, axis, [(i, (i + by) % size) for i in range(size)])  200 us
    ppermute x81, starting transfers between devices, shifted(): lax.ppermute(value, axis, [(i, (i + by) % size) for i in range(size)])  76.3 us
    pallas_call x2, Pallas kernels, expert_call(): pl.pallas_call(functools.partial(expert_kernel, count, width, capacity, e...  69.3 us
    dot_general x22, matrix products, product(): return jnp.dot(first_arg, second_arg, preferred_element_type=F32)  46.8 us
    dot_general x9, matrix products, mm(): return jnp.einsum(spec, first_arg, second_arg, preferred_element_type=F32)  31.7 us
    convert_element_type x24, other arithmetic, ring_reduce(): (other.astype(F32) + pick(value, index - step, at).astype(F32)).astype(BF)  24 us
    squeeze x28, local copies, waits for them, and re-layouts, pick(): lax.dynamic_index_in_dim(value, index % value.shape[axis], axis, False)  16.4 us
  transfers between devices with their start and end apart: 82, of which 28 were waited for; matrix products, arithmetic and copies ran while one was open for 38% of the time, Pallas kernels for 12%

profile of v4, /device:TPU:0, one launch (start us, length us, event | category | flops | bytes accessed | tf_op | source)
XLA Modules:
  0.0 676.1 jit_solution(8264954558387929091)
XLA Ops:
  25.5 18.6 %collective-permute-done.2.refs_2_ = bf16[320,2048]{1,0:T(8,128)(2,1)} collective-permute-done((bf16[320,2048]{1,0:T(8,128)(2,1)}, bf16[320,2048]{1,0:T(8,128)(2,1)}, u32[]{:S(2)}, u32[]{:S(2)}) %collective-permute-start.2) | collective-permute-done | bytes 1310752 | tf_op jit(solution)/shard_map/ppermute | solution.py:242
  68.1 5.1 place.2
  74.9 4.0 slice_bitcast_fusion.1
  85.0 3.7 copy.253
  115.8 20.8 %collective-permute-done.17.refs_6_ = bf16[256,1408]{1,0:T(8,128)(2,1)} collective-permute-done((bf16[256,1408]{1,0:T(8,128)(2,1)}, bf16[256,1408]{1,0:T(8,128)(2,1)}, u32[]{:S(2)}, u32[]{:S(2)}) %collective-permute-start.17) | collective-permute-done | bytes 720928 | tf_op jit(solution)/shard_map/ppermute | solution.py:242
  138.8 5.1 place.3
  198.9 10.2 %collective-permute-done.20.refs_2_ = bf16[256,1408]{1,0:T(8,128)(2,1)} collective-permute-done((bf16[256,1408]{1,0:T(8,128)(2,1)}, bf16[256,1408]{1,0:T(8,128)(2,1)}, u32[]{:S(2)}, u32[]{:S(2)}) %collective-permute-start.20) | collective-permute-done | bytes 720928 | tf_op jit(solution)/shard_map/ppermute | solution.py:242
  225.6 34.6 %experts.2 = (bf16[256,2688]{1,0:T(8,128)(2,1)}, bf16[256,2688]{1,0:T(8,128)(2,1)}, bf16[256,2688]{1,0:T(8,128)(2,1)}, bf16[256,2688]{1,0:T(8,128)(2,1)}, bf16[2...) custom-call(s32[1]{0:T(128)} %bitcast.20.me_ref, ...), custom_call_target="tpu_custom_call" | custom-call | flops 16441671680 | bytes 62914560 | tf_op jit(solution)/shard_map/experts/pallas_call | solution.py:133
  269.4 9.7 %collective-permute-done.76 = bf16[2,224,640]{2,1,0:T(8,128)(2,1)S(1)} collective-permute-done((bf16[2,224,640]{2,1,0:T(8,128)(2,1)S(1)}, bf16[2,224,640]{2,1,0:T(8,128)(2,1)S(1)}, u32[]{:S(2)}, u32[]{:S(2)}) %collective-permute-start.76) | collective-permute-done | bytes 573472 | tf_op jit(solution)/shard_map/ppermute | solution.py:242
  287.1 34.7 %experts.3 = (bf16[256,2688]{1,0:T(8,128)(2,1)}, bf16[256,2688]{1,0:T(8,128)(2,1)}, bf16[256,2688]{1,0:T(8,128)(2,1)}, bf16[256,2688]{1,0:T(8,128)(2,1)}, bf16[2...) custom-call(s32[1]{0:T(128)} %bitcast.20.me_ref, ...), custom_call_target="tpu_custom_call", output_to_operand_aliasing={{4}: (13, {}), {5}: (14, {}), {6}: (15, {}), {7}: (16, {}),... | custom-call | flops 16441671680 | bytes 62914560 | tf_op jit(solution)/shard_map/experts/pallas_call | solution.py:133
  332.3 9.0 %convolution_convert_fusion.2 = bf16[2,1280,896]{2,1,0:T(8,128)(2,1)S(1)} fusion(bf16[2,1024,1280]{2,1,0:T(8,128)(2,1)} %get-tuple-element.100, bf16[2,1024,896]{2,1,0:T(8,128)(2,1)} %get-tuple-element.101), kind=kOutput, calls=%fused_computation.3 | convolution fusion | flops 4699914240 | bytes 13500416 | tf_op jit(solution)/shard_map/erd,erf->edf/dot_general | solution.py:196
  341.3 8.4 %convolution_convert_fusion = bf16[2,1280,896]{2,1,0:T(8,128)(2,1)S(1)} fusion(bf16[2,1024,1280]{2,1,0:T(8,128)(2,1)} %get-tuple-element.100, bf16[2,1024,896]{2,1,0:T(8,128)(2,1)S(1)} %copy-done.95), kind=kOutput, calls=%fused_computation.1 | convolution fusion | flops 4699914240 | bytes 13500416 | tf_op jit(solution)/shard_map/erd,erf->edf/dot_general | solution.py:196
  354.6 7.8 %convolution_convert_fusion.1 = bf16[2,896,1280]{2,1,0:T(8,128)(2,1)S(1)} fusion(bf16[2,1024,896]{2,1,0:T(8,128)(2,1)S(1)} %copy-done.94, bf16[2,1024,1280]{2,1,0:T(8,128)(2,1)} %get-tuple-element.113), kind=kOutput, calls=%fused_computation.2 | convolution fusion | flops 4699914240 | bytes 13500416 | tf_op jit(solution)/shard_map/erf,erd->efd/dot_general | solution.py:196
  372.2 7.4 %all-reduce.5.cloned.1.call-done = bf16[320,1344]{1,0:T(8,128)(2,1)} async-done(((bf16[320,1344]{1,0:T(8,128)(2,1)}), bf16[320,1344]{1,0:T(8,128)(2,1)}) %all-reduce.5.cloned.1.call-update) | async-done | bytes 860176 | tf_op jit(solution)/shard_map/psum | solution.py:588
  385.0 5.0 collective-permute-done.33
  416.1 22.0 %collective-permute-done.30 = bf16[256,1408]{1,0:T(8,128)(2,1)} collective-permute-done((bf16[256,1408]{1,0:T(8,128)(2,1)}, bf16[256,1408]{1,0:T(8,128)(2,1)}, u32[]{:S(2)}, u32[]{:S(2)}) %collective-permute-start.30) | collective-permute-done | bytes 720928 | tf_op jit(solution)/shard_map/ppermute | solution.py:242
  491.3 4.5 collective-permute-done.47
  495.9 4.0 collective-permute-start.37
  503.9 8.8 %collective-permute-done.37 = bf16[256,1280]{1,0:T(8,128)(2,1)S(1)} collective-permute-done((bf16[256,1280]{1,0:T(8,128)(2,1)S(1)}, bf16[256,1280]{1,0:T(8,128)(2,1)S(1)}, u32[]{:S(2)}, u32[]{:S(2)}) %collective-permute-start.37) | collective-permute-done | bytes 655392 | tf_op jit(solution)/shard_map/ppermute | solution.py:242
  517.0 4.0 copy.288
  531.2 7.8 %collective-permute-done.80 = bf16[224,1280]{1,0:T(8,128)(2,1)S(1)} collective-permute-done((bf16[224,1280]{1,0:T(8,128)(2,1)S(1)}, bf16[224,1280]{1,0:T(8,128)(2,1)S(1)}, u32[]{:S(2)}, u32[]{:S(2)}) %collective-permute-start.80) | collective-permute-done | bytes 573472 | tf_op jit(solution)/shard_map/ppermute | solution.py:242
  542.3 10.9 %collective-permute-done.48 = bf16[2,320,640]{2,1,0:T(8,128)(2,1)S(1)} collective-permute-done((bf16[2,320,640]{2,1,0:T(8,128)(2,1)S(1)}, bf16[2,320,640]{2,1,0:T(8,128)(2,1)S(1)}, u32[]{:S(2)}, u32[]{:S(2)}) %collective-permute-start.48) | collective-permute-done | bytes 819232 | tf_op jit(solution)/shard_map/ppermute | solution.py:242
  559.6 5.3 collective-permute-done.49
  579.6 9.2 %collective-permute-done.65 = bf16[80,1280]{1,0:T(8,128)(2,1)S(1)} collective-permute-done((bf16[80,1280]{1,0:T(8,128)(2,1)}, bf16[80,1280]{1,0:T(8,128)(2,1)S(1)}, u32[]{:S(2)}, u32[]{:S(2)}) %collective-permute-start.65) | collective-permute-done | bytes 204832 | tf_op jit(solution)/shard_map/ppermute | solution.py:242
  592.7 6.1 collective-permute-done.67
  598.8 7.2 %collective-permute-done.68 = bf16[80,1280]{1,0:T(8,128)(2,1)S(1)} collective-permute-done((bf16[80,1280]{1,0:T(8,128)(2,1)S(1)}, bf16[80,1280]{1,0:T(8,128)(2,1)S(1)}, u32[]{:S(2)}, u32[]{:S(2)}) %collective-permute-start.68) | collective-permute-done | bytes 204832 | tf_op jit(solution)/shard_map/ppermute | solution.py:242
  607.5 6.9 %collective-permute-done.55 = bf16[2,320,768]{2,1,0:T(8,128)(2,1)S(1)} collective-permute-done((bf16[2,320,768]{2,1,0:T(8,128)(2,1)S(1)}, bf16[2,320,768]{2,1,0:T(8,128)(2,1)S(1)}, u32[]{:S(2)}, u32[]{:S(2)}) %collective-permute-start.55) | collective-permute-done | bytes 983072 | tf_op jit(solution)/shard_map/ppermute | solution.py:242
  624.0 3.8 collective-permute-start.59
  627.9 4.1 collective-permute-done.57
  632.8 10.4 %collective-permute-done.58 = bf16[80,1408]{1,0:T(8,128)(2,1)S(1)} collective-permute-done((bf16[80,1408]{1,0:T(8,128)(2,1)S(1)}, bf16[80,1408]{1,0:T(8,128)(2,1)S(1)}, u32[]{:S(2)}, u32[]{:S(2)}) %collective-permute-start.58) | collective-permute-done | bytes 225312 | tf_op jit(solution)/shard_map/ppermute | solution.py:242
  645.5 5.8 collective-permute-done.60
  651.4 9.9 %collective-permute-done.61 = bf16[80,1408]{1,0:T(8,128)(2,1)S(1)} collective-permute-done((bf16[80,1408]{1,0:T(8,128)(2,1)S(1)}, bf16[80,1408]{1,0:T(8,128)(2,1)S(1)}, u32[]{:S(2)}, u32[]{:S(2)}) %collective-permute-start.61) | collective-permute-done | bytes 225312 | tf_op jit(solution)/shard_map/ppermute | solution.py:242
  (621 shorter events, 341.7 us)
Async XLA Ops:
  7.2 372.4 %all-reduce.5.cloned.1.call-start = ((), (), s32[]{:S(2)}) async-start(), calls=%async_computation | async-start | bytes 1802240 | tf_op jit(solution)/shard_map/psum | solution.py:588
  12.1 32.1 %collective-permute-start.2 = (bf16[320,2048]{1,0:T(8,128)(2,1)}, bf16[320,2048]{1,0:T(8,128)(2,1)}, u32[]{:S(2)}, u32[]{:S(2)}) collective-permute-start(bf16[320,2048]{1,0:T(8,128)(2,1)} %fusion.33.refs_0_), channel_id=1, source_target_pairs={{0,16},{16,0},{1,17},{17,1},{2,18},{18,2},{3,19},{19,3},{4,20},{20... | collective-permute-start | bytes 3932168 | tf_op jit(solution)/shard_map/ppermute | solution.py:242
  15.1 32.8 %collective-permute-start.1 = (bf16[320,2048]{1,0:T(8,128)(2,1)}, bf16[320,2048]{1,0:T(8,128)(2,1)}, u32[]{:S(2)}, u32[]{:S(2)}) collective-permute-start(bf16[320,2048]{1,0:T(8,128)(2,1)} %fusion.33.refs_0_), channel_id=1, source_target_pairs={{0,8},{8,0},{1,9},{9,1},{2,10},{10,2},{3,11},{11,3},{4,12},{12,4},... | collective-permute-start | bytes 3932168 | tf_op jit(solution)/shard_map/ppermute | solution.py:242
  52.3 50.7 %collective-permute-start.13 = (bf16[256,1408]{1,0:T(8,128)(2,1)}, bf16[256,1408]{1,0:T(8,128)(2,1)}, u32[]{:S(2)}, u32[]{:S(2)}) collective-permute-start(bf16[256,1408]{1,0:T(8,128)(2,1)} %pad_maximum_fusion.8.refs_4_), channel_id=1, source_target_pairs={{0,4},{2,6},{4,0},{6,2},{1,5},{3,7},{5,1},{7,3},{8,12},{10,14},{12... | collective-permute-start | bytes 2162696 | tf_op jit(solution)/shard_map/ppermute | solution.py:242
  54.9 51.1 %collective-permute-start.12 = (bf16[256,1408]{1,0:T(8,128)(2,1)}, bf16[256,1408]{1,0:T(8,128)(2,1)}, u32[]{:S(2)}, u32[]{:S(2)}) collective-permute-start(bf16[256,1408]{1,0:T(8,128)(2,1)} %pad_maximum_fusion.8.refs_4_), channel_id=1, source_target_pairs={{0,1},{1,0},{2,3},{3,2},{4,5},{5,4},{6,7},{7,6},{8,9},{9,8},{10,11... | collective-permute-start | bytes 2162696 | tf_op jit(solution)/shard_map/ppermute | solution.py:242
  67.0 42.0 %collective-permute-start.7 = (bf16[320,1984]{1,0:T(8,128)(2,1)}, bf16[320,1984]{1,0:T(8,128)(2,1)}, u32[]{:S(2)}, u32[]{:S(2)}) collective-permute-start(bf16[320,1984]{1,0:T(8,128)(2,1)} %concatenate.126.refs_0_), channel_id=1, source_target_pairs={{0,16},{16,0},{1,17},{17,1},{2,18},{18,2},{3,19},{19,3},{4,20},{20... | collective-permute-start | bytes 3809288 | tf_op jit(solution)/shard_map/ppermute | solution.py:242
  67.6 44.1 %collective-permute-start.6 = (bf16[320,1984]{1,0:T(8,128)(2,1)}, bf16[320,1984]{1,0:T(8,128)(2,1)}, u32[]{:S(2)}, u32[]{:S(2)}) collective-permute-start(bf16[320,1984]{1,0:T(8,128)(2,1)} %concatenate.126.refs_0_), channel_id=1, source_target_pairs={{0,8},{8,0},{1,9},{9,1},{2,10},{10,2},{3,11},{11,3},{4,12},{12,4},... | collective-permute-start | bytes 3809288 | tf_op jit(solution)/shard_map/ppermute | solution.py:242
  102.9 33.7 %collective-permute-start.17 = (bf16[256,1408]{1,0:T(8,128)(2,1)}, bf16[256,1408]{1,0:T(8,128)(2,1)}, u32[]{:S(2)}, u32[]{:S(2)}) collective-permute-start(bf16[256,1408]{1,0:T(8,128)(2,1)} %pad_maximum_fusion.8.refs_4_), channel_id=1, source_target_pairs={{0,6},{2,0},{4,2},{6,4},{1,7},{3,1},{5,3},{7,5},{8,14},{10,8},{12,... | collective-permute-start | bytes 2162696 | tf_op jit(solution)/shard_map/ppermute | solution.py:242
  106.9 45.5 %collective-permute-start.14 = (bf16[256,1408]{1,0:T(8,128)(2,1)}, bf16[256,1408]{1,0:T(8,128)(2,1)}, u32[]{:S(2)}, u32[]{:S(2)}) collective-permute-start(bf16[256,1408]{1,0:T(8,128)(2,1)} %collective-permute-done.13.refs_6_), channel_id=1, source_target_pairs={{0,1},{1,0},{2,3},{3,2},{4,5},{5,4},{6,7},{7,6},{8,9},{9,8},{10,11... | collective-permute-start | bytes 2162696 | tf_op jit(solution)/shard_map/ppermute | solution.py:242
  173.9 35.2 %collective-permute-start.20 = (bf16[256,1408]{1,0:T(8,128)(2,1)}, bf16[256,1408]{1,0:T(8,128)(2,1)}, u32[]{:S(2)}, u32[]{:S(2)}) collective-permute-start(bf16[256,1408]{1,0:T(8,128)(2,1)} %concatenate.131.refs_0_), channel_id=1, source_target_pairs={{0,4},{2,6},{4,0},{6,2},{1,5},{3,7},{5,1},{7,3},{8,12},{10,14},{12... | collective-permute-start | bytes 2162696 | tf_op jit(solution)/shard_map/ppermute | solution.py:242
  209.1 71.5 %collective-permute-start.27 = (bf16[256,1408]{1,0:T(8,128)(2,1)}, bf16[256,1408]{1,0:T(8,128)(2,1)}, u32[]{:S(2)}, u32[]{:S(2)}) collective-permute-start(bf16[256,1408]{1,0:T(8,128)(2,1)} %concatenate.131.refs_0_), channel_id=1, source_target_pairs={{0,6},{2,0},{4,2},{6,4},{1,7},{3,1},{5,3},{7,5},{8,14},{10,8},{12,... | collective-permute-start | bytes 2162696 | tf_op jit(solution)/shard_map/ppermute | solution.py:242
  211.1 69.5 %collective-permute-start.25 = (bf16[256,1408]{1,0:T(8,128)(2,1)}, bf16[256,1408]{1,0:T(8,128)(2,1)}, u32[]{:S(2)}, u32[]{:S(2)}) collective-permute-start(bf16[256,1408]{1,0:T(8,128)(2,1)} %concatenate.131.refs_0_), channel_id=1, source_target_pairs={{0,2},{2,4},{4,6},{6,0},{1,3},{3,5},{5,7},{7,1},{8,10},{10,12},{12... | collective-permute-start | bytes 2162696 | tf_op jit(solution)/shard_map/ppermute | solution.py:242
  216.7 46.6 %collective-permute-start.73 = (bf16[2,320,448]{2,1,0:T(8,128)(2,1)}, bf16[2,320,448]{2,1,0:T(8,128)(2,1)}, u32[]{:S(2)}, u32[]{:S(2)}) collective-permute-start(bf16[2,320,448]{2,1,0:T(8,128)(2,1)} %dynamic-slice_bitcast_fusion.10), channel_id=1, source_target_pairs={{0,8},{8,0},{1,9},{9,1},{2,10},{10,2},{3,11},{11,3},{4,12},{12,4},... | collective-permute-start | bytes 1720328 | tf_op jit(solution)/shard_map/ppermute | solution.py:242
  221.3 44.5 %collective-permute-start.71 = (bf16[2,320,448]{2,1,0:T(8,128)(2,1)}, bf16[2,320,448]{2,1,0:T(8,128)(2,1)}, u32[]{:S(2)}, u32[]{:S(2)}) collective-permute-start(bf16[2,320,448]{2,1,0:T(8,128)(2,1)} %dynamic-slice_bitcast_fusion.11), channel_id=1, source_target_pairs={{0,16},{16,0},{1,17},{17,1},{2,18},{18,2},{3,19},{19,3},{4,20},{20... | collective-permute-start | bytes 1720328 | tf_op jit(solution)/shard_map/ppermute | solution.py:242
  265.8 57.9 %collective-permute-start.74 = (bf16[320,448]{1,0:T(8,128)(2,1)}, bf16[320,448]{1,0:T(8,128)(2,1)}, u32[]{:S(2)}, u32[]{:S(2)}) collective-permute-start(bf16[320,448]{1,0:T(8,128)(2,1)} %dynamic-slice_bitcast_fusion.23), channel_id=1, source_target_pairs={{0,16},{16,0},{1,17},{17,1},{2,18},{18,2},{3,19},{19,3},{4,20},{20... | collective-permute-start | bytes 860168 | tf_op jit(solution)/shard_map/ppermute | solution.py:242
  279.1 46.4 %collective-permute-start.72 = (bf16[320,448]{1,0:T(8,128)(2,1)}, bf16[320,448]{1,0:T(8,128)(2,1)}, u32[]{:S(2)}, u32[]{:S(2)}) collective-permute-start(bf16[320,448]{1,0:T(8,128)(2,1)} %dynamic-slice_bitcast_fusion.24), channel_id=1, source_target_pairs={{0,8},{8,0},{1,9},{9,1},{2,10},{10,2},{3,11},{11,3},{4,12},{12,4},... | collective-permute-start | bytes 860168 | tf_op jit(solution)/shard_map/ppermute | solution.py:242
  280.6 81.9 %collective-permute-start.22 = (bf16[256,2688]{1,0:T(8,128)(2,1)}, bf16[256,2688]{1,0:T(8,128)(2,1)}, u32[]{:S(2)}, u32[]{:S(2)}) collective-permute-start(bf16[256,2688]{1,0:T(8,128)(2,1)} %fusion.29), channel_id=1, source_target_pairs={{0,1},{1,0},{2,3},{3,2},{4,5},{5,4},{6,7},{7,6},{8,9},{9,8},{10,11... | collective-permute-start | bytes 4128776 | tf_op jit(solution)/shard_map/ppermute | solution.py:242
  285.1 36.8 %collective-permute-start.77 = (bf16[224,640]{1,0:T(8,128)(2,1)}, bf16[224,640]{1,0:T(8,128)(2,1)}, u32[]{:S(2)}, u32[]{:S(2)}) collective-permute-start(bf16[224,640]{1,0:T(8,128)(2,1)} %dynamic-slice_bitcast_fusion.25), channel_id=1, source_target_pairs={{0,8},{8,0},{1,9},{9,1},{2,10},{10,2},{3,11},{11,3},{4,12},{12,4},... | collective-permute-start | bytes 860168 | tf_op jit(solution)/shard_map/ppermute | solution.py:242
  286.6 129.6 %collective-permute-start.24 = (bf16[256,1408]{1,0:T(8,128)(2,1)}, bf16[256,1408]{1,0:T(8,128)(2,1)}, u32[]{:S(2)}, u32[]{:S(2)}) collective-permute-start(bf16[256,1408]{1,0:T(8,128)(2,1)} %slice.383), channel_id=1, source_target_pairs={{0,4},{2,6},{4,0},{6,2},{1,5},{3,7},{5,1},{7,3},{8,12},{10,14},{12... | collective-permute-start | bytes 2162696 | tf_op jit(solution)/shard_map/ppermute | solution.py:242
  331.7 64.1 %collective-permute-start.29 = (bf16[256,2688]{1,0:T(8,128)(2,1)}, bf16[256,2688]{1,0:T(8,128)(2,1)}, u32[]{:S(2)}, u32[]{:S(2)}) collective-permute-start(bf16[256,2688]{1,0:T(8,128)(2,1)} %get-tuple-element.97), channel_id=1, source_target_pairs={{0,1},{1,0},{2,3},{3,2},{4,5},{5,4},{6,7},{7,6},{8,9},{9,8},{10,11... | collective-permute-start | bytes 4128776 | tf_op jit(solution)/shard_map/ppermute | solution.py:242
  331.8 68.1 %collective-permute-start.31 = (bf16[256,2688]{1,0:T(8,128)(2,1)}, bf16[256,2688]{1,0:T(8,128)(2,1)}, u32[]{:S(2)}, u32[]{:S(2)}) collective-permute-start(bf16[256,2688]{1,0:T(8,128)(2,1)} %get-tuple-element.99), channel_id=1, source_target_pairs={{0,1},{1,0},{2,3},{3,2},{4,5},{5,4},{6,7},{7,6},{8,9},{9,8},{10,11... | collective-permute-start | bytes 4128776 | tf_op jit(solution)/shard_map/ppermute | solution.py:242
  393.7 52.6 %collective-permute-start.41 = (bf16[2,320,896]{2,1,0:T(8,128)(2,1)}, bf16[2,320,896]{2,1,0:T(8,128)(2,1)}, u32[]{:S(2)}, u32[]{:S(2)}) collective-permute-start(bf16[2,320,896]{2,1,0:T(8,128)(2,1)} %dynamic-slice_bitcast_fusion.2), channel_id=1, source_target_pairs={{0,8},{8,0},{1,9},{9,1},{2,10},{10,2},{3,11},{11,3},{4,12},{12,4},... | collective-permute-start | bytes 3440648 | tf_op jit(solution)/shard_map/ppermute | solution.py:242
  395.9 54.3 %collective-permute-start.40 = (bf16[2,320,896]{2,1,0:T(8,128)(2,1)}, bf16[2,320,896]{2,1,0:T(8,128)(2,1)}, u32[]{:S(2)}, u32[]{:S(2)}) collective-permute-start(bf16[2,320,896]{2,1,0:T(8,128)(2,1)} %dynamic-slice_bitcast_fusion.3), channel_id=1, source_target_pairs={{0,16},{16,0},{1,17},{17,1},{2,18},{18,2},{3,19},{19,3},{4,20},{20... | collective-permute-start | bytes 3440648 | tf_op jit(solution)/shard_map/ppermute | solution.py:242
  403.4 34.7 %collective-permute-start.30 = (bf16[256,1408]{1,0:T(8,128)(2,1)}, bf16[256,1408]{1,0:T(8,128)(2,1)}, u32[]{:S(2)}, u32[]{:S(2)}) collective-permute-start(bf16[256,1408]{1,0:T(8,128)(2,1)} %slice.385), channel_id=1, source_target_pairs={{0,6},{2,0},{4,2},{6,4},{1,7},{3,1},{5,3},{7,5},{8,14},{10,8},{12,... | collective-permute-start | bytes 2162696 | tf_op jit(solution)/shard_map/ppermute | solution.py:242
  446.3 32.4 %collective-permute-start.35 = (bf16[256,1280]{1,0:T(8,128)(2,1)}, bf16[256,1280]{1,0:T(8,128)(2,1)}, u32[]{:S(2)}, u32[]{:S(2)}) collective-permute-start(bf16[256,1280]{1,0:T(8,128)(2,1)} %slice.381), channel_id=1, source_target_pairs={{0,4},{2,6},{4,0},{6,2},{1,5},{3,7},{5,1},{7,3},{8,12},{10,14},{12... | collective-permute-start | bytes 1966088 | tf_op jit(solution)/shard_map/ppermute | solution.py:242
  453.6 67.4 %collective-permute-start.43 = (bf16[2,224,1280]{2,1,0:T(8,128)(2,1)}, bf16[2,224,1280]{2,1,0:T(8,128)(2,1)}, u32[]{:S(2)}, u32[]{:S(2)}) collective-permute-start(bf16[2,224,1280]{2,1,0:T(8,128)(2,1)} %dynamic-slice_bitcast_fusion), channel_id=1, source_target_pairs={{0,8},{8,0},{1,9},{9,1},{2,10},{10,2},{3,11},{11,3},{4,12},{12,4},... | collective-permute-start | bytes 3440648 | tf_op jit(solution)/shard_map/ppermute | solution.py:242
  455.9 68.8 %collective-permute-start.42 = (bf16[2,224,1280]{2,1,0:T(8,128)(2,1)}, bf16[2,224,1280]{2,1,0:T(8,128)(2,1)}, u32[]{:S(2)}, u32[]{:S(2)}) collective-permute-start(bf16[2,224,1280]{2,1,0:T(8,128)(2,1)} %dynamic-slice_bitcast_fusion.1), channel_id=1, source_target_pairs={{0,16},{16,0},{1,17},{17,1},{2,18},{18,2},{3,19},{19,3},{4,20},{20... | collective-permute-start | bytes 3440648 | tf_op jit(solution)/shard_map/ppermute | solution.py:242
  458.2 37.7 %collective-permute-start.47 = (bf16[320,896]{1,0:T(8,128)(2,1)}, bf16[320,896]{1,0:T(8,128)(2,1)}, u32[]{:S(2)}, u32[]{:S(2)}) collective-permute-start(bf16[320,896]{1,0:T(8,128)(2,1)} %dynamic-slice_bitcast_fusion.15), channel_id=1, source_target_pairs={{0,16},{16,0},{1,17},{17,1},{2,18},{18,2},{3,19},{19,3},{4,20},{20... | collective-permute-start | bytes 1720328 | tf_op jit(solution)/shard_map/ppermute | solution.py:242
  461.5 38.3 %collective-permute-start.46 = (bf16[320,896]{1,0:T(8,128)(2,1)}, bf16[320,896]{1,0:T(8,128)(2,1)}, u32[]{:S(2)}, u32[]{:S(2)}) collective-permute-start(bf16[320,896]{1,0:T(8,128)(2,1)} %dynamic-slice_bitcast_fusion.16), channel_id=1, source_target_pairs={{0,8},{8,0},{1,9},{9,1},{2,10},{10,2},{3,11},{11,3},{4,12},{12,4},... | collective-permute-start | bytes 1720328 | tf_op jit(solution)/shard_map/ppermute | solution.py:242
  478.7 48.7 %collective-permute-start.39 = (bf16[640,640]{1,0:T(8,128)(2,1)}, bf16[640,640]{1,0:T(8,128)(2,1)}, u32[]{:S(2)}, u32[]{:S(2)}) collective-permute-start(bf16[640,640]{1,0:T(8,128)(2,1)} %get-tuple-element.264), channel_id=1, source_target_pairs={{0,1},{1,0},{2,3},{3,2},{4,5},{5,4},{6,7},{7,6},{8,9},{9,8},{10,11... | collective-permute-start | bytes 2457608 | tf_op jit(solution)/shard_map/ppermute | solution.py:242
  513.4 51.5 %collective-permute-start.38 = (bf16[256,1280]{1,0:T(8,128)(2,1)}, bf16[256,1280]{1,0:T(8,128)(2,1)}, u32[]{:S(2)}, u32[]{:S(2)}) collective-permute-start(bf16[256,1280]{1,0:T(8,128)(2,1)} %slice.395), channel_id=1, source_target_pairs={{0,2},{2,4},{4,6},{6,0},{1,3},{3,5},{5,7},{7,1},{8,10},{10,12},{12... | collective-permute-start | bytes 1966088 | tf_op jit(solution)/shard_map/ppermute | solution.py:242
  627.9 33.9 %collective-permute-start.70 = (bf16[320,1280]{1,0:T(8,128)(2,1)S(1)}, bf16[320,1280]{1,0:T(8,128)(2,1)S(1)}, u32[]{:S(2)}, u32[]{:S(2)}) collective-permute-start(bf16[320,1280]{1,0:T(8,128)(2,1)S(1)} %bitcast.413), channel_id=1, source_target_pairs={{0,1},{1,0},{2,3},{3,2},{4,5},{5,4},{6,7},{7,6},{8,9},{9,8},{10,11... | collective-permute-start | bytes 2457608 | tf_op jit(solution)/shard_map/ppermute | solution.py:242
  (150 other events, 1429.8 us)
Sparse Core Ops, SparseCore 0:
  331.9 47.6 all-reduce.4

commit v5 on v4

--- a/solution.py
+++ b/solution.py
@@ -321,17 +321,30 @@
     return [ring_reduce(v, o[1], 0, late) for v, o in zip(values, orders)]
 
 
-def reduce_level(value):
+def crossed(value, bit):
+    depth = lax.axis_size("z")
+    return lax.ppermute(value, "z", [(i, i ^ bit) for i in range(depth)])
+
+
+def reduce_level(value, late=((), (), (), ())):
     depth, level = lax.axis_size("z"), lax.axis_index("z")
     rows, cols = value.shape
-    parts = value.reshape(depth, rows // depth, cols)
-    total = pick(parts, level, 0).astype(F32)
-    for step in range(1, depth):
-        total += shifted(pick(parts, level + step, 0), "z", step).astype(F32)
-    mine = total.astype(BF)
-    found = [mine] + [shifted(mine, "z", step) for step in range(1, depth)]
-    turned = jnp.stack(found[::-1] * 2)
-    return lax.dynamic_slice_in_dim(turned, depth - 1 - level, depth, 0).reshape(rows, cols)
+    bits = depth.bit_length() - 1
+    hold = lambda piece, first: after(piece, *first) if first else piece
+    moving = value.reshape(*(2,) * bits, rows // depth, cols)
+    for i in range(bits):
+        mine = (level >> i) & 1
+        at = bits - 1 - i
+        other = hold(crossed(pick(moving, 1 - mine, at), 1 << i), late[i])
+        moving = (other.astype(F32) + pick(moving, mine, at).astype(F32)).astype(BF)
+    for i in reversed(range(bits)):
+        mine = (level >> i) & 1
+        other = hold(crossed(moving, 1 << i), late[2 * bits - 1 - i])
+        at = bits - 1 - i
+        moving = jnp.where(
+            mine == 0, jnp.stack([moving, other], at), jnp.stack([other, moving], at)
+        )
+    return moving.reshape(rows, cols)
 
 
 def body(
@@ -386,29 +399,19 @@
         + [half(later[3], core, 1).reshape(rows, narrow)],
         axis=1,
     )
-    second_full, _, _ = gather_dp(after(second_shard, *first_far))
+    second_full, second_near, _ = gather_dp(after(second_shard, *first_far))
 
     chosen = (expert_ids[:, :, None] == jnp.arange(experts, dtype=jnp.int32)).any(axis=1)
     chosen_low = jnp.pad(chosen.astype(BF), ((0, 0), (0, 128 - experts)))
 
     levels = [0, depth // 2] + [step for step in range(1, depth) if step != depth // 2]
 
-    def spread_out(mine, paired, *filler):
-        found = {0: mine, levels[1]: shifted(mine, "z", levels[1])}
-        mine = after(mine, found[levels[1]], *filler)
-        for step in levels[2:]:
-            found[step] = shifted(mine, "z", step)
-        rest = [piece for step in levels[1:] for piece in (found[step], swap(found[step]))]
-        return [found[0], paired, *rest]
-
     grads_sent = jnp.concatenate([later[4], chosen_low], axis=1)
-    grads_all = spread_out(grads_sent, swap(grads_sent))
-    own = me * EXP_DEV + jnp.arange(EXP_DEV)
-    own_hot = (own[:, None] == jnp.arange(experts)[None, :]).astype(F32)
-    marks = jnp.stack([piece[:, width : width + experts] for piece in grads_all]).astype(F32)
-    mask = mm("ste,oe->ost", marks, own_hot)
-    slots = jnp.where(mask > 0, jnp.cumsum(mask, axis=2) - 1.0, -1.0).astype(jnp.int32)
-    slots = slots[:, :, None, :]
+    grads_pair = swap(grads_sent)
+    grads_far = {levels[1]: shifted(grads_sent, "z", levels[1])}
+    grads_next = after(grads_sent, grads_far[levels[1]])
+    for step in levels[2:]:
+        grads_far[step] = shifted(grads_next, "z", step)
 
     query_half = first_full[:, :wide]
     key_half = first_full[:, wide : 2 * wide]
@@ -443,7 +446,7 @@
     exps = jnp.exp(scores - row_max)
     attn_probs = exps / jnp.sum(exps, axis=-1, keepdims=True)
     probs_low = attn_probs.astype(BF)
-    context = flat(mm("shqk,skhd->sqhd", probs_low, values).astype(BF))
+    context = flat(mm("shqk,skhd->sqhd", probs_low, after(values, *second_near)).astype(BF))
     out_partial = product(context, output_half).reshape(2, length, width)
     attn_out = out_partial[0] + swap(out_partial[1].astype(BF)).astype(F32)
     residual = token_f[0] + attn_out
@@ -456,9 +459,20 @@
         [ffn_in, gates_high, gates_low, jnp.zeros((length, 128 - 2 * experts), BF)], axis=1
     )
     sent_other = swap(sent)
+    rows_far = {levels[1]: shifted(sent, "z", levels[1])}
+    grads_late = after([grads_far[step] for step in levels[1:]], sent)
+    grads_all = [grads_sent, grads_pair]
+    for piece in grads_late:
+        grads_all += [piece, swap(piece)]
+    own = me * EXP_DEV + jnp.arange(EXP_DEV)
+    own_hot = (own[:, None] == jnp.arange(experts)[None, :]).astype(F32)
+    named = jnp.stack([piece[:, width : width + experts] for piece in grads_all]).astype(F32)
+    mask = mm("ste,oe->ost", named, own_hot)
+    slots = jnp.where(mask > 0, jnp.cumsum(mask, axis=2) - 1.0, -1.0).astype(jnp.int32)
+    slots = slots[:, :, None, :]
 
     ffn_two = jnp.stack([ffn_in, sent_other[:, :width]]).reshape(2 * length, width)
-    grad_two = jnp.stack([out_grad, grads_all[1][:, :width]]).reshape(2 * length, width)
+    grad_two = jnp.stack([out_grad, grads_pair[:, :width]]).reshape(2 * length, width)
     shared_gate_act = product(ffn_two, gate_half)
     shared_up_act = product(ffn_two, up_half)
     shared_hidden = (jax.nn.silu(shared_gate_act) * shared_up_act).astype(BF)
@@ -476,14 +490,25 @@
         .astype(BF)
         .reshape(2, length, width)
     )
-    rows_all = spread_out(sent, sent_other, shared_gate_grad, shared_in_grad)
     shared_both = jnp.concatenate(
         [shared_in_grad, jnp.zeros((2, length, 128), BF), shared_out], axis=2
     )
     turn = lambda grad: joined(half(grad, core, 1), swap(half(grad, 1 - core, 1)), core, 0)
     shares = lambda value: value.reshape(side, side, value.shape[0] // dp, -1)
-    shared_orders = ("yx", "xy", "yx")
-    shared_part = [shares(g) for g in (shared_gate_grad, shared_up_grad, turn(shared_down_grad))]
+    down_turned = turn(shared_down_grad).reshape(width, narrow)
+    cut = narrow // 2
+    shared_part = [
+        jnp.concatenate([shared_gate_grad, down_turned[:, :cut]], axis=1),
+        jnp.concatenate([shared_up_grad, down_turned[:, cut:]], axis=1),
+    ]
+    sent_next = after(sent, rows_far[levels[1]], shared_in_grad, *shared_part)
+    for step in levels[2:]:
+        rows_far[step] = shifted(sent_next, "z", step)
+    rows_all = [sent, sent_other]
+    for step in levels[1:]:
+        rows_all += [rows_far[step], swap(rows_far[step])]
+    both = ("yx", "xy")
+    shared_part = [shares(part) for part in shared_part]
 
     place_me = me.reshape(1).astype(jnp.int32)
     block = owners // 2
@@ -492,12 +517,12 @@
         expert_gate, expert_up, expert_down, owners, 0,
     )
     wider = width + 128
-    shared_part = stage_one(shared_part, shared_orders, late=(near[block],))
+    shared_one = stage_one(shared_part, both, late=(near[block],))
     chips = [None] * depth
     for place_at in range(1, depth // 2):
         chips[place_at] = near[2 * place_at].astype(F32) + swap(near[2 * place_at + 1]).astype(F32)
     sent_back = [None] + [chips[i][:, :wider].astype(BF) for i in range(1, depth // 2)]
-    far_slots = after(slots[:, block:], *sent_back[1:])
+    far_slots = after(slots[:, block:], *sent_back[1:], *shared_one)
     far = expert_call(
         place_me, far_slots, rows_all[block:], grads_all[block:],
         expert_gate, expert_up, expert_down, owners, 1, near[block:],
@@ -508,23 +533,24 @@
         chips[place_at] = mine.astype(F32) + swap(other).astype(F32)
         sent_back.append(chips[place_at][:, :wider].astype(BF))
     back_in = [shifted(sent_back[i], "z", -levels[i]) for i in range(1, depth)]
-    shared_part = stage_two(shared_part, shared_orders, late=(far[block],))
+    chips[0] = (near[0].astype(F32) + shared_both[0].astype(F32)) + swap(
+        near[1] + shared_both[1]
+    ).astype(F32)
+    back = chips[0][:, :wider]
+    for piece in back_in[: depth // 2 - 1]:
+        back += after(piece, far[block]).astype(F32)
+    shared_two = stage_two(shared_one, both, late=(far[block],))
+    routed_gate_grad = after(routed_gate_grad, *sent_back[depth // 2 :], back)
 
     gate_grad = mm("erd,erf->edf", expert_in, routed_gate_grad).astype(BF)
     up_grad = mm("erd,erf->edf", expert_in, routed_up_grad).astype(BF)
     down_grad = mm("erf,erd->efd", routed_hidden, res_grad).astype(BF)
-    both = ("yx", "xy")
     blocks = [
         [grad[e].reshape(side, side, grad.shape[1] // dp, grad.shape[2]) for e in range(EXP_DEV)]
         for grad in (gate_grad, up_grad, down_grad)
     ]
-    gate_one = stage_one(blocks[0], both)
-    back_in = after(back_in, *gate_one)
-    chips[0] = (near[0].astype(F32) + shared_both[0].astype(F32)) + swap(
-        near[1] + shared_both[1]
-    ).astype(F32)
-    back = chips[0][:, :wider]
-    for piece in back_in:
+    gate_one = stage_one(blocks[0], both, shared_two)
+    for piece in after(back_in[depth // 2 - 1 :], *gate_one):
         back += piece.astype(F32)
 
     probs_grad = back[:, width : width + experts] + back[:, width + experts : width + 2 * experts]
@@ -542,8 +568,6 @@
         - residual * norm_two**3 * jnp.mean(upstream_two * residual, axis=-1, keepdims=True)
     )
     residual_low = residual_grad.astype(BF)
-    up_one = stage_one(blocks[1], both, gate_one, (residual_low,))
-    gate_two = stage_two(gate_one, both, (back,), ())
     attn_grad_two = two(residual_low).reshape(2 * length, width)
     output_grad = product(context.T, attn_grad_two).astype(BF)
     output_grad = turn(output_grad)
@@ -552,8 +576,6 @@
     probs_grad_att = mm("sqhd,skhd->shqk", context_grad, values)
     row_delta = jnp.sum(attn_probs * probs_grad_att, axis=-1, keepdims=True)
     scores_grad = (attn_probs * (probs_grad_att - row_delta)).astype(BF)
-    down_one = stage_one(blocks[2], both, up_one, (scores_grad,))
-    up_two = stage_two(up_one, both, gate_two, (scores_grad,))
     query_grad = mm("shqk,skhd->sqhd", scores_grad, key_rot) * score_scale
     key_grad = mm("shqk,sqhd->skhd", scores_grad, query_rot) * score_scale
     query_pre_grad = flat(rotate(query_grad, cosine, -sine_part).astype(BF))
@@ -579,24 +601,27 @@
         [router_grad, attn_gain_grad[:, None], ffn_gain_grad[:, None]], axis=1
     ).astype(BF)
     small_grads = jnp.pad(small_grads, ((0, 0), (0, 128 - small_grads.shape[1])))
-    early = stage_one([shares(output_grad), shares(value_wgrad)], both, (*down_one, *up_two))
-    down_two = stage_two(down_one, both)
-    early = stage_two(early, both)
+    marks = ((value_grad,), (scores_grad,), (query_wgrad,), ())
+    up_one = stage_one(blocks[1], both, gate_one, marks[0])
+    gate_two = stage_two(gate_one, both, up_one, marks[1])
+    early = [shares(output_grad), shares(value_wgrad)]
+    early_one = stage_one(early, both, gate_two, marks[2])
+    early_two = stage_two(early_one, both)
     late = [shares(query_wgrad), shares(jnp.concatenate([key_wgrad, small_grads], axis=1))]
-    late = stage_two(stage_one(late, both, early), both)
+    late_one = stage_one(late, both, early_one)
+    late_two = stage_two(late_one, both, early_two)
+    up_two = stage_two(up_one, both, late_one)
+    down_two = stage_two(stage_one(blocks[2], both, late_two), both)
     expert_shares = [jnp.stack(pair).astype(F32) for pair in (gate_two, up_two, down_two)]
-    shared_share = lax.psum(
-        jnp.concatenate([*shared_part[:2], shared_part[2].reshape(rows, narrow)], axis=1), "z"
-    )
-    early_share = reduce_level(jnp.concatenate(early, axis=1))
-    late_share = reduce_level(jnp.concatenate(late, axis=1))
+    shared_share = reduce_level(after(jnp.concatenate(shared_two, axis=1), back), marks)
+    early_share = reduce_level(jnp.concatenate(early_two, axis=1))
+    late_share = reduce_level(jnp.concatenate(late_two, axis=1))
 
     moe_out = chips[0][:, wider:]
+    piece = back
     for i in range(1, depth):
-        moving = after(chips[i][:, wider:].astype(BF), back)
-        if i > 1:
-            moving = after(moving, piece)
-        piece = after(shifted(moving, "z", -levels[i]), (scores_grad, query_wgrad, early[0])[min(i - 1, 2)])
+        moving = after(chips[i][:, wider:].astype(BF), piece)
+        piece = after(shifted(moving, "z", -levels[i]), *marks[min(i - 1, 2)])
         moe_out += piece.astype(F32)
 
     early_other, late_other, shared_other = swap(early_share), swap(late_share), swap(shared_share)
@@ -604,12 +629,10 @@
         mine[:, start : start + size], other[:, start : start + size], core, 1
     ).astype(F32)
     small_sum = late_share[:, 2 * wide :].astype(F32) + late_other[:, 2 * wide :].astype(F32)
-    down_rows = joined(
-        shared_share[:, 2 * narrow :].reshape(-1, wide),
-        shared_other[:, 2 * narrow :].reshape(-1, wide),
-        core,
-        1,
-    ).astype(F32)
+    down_cols = lambda share: jnp.concatenate(
+        [share[:, narrow : narrow + cut], share[:, 2 * narrow + cut :]], axis=1
+    ).reshape(-1, wide)
+    down_rows = joined(down_cols(shared_share), down_cols(shared_other), core, 1).astype(F32)
 
     stream_out = residual + moe_out
     stat_rms = jnp.stack(
@@ -630,7 +653,7 @@
         small_sum[:, experts + 1],
         small_sum[:, :experts],
         column(shared_share, shared_other, 0, narrow),
-        column(shared_share, shared_other, narrow, narrow),
+        column(shared_share, shared_other, narrow + cut, narrow),
         down_rows,
         *expert_shares,
         stat_rms,

time: 682 us -> 650 us (0.953)
  waiting for transfers between devices: 208 us -> 173 us
  between operations: 19.6 us -> 6.17 us
  starting transfers between devices: 76.3 us -> 88.6 us
    ppermute x81 -> x67, waiting for transfers between devices: 200 us -> 125 us  [shifted(): lax.ppermute(value, axis, [(i, (i + by) % size) for i in range(size)])]
    ppermute x0 -> x12, waiting for transfers between devices: none -> 47.7 us  [crossed(): return lax.ppermute(value, 'z', [(i, i ^ bit) for i in range(depth)])]
    ppermute x0 -> x12, starting transfers between devices: none -> 18.8 us  [crossed(): return lax.ppermute(value, 'z', [(i, i ^ bit) for i in range(depth)])]
    psum x1 -> x0, waiting for transfers between devices: 7.38 us -> none  [body(): lax.psum(jnp.concatenate([*shared_part[:2], shared_part[2].reshape(rows,...]
    ppermute x81 -> x67, starting transfers between devices: 76.3 us -> 69.8 us  [shifted(): lax.ppermute(value, axis, [(i, (i + by) % size) for i in range(size)])]
    convert_element_type x24 -> x20, other arithmetic: 24 us -> 19.4 us  [ring_reduce(): (other.astype(F32) + pick(value, index - step, at).astype(F32)).astype(BF)]
    squeeze x28 -> x30, local copies, waits for them, and re-layouts: 16.4 us -> 11.8 us  [pick(): lax.dynamic_index_in_dim(value, index % value.shape[axis], axis, False)]
    unnamed x222 -> x220, local copies, waits for them, and re-layouts: 13.1 us -> 16.3 us
  transfers between devices with their start and end apart: 82 -> 79, of which waited for: 28 -> 25; matrix products, arithmetic and copies ran while one was open for 38% -> 41% of each run, Pallas kernels for 12% -> 12%
where the time goes in v5:
time: 650 us; the launch traced here: 644 us
  waiting for transfers between devices  173 us (27%)
  local copies, waits for them, and re-layouts  126 us (19%)
  other arithmetic  92.3 us (14%)
  starting transfers between devices  88.6 us (14%)
  Pallas kernels  79.7 us (12%)
  matrix products  78.1 us (12%)
    ppermute x67, waiting for transfers between devices, shifted(): lax.ppermute(value, axis, [(i, (i + by) % size) for i in range(size)])  125 us
    ppermute x67, starting transfers between devices, shifted(): lax.ppermute(value, axis, [(i, (i + by) % size) for i in range(size)])  69.8 us
    pallas_call x2, Pallas kernels, expert_call(): pl.pallas_call(functools.partial(expert_kernel, count, width, capacity, e...  69.4 us
    ppermute x12, waiting for transfers between devices, crossed(): return lax.ppermute(value, 'z', [(i, i ^ bit) for i in range(depth)])  47.7 us
    dot_general x22, matrix products, product(): return jnp.dot(first_arg, second_arg, preferred_element_type=F32)  40.5 us
    dot_general x9, matrix products, mm(): return jnp.einsum(spec, first_arg, second_arg, preferred_element_type=F32)  32.7 us
    convert_element_type x20, other arithmetic, ring_reduce(): (other.astype(F32) + pick(value, index - step, at).astype(F32)).astype(BF)  19.4 us
    ppermute x12, starting transfers between devices, crossed(): return lax.ppermute(value, 'z', [(i, i ^ bit) for i in range(depth)])  18.8 us
  transfers between devices with their start and end apart: 79, of which 25 were waited for; matrix products, arithmetic and copies ran while one was open for 41% of the time, Pallas kernels for 12%

profile of v5, /device:TPU:0, one launch (start us, length us, event | category | flops | bytes accessed | tf_op | source)
XLA Modules:
  0.0 643.7 jit_solution(14720709339951991593)
XLA Ops:
  18.9 18.7 %collective-permute-done.2.refs_2_ = bf16[320,2048]{1,0:T(8,128)(2,1)} collective-permute-done((bf16[320,2048]{1,0:T(8,128)(2,1)}, bf16[320,2048]{1,0:T(8,128)(2,1)}, u32[]{:S(2)}, u32[]{:S(2)}) %collective-permute-start.2) | collective-permute-done | bytes 1310752 | tf_op jit(solution)/shard_map/ppermute | solution.py:242
  56.8 3.9 concatenate.178.refs_0_
  61.7 5.2 place.2
  66.9 3.9 slice_bitcast_fusion.1
  83.4 8.8 %collective-permute-done.6.refs_2_ = bf16[320,1984]{1,0:T(8,128)(2,1)} collective-permute-done((bf16[320,1984]{1,0:T(8,128)(2,1)}, bf16[320,1984]{1,0:T(8,128)(2,1)}, u32[]{:S(2)}, u32[]{:S(2)}) %collective-permute-start.6) | collective-permute-done | bytes 1269792 | tf_op jit(solution)/shard_map/ppermute | solution.py:242
  99.0 10.5 %collective-permute-done.9.refs_4_ = bf16[160,1984]{1,0:T(8,128)(2,1)S(1)} collective-permute-done((bf16[160,1984]{1,0:T(8,128)(2,1)S(1)}, bf16[160,1984]{1,0:T(8,128)(2,1)S(1)}, u32[]{:S(2)}, u32[]{:S(2)}) %collective-permute-start.9) | collective-permute-done | bytes 634912 | tf_op jit(solution)/shard_map/ppermute | solution.py:242
  111.1 5.2 place.3
  134.1 13.1 %collective-permute-start.14 = (bf16[256,1408]{1,0:T(8,128)(2,1)}, bf16[256,1408]{1,0:T(8,128)(2,1)}, u32[]{:S(2)}, u32[]{:S(2)}) collective-permute-start(bf16[256,1408]{1,0:T(8,128)(2,1)} %pad_maximum_fusion.11.refs_4_), channel_id=1, source_target_pairs={{0,2},{2,4},{4,6},{6,0},{1,3},{3,5},{5,7},{7,1},{8,10},{10,12},{12... | collective-permute-start | bytes 2162696 | tf_op jit(solution)/shard_map/ppermute | solution.py:242
  163.1 3.9 collective-permute-done.15.refs_6_
  218.9 3.7 copy.289
  225.2 3.7 copy.287
  236.3 34.8 %experts.2 = (bf16[256,2688]{1,0:T(8,128)(2,1)}, bf16[256,2688]{1,0:T(8,128)(2,1)}, bf16[256,2688]{1,0:T(8,128)(2,1)}, bf16[256,2688]{1,0:T(8,128)(2,1)}, bf16[2...) custom-call(s32[1]{0:T(128)} %bitcast.20.me_ref, ...), custom_call_target="tpu_custom_call" | custom-call | flops 16441671680 | bytes 62914560 | tf_op jit(solution)/shard_map/experts/pallas_call | solution.py:133
  282.5 34.6 %experts.3 = (bf16[256,2688]{1,0:T(8,128)(2,1)}, bf16[256,2688]{1,0:T(8,128)(2,1)}, bf16[256,2688]{1,0:T(8,128)(2,1)}, bf16[256,2688]{1,0:T(8,128)(2,1)}, bf16[2...) custom-call(s32[1]{0:T(128)} %bitcast.20.me_ref, ...), custom_call_target="tpu_custom_call", output_to_operand_aliasing={{4}: (13, {}), {5}: (14, {}), {6}: (15, {}), {7}: (16, {}),... | custom-call | flops 16441671680 | bytes 62914560 | tf_op jit(solution)/shard_map/experts/pallas_call | solution.py:133
  317.1 9.1 %convolution_convert_fusion.1 = bf16[2,1280,896]{2,1,0:T(8,128)(2,1)S(1)} fusion(bf16[2,1024,1280]{2,1,0:T(8,128)(2,1)} %get-tuple-element.111, bf16[2,1024,896]{2,1,0:T(8,128)(2,1)} %get-tuple-element.131), kind=kOutput, calls=%fused_computation.2 | convolution fusion | flops 4699914240 | bytes 13500416 | tf_op jit(solution)/shard_map/erd,erf->edf/dot_general | solution.py:196
  326.8 8.7 %convolution_convert_fusion = bf16[2,896,1280]{2,1,0:T(8,128)(2,1)S(1)} fusion(bf16[2,1024,896]{2,1,0:T(8,128)(2,1)} %get-tuple-element.154, bf16[2,1024,1280]{2,1,0:T(8,128)(2,1)} %get-tuple-element.155), kind=kOutput, calls=%fused_computation.1 | convolution fusion | flops 4699914240 | bytes 13500416 | tf_op jit(solution)/shard_map/erf,erd->efd/dot_general | solution.py:196
  348.6 8.2 %convolution_convert_fusion.2 = bf16[2,1280,896]{2,1,0:T(8,128)(2,1)S(1)} fusion(bf16[2,1024,1280]{2,1,0:T(8,128)(2,1)S(1)} %copy-done.98, bf16[2,1024,896]{2,1,0:T(8,128)(2,1)} %get-tuple-element.118), kind=kOutput, calls=%fused_computation.3 | convolution fusion | flops 4699914240 | bytes 13500416 | tf_op jit(solution)/shard_map/erd,erf->edf/dot_general | solution.py:196
  368.7 15.8 %collective-permute-done.38 = bf16[2,320,896]{2,1,0:T(8,128)(2,1)S(1)} collective-permute-done((bf16[2,320,896]{2,1,0:T(8,128)(2,1)S(1)}, bf16[2,320,896]{2,1,0:T(8,128)(2,1)S(1)}, u32[]{:S(2)}, u32[]{:S(2)}) %collective-permute-start.38) | collective-permute-done | bytes 1146912 | tf_op jit(solution)/shard_map/ppermute | solution.py:242
  387.2 9.8 %collective-permute-done.33 = bf16[256,1408]{1,0:T(8,128)(2,1)S(1)} collective-permute-done((bf16[256,1408]{1,0:T(8,128)(2,1)S(1)}, bf16[256,1408]{1,0:T(8,128)(2,1)S(1)}, u32[]{:S(2)}, u32[]{:S(2)}) %collective-permute-start.33) | collective-permute-done | bytes 720928 | tf_op jit(solution)/shard_map/ppermute | solution.py:242
  429.1 11.6 %collective-permute-done.40 = bf16[256,1280]{1,0:T(8,128)(2,1)} collective-permute-done((bf16[256,1280]{1,0:T(8,128)(2,1)}, bf16[256,1280]{1,0:T(8,128)(2,1)}, u32[]{:S(2)}, u32[]{:S(2)}) %collective-permute-start.40) | collective-permute-done | bytes 655392 | tf_op jit(solution)/shard_map/ppermute | solution.py:242
  453.7 12.2 %collective-permute-done.70 = bf16[80,1344]{1,0:T(8,128)(2,1)S(1)} collective-permute-done((bf16[80,1344]{1,0:T(8,128)(2,1)S(1)}, bf16[80,1344]{1,0:T(8,128)(2,1)S(1)}, u32[]{:S(2)}, u32[]{:S(2)}) %collective-permute-start.70) | collective-permute-done | bytes 215072 | tf_op jit(solution)/shard_map/ppermute | solution.py:326
  467.7 4.5 collective-permute-start.71
  484.8 4.1 copy.302
  517.7 6.1 collective-permute-done.51
  531.9 5.8 collective-permute-done.55
  544.6 9.2 %collective-permute-done.52 = bf16[2,320,640]{2,1,0:T(8,128)(2,1)S(1)} collective-permute-done((bf16[2,320,640]{2,1,0:T(8,128)(2,1)S(1)}, bf16[2,320,640]{2,1,0:T(8,128)(2,1)S(1)}, u32[]{:S(2)}, u32[]{:S(2)}) %collective-permute-start.52) | collective-permute-done | bytes 819232 | tf_op jit(solution)/shard_map/ppermute | solution.py:242
  557.2 6.6 %collective-permute-done.53 = bf16[2,320,768]{2,1,0:T(8,128)(2,1)S(1)} collective-permute-done((bf16[2,320,768]{2,1,0:T(8,128)(2,1)S(1)}, bf16[2,320,768]{2,1,0:T(8,128)(2,1)S(1)}, u32[]{:S(2)}, u32[]{:S(2)}) %collective-permute-start.53) | collective-permute-done | bytes 983072 | tf_op jit(solution)/shard_map/ppermute | solution.py:242
  569.6 6.7 %collective-permute-done.65 = bf16[80,1280]{1,0:T(8,128)(2,1)S(1)} collective-permute-done((bf16[80,1280]{1,0:T(8,128)(2,1)S(1)}, bf16[80,1280]{1,0:T(8,128)(2,1)S(1)}, u32[]{:S(2)}, u32[]{:S(2)}) %collective-permute-start.65) | collective-permute-done | bytes 204832 | tf_op jit(solution)/shard_map/ppermute | solution.py:326
  582.4 6.8 %collective-permute-done.74 = bf16[320,896]{1,0:T(8,128)(2,1)S(1)} collective-permute-done((bf16[320,896]{1,0:T(8,128)(2,1)S(1)}, bf16[320,896]{1,0:T(8,128)(2,1)S(1)}, u32[]{:S(2)}, u32[]{:S(2)}) %collective-permute-start.74) | collective-permute-done | bytes 573472 | tf_op jit(solution)/shard_map/ppermute | solution.py:242
  598.2 8.7 %collective-permute-done.59 = bf16[80,1408]{1,0:T(8,128)(2,1)S(1)} collective-permute-done((bf16[80,1408]{1,0:T(8,128)(2,1)S(1)}, bf16[80,1408]{1,0:T(8,128)(2,1)S(1)}, u32[]{:S(2)}, u32[]{:S(2)}) %collective-permute-start.59) | collective-permute-done | bytes 225312 | tf_op jit(solution)/shard_map/ppermute | solution.py:326
  607.2 12.2 %collective-permute-done.60 = bf16[80,1408]{1,0:T(8,128)(2,1)S(1)} collective-permute-done((bf16[80,1408]{1,0:T(8,128)(2,1)S(1)}, bf16[80,1408]{1,0:T(8,128)(2,1)S(1)}, u32[]{:S(2)}, u32[]{:S(2)}) %collective-permute-start.60) | collective-permute-done | bytes 225312 | tf_op jit(solution)/shard_map/ppermute | solution.py:326
  626.3 3.7 collective-permute-done.61
  630.4 5.6 collective-permute-done.78
  (631 shorter events, 332.2 us)
Async XLA Ops:
  5.5 32.1 %collective-permute-start.2 = (bf16[320,2048]{1,0:T(8,128)(2,1)}, bf16[320,2048]{1,0:T(8,128)(2,1)}, u32[]{:S(2)}, u32[]{:S(2)}) collective-permute-start(bf16[320,2048]{1,0:T(8,128)(2,1)} %fusion.33.refs_0_), channel_id=1, source_target_pairs={{0,16},{16,0},{1,17},{17,1},{2,18},{18,2},{3,19},{19,3},{4,20},{20... | collective-permute-start | bytes 3932168 | tf_op jit(solution)/shard_map/ppermute | solution.py:242
  8.5 32.8 %collective-permute-start.1 = (bf16[320,2048]{1,0:T(8,128)(2,1)}, bf16[320,2048]{1,0:T(8,128)(2,1)}, u32[]{:S(2)}, u32[]{:S(2)}) collective-permute-start(bf16[320,2048]{1,0:T(8,128)(2,1)} %fusion.33.refs_0_), channel_id=1, source_target_pairs={{0,8},{8,0},{1,9},{9,1},{2,10},{10,2},{3,11},{11,3},{4,12},{12,4},... | collective-permute-start | bytes 3932168 | tf_op jit(solution)/shard_map/ppermute | solution.py:242
  45.7 87.4 %collective-permute-start.13 = (bf16[256,1408]{1,0:T(8,128)(2,1)}, bf16[256,1408]{1,0:T(8,128)(2,1)}, u32[]{:S(2)}, u32[]{:S(2)}) collective-permute-start(bf16[256,1408]{1,0:T(8,128)(2,1)} %pad_maximum_fusion.11.refs_4_), channel_id=1, source_target_pairs={{0,4},{2,6},{4,0},{6,2},{1,5},{3,7},{5,1},{7,3},{8,12},{10,14},{12... | collective-permute-start | bytes 2162696 | tf_op jit(solution)/shard_map/ppermute | solution.py:242
  48.3 98.9 %collective-permute-start.12 = (bf16[256,1408]{1,0:T(8,128)(2,1)}, bf16[256,1408]{1,0:T(8,128)(2,1)}, u32[]{:S(2)}, u32[]{:S(2)}) collective-permute-start(bf16[256,1408]{1,0:T(8,128)(2,1)} %pad_maximum_fusion.11.refs_4_), channel_id=1, source_target_pairs={{0,1},{1,0},{2,3},{3,2},{4,5},{5,4},{6,7},{7,6},{8,9},{9,8},{10,11... | collective-permute-start | bytes 2162696 | tf_op jit(solution)/shard_map/ppermute | solution.py:242
  60.6 31.5 %collective-permute-start.6 = (bf16[320,1984]{1,0:T(8,128)(2,1)}, bf16[320,1984]{1,0:T(8,128)(2,1)}, u32[]{:S(2)}, u32[]{:S(2)}) collective-permute-start(bf16[320,1984]{1,0:T(8,128)(2,1)} %concatenate.178.refs_0_), channel_id=1, source_target_pairs={{0,16},{16,0},{1,17},{17,1},{2,18},{18,2},{3,19},{19,3},{4,20},{20... | collective-permute-start | bytes 3809288 | tf_op jit(solution)/shard_map/ppermute | solution.py:242
  61.2 32.7 %collective-permute-start.5 = (bf16[320,1984]{1,0:T(8,128)(2,1)}, bf16[320,1984]{1,0:T(8,128)(2,1)}, u32[]{:S(2)}, u32[]{:S(2)}) collective-permute-start(bf16[320,1984]{1,0:T(8,128)(2,1)} %concatenate.178.refs_0_), channel_id=1, source_target_pairs={{0,8},{8,0},{1,9},{9,1},{2,10},{10,2},{3,11},{11,3},{4,12},{12,4},... | collective-permute-start | bytes 3809288 | tf_op jit(solution)/shard_map/ppermute | solution.py:242
  123.5 27.6 %collective-permute-start.10 = (bf16[1088,640]{1,0:T(8,128)(2,1)}, bf16[1088,640]{1,0:T(8,128)(2,1)}, u32[]{:S(2)}, u32[]{:S(2)}) collective-permute-start(bf16[1088,640]{1,0:T(8,128)(2,1)} %pad_maximum_fusion.4), channel_id=1, source_target_pairs={{0,1},{1,0},{2,3},{3,2},{4,5},{5,4},{6,7},{7,6},{8,9},{9,8},{10,11... | collective-permute-start | bytes 4177928 | tf_op jit(solution)/shard_map/ppermute | solution.py:242
  133.1 33.8 %collective-permute-start.15 = (bf16[256,1408]{1,0:T(8,128)(2,1)}, bf16[256,1408]{1,0:T(8,128)(2,1)}, u32[]{:S(2)}, u32[]{:S(2)}) collective-permute-start(bf16[256,1408]{1,0:T(8,128)(2,1)} %pad_maximum_fusion.11.refs_4_), channel_id=1, source_target_pairs={{0,6},{2,0},{4,2},{6,4},{1,7},{3,1},{5,3},{7,5},{8,14},{10,8},{12,... | collective-permute-start | bytes 2162696 | tf_op jit(solution)/shard_map/ppermute | solution.py:242
  134.1 32.8 %collective-permute-start.14 = (bf16[256,1408]{1,0:T(8,128)(2,1)}, bf16[256,1408]{1,0:T(8,128)(2,1)}, u32[]{:S(2)}, u32[]{:S(2)}) collective-permute-start(bf16[256,1408]{1,0:T(8,128)(2,1)} %pad_maximum_fusion.11.refs_4_), channel_id=1, source_target_pairs={{0,2},{2,4},{4,6},{6,0},{1,3},{3,5},{5,7},{7,1},{8,10},{10,12},{12... | collective-permute-start | bytes 2162696 | tf_op jit(solution)/shard_map/ppermute | solution.py:242
  170.0 35.5 %collective-permute-start.20 = (bf16[256,1408]{1,0:T(8,128)(2,1)}, bf16[256,1408]{1,0:T(8,128)(2,1)}, u32[]{:S(2)}, u32[]{:S(2)}) collective-permute-start(bf16[256,1408]{1,0:T(8,128)(2,1)} %concatenate.185.refs_0_), channel_id=1, source_target_pairs={{0,4},{2,6},{4,0},{6,2},{1,5},{3,7},{5,1},{7,3},{8,12},{10,14},{12... | collective-permute-start | bytes 2162696 | tf_op jit(solution)/shard_map/ppermute | solution.py:242
  205.5 30.8 %collective-permute-start.21 = (bf16[256,1408]{1,0:T(8,128)(2,1)}, bf16[256,1408]{1,0:T(8,128)(2,1)}, u32[]{:S(2)}, u32[]{:S(2)}) collective-permute-start(bf16[256,1408]{1,0:T(8,128)(2,1)} %collective-permute-done.20.refs_2_), channel_id=1, source_target_pairs={{0,1},{1,0},{2,3},{3,2},{4,5},{5,4},{6,7},{7,6},{8,9},{9,8},{10,11... | collective-permute-start | bytes 2162696 | tf_op jit(solution)/shard_map/ppermute | solution.py:242
  228.9 45.4 %collective-permute-start.30 = (bf16[256,1408]{1,0:T(8,128)(2,1)}, bf16[256,1408]{1,0:T(8,128)(2,1)}, u32[]{:S(2)}, u32[]{:S(2)}) collective-permute-start(bf16[256,1408]{1,0:T(8,128)(2,1)} %concatenate.185.refs_0_), channel_id=1, source_target_pairs={{0,6},{2,0},{4,2},{6,4},{1,7},{3,1},{5,3},{7,5},{8,14},{10,8},{12,... | collective-permute-start | bytes 2162696 | tf_op jit(solution)/shard_map/ppermute | solution.py:242
  231.1 43.7 %collective-permute-start.28 = (bf16[256,1408]{1,0:T(8,128)(2,1)}, bf16[256,1408]{1,0:T(8,128)(2,1)}, u32[]{:S(2)}, u32[]{:S(2)}) collective-permute-start(bf16[256,1408]{1,0:T(8,128)(2,1)} %concatenate.185.refs_0_), channel_id=1, source_target_pairs={{0,2},{2,4},{4,6},{6,0},{1,3},{3,5},{5,7},{7,1},{8,10},{10,12},{12... | collective-permute-start | bytes 2162696 | tf_op jit(solution)/shard_map/ppermute | solution.py:242
  233.3 41.6 %collective-permute-start.27 = (bf16[2,320,672]{2,1,0:T(8,128)(2,1)}, bf16[2,320,672]{2,1,0:T(8,128)(2,1)}, u32[]{:S(2)}, u32[]{:S(2)}) collective-permute-start(bf16[2,320,672]{2,1,0:T(8,128)(2,1)} %dynamic-slice_bitcast_fusion.7), channel_id=1, source_target_pairs={{0,8},{8,0},{1,9},{9,1},{2,10},{10,2},{3,11},{11,3},{4,12},{12,4},... | collective-permute-start | bytes 2580488 | tf_op jit(solution)/shard_map/ppermute | solution.py:242
  235.8 39.5 %collective-permute-start.26 = (bf16[2,320,672]{2,1,0:T(8,128)(2,1)}, bf16[2,320,672]{2,1,0:T(8,128)(2,1)S(1)}, u32[]{:S(2)}, u32[]{:S(2)}) collective-permute-start(bf16[2,320,672]{2,1,0:T(8,128)(2,1)} %dynamic-slice_bitcast_fusion.8), channel_id=1, source_target_pairs={{0,16},{16,0},{1,17},{17,1},{2,18},{18,2},{3,19},{19,3},{4,20},{20... | collective-permute-start | bytes 2580488 | tf_op jit(solution)/shard_map/ppermute | solution.py:242
  274.3 61.3 %collective-permute-start.22 = (bf16[256,2688]{1,0:T(8,128)(2,1)}, bf16[256,2688]{1,0:T(8,128)(2,1)}, u32[]{:S(2)}, u32[]{:S(2)}) collective-permute-start(bf16[256,2688]{1,0:T(8,128)(2,1)} %fusion.29), channel_id=1, source_target_pairs={{0,1},{1,0},{2,3},{3,2},{4,5},{5,4},{6,7},{7,6},{8,9},{9,8},{10,11... | collective-permute-start | bytes 4128776 | tf_op jit(solution)/shard_map/ppermute | solution.py:242
  277.0 60.5 %collective-permute-start.37 = (bf16[320,672]{1,0:T(8,128)(2,1)S(1)}, bf16[320,672]{1,0:T(8,128)(2,1)}, u32[]{:S(2)}, u32[]{:S(2)}) collective-permute-start(bf16[320,672]{1,0:T(8,128)(2,1)S(1)} %dynamic-slice_bitcast_fusion.19), channel_id=1, source_target_pairs={{0,16},{16,0},{1,17},{17,1},{2,18},{18,2},{3,19},{19,3},{4,20},{20... | collective-permute-start | bytes 1290248 | tf_op jit(solution)/shard_map/ppermute | solution.py:242
  279.7 46.5 %collective-permute-start.36 = (bf16[320,672]{1,0:T(8,128)(2,1)}, bf16[320,672]{1,0:T(8,128)(2,1)}, u32[]{:S(2)}, u32[]{:S(2)}) collective-permute-start(bf16[320,672]{1,0:T(8,128)(2,1)} %dynamic-slice_bitcast_fusion.20), channel_id=1, source_target_pairs={{0,8},{8,0},{1,9},{9,1},{2,10},{10,2},{3,11},{11,3},{4,12},{12,4},... | collective-permute-start | bytes 1290248 | tf_op jit(solution)/shard_map/ppermute | solution.py:242
  281.5 59.5 %collective-permute-start.24 = (bf16[256,1408]{1,0:T(8,128)(2,1)}, bf16[256,1408]{1,0:T(8,128)(2,1)}, u32[]{:S(2)}, u32[]{:S(2)}) collective-permute-start(bf16[256,1408]{1,0:T(8,128)(2,1)} %slice.396), channel_id=1, source_target_pairs={{0,4},{2,6},{4,0},{6,2},{1,5},{3,7},{5,1},{7,3},{8,12},{10,14},{12... | collective-permute-start | bytes 2162696 | tf_op jit(solution)/shard_map/ppermute | solution.py:242
  357.3 27.3 %collective-permute-start.38 = (bf16[2,320,896]{2,1,0:T(8,128)(2,1)S(1)}, bf16[2,320,896]{2,1,0:T(8,128)(2,1)S(1)}, u32[]{:S(2)}, u32[]{:S(2)}) collective-permute-start(bf16[2,320,896]{2,1,0:T(8,128)(2,1)S(1)} %dynamic-slice_bitcast_fusion.5), channel_id=1, source_target_pairs={{0,16},{16,0},{1,17},{17,1},{2,18},{18,2},{3,19},{19,3},{4,20},{20... | collective-permute-start | bytes 3440648 | tf_op jit(solution)/shard_map/ppermute | solution.py:242
  358.3 27.5 %collective-permute-start.39 = (bf16[2,320,896]{2,1,0:T(8,128)(2,1)S(1)}, bf16[2,320,896]{2,1,0:T(8,128)(2,1)S(1)}, u32[]{:S(2)}, u32[]{:S(2)}) collective-permute-start(bf16[2,320,896]{2,1,0:T(8,128)(2,1)S(1)} %dynamic-slice_bitcast_fusion.4), channel_id=1, source_target_pairs={{0,8},{8,0},{1,9},{9,1},{2,10},{10,2},{3,11},{11,3},{4,12},{12,4},... | collective-permute-start | bytes 3440648 | tf_op jit(solution)/shard_map/ppermute | solution.py:242
  362.3 34.6 %collective-permute-start.33 = (bf16[256,1408]{1,0:T(8,128)(2,1)S(1)}, bf16[256,1408]{1,0:T(8,128)(2,1)S(1)}, u32[]{:S(2)}, u32[]{:S(2)}) collective-permute-start(bf16[256,1408]{1,0:T(8,128)(2,1)S(1)} %copy-done.68), channel_id=1, source_target_pairs={{0,6},{2,0},{4,2},{6,4},{1,7},{3,1},{5,3},{7,5},{8,14},{10,8},{12,... | collective-permute-start | bytes 2162696 | tf_op jit(solution)/shard_map/ppermute | solution.py:242
  365.2 31.8 %collective-permute-start.35 = (bf16[256,1408]{1,0:T(8,128)(2,1)S(1)}, bf16[256,1408]{1,0:T(8,128)(2,1)S(1)}, u32[]{:S(2)}, u32[]{:S(2)}) collective-permute-start(bf16[256,1408]{1,0:T(8,128)(2,1)S(1)} %copy-done.69), channel_id=1, source_target_pairs={{0,2},{2,4},{4,6},{6,0},{1,3},{3,5},{5,7},{7,1},{8,10},{10,12},{12... | collective-permute-start | bytes 2162696 | tf_op jit(solution)/shard_map/ppermute | solution.py:242
  402.9 37.7 %collective-permute-start.40 = (bf16[256,1280]{1,0:T(8,128)(2,1)}, bf16[256,1280]{1,0:T(8,128)(2,1)}, u32[]{:S(2)}, u32[]{:S(2)}) collective-permute-start(bf16[256,1280]{1,0:T(8,128)(2,1)} %slice.394), channel_id=1, source_target_pairs={{0,4},{2,6},{4,0},{6,2},{1,5},{3,7},{5,1},{7,3},{8,12},{10,14},{12... | collective-permute-start | bytes 1966088 | tf_op jit(solution)/shard_map/ppermute | solution.py:242
  405.5 69.3 %collective-permute-start.47 = (bf16[2,320,896]{2,1,0:T(8,128)(2,1)}, bf16[2,320,896]{2,1,0:T(8,128)(2,1)}, u32[]{:S(2)}, u32[]{:S(2)}) collective-permute-start(bf16[2,320,896]{2,1,0:T(8,128)(2,1)} %dynamic-slice_bitcast_fusion.2), channel_id=1, source_target_pairs={{0,8},{8,0},{1,9},{9,1},{2,10},{10,2},{3,11},{11,3},{4,12},{12,4},... | collective-permute-start | bytes 3440648 | tf_op jit(solution)/shard_map/ppermute | solution.py:242
  407.1 60.6 %collective-permute-start.46 = (bf16[2,320,896]{2,1,0:T(8,128)(2,1)}, bf16[2,320,896]{2,1,0:T(8,128)(2,1)}, u32[]{:S(2)}, u32[]{:S(2)}) collective-permute-start(bf16[2,320,896]{2,1,0:T(8,128)(2,1)} %dynamic-slice_bitcast_fusion.3), channel_id=1, source_target_pairs={{0,16},{16,0},{1,17},{17,1},{2,18},{18,2},{3,19},{19,3},{4,20},{20... | collective-permute-start | bytes 3440648 | tf_op jit(solution)/shard_map/ppermute | solution.py:242
  424.3 26.9 %collective-permute-start.69 = (bf16[80,1344]{1,0:T(8,128)(2,1)S(1)}, bf16[80,1344]{1,0:T(8,128)(2,1)S(1)}, u32[]{:S(2)}, u32[]{:S(2)}) collective-permute-start(bf16[80,1344]{1,0:T(8,128)(2,1)S(1)} %dynamic-slice_bitcast_fusion.27), channel_id=1, source_target_pairs={{0,4},{2,6},{4,0},{6,2},{1,5},{3,7},{5,1},{7,3},{8,12},{10,14},{12... | collective-permute-start | bytes 645128 | tf_op jit(solution)/shard_map/ppermute | solution.py:326
  440.7 40.2 %collective-permute-start.42 = (bf16[256,1280]{1,0:T(8,128)(2,1)S(1)}, bf16[256,1280]{1,0:T(8,128)(2,1)S(1)}, u32[]{:S(2)}, u32[]{:S(2)}) collective-permute-start(bf16[256,1280]{1,0:T(8,128)(2,1)S(1)} %copy-done.75), channel_id=1, source_target_pairs={{0,6},{2,0},{4,2},{6,4},{1,7},{3,1},{5,3},{7,5},{8,14},{10,8},{12,... | collective-permute-start | bytes 1966088 | tf_op jit(solution)/shard_map/ppermute | solution.py:242
  442.9 46.0 %collective-permute-start.45 = (bf16[640,640]{1,0:T(8,128)(2,1)}, bf16[640,640]{1,0:T(8,128)(2,1)}, u32[]{:S(2)}, u32[]{:S(2)}) collective-permute-start(bf16[640,640]{1,0:T(8,128)(2,1)} %get-tuple-element.282), channel_id=1, source_target_pairs={{0,1},{1,0},{2,3},{3,2},{4,5},{5,4},{6,7},{7,6},{8,9},{9,8},{10,11... | collective-permute-start | bytes 2457608 | tf_op jit(solution)/shard_map/ppermute | solution.py:242
  481.4 26.1 %collective-permute-start.43 = (bf16[256,1280]{1,0:T(8,128)(2,1)}, bf16[256,1280]{1,0:T(8,128)(2,1)}, u32[]{:S(2)}, u32[]{:S(2)}) collective-permute-start(bf16[256,1280]{1,0:T(8,128)(2,1)} %slice.408), channel_id=1, source_target_pairs={{0,2},{2,4},{4,6},{6,0},{1,3},{3,5},{5,7},{7,1},{8,10},{10,12},{12... | collective-permute-start | bytes 1966088 | tf_op jit(solution)/shard_map/ppermute | solution.py:242
  581.5 40.9 %collective-permute-start.77 = (bf16[2,224,1280]{2,1,0:T(8,128)(2,1)S(1)}, bf16[2,224,1280]{2,1,0:T(8,128)(2,1)S(1)}, u32[]{:S(2)}, u32[]{:S(2)}) collective-permute-start(bf16[2,224,1280]{2,1,0:T(8,128)(2,1)S(1)} %dynamic-slice_bitcast_fusion), channel_id=1, source_target_pairs={{0,8},{8,0},{1,9},{9,1},{2,10},{10,2},{3,11},{11,3},{4,12},{12,4},... | collective-permute-start | bytes 3440648 | tf_op jit(solution)/shard_map/ppermute | solution.py:242
  589.2 34.1 %collective-permute-start.75 = (bf16[2,224,1280]{2,1,0:T(8,128)(2,1)S(1)}, bf16[2,224,1280]{2,1,0:T(8,128)(2,1)S(1)}, u32[]{:S(2)}, u32[]{:S(2)}) collective-permute-start(bf16[2,224,1280]{2,1,0:T(8,128)(2,1)S(1)} %dynamic-slice_bitcast_fusion.1), channel_id=1, source_target_pairs={{0,16},{16,0},{1,17},{17,1},{2,18},{18,2},{3,19},{19,3},{4,20},{20... | collective-permute-start | bytes 3440648 | tf_op jit(solution)/shard_map/ppermute | solution.py:242
  (152 other events, 1485.2 us)

commit v6 on v5

--- a/solution.py
+++ b/solution.py
@@ -409,9 +409,10 @@
     grads_sent = jnp.concatenate([later[4], chosen_low], axis=1)
     grads_pair = swap(grads_sent)
     grads_far = {levels[1]: shifted(grads_sent, "z", levels[1])}
-    grads_next = after(grads_sent, grads_far[levels[1]])
+    turn_at = after(grads_sent, grads_far[levels[1]])
     for step in levels[2:]:
-        grads_far[step] = shifted(grads_next, "z", step)
+        grads_far[step] = shifted(turn_at, "z", step)
+        turn_at = after(turn_at, grads_far[step])
 
     query_half = first_full[:, :wide]
     key_half = first_full[:, wide : 2 * wide]
@@ -440,13 +441,14 @@
     key_rot = rotate(by_head(product(attn_in, key_half)), cosine, sine_part).astype(BF)
     values = by_head(product(attn_in, value_half).astype(BF))
     allowed = jnp.stack([allowed_mask(length, starts_two[i], piece_len) for i in range(2)])
-    scores = mm("sqhd,skhd->shqk", query_rot, key_rot) * score_scale
+    key_met = after(key_rot, grads_far[levels[1]])
+    scores = mm("sqhd,skhd->shqk", query_rot, key_met) * score_scale
     scores = jnp.where(allowed[:, None], scores, -1e30)
     row_max = jnp.max(scores, axis=-1, keepdims=True)
     exps = jnp.exp(scores - row_max)
     attn_probs = exps / jnp.sum(exps, axis=-1, keepdims=True)
     probs_low = attn_probs.astype(BF)
-    context = flat(mm("shqk,skhd->sqhd", probs_low, after(values, *second_near)).astype(BF))
+    context = flat(mm("shqk,skhd->sqhd", probs_low, after(values, grads_far[levels[2]], *second_near)).astype(BF))
     out_partial = product(context, output_half).reshape(2, length, width)
     attn_out = out_partial[0] + swap(out_partial[1].astype(BF)).astype(F32)
     residual = token_f[0] + attn_out
@@ -478,13 +480,10 @@
     shared_hidden = (jax.nn.silu(shared_gate_act) * shared_up_act).astype(BF)
     shared_out = product(shared_hidden, down_half).astype(BF).reshape(2, length, width)
     shared_hidden_grad = product(grad_two, down_half.T)
-    shared_down_grad = product(shared_hidden.T, grad_two).astype(BF)
     shared_gate_act_grad = (shared_hidden_grad * shared_up_act * silu_grad(shared_gate_act)).astype(
         BF
     )
     shared_up_act_grad = (shared_hidden_grad * jax.nn.silu(shared_gate_act)).astype(BF)
-    shared_gate_grad = product(ffn_two.T, shared_gate_act_grad).astype(BF)
-    shared_up_grad = product(ffn_two.T, shared_up_act_grad).astype(BF)
     shared_in_grad = (
         (product(shared_gate_act_grad, gate_half.T) + product(shared_up_act_grad, up_half.T))
         .astype(BF)
@@ -495,20 +494,13 @@
     )
     turn = lambda grad: joined(half(grad, core, 1), swap(half(grad, 1 - core, 1)), core, 0)
     shares = lambda value: value.reshape(side, side, value.shape[0] // dp, -1)
-    down_turned = turn(shared_down_grad).reshape(width, narrow)
-    cut = narrow // 2
-    shared_part = [
-        jnp.concatenate([shared_gate_grad, down_turned[:, :cut]], axis=1),
-        jnp.concatenate([shared_up_grad, down_turned[:, cut:]], axis=1),
-    ]
-    sent_next = after(sent, rows_far[levels[1]], shared_in_grad, *shared_part)
+    sent_next = after(sent, rows_far[levels[1]], shared_in_grad, shared_out)
     for step in levels[2:]:
         rows_far[step] = shifted(sent_next, "z", step)
     rows_all = [sent, sent_other]
     for step in levels[1:]:
         rows_all += [rows_far[step], swap(rows_far[step])]
     both = ("yx", "xy")
-    shared_part = [shares(part) for part in shared_part]
 
     place_me = me.reshape(1).astype(jnp.int32)
     block = owners // 2
@@ -517,50 +509,61 @@
         expert_gate, expert_up, expert_down, owners, 0,
     )
     wider = width + 128
-    shared_one = stage_one(shared_part, both, late=(near[block],))
+    gate_low, up_low, hidden_low, grad_low = after(
+        [shared_gate_act_grad, shared_up_act_grad, shared_hidden, grad_two], near[block]
+    )
+    shared_down_grad = product(hidden_low.T, grad_low).astype(BF)
+    shared_gate_grad = product(ffn_two.T, gate_low).astype(BF)
+    shared_up_grad = product(ffn_two.T, up_low).astype(BF)
+    down_shares = turn(shared_down_grad).reshape(side, side, rows, narrow)
+    cut = (rows // 2 + 15) // 16 * 16
+    shared_part = [
+        jnp.concatenate([shares(shared_gate_grad), down_shares[:, :, :cut]], axis=2),
+        jnp.concatenate([shares(shared_up_grad), down_shares[:, :, cut:]], axis=2),
+    ]
     chips = [None] * depth
     for place_at in range(1, depth // 2):
         chips[place_at] = near[2 * place_at].astype(F32) + swap(near[2 * place_at + 1]).astype(F32)
     sent_back = [None] + [chips[i][:, :wider].astype(BF) for i in range(1, depth // 2)]
-    far_slots = after(slots[:, block:], *sent_back[1:], *shared_one)
+    far_slots = after(slots[:, block:], *sent_back[1:], *shared_part)
     far = expert_call(
         place_me, far_slots, rows_all[block:], grads_all[block:],
         expert_gate, expert_up, expert_down, owners, 1, near[block:],
     )
     expert_in, res_grad, routed_hidden, routed_gate_grad, routed_up_grad = far[block:]
-    for place_at in range(depth // 2, depth):
-        mine, other = far[2 * place_at - block], far[2 * place_at - block + 1]
-        chips[place_at] = mine.astype(F32) + swap(other).astype(F32)
-        sent_back.append(chips[place_at][:, :wider].astype(BF))
+    gate_grad = mm("erd,erf->edf", expert_in, routed_gate_grad).astype(BF)
+    met = after([swap(far[i]) for i in range(1, block, 2)], gate_grad)
+    for i, other in enumerate(met):
+        chips[depth // 2 + i] = far[2 * i].astype(F32) + other.astype(F32)
+        sent_back.append(chips[depth // 2 + i][:, :wider].astype(BF))
     back_in = [shifted(sent_back[i], "z", -levels[i]) for i in range(1, depth)]
+    shared_one = stage_one(shared_part, both, late=(gate_grad,))
     chips[0] = (near[0].astype(F32) + shared_both[0].astype(F32)) + swap(
         near[1] + shared_both[1]
     ).astype(F32)
     back = chips[0][:, :wider]
     for piece in back_in[: depth // 2 - 1]:
-        back += after(piece, far[block]).astype(F32)
-    shared_two = stage_two(shared_one, both, late=(far[block],))
-    routed_gate_grad = after(routed_gate_grad, *sent_back[depth // 2 :], back)
-
-    gate_grad = mm("erd,erf->edf", expert_in, routed_gate_grad).astype(BF)
+        back += after(piece, gate_grad).astype(F32)
+
+    routed_up_grad = after(routed_up_grad, *sent_back[depth // 2 :], *shared_one, back)
     up_grad = mm("erd,erf->edf", expert_in, routed_up_grad).astype(BF)
-    down_grad = mm("erf,erd->efd", routed_hidden, res_grad).astype(BF)
+    shared_two = stage_two(shared_one, both, late=(up_grad,))
+    down_grad = mm("erf,erd->efd", routed_hidden, after(res_grad, *shared_two)).astype(BF)
     blocks = [
         [grad[e].reshape(side, side, grad.shape[1] // dp, grad.shape[2]) for e in range(EXP_DEV)]
         for grad in (gate_grad, up_grad, down_grad)
     ]
     gate_one = stage_one(blocks[0], both, shared_two)
-    for piece in after(back_in[depth // 2 - 1 :], *gate_one):
+    for piece in after(back_in[depth // 2 - 1 :], down_grad, *gate_one):
         back += piece.astype(F32)
 
     probs_grad = back[:, width : width + experts] + back[:, width + experts : width + 2 * experts]
     logits_grad = router_probs * (
         probs_grad - jnp.sum(router_probs * probs_grad, axis=-1, keepdims=True)
     )
-    router_grad = product_high(ffn_in.astype(F32).T, logits_grad)
     router_in_grad = product_high(logits_grad, router_full.astype(F32).T)
     ffn_in_grad = back[:, :width] + router_in_grad
-    ffn_gain_grad = jnp.sum(ffn_in_grad * residual * norm_two, axis=0)
+    ffn_gain_terms = ffn_in_grad * residual * norm_two
     upstream_two = ffn_in_grad * gain_two_f
     residual_grad = (
         out_grad.astype(F32)
@@ -573,16 +576,20 @@
     output_grad = turn(output_grad)
     context_grad = by_head(product(attn_grad_two, output_half.T).astype(BF))
     value_grad = flat(mm("shqk,sqhd->skhd", probs_low, context_grad).astype(BF))
-    probs_grad_att = mm("sqhd,skhd->shqk", context_grad, values)
+    up_one = stage_one(blocks[1], both, gate_one, (value_grad,))
+    context_late = after(context_grad, *up_one)
+    value_wgrad = product(attn_in.T, value_grad).astype(BF)
+    probs_grad_att = mm("sqhd,skhd->shqk", context_late, values)
     row_delta = jnp.sum(attn_probs * probs_grad_att, axis=-1, keepdims=True)
     scores_grad = (attn_probs * (probs_grad_att - row_delta)).astype(BF)
+    early = [shares(output_grad), shares(value_wgrad)]
+    scores_grad = after(scores_grad, *early)
     query_grad = mm("shqk,skhd->sqhd", scores_grad, key_rot) * score_scale
     key_grad = mm("shqk,sqhd->skhd", scores_grad, query_rot) * score_scale
     query_pre_grad = flat(rotate(query_grad, cosine, -sine_part).astype(BF))
     key_pre_grad = flat(rotate(key_grad, cosine, -sine_part).astype(BF))
     query_wgrad = product(attn_in.T, query_pre_grad).astype(BF)
     key_wgrad = product(attn_in.T, key_pre_grad).astype(BF)
-    value_wgrad = product(attn_in.T, value_grad).astype(BF)
     in_partial = (
         product(query_pre_grad, query_half.T)
         + product(key_pre_grad, key_half.T)
@@ -590,22 +597,24 @@
     ).reshape(2, length, width)
     attn_in_grad = in_partial[0] + swap(in_partial[1].astype(BF)).astype(F32)
     token_mine, norm_mine = token_f[0], norm_one[0]
-    attn_gain_grad = jnp.sum(attn_in_grad * token_mine * norm_mine, axis=0)
+    attn_gain_terms = attn_in_grad * token_mine * norm_mine
     upstream_one = attn_in_grad * gain_one_f
     tokens_grad = (
         residual_grad
         + norm_mine * upstream_one
         - token_mine * norm_mine**3 * jnp.mean(upstream_one * token_mine, axis=-1, keepdims=True)
     )
-    small_grads = jnp.concatenate(
-        [router_grad, attn_gain_grad[:, None], ffn_gain_grad[:, None]], axis=1
+    lanes = jnp.arange(128)
+    unit = lambda lane: jnp.broadcast_to((lanes == lane).astype(F32), (length, 128))
+    small_grads = (
+        product_high(ffn_in.astype(F32).T, jnp.pad(logits_grad, ((0, 0), (0, 128 - experts))))
+        + product_high(ffn_gain_terms.T, unit(experts + 1))
+        + product_high(attn_gain_terms.T, unit(experts))
     ).astype(BF)
-    small_grads = jnp.pad(small_grads, ((0, 0), (0, 128 - small_grads.shape[1])))
-    marks = ((value_grad,), (scores_grad,), (query_wgrad,), ())
-    up_one = stage_one(blocks[1], both, gate_one, marks[0])
-    gate_two = stage_two(gate_one, both, up_one, marks[1])
-    early = [shares(output_grad), shares(value_wgrad)]
-    early_one = stage_one(early, both, gate_two, marks[2])
+
+    done_wgrads = (query_wgrad, key_wgrad)
+    gate_two = stage_two(gate_one, both, up_one, done_wgrads)
+    early_one = stage_one(early, both, up_one, done_wgrads)
     early_two = stage_two(early_one, both)
     late = [shares(query_wgrad), shares(jnp.concatenate([key_wgrad, small_grads], axis=1))]
     late_one = stage_one(late, both, early_one)
@@ -613,15 +622,18 @@
     up_two = stage_two(up_one, both, late_one)
     down_two = stage_two(stage_one(blocks[2], both, late_two), both)
     expert_shares = [jnp.stack(pair).astype(F32) for pair in (gate_two, up_two, down_two)]
-    shared_share = reduce_level(after(jnp.concatenate(shared_two, axis=1), back), marks)
+    shared_share = reduce_level(
+        after(jnp.concatenate(shared_two, axis=0), back),
+        ((value_grad,), done_wgrads, early_two, late_one),
+    )
     early_share = reduce_level(jnp.concatenate(early_two, axis=1))
     late_share = reduce_level(jnp.concatenate(late_two, axis=1))
 
     moe_out = chips[0][:, wider:]
     piece = back
     for i in range(1, depth):
-        moving = after(chips[i][:, wider:].astype(BF), piece)
-        piece = after(shifted(moving, "z", -levels[i]), *marks[min(i - 1, 2)])
+        moving = after(chips[i][:, wider:].astype(BF), piece, *(early_two if i > 1 else ()))
+        piece = after(shifted(moving, "z", -levels[i]), *((value_grad,), late_one, late_two)[min(i - 1, 2)])
         moe_out += piece.astype(F32)
 
     early_other, late_other, shared_other = swap(early_share), swap(late_share), swap(shared_share)
@@ -629,10 +641,14 @@
         mine[:, start : start + size], other[:, start : start + size], core, 1
     ).astype(F32)
     small_sum = late_share[:, 2 * wide :].astype(F32) + late_other[:, 2 * wide :].astype(F32)
-    down_cols = lambda share: jnp.concatenate(
-        [share[:, narrow : narrow + cut], share[:, 2 * narrow + cut :]], axis=1
+    first_rows = rows + cut
+    down_part = lambda share: jnp.concatenate(
+        [share[rows:first_rows], share[first_rows + rows :]], axis=0
     ).reshape(-1, wide)
-    down_rows = joined(down_cols(shared_share), down_cols(shared_other), core, 1).astype(F32)
+    down_rows = joined(down_part(shared_share), down_part(shared_other), core, 1).astype(F32)
+    unit_cols = lambda start: joined(
+        shared_share[start : start + rows], shared_other[start : start + rows], core, 1
+    ).astype(F32)
 
     stream_out = residual + moe_out
     stat_rms = jnp.stack(
@@ -652,8 +668,8 @@
         small_sum[:, experts],
         small_sum[:, experts + 1],
         small_sum[:, :experts],
-        column(shared_share, shared_other, 0, narrow),
-        column(shared_share, shared_other, narrow + cut, narrow),
+        unit_cols(0),
+        unit_cols(first_rows),
         down_rows,
         *expert_shares,
         stat_rms,

time: 650 us -> 687 us (1.057)
  local copies, waits for them, and re-layouts: 126 us -> 148 us
  waiting for transfers between devices: 173 us -> 193 us
  starting transfers between devices: 88.6 us -> 74.4 us
    ppermute x67, waiting for transfers between devices: 125 us -> 147 us  [shifted(): lax.ppermute(value, axis, [(i, (i + by) % size) for i in range(size)])]
    ppermute x67, starting transfers between devices: 69.8 us -> 53.6 us  [shifted(): lax.ppermute(value, axis, [(i, (i + by) % size) for i in range(size)])]
    unnamed x220 -> x238, local copies, waits for them, and re-layouts: 16.3 us -> 23.9 us
    convert_element_type x20 -> x18, other arithmetic: 19.4 us -> 20.4 us  [ring_reduce(): (other.astype(F32) + pick(value, index - step, at).astype(F32)).astype(BF)]
  transfers between devices with their start and end apart: 79 -> 79, of which waited for: 25 -> 25; matrix products, arithmetic and copies ran while one was open for 41% -> 42% of each run, Pallas kernels for 12% -> 12%
where the time goes in v6:
time: 687 us; the launch traced here: 675 us
  waiting for transfers between devices  193 us (28%)
  local copies, waits for them, and re-layouts  148 us (22%)
  other arithmetic  94.1 us (14%)
  matrix products  80.1 us (12%)
  Pallas kernels  79.3 us (12%)
  starting transfers between devices  74.4 us (11%)
    ppermute x67, waiting for transfers between devices, shifted(): lax.ppermute(value, axis, [(i, (i + by) % size) for i in range(size)])  147 us
    pallas_call x2, Pallas kernels, expert_call(): pl.pallas_call(functools.partial(expert_kernel, count, width, capacity, e...  69 us
    ppermute x67, starting transfers between devices, shifted(): lax.ppermute(value, axis, [(i, (i + by) % size) for i in range(size)])  53.6 us
    ppermute x12, waiting for transfers between devices, crossed(): return lax.ppermute(value, 'z', [(i, i ^ bit) for i in range(depth)])  46.6 us
    dot_general x22, matrix products, product(): return jnp.dot(first_arg, second_arg, preferred_element_type=F32)  40 us
    dot_general x9, matrix products, mm(): return jnp.einsum(spec, first_arg, second_arg, preferred_element_type=F32)  31 us
    unnamed x238, local copies, waits for them, and re-layouts  23.9 us
    ppermute x12, starting transfers between devices, crossed(): return lax.ppermute(value, 'z', [(i, i ^ bit) for i in range(depth)])  20.9 us
  transfers between devices with their start and end apart: 79, of which 25 were waited for; matrix products, arithmetic and copies ran while one was open for 42% of the time, Pallas kernels for 12%

profile of v6, /device:TPU:0, one launch (start us, length us, event | category | flops | bytes accessed | tf_op | source)
XLA Modules:
  0.0 675.5 jit_solution(11258500322698519697)
XLA Ops:
  20.0 17.6 %collective-permute-done.2.refs_2_ = bf16[320,2048]{1,0:T(8,128)(2,1)} collective-permute-done((bf16[320,2048]{1,0:T(8,128)(2,1)}, bf16[320,2048]{1,0:T(8,128)(2,1)}, u32[]{:S(2)}, u32[]{:S(2)}) %collective-permute-start.2) | collective-permute-done | bytes 1310752 | tf_op jit(solution)/shard_map/ppermute | solution.py:242
  61.4 5.2 place.2
  68.2 4.0 slice_bitcast_fusion.1
  73.7 3.5 copy.349
  85.2 6.3 collective-permute-done.8.refs_2_
  103.1 5.6 collective-permute-done.11.refs_4_
  110.2 5.1 place.3
  125.9 3.7 fusion.158
  130.7 14.2 %collective-permute-done.6.refs_4_ = bf16[256,1408]{1,0:T(8,128)(2,1)} collective-permute-done((bf16[256,1408]{1,0:T(8,128)(2,1)}, bf16[256,1408]{1,0:T(8,128)(2,1)}, u32[]{:S(2)}, u32[]{:S(2)}) %collective-permute-start.6) | collective-permute-done | bytes 720928 | tf_op jit(solution)/shard_map/ppermute | solution.py:242
  158.1 12.1 %collective-permute-done.15.refs_6_ = bf16[256,1408]{1,0:T(8,128)(2,1)} collective-permute-done((bf16[256,1408]{1,0:T(8,128)(2,1)}, bf16[256,1408]{1,0:T(8,128)(2,1)}, u32[]{:S(2)}, u32[]{:S(2)}) %collective-permute-start.15) | collective-permute-done | bytes 720928 | tf_op jit(solution)/shard_map/ppermute | solution.py:242
  186.9 21.0 %collective-permute-done.20.refs_2_ = bf16[256,1408]{1,0:T(8,128)(2,1)} collective-permute-done((bf16[256,1408]{1,0:T(8,128)(2,1)}, bf16[256,1408]{1,0:T(8,128)(2,1)}, u32[]{:S(2)}, u32[]{:S(2)}) %collective-permute-start.20) | collective-permute-done | bytes 720928 | tf_op jit(solution)/shard_map/ppermute | solution.py:242
  223.4 34.6 %experts.2 = (bf16[256,2688]{1,0:T(8,128)(2,1)}, bf16[256,2688]{1,0:T(8,128)(2,1)}, bf16[256,2688]{1,0:T(8,128)(2,1)}, bf16[256,2688]{1,0:T(8,128)(2,1)}, bf16[2...) custom-call(s32[1]{0:T(128)} %bitcast.20.me_ref, ...), custom_call_target="tpu_custom_call" | custom-call | flops 16441671680 | bytes 62914560 | tf_op jit(solution)/shard_map/experts/pallas_call | solution.py:133
  273.1 3.9 select_n.504
  293.9 34.4 %experts.3 = (bf16[256,2688]{1,0:T(8,128)(2,1)}, bf16[256,2688]{1,0:T(8,128)(2,1)}, bf16[256,2688]{1,0:T(8,128)(2,1)}, bf16[256,2688]{1,0:T(8,128)(2,1)}, bf16[2...) custom-call(s32[1]{0:T(128)} %bitcast.20.me_ref, ...), custom_call_target="tpu_custom_call", output_to_operand_aliasing={{4}: (13, {}), {5}: (14, {}), {6}: (15, {}), {7}: (16, {}),... | custom-call | flops 16441671680 | bytes 62914560 | tf_op jit(solution)/shard_map/experts/pallas_call | solution.py:133
  328.4 9.1 %convolution_convert_fusion.2 = bf16[2,1280,896]{2,1,0:T(8,128)(2,1)S(1)} fusion(bf16[2,1024,1280]{2,1,0:T(8,128)(2,1)} %get-tuple-element.127, bf16[2,1024,896]{2,1,0:T(8,128)(2,1)} %get-tuple-element.128), kind=kOutput, calls=%fused_computation.4 | convolution fusion | flops 4699914240 | bytes 13500416 | tf_op jit(solution)/shard_map/erd,erf->edf/dot_general | solution.py:196
  366.0 6.2 convolution_convert_fusion.1
  376.7 8.6 %convolution_convert_fusion = bf16[2,896,1280]{2,1,0:T(8,128)(2,1)S(1)} fusion(bf16[2,1024,896]{2,1,0:T(8,128)(2,1)} %get-tuple-element.136, bf16[2,1024,1280]{2,1,0:T(8,128)(2,1)} %get-tuple-element.144), kind=kOutput, calls=%fused_computation.2 | convolution fusion | flops 4699914240 | bytes 13500416 | tf_op jit(solution)/shard_map/erf,erd->efd/dot_general | solution.py:196
  388.5 14.4 %collective-permute-done.38 = bf16[2,320,896]{2,1,0:T(8,128)(2,1)} collective-permute-done((bf16[2,320,896]{2,1,0:T(8,128)(2,1)S(1)}, bf16[2,320,896]{2,1,0:T(8,128)(2,1)}, u32[]{:S(2)}, u32[]{:S(2)}) %collective-permute-start.38) | collective-permute-done | bytes 1146912 | tf_op jit(solution)/shard_map/ppermute | solution.py:242
  437.8 15.5 %collective-permute-done.40 = bf16[256,1280]{1,0:T(8,128)(2,1)} collective-permute-done((bf16[256,1280]{1,0:T(8,128)(2,1)}, bf16[256,1280]{1,0:T(8,128)(2,1)}, u32[]{:S(2)}, u32[]{:S(2)}) %collective-permute-start.40) | collective-permute-done | bytes 655392 | tf_op jit(solution)/shard_map/ppermute | solution.py:242
  486.0 9.4 %collective-permute-done.47 = bf16[2,320,640]{2,1,0:T(8,128)(2,1)S(1)} collective-permute-done((bf16[2,320,640]{2,1,0:T(8,128)(2,1)S(1)}, bf16[2,320,640]{2,1,0:T(8,128)(2,1)S(1)}, u32[]{:S(2)}, u32[]{:S(2)}) %collective-permute-start.47) | collective-permute-done | bytes 819232 | tf_op jit(solution)/shard_map/ppermute | solution.py:242
  500.8 3.9 copy.393
  518.2 4.0 collective-permute-done.61
  523.9 5.1 collective-permute-done.51
  529.2 4.6 collective-permute-done.52
  539.6 4.2 select_n.548
  555.1 10.7 %collective-permute-start.63 = (bf16[80,1280]{1,0:T(8,128)(2,1)S(1)}, bf16[80,1280]{1,0:T(8,128)(2,1)S(1)}, u32[]{:S(2)}, u32[]{:S(2)}) collective-permute-start(bf16[80,1280]{1,0:T(8,128)(2,1)S(1)} %fusion.106), channel_id=1, source_target_pairs={{0,4},{2,6},{4,0},{6,2},{1,5},{3,7},{5,1},{7,3},{8,12},{10,14},{12... | collective-permute-start | bytes 614408 | tf_op jit(solution)/shard_map/ppermute | solution.py:326
  568.8 6.5 collective-permute-done.63
  585.1 4.5 collective-permute-done.73
  592.3 11.3 %collective-permute-done.64 = bf16[2,80,1280]{2,1,0:T(8,128)(2,1)S(1)} collective-permute-done((bf16[2,80,1280]{2,1,0:T(8,128)(2,1)S(1)}, bf16[2,80,1280]{2,1,0:T(8,128)(2,1)S(1)}, u32[]{:S(2)}, u32[]{:S(2)}) %collective-permute-start.64) | collective-permute-done | bytes 409632 | tf_op jit(solution)/shard_map/ppermute | solution.py:326
  622.4 9.1 %collective-permute-done.57 = bf16[80,1408]{1,0:T(8,128)(2,1)} collective-permute-done((bf16[80,1408]{1,0:T(8,128)(2,1)}, bf16[80,1408]{1,0:T(8,128)(2,1)}, u32[]{:S(2)}, u32[]{:S(2)}) %collective-permute-start.57) | collective-permute-done | bytes 225312 | tf_op jit(solution)/shard_map/ppermute | solution.py:326
  633.8 11.7 %collective-permute-done.58 = bf16[80,1408]{1,0:T(8,128)(2,1)S(1)} collective-permute-done((bf16[80,1408]{1,0:T(8,128)(2,1)S(1)}, bf16[80,1408]{1,0:T(8,128)(2,1)S(1)}, u32[]{:S(2)}, u32[]{:S(2)}) %collective-permute-start.58) | collective-permute-done | bytes 225312 | tf_op jit(solution)/shard_map/ppermute | solution.py:326
  658.0 8.9 %collective-permute-done.78 = bf16[224,1280]{1,0:T(8,128)(2,1)S(1)} collective-permute-done((bf16[224,1280]{1,0:T(8,128)(2,1)S(1)}, bf16[224,1280]{1,0:T(8,128)(2,1)S(1)}, u32[]{:S(2)}, u32[]{:S(2)}) %collective-permute-start.78) | collective-permute-done | bytes 573472 | tf_op jit(solution)/shard_map/ppermute | solution.py:242
  (658 shorter events, 350.3 us)
Async XLA Ops:
  5.5 32.1 %collective-permute-start.2 = (bf16[320,2048]{1,0:T(8,128)(2,1)}, bf16[320,2048]{1,0:T(8,128)(2,1)}, u32[]{:S(2)}, u32[]{:S(2)}) collective-permute-start(bf16[320,2048]{1,0:T(8,128)(2,1)} %fusion.38.refs_0_), channel_id=1, source_target_pairs={{0,16},{16,0},{1,17},{17,1},{2,18},{18,2},{3,19},{19,3},{4,20},{20... | collective-permute-start | bytes 3932168 | tf_op jit(solution)/shard_map/ppermute | solution.py:242
  8.5 32.8 %collective-permute-start.1 = (bf16[320,2048]{1,0:T(8,128)(2,1)}, bf16[320,2048]{1,0:T(8,128)(2,1)}, u32[]{:S(2)}, u32[]{:S(2)}) collective-permute-start(bf16[320,2048]{1,0:T(8,128)(2,1)} %fusion.38.refs_0_), channel_id=1, source_target_pairs={{0,8},{8,0},{1,9},{9,1},{2,10},{10,2},{3,11},{11,3},{4,12},{12,4},... | collective-permute-start | bytes 3932168 | tf_op jit(solution)/shard_map/ppermute | solution.py:242
  45.7 77.4 %collective-permute-start.14 = (bf16[256,1408]{1,0:T(8,128)(2,1)}, bf16[256,1408]{1,0:T(8,128)(2,1)}, u32[]{:S(2)}, u32[]{:S(2)}) collective-permute-start(bf16[256,1408]{1,0:T(8,128)(2,1)} %pad_maximum_fusion.11.refs_4_), channel_id=1, source_target_pairs={{0,1},{1,0},{2,3},{3,2},{4,5},{5,4},{6,7},{7,6},{8,9},{9,8},{10,11... | collective-permute-start | bytes 2162696 | tf_op jit(solution)/shard_map/ppermute | solution.py:242
  45.7 78.4 %collective-permute-start.5 = (bf16[256,1408]{1,0:T(8,128)(2,1)}, bf16[256,1408]{1,0:T(8,128)(2,1)}, u32[]{:S(2)}, u32[]{:S(2)}) collective-permute-start(bf16[256,1408]{1,0:T(8,128)(2,1)} %pad_maximum_fusion.11.refs_4_), channel_id=1, source_target_pairs={{0,4},{2,6},{4,0},{6,2},{1,5},{3,7},{5,1},{7,3},{8,12},{10,14},{12... | collective-permute-start | bytes 2162696 | tf_op jit(solution)/shard_map/ppermute | solution.py:242
  60.2 31.2 %collective-permute-start.8 = (bf16[320,1984]{1,0:T(8,128)(2,1)}, bf16[320,1984]{1,0:T(8,128)(2,1)}, u32[]{:S(2)}, u32[]{:S(2)}) collective-permute-start(bf16[320,1984]{1,0:T(8,128)(2,1)} %concatenate.175.refs_0_), channel_id=1, source_target_pairs={{0,16},{16,0},{1,17},{17,1},{2,18},{18,2},{3,19},{19,3},{4,20},{20... | collective-permute-start | bytes 3809288 | tf_op jit(solution)/shard_map/ppermute | solution.py:242
  60.8 32.4 %collective-permute-start.7 = (bf16[320,1984]{1,0:T(8,128)(2,1)}, bf16[320,1984]{1,0:T(8,128)(2,1)}, u32[]{:S(2)}, u32[]{:S(2)}) collective-permute-start(bf16[320,1984]{1,0:T(8,128)(2,1)} %concatenate.175.refs_0_), channel_id=1, source_target_pairs={{0,8},{8,0},{1,9},{9,1},{2,10},{10,2},{3,11},{11,3},{4,12},{12,4},... | collective-permute-start | bytes 3809288 | tf_op jit(solution)/shard_map/ppermute | solution.py:242
  171.1 39.3 %collective-permute-start.16 = (bf16[256,1408]{1,0:T(8,128)(2,1)}, bf16[256,1408]{1,0:T(8,128)(2,1)}, u32[]{:S(2)}, u32[]{:S(2)}) collective-permute-start(bf16[256,1408]{1,0:T(8,128)(2,1)} %collective-permute-done.5.refs_6_), channel_id=1, source_target_pairs={{0,1},{1,0},{2,3},{3,2},{4,5},{5,4},{6,7},{7,6},{8,9},{9,8},{10,11... | collective-permute-start | bytes 2162696 | tf_op jit(solution)/shard_map/ppermute | solution.py:242
  171.9 39.4 %collective-permute-start.17 = (bf16[256,1408]{1,0:T(8,128)(2,1)}, bf16[256,1408]{1,0:T(8,128)(2,1)}, u32[]{:S(2)}, u32[]{:S(2)}) collective-permute-start(bf16[256,1408]{1,0:T(8,128)(2,1)} %collective-permute-done.6.refs_4_), channel_id=1, source_target_pairs={{0,1},{1,0},{2,3},{3,2},{4,5},{5,4},{6,7},{7,6},{8,9},{9,8},{10,11... | collective-permute-start | bytes 2162696 | tf_op jit(solution)/shard_map/ppermute | solution.py:242
  173.3 39.0 %collective-permute-start.18 = (bf16[256,1408]{1,0:T(8,128)(2,1)}, bf16[256,1408]{1,0:T(8,128)(2,1)}, u32[]{:S(2)}, u32[]{:S(2)}) collective-permute-start(bf16[256,1408]{1,0:T(8,128)(2,1)} %collective-permute-done.15.refs_6_), channel_id=1, source_target_pairs={{0,1},{1,0},{2,3},{3,2},{4,5},{5,4},{6,7},{7,6},{8,9},{9,8},{10,11... | collective-permute-start | bytes 2162696 | tf_op jit(solution)/shard_map/ppermute | solution.py:242
  173.8 34.2 %collective-permute-start.20 = (bf16[256,1408]{1,0:T(8,128)(2,1)}, bf16[256,1408]{1,0:T(8,128)(2,1)}, u32[]{:S(2)}, u32[]{:S(2)}) collective-permute-start(bf16[256,1408]{1,0:T(8,128)(2,1)} %concatenate.181.refs_0_), channel_id=1, source_target_pairs={{0,4},{2,6},{4,0},{6,2},{1,5},{3,7},{5,1},{7,3},{8,12},{10,14},{12... | collective-permute-start | bytes 2162696 | tf_op jit(solution)/shard_map/ppermute | solution.py:242
  207.9 63.2 %collective-permute-start.28 = (bf16[256,1408]{1,0:T(8,128)(2,1)}, bf16[256,1408]{1,0:T(8,128)(2,1)}, u32[]{:S(2)}, u32[]{:S(2)}) collective-permute-start(bf16[256,1408]{1,0:T(8,128)(2,1)} %concatenate.181.refs_0_), channel_id=1, source_target_pairs={{0,6},{2,0},{4,2},{6,4},{1,7},{3,1},{5,3},{7,5},{8,14},{10,8},{12,... | collective-permute-start | bytes 2162696 | tf_op jit(solution)/shard_map/ppermute | solution.py:242
  210.1 61.0 %collective-permute-start.26 = (bf16[256,1408]{1,0:T(8,128)(2,1)}, bf16[256,1408]{1,0:T(8,128)(2,1)}, u32[]{:S(2)}, u32[]{:S(2)}) collective-permute-start(bf16[256,1408]{1,0:T(8,128)(2,1)} %concatenate.181.refs_0_), channel_id=1, source_target_pairs={{0,2},{2,4},{4,6},{6,0},{1,3},{3,5},{5,7},{7,1},{8,10},{10,12},{12... | collective-permute-start | bytes 2162696 | tf_op jit(solution)/shard_map/ppermute | solution.py:242
  270.6 69.7 %collective-permute-start.22 = (bf16[256,2688]{1,0:T(8,128)(2,1)}, bf16[256,2688]{1,0:T(8,128)(2,1)}, u32[]{:S(2)}, u32[]{:S(2)}) collective-permute-start(bf16[256,2688]{1,0:T(8,128)(2,1)} %fusion.34), channel_id=1, source_target_pairs={{0,1},{1,0},{2,3},{3,2},{4,5},{5,4},{6,7},{7,6},{8,9},{9,8},{10,11... | collective-permute-start | bytes 4128776 | tf_op jit(solution)/shard_map/ppermute | solution.py:242
  283.5 61.2 %collective-permute-start.34 = (bf16[2,480,448]{1,2,0:T(8,128)(2,1)}, bf16[2,480,448]{1,2,0:T(8,128)(2,1)}, u32[]{:S(2)}, u32[]{:S(2)}) collective-permute-start(bf16[2,480,448]{1,2,0:T(8,128)(2,1)} %bitcast.453), channel_id=1, source_target_pairs={{0,16},{16,0},{1,17},{17,1},{2,18},{18,2},{3,19},{19,3},{4,20},{20... | collective-permute-start | bytes 2580488 | tf_op jit(solution)/shard_map/ppermute | solution.py:242
  288.2 56.5 %collective-permute-start.36 = (bf16[2,480,448]{1,2,0:T(8,128)(2,1)}, bf16[2,480,448]{1,2,0:T(8,128)(2,1)}, u32[]{:S(2)}, u32[]{:S(2)}) collective-permute-start(bf16[2,480,448]{1,2,0:T(8,128)(2,1)} %bitcast.454), channel_id=1, source_target_pairs={{0,8},{8,0},{1,9},{9,1},{2,10},{10,2},{3,11},{11,3},{4,12},{12,4},... | collective-permute-start | bytes 2580488 | tf_op jit(solution)/shard_map/ppermute | solution.py:242
  293.6 60.0 %collective-permute-start.24 = (bf16[256,1408]{1,0:T(8,128)(2,1)}, bf16[256,1408]{1,0:T(8,128)(2,1)}, u32[]{:S(2)}, u32[]{:S(2)}) collective-permute-start(bf16[256,1408]{1,0:T(8,128)(2,1)} %slice.396), channel_id=1, source_target_pairs={{0,4},{2,6},{4,0},{6,2},{1,5},{3,7},{5,1},{7,3},{8,12},{10,14},{12... | collective-permute-start | bytes 2162696 | tf_op jit(solution)/shard_map/ppermute | solution.py:242
  362.2 45.7 %collective-permute-start.32 = (bf16[256,1408]{1,0:T(8,128)(2,1)}, bf16[256,1408]{1,0:T(8,128)(2,1)}, u32[]{:S(2)}, u32[]{:S(2)}) collective-permute-start(bf16[256,1408]{1,0:T(8,128)(2,1)} %slice.400), channel_id=1, source_target_pairs={{0,6},{2,0},{4,2},{6,4},{1,7},{3,1},{5,3},{7,5},{8,14},{10,8},{12,... | collective-permute-start | bytes 2162696 | tf_op jit(solution)/shard_map/ppermute | solution.py:242
  365.5 42.5 %collective-permute-start.33 = (bf16[256,1408]{1,0:T(8,128)(2,1)}, bf16[256,1408]{1,0:T(8,128)(2,1)}, u32[]{:S(2)}, u32[]{:S(2)}) collective-permute-start(bf16[256,1408]{1,0:T(8,128)(2,1)} %slice.401), channel_id=1, source_target_pairs={{0,2},{2,4},{4,6},{6,0},{1,3},{3,5},{5,7},{7,1},{8,10},{10,12},{12... | collective-permute-start | bytes 2162696 | tf_op jit(solution)/shard_map/ppermute | solution.py:242
  374.7 30.7 %collective-permute-start.39 = (bf16[2,320,896]{2,1,0:T(8,128)(2,1)S(1)}, bf16[2,320,896]{2,1,0:T(8,128)(2,1)}, u32[]{:S(2)}, u32[]{:S(2)}) collective-permute-start(bf16[2,320,896]{2,1,0:T(8,128)(2,1)S(1)} %dynamic-slice_bitcast_fusion.4), channel_id=1, source_target_pairs={{0,8},{8,0},{1,9},{9,1},{2,10},{10,2},{3,11},{11,3},{4,12},{12,4},... | collective-permute-start | bytes 3440648 | tf_op jit(solution)/shard_map/ppermute | solution.py:242
  415.1 38.2 %collective-permute-start.40 = (bf16[256,1280]{1,0:T(8,128)(2,1)}, bf16[256,1280]{1,0:T(8,128)(2,1)}, u32[]{:S(2)}, u32[]{:S(2)}) collective-permute-start(bf16[256,1280]{1,0:T(8,128)(2,1)} %slice.394), channel_id=1, source_target_pairs={{0,4},{2,6},{4,0},{6,2},{1,5},{3,7},{5,1},{7,3},{8,12},{10,14},{12... | collective-permute-start | bytes 1966088 | tf_op jit(solution)/shard_map/ppermute | solution.py:242
  418.0 38.0 %collective-permute-start.44 = (bf16[2,320,896]{2,1,0:T(8,128)(2,1)}, bf16[2,320,896]{2,1,0:T(8,128)(2,1)}, u32[]{:S(2)}, u32[]{:S(2)}) collective-permute-start(bf16[2,320,896]{2,1,0:T(8,128)(2,1)} %dynamic-slice_bitcast_fusion.2), channel_id=1, source_target_pairs={{0,8},{8,0},{1,9},{9,1},{2,10},{10,2},{3,11},{11,3},{4,12},{12,4},... | collective-permute-start | bytes 3440648 | tf_op jit(solution)/shard_map/ppermute | solution.py:242
  419.7 39.5 %collective-permute-start.43 = (bf16[2,320,896]{2,1,0:T(8,128)(2,1)}, bf16[2,320,896]{2,1,0:T(8,128)(2,1)}, u32[]{:S(2)}, u32[]{:S(2)}) collective-permute-start(bf16[2,320,896]{2,1,0:T(8,128)(2,1)} %dynamic-slice_bitcast_fusion.3), channel_id=1, source_target_pairs={{0,16},{16,0},{1,17},{17,1},{2,18},{18,2},{3,19},{19,3},{4,20},{20... | collective-permute-start | bytes 3440648 | tf_op jit(solution)/shard_map/ppermute | solution.py:242
  436.7 41.4 %collective-permute-start.67 = (bf16[240,448]{1,0:T(8,128)(2,1)S(1)}, bf16[240,448]{1,0:T(8,128)(2,1)S(1)}, u32[]{:S(2)}, u32[]{:S(2)}) collective-permute-start(bf16[240,448]{1,0:T(8,128)(2,1)S(1)} %dynamic-slice_bitcast_fusion.25), channel_id=1, source_target_pairs={{0,4},{2,6},{4,0},{6,2},{1,5},{3,7},{5,1},{7,3},{8,12},{10,14},{12... | collective-permute-start | bytes 645128 | tf_op jit(solution)/shard_map/ppermute | solution.py:326
  478.8 33.6 %collective-permute-start.68 = (bf16[240,448]{1,0:T(8,128)(2,1)}, bf16[240,448]{1,0:T(8,128)(2,1)}, u32[]{:S(2)}, u32[]{:S(2)}) collective-permute-start(bf16[240,448]{1,0:T(8,128)(2,1)} %fusion.103), channel_id=1, source_target_pairs={{0,4},{2,6},{4,0},{6,2},{1,5},{3,7},{5,1},{7,3},{8,12},{10,14},{12... | collective-permute-start | bytes 645128 | tf_op jit(solution)/shard_map/ppermute | solution.py:326
  515.5 52.4 %collective-permute-start.49 = (bf16[256,1280]{1,0:T(8,128)(2,1)}, bf16[256,1280]{1,0:T(8,128)(2,1)}, u32[]{:S(2)}, u32[]{:S(2)}) collective-permute-start(bf16[256,1280]{1,0:T(8,128)(2,1)} %slice.407), channel_id=1, source_target_pairs={{0,6},{2,0},{4,2},{6,4},{1,7},{3,1},{5,3},{7,5},{8,14},{10,8},{12,... | collective-permute-start | bytes 1966088 | tf_op jit(solution)/shard_map/ppermute | solution.py:242
  522.3 31.8 %collective-permute-start.62 = (bf16[80,1280]{1,0:T(8,128)(2,1)S(1)}, bf16[80,1280]{1,0:T(8,128)(2,1)}, u32[]{:S(2)}, u32[]{:S(2)}) collective-permute-start(bf16[80,1280]{1,0:T(8,128)(2,1)S(1)} %dynamic-slice_bitcast_fusion.27), channel_id=1, source_target_pairs={{0,4},{2,6},{4,0},{6,2},{1,5},{3,7},{5,1},{7,3},{8,12},{10,14},{12... | collective-permute-start | bytes 614408 | tf_op jit(solution)/shard_map/ppermute | solution.py:326
  545.0 66.5 %collective-permute-start.70 = (bf16[960,448]{0,1:T(8,128)(2,1)}, bf16[960,448]{0,1:T(8,128)(2,1)}, u32[]{:S(2)}, u32[]{:S(2)}) collective-permute-start(bf16[960,448]{0,1:T(8,128)(2,1)} %select_n.548), channel_id=1, source_target_pairs={{0,1},{1,0},{2,3},{3,2},{4,5},{5,4},{6,7},{7,6},{8,9},{9,8},{10,11... | collective-permute-start | bytes 2580488 | tf_op jit(solution)/shard_map/ppermute | solution.py:242
  545.9 30.6 %collective-permute-start.54 = (bf16[320,640]{1,0:T(8,128)(2,1)}, bf16[320,640]{1,0:T(8,128)(2,1)}, u32[]{:S(2)}, u32[]{:S(2)}) collective-permute-start(bf16[320,640]{1,0:T(8,128)(2,1)} %dynamic-slice_bitcast_fusion.22), channel_id=1, source_target_pairs={{0,8},{8,0},{1,9},{9,1},{2,10},{10,2},{3,11},{11,3},{4,12},{12,4},... | collective-permute-start | bytes 1228808 | tf_op jit(solution)/shard_map/ppermute | solution.py:242
  582.9 32.8 %collective-permute-start.56 = (bf16[2,80,1408]{2,1,0:T(8,128)(2,1)}, bf16[2,80,1408]{2,1,0:T(8,128)(2,1)}, u32[]{:S(2)}, u32[]{:S(2)}) collective-permute-start(bf16[2,80,1408]{2,1,0:T(8,128)(2,1)} %dynamic-slice_bitcast_fusion.20), channel_id=1, source_target_pairs={{0,2},{2,0},{4,6},{6,4},{1,3},{3,1},{5,7},{7,5},{8,10},{10,8},{12,... | collective-permute-start | bytes 1351688 | tf_op jit(solution)/shard_map/ppermute | solution.py:326
  589.5 60.1 %collective-permute-start.77 = (bf16[2,224,1280]{2,1,0:T(8,128)(2,1)}, bf16[2,224,1280]{2,1,0:T(8,128)(2,1)}, u32[]{:S(2)}, u32[]{:S(2)}) collective-permute-start(bf16[2,224,1280]{2,1,0:T(8,128)(2,1)} %dynamic-slice_bitcast_fusion), channel_id=1, source_target_pairs={{0,8},{8,0},{1,9},{9,1},{2,10},{10,2},{3,11},{11,3},{4,12},{12,4},... | collective-permute-start | bytes 3440648 | tf_op jit(solution)/shard_map/ppermute | solution.py:242
  603.6 49.5 %collective-permute-start.75 = (bf16[2,224,1280]{2,1,0:T(8,128)(2,1)}, bf16[2,224,1280]{2,1,0:T(8,128)(2,1)}, u32[]{:S(2)}, u32[]{:S(2)}) collective-permute-start(bf16[2,224,1280]{2,1,0:T(8,128)(2,1)} %dynamic-slice_bitcast_fusion.1), channel_id=1, source_target_pairs={{0,16},{16,0},{1,17},{17,1},{2,18},{18,2},{3,19},{19,3},{4,20},{20... | collective-permute-start | bytes 3440648 | tf_op jit(solution)/shard_map/ppermute | solution.py:242
  605.8 39.9 %collective-permute-start.65 = (bf16[320,1280]{1,0:T(8,128)(2,1)S(1)}, bf16[320,1280]{1,0:T(8,128)(2,1)}, u32[]{:S(2)}, u32[]{:S(2)}) collective-permute-start(bf16[320,1280]{1,0:T(8,128)(2,1)S(1)} %bitcast.420), channel_id=1, source_target_pairs={{0,1},{1,0},{2,3},{3,2},{4,5},{5,4},{6,7},{7,6},{8,9},{9,8},{10,11... | collective-permute-start | bytes 2457608 | tf_op jit(solution)/shard_map/ppermute | solution.py:242
  (161 other events, 1519.0 us)

commit v7 on v6

--- a/solution.py
+++ b/solution.py
@@ -297,7 +297,8 @@
             kept = ring_gather(along[order[0]][first][start:stop], order[1])
             for second in range(1, side):
                 add(kept[second], start, {order[0]: first, order[1]: second})
-    return place(pieces, offsets, rows * side * side), pieces[1:near], pieces[near:]
+    full = lambda last: place(pieces[:near] + last, offsets, rows * side * side)
+    return full, pieces[1:near], pieces[near:]
 
 
 def ring_reduce(value, axis, at, late):
@@ -385,12 +386,13 @@
 
     small = jnp.concatenate([router_weight, attn_gain[:, None], ffn_gain[:, None]], axis=1)
     small = jnp.pad(small, ((0, 0), (0, 128 - small.shape[1])))
-    first_full, first_near, first_far = gather_dp(
+    first_join, first_near, first_far = gather_dp(
         jnp.concatenate(
             [half(query_weight, core, 1), half(key_weight, core, 1), half(value_weight, core, 1), small],
             axis=1,
         )
     )
+    first_full = first_join(first_far)
     tokens_two = two(tokens)
     starts_two = two(piece_starts[0])
     later = after([output_weight, shared_gate, shared_up, shared_down, out_grad], *first_near)
@@ -399,7 +401,7 @@
         + [half(later[3], core, 1).reshape(rows, narrow)],
         axis=1,
     )
-    second_full, second_near, _ = gather_dp(after(second_shard, *first_far))
+    second_join, second_near, second_far = gather_dp(after(second_shard, *first_far))
 
     chosen = (expert_ids[:, :, None] == jnp.arange(experts, dtype=jnp.int32)).any(axis=1)
     chosen_low = jnp.pad(chosen.astype(BF), ((0, 0), (0, 128 - experts)))
@@ -410,7 +412,7 @@
     grads_pair = swap(grads_sent)
     grads_far = {levels[1]: shifted(grads_sent, "z", levels[1])}
     turn_at = after(grads_sent, grads_far[levels[1]])
-    for step in levels[2:]:
+    for step in levels[2:-1]:
         grads_far[step] = shifted(turn_at, "z", step)
         turn_at = after(turn_at, grads_far[step])
 
@@ -421,16 +423,6 @@
     router_full = small_full[:, :experts]
     gain_one_f = small_full[:, experts].astype(F32)
     gain_two_f = small_full[:, experts + 1].astype(F32)
-    output_cols = second_full[:, :wide]
-    gate_half = second_full[:, wide : wide + narrow]
-    up_half = second_full[:, wide + narrow : wide + 2 * narrow]
-    down_cols = second_full[:, wide + 2 * narrow :].reshape(hidden, wide)
-    met = swap(
-        jnp.concatenate([half(output_cols, 1 - core, 0), half(down_cols, 1 - core, 0)], axis=0)
-    )
-    output_half = joined(half(output_cols, core, 0), met[:wide], core, 1)
-    down_half = joined(half(down_cols, core, 0), met[wide:], core, 1)
-
     token_f = tokens_two.astype(F32)
     norm_one = lax.rsqrt(jnp.mean(token_f * token_f, axis=-1, keepdims=True) + 1e-06)
     attn_in = (token_f * norm_one * gain_one_f).astype(BF).reshape(2 * length, width)
@@ -439,17 +431,28 @@
     flat = lambda value: value.reshape(2 * length, wide)
     query_rot = rotate(by_head(product(attn_in, query_half)), cosine, sine_part).astype(BF)
     key_rot = rotate(by_head(product(attn_in, key_half)), cosine, sine_part).astype(BF)
-    values = by_head(product(attn_in, value_half).astype(BF))
+    value_in = after(attn_in, grads_far[levels[1]])
+    values = by_head(product(value_in, value_half).astype(BF))
     allowed = jnp.stack([allowed_mask(length, starts_two[i], piece_len) for i in range(2)])
-    key_met = after(key_rot, grads_far[levels[1]])
-    scores = mm("sqhd,skhd->shqk", query_rot, key_met) * score_scale
+    scores = mm("sqhd,skhd->shqk", query_rot, key_rot) * score_scale
     scores = jnp.where(allowed[:, None], scores, -1e30)
     row_max = jnp.max(scores, axis=-1, keepdims=True)
     exps = jnp.exp(scores - row_max)
     attn_probs = exps / jnp.sum(exps, axis=-1, keepdims=True)
     probs_low = attn_probs.astype(BF)
-    context = flat(mm("shqk,skhd->sqhd", probs_low, after(values, grads_far[levels[2]], *second_near)).astype(BF))
-    out_partial = product(context, output_half).reshape(2, length, width)
+    second_full = second_join(after(second_far, probs_low))
+    output_cols = second_full[:, :wide]
+    gate_half = second_full[:, wide : wide + narrow]
+    up_half = second_full[:, wide + narrow : wide + 2 * narrow]
+    down_cols = second_full[:, wide + 2 * narrow :].reshape(hidden, wide)
+    met = swap(
+        jnp.concatenate([half(output_cols, 1 - core, 0), half(down_cols, 1 - core, 0)], axis=0)
+    )
+    output_half = joined(half(output_cols, core, 0), met[:wide], core, 1)
+    down_half = joined(half(down_cols, core, 0), met[wide:], core, 1)
+    context = flat(mm("shqk,skhd->sqhd", probs_low, after(values, *second_near)).astype(BF))
+    held = [grads_far[step] for step in levels[2:-1]]
+    out_partial = product(after(context, *held) if held else context, output_half).reshape(2, length, width)
     attn_out = out_partial[0] + swap(out_partial[1].astype(BF)).astype(F32)
     residual = token_f[0] + attn_out
     norm_two = lax.rsqrt(jnp.mean(residual * residual, axis=-1, keepdims=True) + 1e-06)
@@ -462,16 +465,22 @@
     )
     sent_other = swap(sent)
     rows_far = {levels[1]: shifted(sent, "z", levels[1])}
-    grads_late = after([grads_far[step] for step in levels[1:]], sent)
-    grads_all = [grads_sent, grads_pair]
-    for piece in grads_late:
-        grads_all += [piece, swap(piece)]
     own = me * EXP_DEV + jnp.arange(EXP_DEV)
     own_hot = (own[:, None] == jnp.arange(experts)[None, :]).astype(F32)
-    named = jnp.stack([piece[:, width : width + experts] for piece in grads_all]).astype(F32)
-    mask = mm("ste,oe->ost", named, own_hot)
-    slots = jnp.where(mask > 0, jnp.cumsum(mask, axis=2) - 1.0, -1.0).astype(jnp.int32)
-    slots = slots[:, :, None, :]
+
+    def slots_of(pieces):
+        named = jnp.stack([piece[:, width : width + experts] for piece in pieces]).astype(F32)
+        mask = mm("ste,oe->ost", named, own_hot)
+        found = jnp.where(mask > 0, jnp.cumsum(mask, axis=2) - 1.0, -1.0).astype(jnp.int32)
+        return found[:, :, None, :]
+
+    def paired(pieces):
+        return [both for piece in pieces for both in (piece, swap(piece))]
+
+    grads_near = [grads_sent, grads_pair] + paired(
+        after([grads_far[step] for step in levels[1 : depth // 2]], sent)
+    )
+    near_slots = slots_of(grads_near)
 
     ffn_two = jnp.stack([ffn_in, sent_other[:, :width]]).reshape(2 * length, width)
     grad_two = jnp.stack([out_grad, grads_pair[:, :width]]).reshape(2 * length, width)
@@ -484,6 +493,8 @@
         BF
     )
     shared_up_act_grad = (shared_hidden_grad * jax.nn.silu(shared_gate_act)).astype(BF)
+    shared_gate_grad = product(ffn_two.T, shared_gate_act_grad).astype(BF)
+    shared_up_grad = product(ffn_two.T, shared_up_act_grad).astype(BF)
     shared_in_grad = (
         (product(shared_gate_act_grad, gate_half.T) + product(shared_up_act_grad, up_half.T))
         .astype(BF)
@@ -494,66 +505,67 @@
     )
     turn = lambda grad: joined(half(grad, core, 1), swap(half(grad, 1 - core, 1)), core, 0)
     shares = lambda value: value.reshape(side, side, value.shape[0] // dp, -1)
-    sent_next = after(sent, rows_far[levels[1]], shared_in_grad, shared_out)
+    shared_part = [shares(shared_gate_grad), shares(shared_up_grad)]
+    both = ("yx", "xy")
+    rows_near = [sent, sent_other] + paired([rows_far[step] for step in levels[1 : depth // 2]])
+    sent_next = after([sent, grads_sent], rows_far[levels[1]], shared_in_grad, *shared_part)
     for step in levels[2:]:
-        rows_far[step] = shifted(sent_next, "z", step)
-    rows_all = [sent, sent_other]
-    for step in levels[1:]:
-        rows_all += [rows_far[step], swap(rows_far[step])]
-    both = ("yx", "xy")
+        rows_far[step] = shifted(sent_next[0], "z", step)
+    grads_far[levels[-1]] = shifted(sent_next[1], "z", levels[-1])
+    rows_rest = paired([rows_far[step] for step in levels[depth // 2 :]])
+    grads_rest = paired([grads_far[step] for step in levels[depth // 2 :]])
 
     place_me = me.reshape(1).astype(jnp.int32)
     block = owners // 2
     near = expert_call(
-        place_me, slots[:, :block], rows_all[:block], grads_all[:block],
+        place_me, near_slots, rows_near, grads_near,
         expert_gate, expert_up, expert_down, owners, 0,
     )
     wider = width + 128
-    gate_low, up_low, hidden_low, grad_low = after(
-        [shared_gate_act_grad, shared_up_act_grad, shared_hidden, grad_two], near[block]
-    )
-    shared_down_grad = product(hidden_low.T, grad_low).astype(BF)
-    shared_gate_grad = product(ffn_two.T, gate_low).astype(BF)
-    shared_up_grad = product(ffn_two.T, up_low).astype(BF)
-    down_shares = turn(shared_down_grad).reshape(side, side, rows, narrow)
-    cut = (rows // 2 + 15) // 16 * 16
-    shared_part = [
-        jnp.concatenate([shares(shared_gate_grad), down_shares[:, :, :cut]], axis=2),
-        jnp.concatenate([shares(shared_up_grad), down_shares[:, :, cut:]], axis=2),
-    ]
-    chips = [None] * depth
-    for place_at in range(1, depth // 2):
-        chips[place_at] = near[2 * place_at].astype(F32) + swap(near[2 * place_at + 1]).astype(F32)
-    sent_back = [None] + [chips[i][:, :wider].astype(BF) for i in range(1, depth // 2)]
-    far_slots = after(slots[:, block:], *sent_back[1:], *shared_part)
+    shared_one = stage_one(shared_part, both, late=(near[block],))
+    hidden_low = after(shared_hidden, near[block])
+    down_part = [shares(turn(product(hidden_low.T, grad_two).astype(BF)))]
+    summed = lambda mine, other, part: (
+        mine[:, part].astype(F32) + other[:, part].astype(F32)
+    ).astype(BF)
+    to_in, to_out = slice(0, wider), slice(wider, None)
+    others = [swap(near[i]) for i in range(3, block, 2)]
+    mines = [near[i] for i in range(2, block, 2)]
+    sent_back = [summed(m, o, to_in) for m, o in zip(mines, others)]
+    far_slots = after(slots_of(grads_rest), *sent_back, *shared_one, *down_part)
     far = expert_call(
-        place_me, far_slots, rows_all[block:], grads_all[block:],
+        place_me, far_slots, rows_rest, grads_rest,
         expert_gate, expert_up, expert_down, owners, 1, near[block:],
     )
     expert_in, res_grad, routed_hidden, routed_gate_grad, routed_up_grad = far[block:]
     gate_grad = mm("erd,erf->edf", expert_in, routed_gate_grad).astype(BF)
-    met = after([swap(far[i]) for i in range(1, block, 2)], gate_grad)
-    for i, other in enumerate(met):
-        chips[depth // 2 + i] = far[2 * i].astype(F32) + other.astype(F32)
-        sent_back.append(chips[depth // 2 + i][:, :wider].astype(BF))
-    back_in = [shifted(sent_back[i], "z", -levels[i]) for i in range(1, depth)]
-    shared_one = stage_one(shared_part, both, late=(gate_grad,))
-    chips[0] = (near[0].astype(F32) + shared_both[0].astype(F32)) + swap(
+    mines += [far[i] for i in range(0, block, 2)]
+    near_back = [shifted(sent_back[i], "z", -levels[i + 1]) for i in range(depth // 2 - 1)]
+    shared_two = stage_two(shared_one, both, late=(gate_grad,))
+    others += after(
+        [swap(far[i]) for i in range(1, block, 2)], gate_grad, *near_back, *shared_two
+    )
+    sent_back += [
+        summed(m, o, to_in) for m, o in zip(mines[depth // 2 - 1 :], others[depth // 2 - 1 :])
+    ]
+    back_in = near_back + [
+        shifted(sent_back[i], "z", -levels[i + 1]) for i in range(depth // 2 - 1, depth - 1)
+    ]
+    routed_up_grad, res_grad = after([routed_up_grad, res_grad], *sent_back)
+    up_grad = mm("erd,erf->edf", expert_in, routed_up_grad).astype(BF)
+    down_grad = mm("erf,erd->efd", routed_hidden, res_grad).astype(BF)
+    own_chip = (near[0].astype(F32) + shared_both[0].astype(F32)) + swap(
         near[1] + shared_both[1]
     ).astype(F32)
-    back = chips[0][:, :wider]
-    for piece in back_in[: depth // 2 - 1]:
-        back += after(piece, gate_grad).astype(F32)
-
-    routed_up_grad = after(routed_up_grad, *sent_back[depth // 2 :], *shared_one, back)
-    up_grad = mm("erd,erf->edf", expert_in, routed_up_grad).astype(BF)
-    shared_two = stage_two(shared_one, both, late=(up_grad,))
-    down_grad = mm("erf,erd->efd", routed_hidden, after(res_grad, *shared_two)).astype(BF)
+    back = own_chip[:, :wider]
+    for piece in after(back_in[: depth // 2 - 1], up_grad):
+        back += piece.astype(F32)
+
     blocks = [
         [grad[e].reshape(side, side, grad.shape[1] // dp, grad.shape[2]) for e in range(EXP_DEV)]
         for grad in (gate_grad, up_grad, down_grad)
     ]
-    gate_one = stage_one(blocks[0], both, shared_two)
+    gate_one = stage_one(blocks[0], both, (*shared_two, *sent_back[depth // 2 - 1 :]))
     for piece in after(back_in[depth // 2 - 1 :], down_grad, *gate_one):
         back += piece.astype(F32)
 
@@ -577,12 +589,16 @@
     context_grad = by_head(product(attn_grad_two, output_half.T).astype(BF))
     value_grad = flat(mm("shqk,sqhd->skhd", probs_low, context_grad).astype(BF))
     up_one = stage_one(blocks[1], both, gate_one, (value_grad,))
-    context_late = after(context_grad, *up_one)
+    down_one = stage_one(down_part, both[:1], gate_one, (value_grad,))
+    moving = after(summed(mines[0], others[0], to_out), back)
+    arrived = [after(shifted(moving, "z", -levels[1]), value_grad)]
+    context_late = after(context_grad, *up_one, *arrived, *down_one)
     value_wgrad = product(attn_in.T, value_grad).astype(BF)
+    early = [shares(output_grad), shares(value_wgrad)]
+    early_one = stage_one(early, both, up_one)
     probs_grad_att = mm("sqhd,skhd->shqk", context_late, values)
     row_delta = jnp.sum(attn_probs * probs_grad_att, axis=-1, keepdims=True)
     scores_grad = (attn_probs * (probs_grad_att - row_delta)).astype(BF)
-    early = [shares(output_grad), shares(value_wgrad)]
     scores_grad = after(scores_grad, *early)
     query_grad = mm("shqk,skhd->sqhd", scores_grad, key_rot) * score_scale
     key_grad = mm("shqk,sqhd->skhd", scores_grad, query_rot) * score_scale
@@ -595,7 +611,9 @@
         + product(key_pre_grad, key_half.T)
         + product(value_grad, value_half.T)
     ).reshape(2, length, width)
-    attn_in_grad = in_partial[0] + swap(in_partial[1].astype(BF)).astype(F32)
+    gate_two = stage_two(gate_one, both, up_one, (query_wgrad,))
+    shared_down = stage_two(down_one, both[:1], late=(query_wgrad,))
+    attn_in_grad = after(in_partial[0], *early_one, *gate_two, *shared_down) + swap(in_partial[1].astype(BF)).astype(F32)
     token_mine, norm_mine = token_f[0], norm_one[0]
     attn_gain_terms = attn_in_grad * token_mine * norm_mine
     upstream_one = attn_in_grad * gain_one_f
@@ -613,27 +631,24 @@
     ).astype(BF)
 
     done_wgrads = (query_wgrad, key_wgrad)
-    gate_two = stage_two(gate_one, both, up_one, done_wgrads)
-    early_one = stage_one(early, both, up_one, done_wgrads)
     early_two = stage_two(early_one, both)
     late = [shares(query_wgrad), shares(jnp.concatenate([key_wgrad, small_grads], axis=1))]
-    late_one = stage_one(late, both, early_one)
+    late_one = stage_one(late, both)
     late_two = stage_two(late_one, both, early_two)
-    up_two = stage_two(up_one, both, late_one)
+    up_two = stage_two(up_one, both, late_two)
     down_two = stage_two(stage_one(blocks[2], both, late_two), both)
     expert_shares = [jnp.stack(pair).astype(F32) for pair in (gate_two, up_two, down_two)]
-    shared_share = reduce_level(
-        after(jnp.concatenate(shared_two, axis=0), back),
-        ((value_grad,), done_wgrads, early_two, late_one),
-    )
-    early_share = reduce_level(jnp.concatenate(early_two, axis=1))
+    shared_share = reduce_level(after(jnp.concatenate(shared_two, axis=0), back), ((value_grad,), done_wgrads, early_two, late_one))
+    shared_share = after(shared_share, *late_two)
+    early_share = reduce_level(jnp.concatenate([*early_two, *shared_down], axis=0))
     late_share = reduce_level(jnp.concatenate(late_two, axis=1))
 
-    moe_out = chips[0][:, wider:]
-    piece = back
-    for i in range(1, depth):
-        moving = after(chips[i][:, wider:].astype(BF), piece, *(early_two if i > 1 else ()))
-        piece = after(shifted(moving, "z", -levels[i]), *((value_grad,), late_one, late_two)[min(i - 1, 2)])
+    for i in range(1, depth - 1):
+        moving = after(summed(mines[i], others[i], to_out), *early_one, arrived[-1])
+        piece = shifted(moving, "z", -levels[i + 1])
+        arrived.append(after(piece, *(late_one if i < depth - 2 else late_two)))
+    moe_out = own_chip[:, wider:]
+    for piece in arrived:
         moe_out += piece.astype(F32)
 
     early_other, late_other, shared_other = swap(early_share), swap(late_share), swap(shared_share)
@@ -641,13 +656,8 @@
         mine[:, start : start + size], other[:, start : start + size], core, 1
     ).astype(F32)
     small_sum = late_share[:, 2 * wide :].astype(F32) + late_other[:, 2 * wide :].astype(F32)
-    first_rows = rows + cut
-    down_part = lambda share: jnp.concatenate(
-        [share[rows:first_rows], share[first_rows + rows :]], axis=0
-    ).reshape(-1, wide)
-    down_rows = joined(down_part(shared_share), down_part(shared_other), core, 1).astype(F32)
-    unit_cols = lambda start: joined(
-        shared_share[start : start + rows], shared_other[start : start + rows], core, 1
+    stacked = lambda mine, other, start, size: joined(
+        mine[start : start + size], other[start : start + size], core, 1
     ).astype(F32)
 
     stream_out = residual + moe_out
@@ -663,14 +673,14 @@
         tokens_grad.astype(BF),
         column(late_share, late_other, 0, wide),
         column(late_share, late_other, wide, wide),
-        column(early_share, early_other, wide, wide),
-        column(early_share, early_other, 0, wide),
+        stacked(early_share, early_other, rows, rows),
+        stacked(early_share, early_other, 0, rows),
         small_sum[:, experts],
         small_sum[:, experts + 1],
         small_sum[:, :experts],
-        unit_cols(0),
-        unit_cols(first_rows),
-        down_rows,
+        stacked(shared_share, shared_other, 0, rows),
+        stacked(shared_share, shared_other, rows, rows),
+        stacked(early_share, early_other, 2 * rows, early_share.shape[0] - 2 * rows),
         *expert_shares,
         stat_rms,
     )

time: 687 us -> 633 us (0.921)
  local copies, waits for them, and re-layouts: 148 us -> 108 us
  waiting for transfers between devices: 193 us -> 170 us
  other arithmetic: 94.1 us -> 109 us
  starting transfers between devices: 74.4 us -> 66.3 us
    ppermute x67 -> x69, waiting for transfers between devices: 147 us -> 99.4 us  [shifted(): lax.ppermute(value, axis, [(i, (i + by) % size) for i in range(size)])]
    ppermute x12, waiting for transfers between devices: 46.6 us -> 70.3 us  [crossed(): return lax.ppermute(value, 'z', [(i, i ^ bit) for i in range(depth)])]
    convert_element_type x4 -> x14, other arithmetic: 1.53 us -> 21.5 us  [the longest x6 12.3 us: body(): summed = lambda mine, other, part: (mine[:, part].astype(F32) + other[:,...]
    ppermute x12, starting transfers between devices: 20.9 us -> 6.54 us  [crossed(): return lax.ppermute(value, 'z', [(i, i ^ bit) for i in range(depth)])]
    slice x14 -> x11, local copies, waits for them, and re-layouts: 14.4 us -> 2.64 us  [the longest x4 1.32 us: body(): other[start:start + size]]
    unnamed x238 -> x254, local copies, waits for them, and re-layouts: 23.9 us -> 15.7 us
    ppermute x67 -> x69, starting transfers between devices: 53.6 us -> 59.7 us  [shifted(): lax.ppermute(value, axis, [(i, (i + by) % size) for i in range(size)])]
    squeeze x28 -> x32, local copies, waits for them, and re-layouts: 11.2 us -> 16.8 us  [pick(): lax.dynamic_index_in_dim(value, index % value.shape[axis], axis, False)]
  transfers between devices with their start and end apart: 79 -> 81, of which waited for: 25 -> 20; matrix products, arithmetic and copies ran while one was open for 42% -> 43% of each run, Pallas kernels for 12% -> 13%
where the time goes in v7:
time: 633 us; the launch traced here: 623 us
  waiting for transfers between devices  170 us (27%)
  other arithmetic  109 us (17%)
  local copies, waits for them, and re-layouts  108 us (17%)
  matrix products  83.6 us (13%)
  Pallas kernels  79.4 us (13%)
  starting transfers between devices  66.3 us (10%)
  between operations  6.56 us (1%)
    ppermute x69, waiting for transfers between devices, shifted(): lax.ppermute(value, axis, [(i, (i + by) % size) for i in range(size)])  99.4 us
    ppermute x12, waiting for transfers between devices, crossed(): return lax.ppermute(value, 'z', [(i, i ^ bit) for i in range(depth)])  70.3 us
    pallas_call x2, Pallas kernels, expert_call(): pl.pallas_call(functools.partial(expert_kernel, count, width, capacity, e...  69.1 us
    ppermute x69, starting transfers between devices, shifted(): lax.ppermute(value, axis, [(i, (i + by) % size) for i in range(size)])  59.7 us
    dot_general x22, matrix products, product(): return jnp.dot(first_arg, second_arg, preferred_element_type=F32)  45.8 us
    dot_general x10, matrix products, mm(): return jnp.einsum(spec, first_arg, second_arg, preferred_element_type=F32)  29.9 us
    convert_element_type x22, other arithmetic, ring_reduce(): (other.astype(F32) + pick(value, index - step, at).astype(F32)).astype(BF)  23 us
    squeeze x32, local copies, waits for them, and re-layouts, pick(): lax.dynamic_index_in_dim(value, index % value.shape[axis], axis, False)  16.8 us
  transfers between devices with their start and end apart: 81, of which 20 were waited for; matrix products, arithmetic and copies ran while one was open for 43% of the time, Pallas kernels for 13%

profile of v7, /device:TPU:0, one launch (start us, length us, event | category | flops | bytes accessed | tf_op | source)
XLA Modules:
  0.0 622.5 jit_solution(6782235304395617037)
XLA Ops:
  5.5 3.0 collective-permute-start.2
  20.1 17.4 %collective-permute-done.2.refs_2_ = bf16[320,2048]{1,0:T(8,128)(2,1)} collective-permute-done((bf16[320,2048]{1,0:T(8,128)(2,1)}, bf16[320,2048]{1,0:T(8,128)(2,1)}, u32[]{:S(2)}, u32[]{:S(2)}) %collective-permute-start.2) | collective-permute-done | bytes 1310752 | tf_op jit(solution)/shard_map/ppermute | solution.py:242
  55.8 3.5 concatenate.163.refs_0_
  61.0 5.2 place.2
  67.7 4.0 slice_bitcast_fusion.1
  73.2 3.5 copy.287
  76.7 3.9 fusion.45
  80.6 3.5 copy.288
  101.7 6.1 collective-permute-done.11.refs_4_
  109.3 5.2 place.3
  115.8 3.2 reshape.934
  152.6 3.9 multiply_convert_fusion.3
  167.0 3.3 fusion.3
  170.3 11.1 %collective-permute-done.17.refs_2_ = bf16[256,1408]{1,0:T(8,128)(2,1)} collective-permute-done((bf16[256,1408]{1,0:T(8,128)(2,1)}, bf16[256,1408]{1,0:T(8,128)(2,1)}, u32[]{:S(2)}, u32[]{:S(2)}) %collective-permute-start.17) | collective-permute-done | bytes 720928 | tf_op jit(solution)/shard_map/ppermute | solution.py:242
  197.6 3.0 collective-permute-start.23
  200.6 34.5 %experts.2 = (bf16[256,2688]{1,0:T(8,128)(2,1)}, bf16[256,2688]{1,0:T(8,128)(2,1)}, bf16[256,2688]{1,0:T(8,128)(2,1)}, bf16[256,2688]{1,0:T(8,128)(2,1)}, bf16[2...) custom-call(s32[1]{0:T(128)} %bitcast.20.me_ref, ...), custom_call_target="tpu_custom_call" | custom-call | flops 16441671680 | bytes 62914560 | tf_op jit(solution)/shard_map/experts/pallas_call | solution.py:133
  256.4 34.6 %experts.3 = (bf16[256,2688]{1,0:T(8,128)(2,1)}, bf16[256,2688]{1,0:T(8,128)(2,1)}, bf16[256,2688]{1,0:T(8,128)(2,1)}, bf16[256,2688]{1,0:T(8,128)(2,1)}, bf16[2...) custom-call(s32[1]{0:T(128)} %bitcast.20.me_ref, ...), custom_call_target="tpu_custom_call", output_to_operand_aliasing={{4}: (13, {}), {5}: (14, {}), {6}: (15, {}), {7}: (16, {}),... | custom-call | flops 16441671680 | bytes 62914560 | tf_op jit(solution)/shard_map/experts/pallas_call | solution.py:133
  291.1 9.3 %convolution_convert_fusion.2 = bf16[2,1280,896]{2,1,0:T(8,128)(2,1)S(1)} fusion(bf16[2,1024,1280]{2,1,0:T(8,128)(2,1)} %get-tuple-element.126, bf16[2,1024,896]{2,1,0:T(8,128)(2,1)} %get-tuple-element.132), kind=kOutput, calls=%fused_computation.4 | convolution fusion | flops 4699914240 | bytes 13500416 | tf_op jit(solution)/shard_map/erd,erf->edf/dot_general | solution.py:196
  305.1 3.3 add_convert_fusion.5
  312.5 3.0 collective-permute-start.36
  315.6 8.5 %convolution_convert_fusion.1 = bf16[2,1280,896]{2,1,0:T(8,128)(2,1)S(1)} fusion(bf16[2,1024,1280]{2,1,0:T(8,128)(2,1)} %get-tuple-element.126, bf16[2,1024,896]{2,1,0:T(8,128)(2,1)S(1)} %copy-done.120), kind=kOutput, calls=%fused_computation.3 | convolution fusion | flops 4699914240 | bytes 13500416 | tf_op jit(solution)/shard_map/erd,erf->edf/dot_general | solution.py:196
  324.1 8.6 %convolution_convert_fusion = bf16[2,896,1280]{2,1,0:T(8,128)(2,1)S(1)} fusion(bf16[2,1024,896]{2,1,0:T(8,128)(2,1)} %get-tuple-element.140, bf16[2,1024,1280]{2,1,0:T(8,128)(2,1)} %get-tuple-element.141), kind=kOutput, calls=%fused_computation.2 | convolution fusion | flops 4699914240 | bytes 13500416 | tf_op jit(solution)/shard_map/erf,erd->efd/dot_general | solution.py:196
  342.1 20.4 %collective-permute-done.38 = bf16[2,320,896]{2,1,0:T(8,128)(2,1)S(1)} collective-permute-done((bf16[2,320,896]{2,1,0:T(8,128)(2,1)S(1)}, bf16[2,320,896]{2,1,0:T(8,128)(2,1)S(1)}, u32[]{:S(2)}, u32[]{:S(2)}) %collective-permute-start.38) | collective-permute-done | bytes 1146912 | tf_op jit(solution)/shard_map/ppermute | solution.py:242
  397.4 12.5 %collective-permute-done.40 = bf16[256,1280]{1,0:T(8,128)(2,1)} collective-permute-done((bf16[256,1280]{1,0:T(8,128)(2,1)}, bf16[256,1280]{1,0:T(8,128)(2,1)}, u32[]{:S(2)}, u32[]{:S(2)}) %collective-permute-start.40) | collective-permute-done | bytes 655392 | tf_op jit(solution)/shard_map/ppermute | solution.py:242
  439.9 13.3 %collective-permute-done.46 = bf16[2,320,640]{2,1,0:T(8,128)(2,1)S(1)} collective-permute-done((bf16[2,320,640]{2,1,0:T(8,128)(2,1)S(1)}, bf16[2,320,640]{2,1,0:T(8,128)(2,1)S(1)}, u32[]{:S(2)}, u32[]{:S(2)}) %collective-permute-start.46) | collective-permute-done | bytes 819232 | tf_op jit(solution)/shard_map/ppermute | solution.py:242
  462.9 3.9 copy.330
  468.3 12.0 %collective-permute-done.57 = bf16[320,640]{1,0:T(8,128)(2,1)} collective-permute-done((bf16[320,640]{1,0:T(8,128)(2,1)}, bf16[320,640]{1,0:T(8,128)(2,1)}, u32[]{:S(2)}, u32[]{:S(2)}) %collective-permute-start.57) | collective-permute-done | bytes 409632 | tf_op jit(solution)/shard_map/ppermute | solution.py:242
  491.4 11.1 %collective-permute-done.65 = bf16[2,216,640]{2,1,0:T(8,128)(2,1)S(1)} collective-permute-done((bf16[2,216,640]{2,1,0:T(8,128)(2,1)S(1)}, bf16[2,216,640]{2,1,0:T(8,128)(2,1)S(1)}, u32[]{:S(2)}, u32[]{:S(2)}) %collective-permute-start.65) | collective-permute-done | bytes 552992 | tf_op jit(solution)/shard_map/ppermute | solution.py:327
  508.7 27.9 %collective-permute-done.66 = bf16[216,640]{1,0:T(8,128)(2,1)S(1)} collective-permute-done((bf16[216,640]{1,0:T(8,128)(2,1)S(1)}, bf16[216,640]{1,0:T(8,128)(2,1)S(1)}, u32[]{:S(2)}, u32[]{:S(2)}) %collective-permute-start.66) | collective-permute-done | bytes 276512 | tf_op jit(solution)/shard_map/ppermute | solution.py:327
  573.9 7.4 %collective-permute-done.68 = bf16[2,216,640]{2,1,0:T(8,128)(2,1)} collective-permute-done((bf16[2,216,640]{2,1,0:T(8,128)(2,1)}, bf16[2,216,640]{2,1,0:T(8,128)(2,1)}, u32[]{:S(2)}, u32[]{:S(2)}) %collective-permute-start.68) | collective-permute-done | bytes 552992 | tf_op jit(solution)/shard_map/ppermute | solution.py:327
  584.2 12.6 %collective-permute-done.62 = bf16[80,1408]{1,0:T(8,128)(2,1)S(1)} collective-permute-done((bf16[80,1408]{1,0:T(8,128)(2,1)S(1)}, bf16[80,1408]{1,0:T(8,128)(2,1)S(1)}, u32[]{:S(2)}, u32[]{:S(2)}) %collective-permute-start.62) | collective-permute-done | bytes 225312 | tf_op jit(solution)/shard_map/ppermute | solution.py:327
  602.6 6.3 %collective-permute-done.63 = bf16[2,80,1408]{2,1,0:T(8,128)(2,1)S(1)} collective-permute-done((bf16[2,80,1408]{2,1,0:T(8,128)(2,1)S(1)}, bf16[2,80,1408]{2,1,0:T(8,128)(2,1)S(1)}, u32[]{:S(2)}, u32[]{:S(2)}) %collective-permute-start.63) | collective-permute-done | bytes 450592 | tf_op jit(solution)/shard_map/ppermute | solution.py:327
  (682 shorter events, 306.7 us)
Async XLA Ops:
  5.5 32.1 %collective-permute-start.2 = (bf16[320,2048]{1,0:T(8,128)(2,1)}, bf16[320,2048]{1,0:T(8,128)(2,1)}, u32[]{:S(2)}, u32[]{:S(2)}) collective-permute-start(bf16[320,2048]{1,0:T(8,128)(2,1)} %fusion.38.refs_0_), channel_id=1, source_target_pairs={{0,16},{16,0},{1,17},{17,1},{2,18},{18,2},{3,19},{19,3},{4,20},{20... | collective-permute-start | bytes 3932168 | tf_op jit(solution)/shard_map/ppermute | solution.py:242
  8.5 32.8 %collective-permute-start.1 = (bf16[320,2048]{1,0:T(8,128)(2,1)}, bf16[320,2048]{1,0:T(8,128)(2,1)}, u32[]{:S(2)}, u32[]{:S(2)}) collective-permute-start(bf16[320,2048]{1,0:T(8,128)(2,1)} %fusion.38.refs_0_), channel_id=1, source_target_pairs={{0,8},{8,0},{1,9},{9,1},{2,10},{10,2},{3,11},{11,3},{4,12},{12,4},... | collective-permute-start | bytes 3932168 | tf_op jit(solution)/shard_map/ppermute | solution.py:242
  45.7 53.4 %collective-permute-start.14 = (bf16[256,1408]{1,0:T(8,128)(2,1)}, bf16[256,1408]{1,0:T(8,128)(2,1)}, u32[]{:S(2)}, u32[]{:S(2)}) collective-permute-start(bf16[256,1408]{1,0:T(8,128)(2,1)} %pad_maximum_fusion.8.refs_4_), channel_id=1, source_target_pairs={{0,1},{1,0},{2,3},{3,2},{4,5},{5,4},{6,7},{7,6},{8,9},{9,8},{10,11... | collective-permute-start | bytes 2162696 | tf_op jit(solution)/shard_map/ppermute | solution.py:242
  45.7 54.4 %collective-permute-start.5 = (bf16[256,1408]{1,0:T(8,128)(2,1)}, bf16[256,1408]{1,0:T(8,128)(2,1)}, u32[]{:S(2)}, u32[]{:S(2)}) collective-permute-start(bf16[256,1408]{1,0:T(8,128)(2,1)} %pad_maximum_fusion.8.refs_4_), channel_id=1, source_target_pairs={{0,4},{2,6},{4,0},{6,2},{1,5},{3,7},{5,1},{7,3},{8,12},{10,14},{12... | collective-permute-start | bytes 2162696 | tf_op jit(solution)/shard_map/ppermute | solution.py:242
  59.3 31.2 %collective-permute-start.7 = (bf16[320,1984]{1,0:T(8,128)(2,1)}, bf16[320,1984]{1,0:T(8,128)(2,1)}, u32[]{:S(2)}, u32[]{:S(2)}) collective-permute-start(bf16[320,1984]{1,0:T(8,128)(2,1)} %concatenate.163.refs_0_), channel_id=1, source_target_pairs={{0,16},{16,0},{1,17},{17,1},{2,18},{18,2},{3,19},{19,3},{4,20},{20... | collective-permute-start | bytes 3809288 | tf_op jit(solution)/shard_map/ppermute | solution.py:242
  60.4 31.9 %collective-permute-start.6 = (bf16[320,1984]{1,0:T(8,128)(2,1)}, bf16[320,1984]{1,0:T(8,128)(2,1)}, u32[]{:S(2)}, u32[]{:S(2)}) collective-permute-start(bf16[320,1984]{1,0:T(8,128)(2,1)} %concatenate.163.refs_0_), channel_id=1, source_target_pairs={{0,8},{8,0},{1,9},{9,1},{2,10},{10,2},{3,11},{11,3},{4,12},{12,4},... | collective-permute-start | bytes 3809288 | tf_op jit(solution)/shard_map/ppermute | solution.py:242
  146.6 34.8 %collective-permute-start.17 = (bf16[256,1408]{1,0:T(8,128)(2,1)}, bf16[256,1408]{1,0:T(8,128)(2,1)}, u32[]{:S(2)}, u32[]{:S(2)}) collective-permute-start(bf16[256,1408]{1,0:T(8,128)(2,1)} %concatenate.169.refs_0_), channel_id=1, source_target_pairs={{0,4},{2,6},{4,0},{6,2},{1,5},{3,7},{5,1},{7,3},{8,12},{10,14},{12... | collective-permute-start | bytes 2162696 | tf_op jit(solution)/shard_map/ppermute | solution.py:242
  147.8 35.6 %collective-permute-start.15 = (bf16[256,1408]{1,0:T(8,128)(2,1)}, bf16[256,1408]{1,0:T(8,128)(2,1)}, u32[]{:S(2)}, u32[]{:S(2)}) collective-permute-start(bf16[256,1408]{1,0:T(8,128)(2,1)} %collective-permute-done.5.refs_6_), channel_id=1, source_target_pairs={{0,1},{1,0},{2,3},{3,2},{4,5},{5,4},{6,7},{7,6},{8,9},{9,8},{10,11... | collective-permute-start | bytes 2162696 | tf_op jit(solution)/shard_map/ppermute | solution.py:242
  181.4 66.6 %collective-permute-start.30 = (bf16[256,1408]{1,0:T(8,128)(2,1)}, bf16[256,1408]{1,0:T(8,128)(2,1)}, u32[]{:S(2)}, u32[]{:S(2)}) collective-permute-start(bf16[256,1408]{1,0:T(8,128)(2,1)} %concatenate.169.refs_0_), channel_id=1, source_target_pairs={{0,6},{2,0},{4,2},{6,4},{1,7},{3,1},{5,3},{7,5},{8,14},{10,8},{12,... | collective-permute-start | bytes 2162696 | tf_op jit(solution)/shard_map/ppermute | solution.py:242
  182.8 66.0 %collective-permute-start.28 = (bf16[256,1408]{1,0:T(8,128)(2,1)}, bf16[256,1408]{1,0:T(8,128)(2,1)}, u32[]{:S(2)}, u32[]{:S(2)}) collective-permute-start(bf16[256,1408]{1,0:T(8,128)(2,1)} %concatenate.169.refs_0_), channel_id=1, source_target_pairs={{0,2},{2,4},{4,6},{6,0},{1,3},{3,5},{5,7},{7,1},{8,10},{10,12},{12... | collective-permute-start | bytes 2162696 | tf_op jit(solution)/shard_map/ppermute | solution.py:242
  193.3 42.8 %collective-permute-start.26 = (bf16[2,320,448]{2,1,0:T(8,128)(2,1)}, bf16[2,320,448]{2,1,0:T(8,128)(2,1)}, u32[]{:S(2)}, u32[]{:S(2)}) collective-permute-start(bf16[2,320,448]{2,1,0:T(8,128)(2,1)} %dynamic-slice_bitcast_fusion.10), channel_id=1, source_target_pairs={{0,8},{8,0},{1,9},{9,1},{2,10},{10,2},{3,11},{11,3},{4,12},{12,4},... | collective-permute-start | bytes 1720328 | tf_op jit(solution)/shard_map/ppermute | solution.py:242
  194.8 43.8 %collective-permute-start.25 = (bf16[2,320,448]{2,1,0:T(8,128)(2,1)}, bf16[2,320,448]{2,1,0:T(8,128)(2,1)}, u32[]{:S(2)}, u32[]{:S(2)}) collective-permute-start(bf16[2,320,448]{2,1,0:T(8,128)(2,1)} %dynamic-slice_bitcast_fusion.11), channel_id=1, source_target_pairs={{0,16},{16,0},{1,17},{17,1},{2,18},{18,2},{3,19},{19,3},{4,20},{20... | collective-permute-start | bytes 1720328 | tf_op jit(solution)/shard_map/ppermute | solution.py:242
  197.6 37.5 %collective-permute-start.23 = (bf16[256,1408]{1,0:T(8,128)(2,1)}, bf16[256,1408]{1,0:T(8,128)(2,1)}, u32[]{:S(2)}, u32[]{:S(2)}) collective-permute-start(bf16[256,1408]{1,0:T(8,128)(2,1)} %pad_maximum_fusion.8.refs_4_), channel_id=1, source_target_pairs={{0,6},{2,0},{4,2},{6,4},{1,7},{3,1},{5,3},{7,5},{8,14},{10,8},{12,... | collective-permute-start | bytes 2162696 | tf_op jit(solution)/shard_map/ppermute | solution.py:242
  245.8 54.7 %collective-permute-start.35 = (bf16[320,448]{1,0:T(8,128)(2,1)}, bf16[320,448]{1,0:T(8,128)(2,1)}, u32[]{:S(2)}, u32[]{:S(2)}) collective-permute-start(bf16[320,448]{1,0:T(8,128)(2,1)} %dynamic-slice_bitcast_fusion.26), channel_id=1, source_target_pairs={{0,16},{16,0},{1,17},{17,1},{2,18},{18,2},{3,19},{19,3},{4,20},{20... | collective-permute-start | bytes 860168 | tf_op jit(solution)/shard_map/ppermute | solution.py:242
  248.0 53.0 %collective-permute-start.34 = (bf16[320,448]{1,0:T(8,128)(2,1)}, bf16[320,448]{1,0:T(8,128)(2,1)}, u32[]{:S(2)}, u32[]{:S(2)}) collective-permute-start(bf16[320,448]{1,0:T(8,128)(2,1)} %dynamic-slice_bitcast_fusion.27), channel_id=1, source_target_pairs={{0,8},{8,0},{1,9},{9,1},{2,10},{10,2},{3,11},{11,3},{4,12},{12,4},... | collective-permute-start | bytes 860168 | tf_op jit(solution)/shard_map/ppermute | solution.py:242
  253.5 49.6 %collective-permute-start.19 = (bf16[256,2688]{1,0:T(8,128)(2,1)}, bf16[256,2688]{1,0:T(8,128)(2,1)}, u32[]{:S(2)}, u32[]{:S(2)}) collective-permute-start(bf16[256,2688]{1,0:T(8,128)(2,1)} %fusion.34), channel_id=1, source_target_pairs={{0,1},{1,0},{2,3},{3,2},{4,5},{5,4},{6,7},{7,6},{8,9},{9,8},{10,11... | collective-permute-start | bytes 4128776 | tf_op jit(solution)/shard_map/ppermute | solution.py:242
  256.4 52.3 %collective-permute-start.21 = (bf16[256,1408]{1,0:T(8,128)(2,1)}, bf16[256,1408]{1,0:T(8,128)(2,1)}, u32[]{:S(2)}, u32[]{:S(2)}) collective-permute-start(bf16[256,1408]{1,0:T(8,128)(2,1)} %add_convert_fusion.2), channel_id=1, source_target_pairs={{0,4},{2,6},{4,0},{6,2},{1,5},{3,7},{5,1},{7,3},{8,12},{10,14},{12... | collective-permute-start | bytes 2162696 | tf_op jit(solution)/shard_map/ppermute | solution.py:242
  310.7 54.3 %collective-permute-start.37 = (bf16[256,1408]{1,0:T(8,128)(2,1)}, bf16[256,1408]{1,0:T(8,128)(2,1)}, u32[]{:S(2)}, u32[]{:S(2)}) collective-permute-start(bf16[256,1408]{1,0:T(8,128)(2,1)} %add_convert_fusion), channel_id=1, source_target_pairs={{0,2},{2,4},{4,6},{6,0},{1,3},{3,5},{5,7},{7,1},{8,10},{10,12},{12... | collective-permute-start | bytes 2162696 | tf_op jit(solution)/shard_map/ppermute | solution.py:242
  312.5 52.5 %collective-permute-start.36 = (bf16[256,1408]{1,0:T(8,128)(2,1)}, bf16[256,1408]{1,0:T(8,128)(2,1)}, u32[]{:S(2)}, u32[]{:S(2)}) collective-permute-start(bf16[256,1408]{1,0:T(8,128)(2,1)} %add_convert_fusion.1), channel_id=1, source_target_pairs={{0,6},{2,0},{4,2},{6,4},{1,7},{3,1},{5,3},{7,5},{8,14},{10,8},{12,... | collective-permute-start | bytes 2162696 | tf_op jit(solution)/shard_map/ppermute | solution.py:242
  373.5 36.4 %collective-permute-start.40 = (bf16[256,1280]{1,0:T(8,128)(2,1)}, bf16[256,1280]{1,0:T(8,128)(2,1)}, u32[]{:S(2)}, u32[]{:S(2)}) collective-permute-start(bf16[256,1280]{1,0:T(8,128)(2,1)} %add_convert_fusion.5), channel_id=1, source_target_pairs={{0,4},{2,6},{4,0},{6,2},{1,5},{3,7},{5,1},{7,3},{8,12},{10,14},{12... | collective-permute-start | bytes 1966088 | tf_op jit(solution)/shard_map/ppermute | solution.py:242
  376.8 36.0 %collective-permute-start.44 = (bf16[2,320,896]{2,1,0:T(8,128)(2,1)}, bf16[2,320,896]{2,1,0:T(8,128)(2,1)}, u32[]{:S(2)}, u32[]{:S(2)}) collective-permute-start(bf16[2,320,896]{2,1,0:T(8,128)(2,1)} %dynamic-slice_bitcast_fusion.2), channel_id=1, source_target_pairs={{0,8},{8,0},{1,9},{9,1},{2,10},{10,2},{3,11},{11,3},{4,12},{12,4},... | collective-permute-start | bytes 3440648 | tf_op jit(solution)/shard_map/ppermute | solution.py:242
  381.1 34.8 %collective-permute-start.43 = (bf16[2,320,896]{2,1,0:T(8,128)(2,1)}, bf16[2,320,896]{2,1,0:T(8,128)(2,1)}, u32[]{:S(2)}, u32[]{:S(2)}) collective-permute-start(bf16[2,320,896]{2,1,0:T(8,128)(2,1)} %dynamic-slice_bitcast_fusion.3), channel_id=1, source_target_pairs={{0,16},{16,0},{1,17},{17,1},{2,18},{18,2},{3,19},{19,3},{4,20},{20... | collective-permute-start | bytes 3440648 | tf_op jit(solution)/shard_map/ppermute | solution.py:242
  393.3 41.8 %collective-permute-start.71 = (bf16[160,448]{1,0:T(8,128)(2,1)S(1)}, bf16[160,448]{1,0:T(8,128)(2,1)S(1)}, u32[]{:S(2)}, u32[]{:S(2)}) collective-permute-start(bf16[160,448]{1,0:T(8,128)(2,1)S(1)} %dynamic-slice_bitcast_fusion.31), channel_id=1, source_target_pairs={{0,4},{2,6},{4,0},{6,2},{1,5},{3,7},{5,1},{7,3},{8,12},{10,14},{12... | collective-permute-start | bytes 430088 | tf_op jit(solution)/shard_map/ppermute | solution.py:327
  396.6 37.4 %collective-permute-start.52 = (bf16[224,640]{1,0:T(8,128)(2,1)S(1)}, bf16[224,640]{1,0:T(8,128)(2,1)S(1)}, u32[]{:S(2)}, u32[]{:S(2)}) collective-permute-start(bf16[224,640]{1,0:T(8,128)(2,1)S(1)} %dynamic-slice_bitcast_fusion.28), channel_id=1, source_target_pairs={{0,8},{8,0},{1,9},{9,1},{2,10},{10,2},{3,11},{11,3},{4,12},{12,4},... | collective-permute-start | bytes 860168 | tf_op jit(solution)/shard_map/ppermute | solution.py:242
  436.0 52.6 %collective-permute-start.72 = (bf16[160,448]{1,0:T(8,128)(2,1)S(1)}, bf16[160,448]{1,0:T(8,128)(2,1)}, u32[]{:S(2)}, u32[]{:S(2)}) collective-permute-start(bf16[160,448]{1,0:T(8,128)(2,1)S(1)} %fusion.103), channel_id=1, source_target_pairs={{0,4},{2,6},{4,0},{6,2},{1,5},{3,7},{5,1},{7,3},{8,12},{10,14},{12... | collective-permute-start | bytes 430088 | tf_op jit(solution)/shard_map/ppermute | solution.py:327
  437.0 50.0 %collective-permute-start.49 = (bf16[2,320,640]{2,1,0:T(8,128)(2,1)}, bf16[2,320,640]{2,1,0:T(8,128)(2,1)}, u32[]{:S(2)}, u32[]{:S(2)}) collective-permute-start(bf16[2,320,640]{2,1,0:T(8,128)(2,1)} %dynamic-slice_bitcast_fusion.7), channel_id=1, source_target_pairs={{0,16},{16,0},{1,17},{17,1},{2,18},{18,2},{3,19},{19,3},{4,20},{20... | collective-permute-start | bytes 2457608 | tf_op jit(solution)/shard_map/ppermute | solution.py:242
  457.5 50.6 %collective-permute-start.47 = (bf16[256,1280]{1,0:T(8,128)(2,1)}, bf16[256,1280]{1,0:T(8,128)(2,1)}, u32[]{:S(2)}, u32[]{:S(2)}) collective-permute-start(bf16[256,1280]{1,0:T(8,128)(2,1)} %add_convert_fusion.4), channel_id=1, source_target_pairs={{0,6},{2,0},{4,2},{6,4},{1,7},{3,1},{5,3},{7,5},{8,14},{10,8},{12,... | collective-permute-start | bytes 1966088 | tf_op jit(solution)/shard_map/ppermute | solution.py:242
  502.7 33.9 %collective-permute-start.66 = (bf16[216,640]{1,0:T(8,128)(2,1)S(1)}, bf16[216,640]{1,0:T(8,128)(2,1)S(1)}, u32[]{:S(2)}, u32[]{:S(2)}) collective-permute-start(bf16[216,640]{1,0:T(8,128)(2,1)S(1)} %dynamic-slice_bitcast_fusion.29), channel_id=1, source_target_pairs={{0,4},{2,6},{4,0},{6,2},{1,5},{3,7},{5,1},{7,3},{8,12},{10,14},{12... | collective-permute-start | bytes 829448 | tf_op jit(solution)/shard_map/ppermute | solution.py:327
  503.7 33.1 %collective-permute-start.58 = (bf16[320,640]{1,0:T(8,128)(2,1)S(1)}, bf16[320,640]{1,0:T(8,128)(2,1)S(1)}, u32[]{:S(2)}, u32[]{:S(2)}) collective-permute-start(bf16[320,640]{1,0:T(8,128)(2,1)S(1)} %dynamic-slice_bitcast_fusion.22), channel_id=1, source_target_pairs={{0,8},{8,0},{1,9},{9,1},{2,10},{10,2},{3,11},{11,3},{4,12},{12,4},... | collective-permute-start | bytes 1228808 | tf_op jit(solution)/shard_map/ppermute | solution.py:242
  508.1 42.5 %collective-permute-start.55 = (bf16[256,1280]{1,0:T(8,128)(2,1)}, bf16[256,1280]{1,0:T(8,128)(2,1)}, u32[]{:S(2)}, u32[]{:S(2)}) collective-permute-start(bf16[256,1280]{1,0:T(8,128)(2,1)} %add_convert_fusion.3), channel_id=1, source_target_pairs={{0,2},{2,4},{4,6},{6,0},{1,3},{3,5},{5,7},{7,1},{8,10},{10,12},{12... | collective-permute-start | bytes 1966088 | tf_op jit(solution)/shard_map/ppermute | solution.py:242
  550.6 46.5 %collective-permute-start.79 = (bf16[2,224,1280]{2,1,0:T(8,128)(2,1)}, bf16[2,224,1280]{2,1,0:T(8,128)(2,1)}, u32[]{:S(2)}, u32[]{:S(2)}) collective-permute-start(bf16[2,224,1280]{2,1,0:T(8,128)(2,1)} %dynamic-slice_bitcast_fusion), channel_id=1, source_target_pairs={{0,8},{8,0},{1,9},{9,1},{2,10},{10,2},{3,11},{11,3},{4,12},{12,4},... | collective-permute-start | bytes 3440648 | tf_op jit(solution)/shard_map/ppermute | solution.py:242
  559.7 40.6 %collective-permute-start.77 = (bf16[2,224,1280]{2,1,0:T(8,128)(2,1)}, bf16[2,224,1280]{2,1,0:T(8,128)(2,1)}, u32[]{:S(2)}, u32[]{:S(2)}) collective-permute-start(bf16[2,224,1280]{2,1,0:T(8,128)(2,1)} %dynamic-slice_bitcast_fusion.1), channel_id=1, source_target_pairs={{0,16},{16,0},{1,17},{17,1},{2,18},{18,2},{3,19},{19,3},{4,20},{20... | collective-permute-start | bytes 3440648 | tf_op jit(solution)/shard_map/ppermute | solution.py:242
  (175 other events, 1804.8 us)

commit v8 on v7

--- a/solution.py
+++ b/solution.py
@@ -551,9 +551,8 @@
     back_in = near_back + [
         shifted(sent_back[i], "z", -levels[i + 1]) for i in range(depth // 2 - 1, depth - 1)
     ]
-    routed_up_grad, res_grad = after([routed_up_grad, res_grad], *sent_back)
+    routed_up_grad = after(routed_up_grad, *sent_back)
     up_grad = mm("erd,erf->edf", expert_in, routed_up_grad).astype(BF)
-    down_grad = mm("erf,erd->efd", routed_hidden, res_grad).astype(BF)
     own_chip = (near[0].astype(F32) + shared_both[0].astype(F32)) + swap(
         near[1] + shared_both[1]
     ).astype(F32)
@@ -561,12 +560,14 @@
     for piece in after(back_in[: depth // 2 - 1], up_grad):
         back += piece.astype(F32)
 
-    blocks = [
-        [grad[e].reshape(side, side, grad.shape[1] // dp, grad.shape[2]) for e in range(EXP_DEV)]
-        for grad in (gate_grad, up_grad, down_grad)
+    in_blocks = lambda grad: [
+        grad[e].reshape(side, side, grad.shape[1] // dp, grad.shape[2]) for e in range(EXP_DEV)
     ]
-    gate_one = stage_one(blocks[0], both, (*shared_two, *sent_back[depth // 2 - 1 :]))
-    for piece in after(back_in[depth // 2 - 1 :], down_grad, *gate_one):
+    gate_first = (*shared_two, *sent_back[depth // 2 - 1 :])
+    gate_one = stage_one(in_blocks(gate_grad), both, gate_first, (back, up_grad))
+    res_grad = after(res_grad, *gate_one)
+    down_grad = mm("erf,erd->efd", routed_hidden, res_grad).astype(BF)
+    for piece in after(back_in[depth // 2 - 1 :], down_grad):
         back += piece.astype(F32)
 
     probs_grad = back[:, width : width + experts] + back[:, width + experts : width + 2 * experts]
@@ -583,19 +584,18 @@
         - residual * norm_two**3 * jnp.mean(upstream_two * residual, axis=-1, keepdims=True)
     )
     residual_low = residual_grad.astype(BF)
-    attn_grad_two = two(residual_low).reshape(2 * length, width)
+    attn_grad_two = two(residual_grad.astype(BF)).reshape(2 * length, width)
     output_grad = product(context.T, attn_grad_two).astype(BF)
     output_grad = turn(output_grad)
     context_grad = by_head(product(attn_grad_two, output_half.T).astype(BF))
     value_grad = flat(mm("shqk,sqhd->skhd", probs_low, context_grad).astype(BF))
-    up_one = stage_one(blocks[1], both, gate_one, (value_grad,))
+    up_one = stage_one(in_blocks(up_grad), both, gate_one, (value_grad,))
     down_one = stage_one(down_part, both[:1], gate_one, (value_grad,))
     moving = after(summed(mines[0], others[0], to_out), back)
     arrived = [after(shifted(moving, "z", -levels[1]), value_grad)]
     context_late = after(context_grad, *up_one, *arrived, *down_one)
     value_wgrad = product(attn_in.T, value_grad).astype(BF)
     early = [shares(output_grad), shares(value_wgrad)]
-    early_one = stage_one(early, both, up_one)
     probs_grad_att = mm("sqhd,skhd->shqk", context_late, values)
     row_delta = jnp.sum(attn_probs * probs_grad_att, axis=-1, keepdims=True)
     scores_grad = (attn_probs * (probs_grad_att - row_delta)).astype(BF)
@@ -613,7 +613,7 @@
     ).reshape(2, length, width)
     gate_two = stage_two(gate_one, both, up_one, (query_wgrad,))
     shared_down = stage_two(down_one, both[:1], late=(query_wgrad,))
-    attn_in_grad = after(in_partial[0], *early_one, *gate_two, *shared_down) + swap(in_partial[1].astype(BF)).astype(F32)
+    attn_in_grad = after(in_partial[0], *gate_two, *shared_down) + swap(in_partial[1].astype(BF)).astype(F32)
     token_mine, norm_mine = token_f[0], norm_one[0]
     attn_gain_terms = attn_in_grad * token_mine * norm_mine
     upstream_one = attn_in_grad * gain_one_f
@@ -631,12 +631,13 @@
     ).astype(BF)
 
     done_wgrads = (query_wgrad, key_wgrad)
+    early_one = stage_one(early, both, up_one, (small_grads,))
     early_two = stage_two(early_one, both)
     late = [shares(query_wgrad), shares(jnp.concatenate([key_wgrad, small_grads], axis=1))]
     late_one = stage_one(late, both)
     late_two = stage_two(late_one, both, early_two)
-    up_two = stage_two(up_one, both, late_two)
-    down_two = stage_two(stage_one(blocks[2], both, late_two), both)
+    up_two = stage_two(up_one, both, late_one)
+    down_two = stage_two(stage_one(in_blocks(down_grad), both, up_two), both)
     expert_shares = [jnp.stack(pair).astype(F32) for pair in (gate_two, up_two, down_two)]
     shared_share = reduce_level(after(jnp.concatenate(shared_two, axis=0), back), ((value_grad,), done_wgrads, early_two, late_one))
     shared_share = after(shared_share, *late_two)
@@ -644,9 +645,9 @@
     late_share = reduce_level(jnp.concatenate(late_two, axis=1))
 
     for i in range(1, depth - 1):
-        moving = after(summed(mines[i], others[i], to_out), *early_one, arrived[-1])
+        moving = after(summed(mines[i], others[i], to_out), arrived[-1])
         piece = shifted(moving, "z", -levels[i + 1])
-        arrived.append(after(piece, *(late_one if i < depth - 2 else late_two)))
+        arrived.append(after(piece, *((query_wgrad,) if i < depth - 2 else early_two)))
     moe_out = own_chip[:, wider:]
     for piece in arrived:
         moe_out += piece.astype(F32)

time: 633 us -> 631 us (level)
  waiting for transfers between devices: 170 us -> 152 us
  Pallas kernels: 79.4 us -> 89.2 us
    ppermute x12, waiting for transfers between devices: 70.3 us -> 43.8 us  [crossed(): return lax.ppermute(value, 'z', [(i, i ^ bit) for i in range(depth)])]
    pallas_call x2, Pallas kernels: 69.1 us -> 78.9 us  [expert_call(): pl.pallas_call(functools.partial(expert_kernel, count, width, capacity, e...]
    ppermute x69, waiting for transfers between devices: 99.4 us -> 108 us  [shifted(): lax.ppermute(value, axis, [(i, (i + by) % size) for i in range(size)])]
    convert_element_type x22 -> x24, other arithmetic: 23 us -> 26.7 us  [ring_reduce(): (other.astype(F32) + pick(value, index - step, at).astype(F32)).astype(BF)]
  transfers between devices with their start and end apart: 81 -> 81, of which waited for: 20 -> 23; matrix products, arithmetic and copies ran while one was open for 43% -> 43% of each run, Pallas kernels for 13% -> 14%
where the time goes in v8:
time: 631 us; the launch traced here: 620 us
  waiting for transfers between devices  152 us (24%)
  other arithmetic  111 us (18%)
  local copies, waits for them, and re-layouts  110 us (17%)
  Pallas kernels  89.2 us (14%)
  matrix products  82.7 us (13%)
  starting transfers between devices  68.7 us (11%)
  between operations  6.47 us (1%)
    ppermute x69, waiting for transfers between devices, shifted(): lax.ppermute(value, axis, [(i, (i + by) % size) for i in range(size)])  108 us
    pallas_call x2, Pallas kernels, expert_call(): pl.pallas_call(functools.partial(expert_kernel, count, width, capacity, e...  78.9 us
    ppermute x69, starting transfers between devices, shifted(): lax.ppermute(value, axis, [(i, (i + by) % size) for i in range(size)])  56.5 us
    dot_general x22, matrix products, product(): return jnp.dot(first_arg, second_arg, preferred_element_type=F32)  44.8 us
    ppermute x12, waiting for transfers between devices, crossed(): return lax.ppermute(value, 'z', [(i, i ^ bit) for i in range(depth)])  43.8 us
    dot_general x10, matrix products, mm(): return jnp.einsum(spec, first_arg, second_arg, preferred_element_type=F32)  29.9 us
    convert_element_type x24, other arithmetic, ring_reduce(): (other.astype(F32) + pick(value, index - step, at).astype(F32)).astype(BF)  26.7 us
    unnamed x254, local copies, waits for them, and re-layouts  19.1 us
  transfers between devices with their start and end apart: 81, of which 23 were waited for; matrix products, arithmetic and copies ran while one was open for 43% of the time, Pallas kernels for 14%

profile of v8, /device:TPU:0, one launch (start us, length us, event | category | flops | bytes accessed | tf_op | source)
XLA Modules:
  0.0 619.7 jit_solution(12857899953990351236)
XLA Ops:
  20.1 17.5 %collective-permute-done.2.refs_2_ = bf16[320,2048]{1,0:T(8,128)(2,1)} collective-permute-done((bf16[320,2048]{1,0:T(8,128)(2,1)}, bf16[320,2048]{1,0:T(8,128)(2,1)}, u32[]{:S(2)}, u32[]{:S(2)}) %collective-permute-start.2) | collective-permute-done | bytes 1310752 | tf_op jit(solution)/shard_map/ppermute | solution.py:242
  55.8 3.5 concatenate.163.refs_0_
  61.0 5.1 place.2
  67.7 4.0 slice_bitcast_fusion.1
  73.2 3.5 copy.287
  76.7 3.9 fusion.43
  80.6 3.5 copy.288
  101.7 6.1 collective-permute-done.11.refs_4_
  109.3 5.2 place.3
  152.4 3.9 multiply_convert_fusion.3
  166.8 3.3 fusion.3
  170.1 11.1 %collective-permute-done.17.refs_2_ = bf16[256,1408]{1,0:T(8,128)(2,1)} collective-permute-done((bf16[256,1408]{1,0:T(8,128)(2,1)}, bf16[256,1408]{1,0:T(8,128)(2,1)}, u32[]{:S(2)}, u32[]{:S(2)}) %collective-permute-start.17) | collective-permute-done | bytes 720928 | tf_op jit(solution)/shard_map/ppermute | solution.py:242
  200.4 44.3 %experts.2 = (bf16[256,2688]{1,0:T(8,128)(2,1)}, bf16[256,2688]{1,0:T(8,128)(2,1)}, bf16[256,2688]{1,0:T(8,128)(2,1)}, bf16[256,2688]{1,0:T(8,128)(2,1)}, bf16[2...) custom-call(s32[1]{0:T(128)} %bitcast.20.me_ref, ...), custom_call_target="tpu_custom_call" | custom-call | flops 16441671680 | bytes 62914560 | tf_op jit(solution)/shard_map/experts/pallas_call | solution.py:133
  266.1 34.6 %experts.3 = (bf16[256,2688]{1,0:T(8,128)(2,1)}, bf16[256,2688]{1,0:T(8,128)(2,1)}, bf16[256,2688]{1,0:T(8,128)(2,1)}, bf16[256,2688]{1,0:T(8,128)(2,1)}, bf16[2...) custom-call(s32[1]{0:T(128)} %bitcast.20.me_ref, ...), custom_call_target="tpu_custom_call", output_to_operand_aliasing={{4}: (13, {}), {5}: (14, {}), {6}: (15, {}), {7}: (16, {}),... | custom-call | flops 16441671680 | bytes 62914560 | tf_op jit(solution)/shard_map/experts/pallas_call | solution.py:133
  300.8 9.3 %convolution_convert_fusion.2 = bf16[2,1280,896]{2,1,0:T(8,128)(2,1)S(1)} fusion(bf16[2,1024,1280]{2,1,0:T(8,128)(2,1)} %get-tuple-element.130, bf16[2,1024,896]{2,1,0:T(8,128)(2,1)} %get-tuple-element.135), kind=kOutput, calls=%fused_computation.4 | convolution fusion | flops 4699914240 | bytes 13500416 | tf_op jit(solution)/shard_map/erd,erf->edf/dot_general | solution.py:196
  314.8 3.2 add_convert_fusion.5
  323.5 3.3 collective-permute-start.36
  326.8 8.5 %convolution_convert_fusion.1 = bf16[2,1280,896]{2,1,0:T(8,128)(2,1)S(1)} fusion(bf16[2,1024,1280]{2,1,0:T(8,128)(2,1)} %get-tuple-element.130, bf16[2,1024,896]{2,1,0:T(8,128)(2,1)S(1)} %copy-done.120), kind=kOutput, calls=%fused_computation.3 | convolution fusion | flops 4699914240 | bytes 13500416 | tf_op jit(solution)/shard_map/erd,erf->edf/dot_general | solution.py:196
  338.9 23.5 %collective-permute-done.39 = bf16[2,320,896]{2,1,0:T(8,128)(2,1)S(1)} collective-permute-done((bf16[2,320,896]{2,1,0:T(8,128)(2,1)S(1)}, bf16[2,320,896]{2,1,0:T(8,128)(2,1)S(1)}, u32[]{:S(2)}, u32[]{:S(2)}) %collective-permute-start.39) | collective-permute-done | bytes 1146912 | tf_op jit(solution)/shard_map/ppermute | solution.py:242
  364.9 8.6 %convolution_convert_fusion = bf16[2,896,1280]{2,1,0:T(8,128)(2,1)S(1)} fusion(bf16[2,1024,896]{2,1,0:T(8,128)(2,1)} %get-tuple-element.143, bf16[2,1024,1280]{2,1,0:T(8,128)(2,1)} %get-tuple-element.149), kind=kOutput, calls=%fused_computation.2 | convolution fusion | flops 4699914240 | bytes 13500416 | tf_op jit(solution)/shard_map/erf,erd->efd/dot_general | solution.py:196
  404.8 12.4 %collective-permute-done.40 = bf16[256,1280]{1,0:T(8,128)(2,1)} collective-permute-done((bf16[256,1280]{1,0:T(8,128)(2,1)}, bf16[256,1280]{1,0:T(8,128)(2,1)}, u32[]{:S(2)}, u32[]{:S(2)}) %collective-permute-start.40) | collective-permute-done | bytes 655392 | tf_op jit(solution)/shard_map/ppermute | solution.py:242
  456.1 3.9 copy.330
  471.4 13.7 %collective-permute-done.56 = bf16[2,320,640]{2,1,0:T(8,128)(2,1)} collective-permute-done((bf16[2,320,640]{2,1,0:T(8,128)(2,1)}, bf16[2,320,640]{2,1,0:T(8,128)(2,1)}, u32[]{:S(2)}, u32[]{:S(2)}) %collective-permute-start.56) | collective-permute-done | bytes 819232 | tf_op jit(solution)/shard_map/ppermute | solution.py:242
  486.9 4.9 collective-permute-done.55
  492.0 5.3 collective-permute-done.53
  519.4 7.8 %collective-permute-done.65 = bf16[2,216,640]{2,1,0:T(8,128)(2,1)S(1)} collective-permute-done((bf16[2,216,640]{2,1,0:T(8,128)(2,1)S(1)}, bf16[2,216,640]{2,1,0:T(8,128)(2,1)S(1)}, u32[]{:S(2)}, u32[]{:S(2)}) %collective-permute-start.65) | collective-permute-done | bytes 552992 | tf_op jit(solution)/shard_map/ppermute | solution.py:327
  531.1 10.6 %collective-permute-done.66 = bf16[216,640]{1,0:T(8,128)(2,1)S(1)} collective-permute-done((bf16[216,640]{1,0:T(8,128)(2,1)S(1)}, bf16[216,640]{1,0:T(8,128)(2,1)S(1)}, u32[]{:S(2)}, u32[]{:S(2)}) %collective-permute-start.66) | collective-permute-done | bytes 276512 | tf_op jit(solution)/shard_map/ppermute | solution.py:327
  572.6 3.1 collective-permute-done.61
  576.7 3.6 collective-permute-start.62
  582.0 8.2 %collective-permute-done.62 = bf16[80,1408]{1,0:T(8,128)(2,1)S(1)} collective-permute-done((bf16[80,1408]{1,0:T(8,128)(2,1)S(1)}, bf16[80,1408]{1,0:T(8,128)(2,1)S(1)}, u32[]{:S(2)}, u32[]{:S(2)}) %collective-permute-start.62) | collective-permute-done | bytes 225312 | tf_op jit(solution)/shard_map/ppermute | solution.py:327
  595.1 6.7 %collective-permute-done.63 = bf16[2,80,1408]{2,1,0:T(8,128)(2,1)S(1)} collective-permute-done((bf16[2,80,1408]{2,1,0:T(8,128)(2,1)S(1)}, bf16[2,80,1408]{2,1,0:T(8,128)(2,1)S(1)}, u32[]{:S(2)}, u32[]{:S(2)}) %collective-permute-start.63) | collective-permute-done | bytes 450592 | tf_op jit(solution)/shard_map/ppermute | solution.py:327
  602.1 4.2 collective-permute-done.80
  (682 shorter events, 322.8 us)
Async XLA Ops:
  5.5 32.1 %collective-permute-start.2 = (bf16[320,2048]{1,0:T(8,128)(2,1)}, bf16[320,2048]{1,0:T(8,128)(2,1)}, u32[]{:S(2)}, u32[]{:S(2)}) collective-permute-start(bf16[320,2048]{1,0:T(8,128)(2,1)} %fusion.36.refs_0_), channel_id=1, source_target_pairs={{0,16},{16,0},{1,17},{17,1},{2,18},{18,2},{3,19},{19,3},{4,20},{20... | collective-permute-start | bytes 3932168 | tf_op jit(solution)/shard_map/ppermute | solution.py:242
  8.5 32.8 %collective-permute-start.1 = (bf16[320,2048]{1,0:T(8,128)(2,1)}, bf16[320,2048]{1,0:T(8,128)(2,1)}, u32[]{:S(2)}, u32[]{:S(2)}) collective-permute-start(bf16[320,2048]{1,0:T(8,128)(2,1)} %fusion.36.refs_0_), channel_id=1, source_target_pairs={{0,8},{8,0},{1,9},{9,1},{2,10},{10,2},{3,11},{11,3},{4,12},{12,4},... | collective-permute-start | bytes 3932168 | tf_op jit(solution)/shard_map/ppermute | solution.py:242
  45.7 53.4 %collective-permute-start.14 = (bf16[256,1408]{1,0:T(8,128)(2,1)}, bf16[256,1408]{1,0:T(8,128)(2,1)}, u32[]{:S(2)}, u32[]{:S(2)}) collective-permute-start(bf16[256,1408]{1,0:T(8,128)(2,1)} %pad_maximum_fusion.8.refs_4_), channel_id=1, source_target_pairs={{0,1},{1,0},{2,3},{3,2},{4,5},{5,4},{6,7},{7,6},{8,9},{9,8},{10,11... | collective-permute-start | bytes 2162696 | tf_op jit(solution)/shard_map/ppermute | solution.py:242
  45.7 54.4 %collective-permute-start.5 = (bf16[256,1408]{1,0:T(8,128)(2,1)}, bf16[256,1408]{1,0:T(8,128)(2,1)}, u32[]{:S(2)}, u32[]{:S(2)}) collective-permute-start(bf16[256,1408]{1,0:T(8,128)(2,1)} %pad_maximum_fusion.8.refs_4_), channel_id=1, source_target_pairs={{0,4},{2,6},{4,0},{6,2},{1,5},{3,7},{5,1},{7,3},{8,12},{10,14},{12... | collective-permute-start | bytes 2162696 | tf_op jit(solution)/shard_map/ppermute | solution.py:242
  59.3 31.2 %collective-permute-start.7 = (bf16[320,1984]{1,0:T(8,128)(2,1)}, bf16[320,1984]{1,0:T(8,128)(2,1)}, u32[]{:S(2)}, u32[]{:S(2)}) collective-permute-start(bf16[320,1984]{1,0:T(8,128)(2,1)} %concatenate.163.refs_0_), channel_id=1, source_target_pairs={{0,16},{16,0},{1,17},{17,1},{2,18},{18,2},{3,19},{19,3},{4,20},{20... | collective-permute-start | bytes 3809288 | tf_op jit(solution)/shard_map/ppermute | solution.py:242
  60.4 31.9 %collective-permute-start.6 = (bf16[320,1984]{1,0:T(8,128)(2,1)}, bf16[320,1984]{1,0:T(8,128)(2,1)}, u32[]{:S(2)}, u32[]{:S(2)}) collective-permute-start(bf16[320,1984]{1,0:T(8,128)(2,1)} %concatenate.163.refs_0_), channel_id=1, source_target_pairs={{0,8},{8,0},{1,9},{9,1},{2,10},{10,2},{3,11},{11,3},{4,12},{12,4},... | collective-permute-start | bytes 3809288 | tf_op jit(solution)/shard_map/ppermute | solution.py:242
  100.1 29.4 %collective-permute-start.9 = (bf16[256,1408]{1,0:T(8,128)(2,1)}, bf16[256,1408]{1,0:T(8,128)(2,1)}, u32[]{:S(2)}, u32[]{:S(2)}) collective-permute-start(bf16[256,1408]{1,0:T(8,128)(2,1)} %pad_maximum_fusion.8.refs_4_), channel_id=1, source_target_pairs={{0,2},{2,4},{4,6},{6,0},{1,3},{3,5},{5,7},{7,1},{8,10},{10,12},{12... | collective-permute-start | bytes 2162696 | tf_op jit(solution)/shard_map/ppermute | solution.py:242
  146.4 34.8 %collective-permute-start.17 = (bf16[256,1408]{1,0:T(8,128)(2,1)}, bf16[256,1408]{1,0:T(8,128)(2,1)}, u32[]{:S(2)}, u32[]{:S(2)}) collective-permute-start(bf16[256,1408]{1,0:T(8,128)(2,1)} %concatenate.169.refs_0_), channel_id=1, source_target_pairs={{0,4},{2,6},{4,0},{6,2},{1,5},{3,7},{5,1},{7,3},{8,12},{10,14},{12... | collective-permute-start | bytes 2162696 | tf_op jit(solution)/shard_map/ppermute | solution.py:242
  147.6 35.6 %collective-permute-start.15 = (bf16[256,1408]{1,0:T(8,128)(2,1)}, bf16[256,1408]{1,0:T(8,128)(2,1)}, u32[]{:S(2)}, u32[]{:S(2)}) collective-permute-start(bf16[256,1408]{1,0:T(8,128)(2,1)} %collective-permute-done.5.refs_6_), channel_id=1, source_target_pairs={{0,1},{1,0},{2,3},{3,2},{4,5},{5,4},{6,7},{7,6},{8,9},{9,8},{10,11... | collective-permute-start | bytes 2162696 | tf_op jit(solution)/shard_map/ppermute | solution.py:242
  181.2 76.5 %collective-permute-start.30 = (bf16[256,1408]{1,0:T(8,128)(2,1)}, bf16[256,1408]{1,0:T(8,128)(2,1)}, u32[]{:S(2)}, u32[]{:S(2)}) collective-permute-start(bf16[256,1408]{1,0:T(8,128)(2,1)} %concatenate.169.refs_0_), channel_id=1, source_target_pairs={{0,6},{2,0},{4,2},{6,4},{1,7},{3,1},{5,3},{7,5},{8,14},{10,8},{12,... | collective-permute-start | bytes 2162696 | tf_op jit(solution)/shard_map/ppermute | solution.py:242
  182.6 75.9 %collective-permute-start.28 = (bf16[256,1408]{1,0:T(8,128)(2,1)}, bf16[256,1408]{1,0:T(8,128)(2,1)}, u32[]{:S(2)}, u32[]{:S(2)}) collective-permute-start(bf16[256,1408]{1,0:T(8,128)(2,1)} %concatenate.169.refs_0_), channel_id=1, source_target_pairs={{0,2},{2,4},{4,6},{6,0},{1,3},{3,5},{5,7},{7,1},{8,10},{10,12},{12... | collective-permute-start | bytes 2162696 | tf_op jit(solution)/shard_map/ppermute | solution.py:242
  193.1 52.6 %collective-permute-start.26 = (bf16[2,320,448]{2,1,0:T(8,128)(2,1)}, bf16[2,320,448]{2,1,0:T(8,128)(2,1)}, u32[]{:S(2)}, u32[]{:S(2)}) collective-permute-start(bf16[2,320,448]{2,1,0:T(8,128)(2,1)} %dynamic-slice_bitcast_fusion.10), channel_id=1, source_target_pairs={{0,8},{8,0},{1,9},{9,1},{2,10},{10,2},{3,11},{11,3},{4,12},{12,4},... | collective-permute-start | bytes 1720328 | tf_op jit(solution)/shard_map/ppermute | solution.py:242
  194.6 53.6 %collective-permute-start.25 = (bf16[2,320,448]{2,1,0:T(8,128)(2,1)}, bf16[2,320,448]{2,1,0:T(8,128)(2,1)}, u32[]{:S(2)}, u32[]{:S(2)}) collective-permute-start(bf16[2,320,448]{2,1,0:T(8,128)(2,1)} %dynamic-slice_bitcast_fusion.11), channel_id=1, source_target_pairs={{0,16},{16,0},{1,17},{17,1},{2,18},{18,2},{3,19},{19,3},{4,20},{20... | collective-permute-start | bytes 1720328 | tf_op jit(solution)/shard_map/ppermute | solution.py:242
  197.4 47.4 %collective-permute-start.23 = (bf16[256,1408]{1,0:T(8,128)(2,1)}, bf16[256,1408]{1,0:T(8,128)(2,1)}, u32[]{:S(2)}, u32[]{:S(2)}) collective-permute-start(bf16[256,1408]{1,0:T(8,128)(2,1)} %pad_maximum_fusion.8.refs_4_), channel_id=1, source_target_pairs={{0,6},{2,0},{4,2},{6,4},{1,7},{3,1},{5,3},{7,5},{8,14},{10,8},{12,... | collective-permute-start | bytes 2162696 | tf_op jit(solution)/shard_map/ppermute | solution.py:242
  255.5 54.7 %collective-permute-start.35 = (bf16[320,448]{1,0:T(8,128)(2,1)}, bf16[320,448]{1,0:T(8,128)(2,1)}, u32[]{:S(2)}, u32[]{:S(2)}) collective-permute-start(bf16[320,448]{1,0:T(8,128)(2,1)} %dynamic-slice_bitcast_fusion.26), channel_id=1, source_target_pairs={{0,16},{16,0},{1,17},{17,1},{2,18},{18,2},{3,19},{19,3},{4,20},{20... | collective-permute-start | bytes 860168 | tf_op jit(solution)/shard_map/ppermute | solution.py:242
  257.7 53.0 %collective-permute-start.34 = (bf16[320,448]{1,0:T(8,128)(2,1)}, bf16[320,448]{1,0:T(8,128)(2,1)}, u32[]{:S(2)}, u32[]{:S(2)}) collective-permute-start(bf16[320,448]{1,0:T(8,128)(2,1)} %dynamic-slice_bitcast_fusion.27), channel_id=1, source_target_pairs={{0,8},{8,0},{1,9},{9,1},{2,10},{10,2},{3,11},{11,3},{4,12},{12,4},... | collective-permute-start | bytes 860168 | tf_op jit(solution)/shard_map/ppermute | solution.py:242
  263.2 49.7 %collective-permute-start.19 = (bf16[256,2688]{1,0:T(8,128)(2,1)}, bf16[256,2688]{1,0:T(8,128)(2,1)}, u32[]{:S(2)}, u32[]{:S(2)}) collective-permute-start(bf16[256,2688]{1,0:T(8,128)(2,1)} %fusion.32), channel_id=1, source_target_pairs={{0,1},{1,0},{2,3},{3,2},{4,5},{5,4},{6,7},{7,6},{8,9},{9,8},{10,11... | collective-permute-start | bytes 4128776 | tf_op jit(solution)/shard_map/ppermute | solution.py:242
  266.1 52.3 %collective-permute-start.21 = (bf16[256,1408]{1,0:T(8,128)(2,1)}, bf16[256,1408]{1,0:T(8,128)(2,1)}, u32[]{:S(2)}, u32[]{:S(2)}) collective-permute-start(bf16[256,1408]{1,0:T(8,128)(2,1)} %add_convert_fusion.2), channel_id=1, source_target_pairs={{0,4},{2,6},{4,0},{6,2},{1,5},{3,7},{5,1},{7,3},{8,12},{10,14},{12... | collective-permute-start | bytes 2162696 | tf_op jit(solution)/shard_map/ppermute | solution.py:242
  322.9 50.6 %collective-permute-start.37 = (bf16[256,1408]{1,0:T(8,128)(2,1)S(1)}, bf16[256,1408]{1,0:T(8,128)(2,1)S(1)}, u32[]{:S(2)}, u32[]{:S(2)}) collective-permute-start(bf16[256,1408]{1,0:T(8,128)(2,1)S(1)} %add_convert_fusion), channel_id=1, source_target_pairs={{0,2},{2,4},{4,6},{6,0},{1,3},{3,5},{5,7},{7,1},{8,10},{10,12},{12... | collective-permute-start | bytes 2162696 | tf_op jit(solution)/shard_map/ppermute | solution.py:242
  323.5 50.1 %collective-permute-start.36 = (bf16[256,1408]{1,0:T(8,128)(2,1)S(1)}, bf16[256,1408]{1,0:T(8,128)(2,1)S(1)}, u32[]{:S(2)}, u32[]{:S(2)}) collective-permute-start(bf16[256,1408]{1,0:T(8,128)(2,1)S(1)} %add_convert_fusion.1), channel_id=1, source_target_pairs={{0,6},{2,0},{4,2},{6,4},{1,7},{3,1},{5,3},{7,5},{8,14},{10,8},{12,... | collective-permute-start | bytes 2162696 | tf_op jit(solution)/shard_map/ppermute | solution.py:242
  380.8 36.4 %collective-permute-start.40 = (bf16[256,1280]{1,0:T(8,128)(2,1)}, bf16[256,1280]{1,0:T(8,128)(2,1)}, u32[]{:S(2)}, u32[]{:S(2)}) collective-permute-start(bf16[256,1280]{1,0:T(8,128)(2,1)} %add_convert_fusion.5), channel_id=1, source_target_pairs={{0,4},{2,6},{4,0},{6,2},{1,5},{3,7},{5,1},{7,3},{8,12},{10,14},{12... | collective-permute-start | bytes 1966088 | tf_op jit(solution)/shard_map/ppermute | solution.py:242
  384.5 37.7 %collective-permute-start.44 = (bf16[2,320,896]{2,1,0:T(8,128)(2,1)}, bf16[2,320,896]{2,1,0:T(8,128)(2,1)}, u32[]{:S(2)}, u32[]{:S(2)}) collective-permute-start(bf16[2,320,896]{2,1,0:T(8,128)(2,1)} %dynamic-slice_bitcast_fusion.2), channel_id=1, source_target_pairs={{0,8},{8,0},{1,9},{9,1},{2,10},{10,2},{3,11},{11,3},{4,12},{12,4},... | collective-permute-start | bytes 3440648 | tf_op jit(solution)/shard_map/ppermute | solution.py:242
  389.3 36.4 %collective-permute-start.43 = (bf16[2,320,896]{2,1,0:T(8,128)(2,1)}, bf16[2,320,896]{2,1,0:T(8,128)(2,1)}, u32[]{:S(2)}, u32[]{:S(2)}) collective-permute-start(bf16[2,320,896]{2,1,0:T(8,128)(2,1)} %dynamic-slice_bitcast_fusion.3), channel_id=1, source_target_pairs={{0,16},{16,0},{1,17},{17,1},{2,18},{18,2},{3,19},{19,3},{4,20},{20... | collective-permute-start | bytes 3440648 | tf_op jit(solution)/shard_map/ppermute | solution.py:242
  400.0 47.1 %collective-permute-start.71 = (bf16[160,448]{1,0:T(8,128)(2,1)S(1)}, bf16[160,448]{1,0:T(8,128)(2,1)S(1)}, u32[]{:S(2)}, u32[]{:S(2)}) collective-permute-start(bf16[160,448]{1,0:T(8,128)(2,1)S(1)} %dynamic-slice_bitcast_fusion.31), channel_id=1, source_target_pairs={{0,4},{2,6},{4,0},{6,2},{1,5},{3,7},{5,1},{7,3},{8,12},{10,14},{12... | collective-permute-start | bytes 430088 | tf_op jit(solution)/shard_map/ppermute | solution.py:327
  404.0 39.5 %collective-permute-start.51 = (bf16[224,640]{1,0:T(8,128)(2,1)S(1)}, bf16[224,640]{1,0:T(8,128)(2,1)S(1)}, u32[]{:S(2)}, u32[]{:S(2)}) collective-permute-start(bf16[224,640]{1,0:T(8,128)(2,1)S(1)} %dynamic-slice_bitcast_fusion.28), channel_id=1, source_target_pairs={{0,8},{8,0},{1,9},{9,1},{2,10},{10,2},{3,11},{11,3},{4,12},{12,4},... | collective-permute-start | bytes 860168 | tf_op jit(solution)/shard_map/ppermute | solution.py:242
  447.8 49.6 %collective-permute-start.72 = (bf16[160,448]{1,0:T(8,128)(2,1)}, bf16[160,448]{1,0:T(8,128)(2,1)}, u32[]{:S(2)}, u32[]{:S(2)}) collective-permute-start(bf16[160,448]{1,0:T(8,128)(2,1)} %fusion.99), channel_id=1, source_target_pairs={{0,4},{2,6},{4,0},{6,2},{1,5},{3,7},{5,1},{7,3},{8,12},{10,14},{12... | collective-permute-start | bytes 430088 | tf_op jit(solution)/shard_map/ppermute | solution.py:327
  449.5 48.9 %collective-permute-start.47 = (bf16[256,1280]{1,0:T(8,128)(2,1)}, bf16[256,1280]{1,0:T(8,128)(2,1)}, u32[]{:S(2)}, u32[]{:S(2)}) collective-permute-start(bf16[256,1280]{1,0:T(8,128)(2,1)} %add_convert_fusion.3), channel_id=1, source_target_pairs={{0,2},{2,4},{4,6},{6,0},{1,3},{3,5},{5,7},{7,1},{8,10},{10,12},{12... | collective-permute-start | bytes 1966088 | tf_op jit(solution)/shard_map/ppermute | solution.py:242
  452.2 32.9 %collective-permute-start.56 = (bf16[2,320,640]{2,1,0:T(8,128)(2,1)}, bf16[2,320,640]{2,1,0:T(8,128)(2,1)}, u32[]{:S(2)}, u32[]{:S(2)}) collective-permute-start(bf16[2,320,640]{2,1,0:T(8,128)(2,1)} %dynamic-slice_bitcast_fusion.7), channel_id=1, source_target_pairs={{0,16},{16,0},{1,17},{17,1},{2,18},{18,2},{3,19},{19,3},{4,20},{20... | collective-permute-start | bytes 2457608 | tf_op jit(solution)/shard_map/ppermute | solution.py:242
  464.2 47.5 %collective-permute-start.57 = (bf16[2,320,768]{2,1,0:T(8,128)(2,1)}, bf16[2,320,768]{2,1,0:T(8,128)(2,1)}, u32[]{:S(2)}, u32[]{:S(2)}) collective-permute-start(bf16[2,320,768]{2,1,0:T(8,128)(2,1)} %dynamic-slice_bitcast_fusion.6), channel_id=1, source_target_pairs={{0,8},{8,0},{1,9},{9,1},{2,10},{10,2},{3,11},{11,3},{4,12},{12,4},... | collective-permute-start | bytes 2949128 | tf_op jit(solution)/shard_map/ppermute | solution.py:242
  552.3 38.1 %collective-permute-start.79 = (bf16[2,224,1280]{2,1,0:T(8,128)(2,1)}, bf16[2,224,1280]{2,1,0:T(8,128)(2,1)}, u32[]{:S(2)}, u32[]{:S(2)}) collective-permute-start(bf16[2,224,1280]{2,1,0:T(8,128)(2,1)} %dynamic-slice_bitcast_fusion), channel_id=1, source_target_pairs={{0,8},{8,0},{1,9},{9,1},{2,10},{10,2},{3,11},{11,3},{4,12},{12,4},... | collective-permute-start | bytes 3440648 | tf_op jit(solution)/shard_map/ppermute | solution.py:242
  553.6 39.8 %collective-permute-start.77 = (bf16[2,224,1280]{2,1,0:T(8,128)(2,1)}, bf16[2,224,1280]{2,1,0:T(8,128)(2,1)}, u32[]{:S(2)}, u32[]{:S(2)}) collective-permute-start(bf16[2,224,1280]{2,1,0:T(8,128)(2,1)} %dynamic-slice_bitcast_fusion.1), channel_id=1, source_target_pairs={{0,16},{16,0},{1,17},{17,1},{2,18},{18,2},{3,19},{19,3},{4,20},{20... | collective-permute-start | bytes 3440648 | tf_op jit(solution)/shard_map/ppermute | solution.py:242
  581.8 29.3 %collective-permute-start.69 = (bf16[864,640]{1,0:T(8,128)(2,1)S(1)}, bf16[864,640]{1,0:T(8,128)(2,1)S(1)}, u32[]{:S(2)}, u32[]{:S(2)}) collective-permute-start(bf16[864,640]{1,0:T(8,128)(2,1)S(1)} %bitcast.421), channel_id=1, source_target_pairs={{0,1},{1,0},{2,3},{3,2},{4,5},{5,4},{6,7},{7,6},{8,9},{9,8},{10,11... | collective-permute-start | bytes 3317768 | tf_op jit(solution)/shard_map/ppermute | solution.py:242
  (174 other events, 1744.9 us)

commit v9 on v7

--- a/solution.py
+++ b/solution.py
@@ -591,15 +591,14 @@
     up_one = stage_one(blocks[1], both, gate_one, (value_grad,))
     down_one = stage_one(down_part, both[:1], gate_one, (value_grad,))
     moving = after(summed(mines[0], others[0], to_out), back)
-    arrived = [after(shifted(moving, "z", -levels[1]), value_grad)]
-    context_late = after(context_grad, *up_one, *arrived, *down_one)
+    context_late = after(context_grad, *up_one, *down_one)
     value_wgrad = product(attn_in.T, value_grad).astype(BF)
     early = [shares(output_grad), shares(value_wgrad)]
-    early_one = stage_one(early, both, up_one)
     probs_grad_att = mm("sqhd,skhd->shqk", context_late, values)
     row_delta = jnp.sum(attn_probs * probs_grad_att, axis=-1, keepdims=True)
     scores_grad = (attn_probs * (probs_grad_att - row_delta)).astype(BF)
-    scores_grad = after(scores_grad, *early)
+    arrived = [after(shifted(moving, "z", -levels[1]), scores_grad)]
+    scores_grad = after(scores_grad, *early, *arrived)
     query_grad = mm("shqk,skhd->sqhd", scores_grad, key_rot) * score_scale
     key_grad = mm("shqk,sqhd->skhd", scores_grad, query_rot) * score_scale
     query_pre_grad = flat(rotate(query_grad, cosine, -sine_part).astype(BF))
@@ -613,7 +612,7 @@
     ).reshape(2, length, width)
     gate_two = stage_two(gate_one, both, up_one, (query_wgrad,))
     shared_down = stage_two(down_one, both[:1], late=(query_wgrad,))
-    attn_in_grad = after(in_partial[0], *early_one, *gate_two, *shared_down) + swap(in_partial[1].astype(BF)).astype(F32)
+    attn_in_grad = after(in_partial[0], *gate_two, *shared_down) + swap(in_partial[1].astype(BF)).astype(F32)
     token_mine, norm_mine = token_f[0], norm_one[0]
     attn_gain_terms = attn_in_grad * token_mine * norm_mine
     upstream_one = attn_in_grad * gain_one_f
@@ -631,12 +630,13 @@
     ).astype(BF)
 
     done_wgrads = (query_wgrad, key_wgrad)
+    early_one = stage_one(early, both, up_one, (small_grads,))
     early_two = stage_two(early_one, both)
     late = [shares(query_wgrad), shares(jnp.concatenate([key_wgrad, small_grads], axis=1))]
     late_one = stage_one(late, both)
     late_two = stage_two(late_one, both, early_two)
-    up_two = stage_two(up_one, both, late_two)
-    down_two = stage_two(stage_one(blocks[2], both, late_two), both)
+    up_two = stage_two(up_one, both, late_one)
+    down_two = stage_two(stage_one(blocks[2], both, up_two), both)
     expert_shares = [jnp.stack(pair).astype(F32) for pair in (gate_two, up_two, down_two)]
     shared_share = reduce_level(after(jnp.concatenate(shared_two, axis=0), back), ((value_grad,), done_wgrads, early_two, late_one))
     shared_share = after(shared_share, *late_two)
@@ -644,9 +644,9 @@
     late_share = reduce_level(jnp.concatenate(late_two, axis=1))
 
     for i in range(1, depth - 1):
-        moving = after(summed(mines[i], others[i], to_out), *early_one, arrived[-1])
+        moving = after(summed(mines[i], others[i], to_out), arrived[-1])
         piece = shifted(moving, "z", -levels[i + 1])
-        arrived.append(after(piece, *(late_one if i < depth - 2 else late_two)))
+        arrived.append(after(piece, *((small_grads,) if i < depth - 2 else early_two)))
     moe_out = own_chip[:, wider:]
     for piece in arrived:
         moe_out += piece.astype(F32)

time: 633 us -> 620 us (0.979)
  waiting for transfers between devices: 170 us -> 126 us
  starting transfers between devices: 66.3 us -> 76.3 us
  Pallas kernels: 79.4 us -> 89.3 us
  other arithmetic: 109 us -> 117 us
    ppermute x12, waiting for transfers between devices: 70.3 us -> 30.7 us  [crossed(): return lax.ppermute(value, 'z', [(i, i ^ bit) for i in range(depth)])]
    pallas_call x2, Pallas kernels: 69.1 us -> 78.9 us  [expert_call(): pl.pallas_call(functools.partial(expert_kernel, count, width, capacity, e...]
    ppermute x12, starting transfers between devices: 6.54 us -> 14 us  [crossed(): return lax.ppermute(value, 'z', [(i, i ^ bit) for i in range(depth)])]
    convert_element_type x22 -> x24, other arithmetic: 23 us -> 26.8 us  [ring_reduce(): (other.astype(F32) + pick(value, index - step, at).astype(F32)).astype(BF)]
    unnamed x254 -> x258, local copies, waits for them, and re-layouts: 15.7 us -> 17.9 us
  transfers between devices with their start and end apart: 81 -> 81, of which waited for: 20 -> 22; matrix products, arithmetic and copies ran while one was open for 43% -> 45% of each run, Pallas kernels for 13% -> 15%
where the time goes in v9:
time: 620 us; the launch traced here: 608 us
  waiting for transfers between devices  126 us (20%)
  other arithmetic  117 us (19%)
  local copies, waits for them, and re-layouts  110 us (18%)
  Pallas kernels  89.3 us (14%)
  matrix products  83.2 us (13%)
  starting transfers between devices  76.3 us (12%)
  between operations  6.41 us (1%)
    ppermute x69, waiting for transfers between devices, shifted(): lax.ppermute(value, axis, [(i, (i + by) % size) for i in range(size)])  95.4 us
    pallas_call x2, Pallas kernels, expert_call(): pl.pallas_call(functools.partial(expert_kernel, count, width, capacity, e...  78.9 us
    ppermute x69, starting transfers between devices, shifted(): lax.ppermute(value, axis, [(i, (i + by) % size) for i in range(size)])  62.3 us
    dot_general x22, matrix products, product(): return jnp.dot(first_arg, second_arg, preferred_element_type=F32)  45.3 us
    ppermute x12, waiting for transfers between devices, crossed(): return lax.ppermute(value, 'z', [(i, i ^ bit) for i in range(depth)])  30.7 us
    dot_general x10, matrix products, mm(): return jnp.einsum(spec, first_arg, second_arg, preferred_element_type=F32)  29.9 us
    convert_element_type x24, other arithmetic, ring_reduce(): (other.astype(F32) + pick(value, index - step, at).astype(F32)).astype(BF)  26.8 us
    unnamed x258, local copies, waits for them, and re-layouts  17.9 us
  transfers between devices with their start and end apart: 81, of which 22 were waited for; matrix products, arithmetic and copies ran while one was open for 45% of the time, Pallas kernels for 15%

profile of v9, /device:TPU:0, one launch (start us, length us, event | category | flops | bytes accessed | tf_op | source)
XLA Modules:
  0.0 608.5 jit_solution(5335251574891995965)
XLA Ops:
  20.1 17.4 %collective-permute-done.2.refs_2_ = bf16[320,2048]{1,0:T(8,128)(2,1)} collective-permute-done((bf16[320,2048]{1,0:T(8,128)(2,1)}, bf16[320,2048]{1,0:T(8,128)(2,1)}, u32[]{:S(2)}, u32[]{:S(2)}) %collective-permute-start.2) | collective-permute-done | bytes 1310752 | tf_op jit(solution)/shard_map/ppermute | solution.py:242
  55.8 3.5 concatenate.163.refs_0_
  61.0 5.2 place.2
  67.7 4.0 slice_bitcast_fusion.1
  73.2 3.5 copy.287
  76.7 3.9 fusion.45
  80.6 3.5 copy.288
  101.7 6.1 %collective-permute-done.11.refs_4_ = bf16[160,1984]{1,0:T(8,128)(2,1)} collective-permute-done((bf16[160,1984]{1,0:T(8,128)(2,1)S(1)}, bf16[160,1984]{1,0:T(8,128)(2,1)}, u32[]{:S(2)}, u32[]{:S(2)}) %collective-permute-start.11) | collective-permute-done | bytes 634912 | tf_op jit(solution)/shard_map/ppermute | solution.py:242
  109.3 5.2 place.3
  152.4 3.9 multiply_convert_fusion.3
  166.8 3.3 fusion.3
  170.1 11.1 %collective-permute-done.17.refs_2_ = bf16[256,1408]{1,0:T(8,128)(2,1)} collective-permute-done((bf16[256,1408]{1,0:T(8,128)(2,1)}, bf16[256,1408]{1,0:T(8,128)(2,1)}, u32[]{:S(2)}, u32[]{:S(2)}) %collective-permute-start.17) | collective-permute-done | bytes 720928 | tf_op jit(solution)/shard_map/ppermute | solution.py:242
  200.4 44.3 %experts.2 = (bf16[256,2688]{1,0:T(8,128)(2,1)}, bf16[256,2688]{1,0:T(8,128)(2,1)}, bf16[256,2688]{1,0:T(8,128)(2,1)}, bf16[256,2688]{1,0:T(8,128)(2,1)}, bf16[2...) custom-call(s32[1]{0:T(128)} %bitcast.20.me_ref, ...), custom_call_target="tpu_custom_call" | custom-call | flops 16441671680 | bytes 62914560 | tf_op jit(solution)/shard_map/experts/pallas_call | solution.py:133
  266.0 34.6 %experts.3 = (bf16[256,2688]{1,0:T(8,128)(2,1)}, bf16[256,2688]{1,0:T(8,128)(2,1)}, bf16[256,2688]{1,0:T(8,128)(2,1)}, bf16[256,2688]{1,0:T(8,128)(2,1)}, bf16[2...) custom-call(s32[1]{0:T(128)} %bitcast.20.me_ref, ...), custom_call_target="tpu_custom_call", output_to_operand_aliasing={{4}: (13, {}), {5}: (14, {}), {6}: (15, {}), {7}: (16, {}),... | custom-call | flops 16441671680 | bytes 62914560 | tf_op jit(solution)/shard_map/experts/pallas_call | solution.py:133
  300.8 9.3 %convolution_convert_fusion.2 = bf16[2,1280,896]{2,1,0:T(8,128)(2,1)S(1)} fusion(bf16[2,1024,1280]{2,1,0:T(8,128)(2,1)} %get-tuple-element.128, bf16[2,1024,896]{2,1,0:T(8,128)(2,1)} %get-tuple-element.134), kind=kOutput, calls=%fused_computation.4 | convolution fusion | flops 4699914240 | bytes 13500416 | tf_op jit(solution)/shard_map/erd,erf->edf/dot_general | solution.py:196
  314.7 3.2 add_convert_fusion.5
  325.2 8.5 %convolution_convert_fusion.1 = bf16[2,1280,896]{2,1,0:T(8,128)(2,1)S(1)} fusion(bf16[2,1024,1280]{2,1,0:T(8,128)(2,1)} %get-tuple-element.128, bf16[2,1024,896]{2,1,0:T(8,128)(2,1)S(1)} %copy-done.122), kind=kOutput, calls=%fused_computation.3 | convolution fusion | flops 4699914240 | bytes 13500416 | tf_op jit(solution)/shard_map/erd,erf->edf/dot_general | solution.py:196
  333.8 8.6 %convolution_convert_fusion = bf16[2,896,1280]{2,1,0:T(8,128)(2,1)S(1)} fusion(bf16[2,1024,896]{2,1,0:T(8,128)(2,1)} %get-tuple-element.142, bf16[2,1024,1280]{2,1,0:T(8,128)(2,1)} %get-tuple-element.143), kind=kOutput, calls=%fused_computation.2 | convolution fusion | flops 4699914240 | bytes 13500416 | tf_op jit(solution)/shard_map/erf,erd->efd/dot_general | solution.py:196
  351.6 20.5 %collective-permute-done.38 = bf16[2,320,896]{2,1,0:T(8,128)(2,1)S(1)} collective-permute-done((bf16[2,320,896]{2,1,0:T(8,128)(2,1)S(1)}, bf16[2,320,896]{2,1,0:T(8,128)(2,1)S(1)}, u32[]{:S(2)}, u32[]{:S(2)}) %collective-permute-start.38) | collective-permute-done | bytes 1146912 | tf_op jit(solution)/shard_map/ppermute | solution.py:242
  410.3 4.5 collective-permute-done.43
  452.4 4.0 copy.330
  467.3 13.6 %collective-permute-done.56 = bf16[2,320,640]{2,1,0:T(8,128)(2,1)} collective-permute-done((bf16[2,320,640]{2,1,0:T(8,128)(2,1)}, bf16[2,320,640]{2,1,0:T(8,128)(2,1)}, u32[]{:S(2)}, u32[]{:S(2)}) %collective-permute-start.56) | collective-permute-done | bytes 819232 | tf_op jit(solution)/shard_map/ppermute | solution.py:242
  483.6 3.3 collective-permute-done.55
  487.0 7.4 %collective-permute-done.53 = bf16[320,640]{1,0:T(8,128)(2,1)S(1)} collective-permute-done((bf16[320,640]{1,0:T(8,128)(2,1)S(1)}, bf16[320,640]{1,0:T(8,128)(2,1)S(1)}, u32[]{:S(2)}, u32[]{:S(2)}) %collective-permute-start.53) | collective-permute-done | bytes 409632 | tf_op jit(solution)/shard_map/ppermute | solution.py:242
  513.6 4.0 collective-permute-done.65
  523.9 8.8 %collective-permute-done.66 = bf16[216,640]{1,0:T(8,128)(2,1)S(1)} collective-permute-done((bf16[216,640]{1,0:T(8,128)(2,1)S(1)}, bf16[216,640]{1,0:T(8,128)(2,1)S(1)}, u32[]{:S(2)}, u32[]{:S(2)}) %collective-permute-start.66) | collective-permute-done | bytes 276512 | tf_op jit(solution)/shard_map/ppermute | solution.py:327
  534.2 3.4 collective-permute-start.60
  564.1 3.1 collective-permute-done.61
  568.2 3.6 collective-permute-start.62
  573.4 7.4 %collective-permute-done.62 = bf16[80,1408]{1,0:T(8,128)(2,1)S(1)} collective-permute-done((bf16[80,1408]{1,0:T(8,128)(2,1)S(1)}, bf16[80,1408]{1,0:T(8,128)(2,1)S(1)}, u32[]{:S(2)}, u32[]{:S(2)}) %collective-permute-start.62) | collective-permute-done | bytes 225312 | tf_op jit(solution)/shard_map/ppermute | solution.py:327
  586.1 6.0 collective-permute-done.63
  592.5 4.0 collective-permute-done.80
  (685 shorter events, 329.3 us)
Async XLA Ops:
  5.5 32.1 %collective-permute-start.2 = (bf16[320,2048]{1,0:T(8,128)(2,1)}, bf16[320,2048]{1,0:T(8,128)(2,1)}, u32[]{:S(2)}, u32[]{:S(2)}) collective-permute-start(bf16[320,2048]{1,0:T(8,128)(2,1)} %fusion.38.refs_0_), channel_id=1, source_target_pairs={{0,16},{16,0},{1,17},{17,1},{2,18},{18,2},{3,19},{19,3},{4,20},{20... | collective-permute-start | bytes 3932168 | tf_op jit(solution)/shard_map/ppermute | solution.py:242
  8.5 32.8 %collective-permute-start.1 = (bf16[320,2048]{1,0:T(8,128)(2,1)}, bf16[320,2048]{1,0:T(8,128)(2,1)}, u32[]{:S(2)}, u32[]{:S(2)}) collective-permute-start(bf16[320,2048]{1,0:T(8,128)(2,1)} %fusion.38.refs_0_), channel_id=1, source_target_pairs={{0,8},{8,0},{1,9},{9,1},{2,10},{10,2},{3,11},{11,3},{4,12},{12,4},... | collective-permute-start | bytes 3932168 | tf_op jit(solution)/shard_map/ppermute | solution.py:242
  45.7 53.4 %collective-permute-start.14 = (bf16[256,1408]{1,0:T(8,128)(2,1)}, bf16[256,1408]{1,0:T(8,128)(2,1)}, u32[]{:S(2)}, u32[]{:S(2)}) collective-permute-start(bf16[256,1408]{1,0:T(8,128)(2,1)} %pad_maximum_fusion.8.refs_4_), channel_id=1, source_target_pairs={{0,1},{1,0},{2,3},{3,2},{4,5},{5,4},{6,7},{7,6},{8,9},{9,8},{10,11... | collective-permute-start | bytes 2162696 | tf_op jit(solution)/shard_map/ppermute | solution.py:242
  45.7 54.4 %collective-permute-start.5 = (bf16[256,1408]{1,0:T(8,128)(2,1)}, bf16[256,1408]{1,0:T(8,128)(2,1)}, u32[]{:S(2)}, u32[]{:S(2)}) collective-permute-start(bf16[256,1408]{1,0:T(8,128)(2,1)} %pad_maximum_fusion.8.refs_4_), channel_id=1, source_target_pairs={{0,4},{2,6},{4,0},{6,2},{1,5},{3,7},{5,1},{7,3},{8,12},{10,14},{12... | collective-permute-start | bytes 2162696 | tf_op jit(solution)/shard_map/ppermute | solution.py:242
  59.3 31.2 %collective-permute-start.7 = (bf16[320,1984]{1,0:T(8,128)(2,1)}, bf16[320,1984]{1,0:T(8,128)(2,1)}, u32[]{:S(2)}, u32[]{:S(2)}) collective-permute-start(bf16[320,1984]{1,0:T(8,128)(2,1)} %concatenate.163.refs_0_), channel_id=1, source_target_pairs={{0,16},{16,0},{1,17},{17,1},{2,18},{18,2},{3,19},{19,3},{4,20},{20... | collective-permute-start | bytes 3809288 | tf_op jit(solution)/shard_map/ppermute | solution.py:242
  60.4 31.9 %collective-permute-start.6 = (bf16[320,1984]{1,0:T(8,128)(2,1)}, bf16[320,1984]{1,0:T(8,128)(2,1)}, u32[]{:S(2)}, u32[]{:S(2)}) collective-permute-start(bf16[320,1984]{1,0:T(8,128)(2,1)} %concatenate.163.refs_0_), channel_id=1, source_target_pairs={{0,8},{8,0},{1,9},{9,1},{2,10},{10,2},{3,11},{11,3},{4,12},{12,4},... | collective-permute-start | bytes 3809288 | tf_op jit(solution)/shard_map/ppermute | solution.py:242
  100.1 29.4 %collective-permute-start.9 = (bf16[256,1408]{1,0:T(8,128)(2,1)}, bf16[256,1408]{1,0:T(8,128)(2,1)}, u32[]{:S(2)}, u32[]{:S(2)}) collective-permute-start(bf16[256,1408]{1,0:T(8,128)(2,1)} %pad_maximum_fusion.8.refs_4_), channel_id=1, source_target_pairs={{0,2},{2,4},{4,6},{6,0},{1,3},{3,5},{5,7},{7,1},{8,10},{10,12},{12... | collective-permute-start | bytes 2162696 | tf_op jit(solution)/shard_map/ppermute | solution.py:242
  146.4 34.8 %collective-permute-start.17 = (bf16[256,1408]{1,0:T(8,128)(2,1)}, bf16[256,1408]{1,0:T(8,128)(2,1)}, u32[]{:S(2)}, u32[]{:S(2)}) collective-permute-start(bf16[256,1408]{1,0:T(8,128)(2,1)} %concatenate.169.refs_0_), channel_id=1, source_target_pairs={{0,4},{2,6},{4,0},{6,2},{1,5},{3,7},{5,1},{7,3},{8,12},{10,14},{12... | collective-permute-start | bytes 2162696 | tf_op jit(solution)/shard_map/ppermute | solution.py:242
  147.6 35.6 %collective-permute-start.15 = (bf16[256,1408]{1,0:T(8,128)(2,1)}, bf16[256,1408]{1,0:T(8,128)(2,1)}, u32[]{:S(2)}, u32[]{:S(2)}) collective-permute-start(bf16[256,1408]{1,0:T(8,128)(2,1)} %collective-permute-done.5.refs_6_), channel_id=1, source_target_pairs={{0,1},{1,0},{2,3},{3,2},{4,5},{5,4},{6,7},{7,6},{8,9},{9,8},{10,11... | collective-permute-start | bytes 2162696 | tf_op jit(solution)/shard_map/ppermute | solution.py:242
  181.2 76.5 %collective-permute-start.30 = (bf16[256,1408]{1,0:T(8,128)(2,1)}, bf16[256,1408]{1,0:T(8,128)(2,1)}, u32[]{:S(2)}, u32[]{:S(2)}) collective-permute-start(bf16[256,1408]{1,0:T(8,128)(2,1)} %concatenate.169.refs_0_), channel_id=1, source_target_pairs={{0,6},{2,0},{4,2},{6,4},{1,7},{3,1},{5,3},{7,5},{8,14},{10,8},{12,... | collective-permute-start | bytes 2162696 | tf_op jit(solution)/shard_map/ppermute | solution.py:242
  182.6 75.9 %collective-permute-start.28 = (bf16[256,1408]{1,0:T(8,128)(2,1)}, bf16[256,1408]{1,0:T(8,128)(2,1)}, u32[]{:S(2)}, u32[]{:S(2)}) collective-permute-start(bf16[256,1408]{1,0:T(8,128)(2,1)} %concatenate.169.refs_0_), channel_id=1, source_target_pairs={{0,2},{2,4},{4,6},{6,0},{1,3},{3,5},{5,7},{7,1},{8,10},{10,12},{12... | collective-permute-start | bytes 2162696 | tf_op jit(solution)/shard_map/ppermute | solution.py:242
  193.1 52.6 %collective-permute-start.26 = (bf16[2,320,448]{2,1,0:T(8,128)(2,1)}, bf16[2,320,448]{2,1,0:T(8,128)(2,1)}, u32[]{:S(2)}, u32[]{:S(2)}) collective-permute-start(bf16[2,320,448]{2,1,0:T(8,128)(2,1)} %dynamic-slice_bitcast_fusion.10), channel_id=1, source_target_pairs={{0,8},{8,0},{1,9},{9,1},{2,10},{10,2},{3,11},{11,3},{4,12},{12,4},... | collective-permute-start | bytes 1720328 | tf_op jit(solution)/shard_map/ppermute | solution.py:242
  194.5 53.7 %collective-permute-start.25 = (bf16[2,320,448]{2,1,0:T(8,128)(2,1)}, bf16[2,320,448]{2,1,0:T(8,128)(2,1)}, u32[]{:S(2)}, u32[]{:S(2)}) collective-permute-start(bf16[2,320,448]{2,1,0:T(8,128)(2,1)} %dynamic-slice_bitcast_fusion.11), channel_id=1, source_target_pairs={{0,16},{16,0},{1,17},{17,1},{2,18},{18,2},{3,19},{19,3},{4,20},{20... | collective-permute-start | bytes 1720328 | tf_op jit(solution)/shard_map/ppermute | solution.py:242
  197.4 47.4 %collective-permute-start.23 = (bf16[256,1408]{1,0:T(8,128)(2,1)}, bf16[256,1408]{1,0:T(8,128)(2,1)}, u32[]{:S(2)}, u32[]{:S(2)}) collective-permute-start(bf16[256,1408]{1,0:T(8,128)(2,1)} %pad_maximum_fusion.8.refs_4_), channel_id=1, source_target_pairs={{0,6},{2,0},{4,2},{6,4},{1,7},{3,1},{5,3},{7,5},{8,14},{10,8},{12,... | collective-permute-start | bytes 2162696 | tf_op jit(solution)/shard_map/ppermute | solution.py:242
  255.4 54.7 %collective-permute-start.35 = (bf16[320,448]{1,0:T(8,128)(2,1)}, bf16[320,448]{1,0:T(8,128)(2,1)}, u32[]{:S(2)}, u32[]{:S(2)}) collective-permute-start(bf16[320,448]{1,0:T(8,128)(2,1)} %dynamic-slice_bitcast_fusion.26), channel_id=1, source_target_pairs={{0,16},{16,0},{1,17},{17,1},{2,18},{18,2},{3,19},{19,3},{4,20},{20... | collective-permute-start | bytes 860168 | tf_op jit(solution)/shard_map/ppermute | solution.py:242
  257.6 53.0 %collective-permute-start.34 = (bf16[320,448]{1,0:T(8,128)(2,1)}, bf16[320,448]{1,0:T(8,128)(2,1)}, u32[]{:S(2)}, u32[]{:S(2)}) collective-permute-start(bf16[320,448]{1,0:T(8,128)(2,1)} %dynamic-slice_bitcast_fusion.27), channel_id=1, source_target_pairs={{0,8},{8,0},{1,9},{9,1},{2,10},{10,2},{3,11},{11,3},{4,12},{12,4},... | collective-permute-start | bytes 860168 | tf_op jit(solution)/shard_map/ppermute | solution.py:242
  263.2 49.6 %collective-permute-start.19 = (bf16[256,2688]{1,0:T(8,128)(2,1)}, bf16[256,2688]{1,0:T(8,128)(2,1)}, u32[]{:S(2)}, u32[]{:S(2)}) collective-permute-start(bf16[256,2688]{1,0:T(8,128)(2,1)} %fusion.34), channel_id=1, source_target_pairs={{0,1},{1,0},{2,3},{3,2},{4,5},{5,4},{6,7},{7,6},{8,9},{9,8},{10,11... | collective-permute-start | bytes 4128776 | tf_op jit(solution)/shard_map/ppermute | solution.py:242
  266.0 52.3 %collective-permute-start.21 = (bf16[256,1408]{1,0:T(8,128)(2,1)}, bf16[256,1408]{1,0:T(8,128)(2,1)}, u32[]{:S(2)}, u32[]{:S(2)}) collective-permute-start(bf16[256,1408]{1,0:T(8,128)(2,1)} %add_convert_fusion.2), channel_id=1, source_target_pairs={{0,4},{2,6},{4,0},{6,2},{1,5},{3,7},{5,1},{7,3},{8,12},{10,14},{12... | collective-permute-start | bytes 2162696 | tf_op jit(solution)/shard_map/ppermute | solution.py:242
  320.3 54.3 %collective-permute-start.37 = (bf16[256,1408]{1,0:T(8,128)(2,1)}, bf16[256,1408]{1,0:T(8,128)(2,1)}, u32[]{:S(2)}, u32[]{:S(2)}) collective-permute-start(bf16[256,1408]{1,0:T(8,128)(2,1)} %add_convert_fusion), channel_id=1, source_target_pairs={{0,2},{2,4},{4,6},{6,0},{1,3},{3,5},{5,7},{7,1},{8,10},{10,12},{12... | collective-permute-start | bytes 2162696 | tf_op jit(solution)/shard_map/ppermute | solution.py:242
  322.2 52.5 %collective-permute-start.36 = (bf16[256,1408]{1,0:T(8,128)(2,1)}, bf16[256,1408]{1,0:T(8,128)(2,1)}, u32[]{:S(2)}, u32[]{:S(2)}) collective-permute-start(bf16[256,1408]{1,0:T(8,128)(2,1)} %add_convert_fusion.1), channel_id=1, source_target_pairs={{0,6},{2,0},{4,2},{6,4},{1,7},{3,1},{5,3},{7,5},{8,14},{10,8},{12,... | collective-permute-start | bytes 2162696 | tf_op jit(solution)/shard_map/ppermute | solution.py:242
  346.4 26.9 %collective-permute-start.39 = (bf16[2,320,896]{2,1,0:T(8,128)(2,1)S(1)}, bf16[2,320,896]{2,1,0:T(8,128)(2,1)S(1)}, u32[]{:S(2)}, u32[]{:S(2)}) collective-permute-start(bf16[2,320,896]{2,1,0:T(8,128)(2,1)S(1)} %dynamic-slice_bitcast_fusion.4), channel_id=1, source_target_pairs={{0,8},{8,0},{1,9},{9,1},{2,10},{10,2},{3,11},{11,3},{4,12},{12,4},... | collective-permute-start | bytes 3440648 | tf_op jit(solution)/shard_map/ppermute | solution.py:242
  383.1 41.8 %collective-permute-start.40 = (bf16[256,1280]{1,0:T(8,128)(2,1)}, bf16[256,1280]{1,0:T(8,128)(2,1)}, u32[]{:S(2)}, u32[]{:S(2)}) collective-permute-start(bf16[256,1280]{1,0:T(8,128)(2,1)} %add_convert_fusion.5), channel_id=1, source_target_pairs={{0,4},{2,6},{4,0},{6,2},{1,5},{3,7},{5,1},{7,3},{8,12},{10,14},{12... | collective-permute-start | bytes 1966088 | tf_op jit(solution)/shard_map/ppermute | solution.py:242
  386.4 28.5 %collective-permute-start.43 = (bf16[2,320,896]{2,1,0:T(8,128)(2,1)}, bf16[2,320,896]{2,1,0:T(8,128)(2,1)}, u32[]{:S(2)}, u32[]{:S(2)}) collective-permute-start(bf16[2,320,896]{2,1,0:T(8,128)(2,1)} %dynamic-slice_bitcast_fusion.2), channel_id=1, source_target_pairs={{0,8},{8,0},{1,9},{9,1},{2,10},{10,2},{3,11},{11,3},{4,12},{12,4},... | collective-permute-start | bytes 3440648 | tf_op jit(solution)/shard_map/ppermute | solution.py:242
  390.7 28.4 %collective-permute-start.42 = (bf16[2,320,896]{2,1,0:T(8,128)(2,1)}, bf16[2,320,896]{2,1,0:T(8,128)(2,1)}, u32[]{:S(2)}, u32[]{:S(2)}) collective-permute-start(bf16[2,320,896]{2,1,0:T(8,128)(2,1)} %dynamic-slice_bitcast_fusion.3), channel_id=1, source_target_pairs={{0,16},{16,0},{1,17},{17,1},{2,18},{18,2},{3,19},{19,3},{4,20},{20... | collective-permute-start | bytes 3440648 | tf_op jit(solution)/shard_map/ppermute | solution.py:242
  404.2 37.7 %collective-permute-start.71 = (bf16[160,448]{1,0:T(8,128)(2,1)S(1)}, bf16[160,448]{1,0:T(8,128)(2,1)S(1)}, u32[]{:S(2)}, u32[]{:S(2)}) collective-permute-start(bf16[160,448]{1,0:T(8,128)(2,1)S(1)} %dynamic-slice_bitcast_fusion.31), channel_id=1, source_target_pairs={{0,4},{2,6},{4,0},{6,2},{1,5},{3,7},{5,1},{7,3},{8,12},{10,14},{12... | collective-permute-start | bytes 430088 | tf_op jit(solution)/shard_map/ppermute | solution.py:327
  406.5 33.6 %collective-permute-start.49 = (bf16[224,640]{1,0:T(8,128)(2,1)S(1)}, bf16[224,640]{1,0:T(8,128)(2,1)S(1)}, u32[]{:S(2)}, u32[]{:S(2)}) collective-permute-start(bf16[224,640]{1,0:T(8,128)(2,1)S(1)} %dynamic-slice_bitcast_fusion.28), channel_id=1, source_target_pairs={{0,8},{8,0},{1,9},{9,1},{2,10},{10,2},{3,11},{11,3},{4,12},{12,4},... | collective-permute-start | bytes 860168 | tf_op jit(solution)/shard_map/ppermute | solution.py:242
  445.5 49.0 %collective-permute-start.72 = (bf16[160,448]{1,0:T(8,128)(2,1)}, bf16[160,448]{1,0:T(8,128)(2,1)}, u32[]{:S(2)}, u32[]{:S(2)}) collective-permute-start(bf16[160,448]{1,0:T(8,128)(2,1)} %fusion.101), channel_id=1, source_target_pairs={{0,4},{2,6},{4,0},{6,2},{1,5},{3,7},{5,1},{7,3},{8,12},{10,14},{12... | collective-permute-start | bytes 430088 | tf_op jit(solution)/shard_map/ppermute | solution.py:327
  448.5 32.5 %collective-permute-start.56 = (bf16[2,320,640]{2,1,0:T(8,128)(2,1)}, bf16[2,320,640]{2,1,0:T(8,128)(2,1)}, u32[]{:S(2)}, u32[]{:S(2)}) collective-permute-start(bf16[2,320,640]{2,1,0:T(8,128)(2,1)} %dynamic-slice_bitcast_fusion.7), channel_id=1, source_target_pairs={{0,16},{16,0},{1,17},{17,1},{2,18},{18,2},{3,19},{19,3},{4,20},{20... | collective-permute-start | bytes 2457608 | tf_op jit(solution)/shard_map/ppermute | solution.py:242
  456.3 45.2 %collective-permute-start.51 = (bf16[256,1280]{1,0:T(8,128)(2,1)}, bf16[256,1280]{1,0:T(8,128)(2,1)S(1)}, u32[]{:S(2)}, u32[]{:S(2)}) collective-permute-start(bf16[256,1280]{1,0:T(8,128)(2,1)} %add_convert_fusion.3), channel_id=1, source_target_pairs={{0,2},{2,4},{4,6},{6,0},{1,3},{3,5},{5,7},{7,1},{8,10},{10,12},{12... | collective-permute-start | bytes 1966088 | tf_op jit(solution)/shard_map/ppermute | solution.py:242
  461.6 45.7 %collective-permute-start.57 = (bf16[2,320,768]{2,1,0:T(8,128)(2,1)}, bf16[2,320,768]{2,1,0:T(8,128)(2,1)}, u32[]{:S(2)}, u32[]{:S(2)}) collective-permute-start(bf16[2,320,768]{2,1,0:T(8,128)(2,1)} %dynamic-slice_bitcast_fusion.6), channel_id=1, source_target_pairs={{0,8},{8,0},{1,9},{9,1},{2,10},{10,2},{3,11},{11,3},{4,12},{12,4},... | collective-permute-start | bytes 2949128 | tf_op jit(solution)/shard_map/ppermute | solution.py:242
  544.3 36.8 %collective-permute-start.79 = (bf16[2,224,1280]{2,1,0:T(8,128)(2,1)}, bf16[2,224,1280]{2,1,0:T(8,128)(2,1)}, u32[]{:S(2)}, u32[]{:S(2)}) collective-permute-start(bf16[2,224,1280]{2,1,0:T(8,128)(2,1)} %dynamic-slice_bitcast_fusion), channel_id=1, source_target_pairs={{0,8},{8,0},{1,9},{9,1},{2,10},{10,2},{3,11},{11,3},{4,12},{12,4},... | collective-permute-start | bytes 3440648 | tf_op jit(solution)/shard_map/ppermute | solution.py:242
  544.3 39.1 %collective-permute-start.77 = (bf16[2,224,1280]{2,1,0:T(8,128)(2,1)}, bf16[2,224,1280]{2,1,0:T(8,128)(2,1)}, u32[]{:S(2)}, u32[]{:S(2)}) collective-permute-start(bf16[2,224,1280]{2,1,0:T(8,128)(2,1)} %dynamic-slice_bitcast_fusion.1), channel_id=1, source_target_pairs={{0,16},{16,0},{1,17},{17,1},{2,18},{18,2},{3,19},{19,3},{4,20},{20... | collective-permute-start | bytes 3440648 | tf_op jit(solution)/shard_map/ppermute | solution.py:242
  (176 other events, 1761.6 us)

commit v10 on v9

--- a/solution.py
+++ b/solution.py
@@ -397,8 +397,9 @@
     starts_two = two(piece_starts[0])
     later = after([output_weight, shared_gate, shared_up, shared_down, out_grad], *first_near)
     second_shard = jnp.concatenate(
-        [half(later[0], core, 1), half(later[1], core, 1), half(later[2], core, 1)]
-        + [half(later[3], core, 1).reshape(rows, narrow)],
+        [half(later[0], core, 1)]
+        + [jnp.pad(half(later[3], core, 1), ((0, rows - shared_down.shape[0]), (0, 0)))]
+        + [half(later[1], core, 1), half(later[2], core, 1)],
         axis=1,
     )
     second_join, second_near, second_far = gather_dp(after(second_shard, *first_far))
@@ -442,9 +443,10 @@
     probs_low = attn_probs.astype(BF)
     second_full = second_join(after(second_far, probs_low))
     output_cols = second_full[:, :wide]
-    gate_half = second_full[:, wide : wide + narrow]
-    up_half = second_full[:, wide + narrow : wide + 2 * narrow]
-    down_cols = second_full[:, wide + 2 * narrow :].reshape(hidden, wide)
+    gate_half = second_full[:, 2 * wide : 2 * wide + narrow]
+    up_half = second_full[:, 2 * wide + narrow :]
+    down_cols = second_full[:, wide : 2 * wide].reshape(dp, rows, wide)
+    down_cols = down_cols[:, : shared_down.shape[0]].reshape(hidden, wide)
     met = swap(
         jnp.concatenate([half(output_cols, 1 - core, 0), half(down_cols, 1 - core, 0)], axis=0)
     )

time: 620 us -> 613 us (0.989)
  Pallas kernels: 89.3 us -> 80.2 us
    pallas_call x2, Pallas kernels: 78.9 us -> 69.6 us  [expert_call(): pl.pallas_call(functools.partial(expert_kernel, count, width, capacity, e...]
  transfers between devices with their start and end apart: 81 -> 81, of which waited for: 22 -> 25; matrix products, arithmetic and copies ran while one was open for 45% -> 46% of each run, Pallas kernels for 15% -> 13%
where the time goes in v10:
time: 613 us; the launch traced here: 604 us
  waiting for transfers between devices  127 us (21%)
  other arithmetic  119 us (19%)
  local copies, waits for them, and re-layouts  107 us (17%)
  matrix products  84.5 us (14%)
  Pallas kernels  80.2 us (13%)
  starting transfers between devices  79.2 us (13%)
  between operations  6.62 us (1%)
    ppermute x69, waiting for transfers between devices, shifted(): lax.ppermute(value, axis, [(i, (i + by) % size) for i in range(size)])  97.6 us
    pallas_call x2, Pallas kernels, expert_call(): pl.pallas_call(functools.partial(expert_kernel, count, width, capacity, e...  69.6 us
    ppermute x69, starting transfers between devices, shifted(): lax.ppermute(value, axis, [(i, (i + by) % size) for i in range(size)])  65.3 us
    dot_general x22, matrix products, product(): return jnp.dot(first_arg, second_arg, preferred_element_type=F32)  46.5 us
    dot_general x10, matrix products, mm(): return jnp.einsum(spec, first_arg, second_arg, preferred_element_type=F32)  29.9 us
    ppermute x12, waiting for transfers between devices, crossed(): return lax.ppermute(value, 'z', [(i, i ^ bit) for i in range(depth)])  29.7 us
    convert_element_type x24, other arithmetic, ring_reduce(): (other.astype(F32) + pick(value, index - step, at).astype(F32)).astype(BF)  26.7 us
    unnamed x258, local copies, waits for them, and re-layouts  16.8 us
  transfers between devices with their start and end apart: 81, of which 25 were waited for; matrix products, arithmetic and copies ran while one was open for 46% of the time, Pallas kernels for 13%

profile of v10, /device:TPU:0, one launch (start us, length us, event | category | flops | bytes accessed | tf_op | source)
XLA Modules:
  0.0 603.8 jit_solution(8760948771815218753)
XLA Ops:
  20.1 17.5 %collective-permute-done.2.refs_2_ = bf16[320,2048]{1,0:T(8,128)(2,1)} collective-permute-done((bf16[320,2048]{1,0:T(8,128)(2,1)}, bf16[320,2048]{1,0:T(8,128)(2,1)}, u32[]{:S(2)}, u32[]{:S(2)}) %collective-permute-start.2) | collective-permute-done | bytes 1310752 | tf_op jit(solution)/shard_map/ppermute | solution.py:242
  51.7 3.6 concatenate.163.refs_0_
  61.0 5.2 place.2
  67.9 4.0 slice_bitcast_fusion.1
  73.3 3.5 copy.287
  76.9 3.9 fusion.45
  80.8 3.5 copy.288
  103.0 3.8 collective-permute-done.11.refs_4_
  110.1 5.4 place.3
  155.3 3.8 multiply_convert_fusion.3
  173.5 7.8 %collective-permute-done.17.refs_2_ = bf16[256,1408]{1,0:T(8,128)(2,1)} collective-permute-done((bf16[256,1408]{1,0:T(8,128)(2,1)}, bf16[256,1408]{1,0:T(8,128)(2,1)}, u32[]{:S(2)}, u32[]{:S(2)}) %collective-permute-start.17) | collective-permute-done | bytes 720928 | tf_op jit(solution)/shard_map/ppermute | solution.py:242
  181.4 3.5 collective-permute-start.30
  199.5 3.8 collective-permute-start.23
  203.3 34.8 %experts.2 = (bf16[256,2688]{1,0:T(8,128)(2,1)}, bf16[256,2688]{1,0:T(8,128)(2,1)}, bf16[256,2688]{1,0:T(8,128)(2,1)}, bf16[256,2688]{1,0:T(8,128)(2,1)}, bf16[2...) custom-call(s32[1]{0:T(128)} %bitcast.22.me_ref, ...), custom_call_target="tpu_custom_call" | custom-call | flops 16441671680 | bytes 62914560 | tf_op jit(solution)/shard_map/experts/pallas_call | solution.py:133
  260.4 34.8 %experts.3 = (bf16[256,2688]{1,0:T(8,128)(2,1)}, bf16[256,2688]{1,0:T(8,128)(2,1)}, bf16[256,2688]{1,0:T(8,128)(2,1)}, bf16[256,2688]{1,0:T(8,128)(2,1)}, bf16[2...) custom-call(s32[1]{0:T(128)} %bitcast.22.me_ref, ...), custom_call_target="tpu_custom_call", output_to_operand_aliasing={{4}: (13, {}), {5}: (14, {}), {6}: (15, {}), {7}: (16, {}),... | custom-call | flops 16441671680 | bytes 62914560 | tf_op jit(solution)/shard_map/experts/pallas_call | solution.py:133
  295.3 9.1 %convolution_convert_fusion.2 = bf16[2,1280,896]{2,1,0:T(8,128)(2,1)S(1)} fusion(bf16[2,1024,1280]{2,1,0:T(8,128)(2,1)} %get-tuple-element.128, bf16[2,1024,896]{2,1,0:T(8,128)(2,1)} %get-tuple-element.134), kind=kOutput, calls=%fused_computation.4 | convolution fusion | flops 4699914240 | bytes 13500416 | tf_op jit(solution)/shard_map/erd,erf->edf/dot_general | solution.py:196
  319.6 8.8 %convolution_convert_fusion.1 = bf16[2,1280,896]{2,1,0:T(8,128)(2,1)S(1)} fusion(bf16[2,1024,1280]{2,1,0:T(8,128)(2,1)} %get-tuple-element.128, bf16[2,1024,896]{2,1,0:T(8,128)(2,1)S(1)} %copy-done.122), kind=kOutput, calls=%fused_computation.3 | convolution fusion | flops 4699914240 | bytes 13500416 | tf_op jit(solution)/shard_map/erd,erf->edf/dot_general | solution.py:196
  328.3 8.6 %convolution_convert_fusion = bf16[2,896,1280]{2,1,0:T(8,128)(2,1)S(1)} fusion(bf16[2,1024,896]{2,1,0:T(8,128)(2,1)} %get-tuple-element.142, bf16[2,1024,1280]{2,1,0:T(8,128)(2,1)} %get-tuple-element.143), kind=kOutput, calls=%fused_computation.2 | convolution fusion | flops 4699914240 | bytes 13500416 | tf_op jit(solution)/shard_map/erf,erd->efd/dot_general | solution.py:196
  346.1 20.5 %collective-permute-done.38 = bf16[2,320,896]{2,1,0:T(8,128)(2,1)S(1)} collective-permute-done((bf16[2,320,896]{2,1,0:T(8,128)(2,1)S(1)}, bf16[2,320,896]{2,1,0:T(8,128)(2,1)S(1)}, u32[]{:S(2)}, u32[]{:S(2)}) %collective-permute-start.38) | collective-permute-done | bytes 1146912 | tf_op jit(solution)/shard_map/ppermute | solution.py:242
  404.5 4.5 collective-permute-done.43
  446.8 4.0 copy.330
  461.2 14.1 %collective-permute-done.56 = bf16[2,320,640]{2,1,0:T(8,128)(2,1)} collective-permute-done((bf16[2,320,640]{2,1,0:T(8,128)(2,1)}, bf16[2,320,640]{2,1,0:T(8,128)(2,1)}, u32[]{:S(2)}, u32[]{:S(2)}) %collective-permute-start.56) | collective-permute-done | bytes 819232 | tf_op jit(solution)/shard_map/ppermute | solution.py:242
  477.3 3.7 collective-permute-done.55
  481.1 7.4 %collective-permute-done.53 = bf16[320,640]{1,0:T(8,128)(2,1)S(1)} collective-permute-done((bf16[320,640]{1,0:T(8,128)(2,1)S(1)}, bf16[320,640]{1,0:T(8,128)(2,1)S(1)}, u32[]{:S(2)}, u32[]{:S(2)}) %collective-permute-start.53) | collective-permute-done | bytes 409632 | tf_op jit(solution)/shard_map/ppermute | solution.py:242
  507.4 3.8 collective-permute-done.65
  517.6 8.3 %collective-permute-done.66 = bf16[216,640]{1,0:T(8,128)(2,1)S(1)} collective-permute-done((bf16[216,640]{1,0:T(8,128)(2,1)S(1)}, bf16[216,640]{1,0:T(8,128)(2,1)S(1)}, u32[]{:S(2)}, u32[]{:S(2)}) %collective-permute-start.66) | collective-permute-done | bytes 276512 | tf_op jit(solution)/shard_map/ppermute | solution.py:327
  527.5 3.4 collective-permute-start.60
  557.3 3.6 collective-permute-done.61
  561.9 3.6 collective-permute-start.62
  567.1 7.4 %collective-permute-done.62 = bf16[80,1408]{1,0:T(8,128)(2,1)S(1)} collective-permute-done((bf16[80,1408]{1,0:T(8,128)(2,1)S(1)}, bf16[80,1408]{1,0:T(8,128)(2,1)S(1)}, u32[]{:S(2)}, u32[]{:S(2)}) %collective-permute-start.62) | collective-permute-done | bytes 225312 | tf_op jit(solution)/shard_map/ppermute | solution.py:327
  580.2 5.5 collective-permute-done.63
  586.2 4.0 collective-permute-done.80
  (682 shorter events, 337.9 us)
Async XLA Ops:
  5.5 32.1 %collective-permute-start.2 = (bf16[320,2048]{1,0:T(8,128)(2,1)}, bf16[320,2048]{1,0:T(8,128)(2,1)}, u32[]{:S(2)}, u32[]{:S(2)}) collective-permute-start(bf16[320,2048]{1,0:T(8,128)(2,1)} %fusion.38.refs_0_), channel_id=1, source_target_pairs={{0,16},{16,0},{1,17},{17,1},{2,18},{18,2},{3,19},{19,3},{4,20},{20... | collective-permute-start | bytes 3932168 | tf_op jit(solution)/shard_map/ppermute | solution.py:242
  8.5 32.8 %collective-permute-start.1 = (bf16[320,2048]{1,0:T(8,128)(2,1)}, bf16[320,2048]{1,0:T(8,128)(2,1)}, u32[]{:S(2)}, u32[]{:S(2)}) collective-permute-start(bf16[320,2048]{1,0:T(8,128)(2,1)} %fusion.38.refs_0_), channel_id=1, source_target_pairs={{0,8},{8,0},{1,9},{9,1},{2,10},{10,2},{3,11},{11,3},{4,12},{12,4},... | collective-permute-start | bytes 3932168 | tf_op jit(solution)/shard_map/ppermute | solution.py:242
  45.7 54.6 %collective-permute-start.14 = (bf16[256,1408]{1,0:T(8,128)(2,1)}, bf16[256,1408]{1,0:T(8,128)(2,1)}, u32[]{:S(2)}, u32[]{:S(2)}) collective-permute-start(bf16[256,1408]{1,0:T(8,128)(2,1)} %pad_maximum_fusion.8.refs_4_), channel_id=1, source_target_pairs={{0,1},{1,0},{2,3},{3,2},{4,5},{5,4},{6,7},{7,6},{8,9},{9,8},{10,11... | collective-permute-start | bytes 2162696 | tf_op jit(solution)/shard_map/ppermute | solution.py:242
  45.7 55.6 %collective-permute-start.5 = (bf16[256,1408]{1,0:T(8,128)(2,1)}, bf16[256,1408]{1,0:T(8,128)(2,1)}, u32[]{:S(2)}, u32[]{:S(2)}) collective-permute-start(bf16[256,1408]{1,0:T(8,128)(2,1)} %pad_maximum_fusion.8.refs_4_), channel_id=1, source_target_pairs={{0,4},{2,6},{4,0},{6,2},{1,5},{3,7},{5,1},{7,3},{8,12},{10,14},{12... | collective-permute-start | bytes 2162696 | tf_op jit(solution)/shard_map/ppermute | solution.py:242
  58.9 30.6 %collective-permute-start.7 = (bf16[320,2176]{1,0:T(8,128)(2,1)}, bf16[320,2176]{1,0:T(8,128)(2,1)}, u32[]{:S(2)}, u32[]{:S(2)}) collective-permute-start(bf16[320,2176]{1,0:T(8,128)(2,1)} %concatenate.163.refs_0_), channel_id=1, source_target_pairs={{0,16},{16,0},{1,17},{17,1},{2,18},{18,2},{3,19},{19,3},{4,20},{20... | collective-permute-start | bytes 4177928 | tf_op jit(solution)/shard_map/ppermute | solution.py:242
  60.4 32.8 %collective-permute-start.6 = (bf16[320,2176]{1,0:T(8,128)(2,1)}, bf16[320,2176]{1,0:T(8,128)(2,1)}, u32[]{:S(2)}, u32[]{:S(2)}) collective-permute-start(bf16[320,2176]{1,0:T(8,128)(2,1)} %concatenate.163.refs_0_), channel_id=1, source_target_pairs={{0,8},{8,0},{1,9},{9,1},{2,10},{10,2},{3,11},{11,3},{4,12},{12,4},... | collective-permute-start | bytes 4177928 | tf_op jit(solution)/shard_map/ppermute | solution.py:242
  146.6 34.7 %collective-permute-start.17 = (bf16[256,1408]{1,0:T(8,128)(2,1)}, bf16[256,1408]{1,0:T(8,128)(2,1)}, u32[]{:S(2)}, u32[]{:S(2)}) collective-permute-start(bf16[256,1408]{1,0:T(8,128)(2,1)} %concatenate.169.refs_0_), channel_id=1, source_target_pairs={{0,4},{2,6},{4,0},{6,2},{1,5},{3,7},{5,1},{7,3},{8,12},{10,14},{12... | collective-permute-start | bytes 2162696 | tf_op jit(solution)/shard_map/ppermute | solution.py:242
  149.9 34.9 %collective-permute-start.15 = (bf16[256,1408]{1,0:T(8,128)(2,1)}, bf16[256,1408]{1,0:T(8,128)(2,1)}, u32[]{:S(2)}, u32[]{:S(2)}) collective-permute-start(bf16[256,1408]{1,0:T(8,128)(2,1)} %collective-permute-done.5.refs_6_), channel_id=1, source_target_pairs={{0,1},{1,0},{2,3},{3,2},{4,5},{5,4},{6,7},{7,6},{8,9},{9,8},{10,11... | collective-permute-start | bytes 2162696 | tf_op jit(solution)/shard_map/ppermute | solution.py:242
  181.4 70.1 %collective-permute-start.30 = (bf16[256,1408]{1,0:T(8,128)(2,1)}, bf16[256,1408]{1,0:T(8,128)(2,1)}, u32[]{:S(2)}, u32[]{:S(2)}) collective-permute-start(bf16[256,1408]{1,0:T(8,128)(2,1)} %concatenate.169.refs_0_), channel_id=1, source_target_pairs={{0,6},{2,0},{4,2},{6,4},{1,7},{3,1},{5,3},{7,5},{8,14},{10,8},{12,... | collective-permute-start | bytes 2162696 | tf_op jit(solution)/shard_map/ppermute | solution.py:242
  184.8 68.1 %collective-permute-start.28 = (bf16[256,1408]{1,0:T(8,128)(2,1)}, bf16[256,1408]{1,0:T(8,128)(2,1)}, u32[]{:S(2)}, u32[]{:S(2)}) collective-permute-start(bf16[256,1408]{1,0:T(8,128)(2,1)} %concatenate.169.refs_0_), channel_id=1, source_target_pairs={{0,2},{2,4},{4,6},{6,0},{1,3},{3,5},{5,7},{7,1},{8,10},{10,12},{12... | collective-permute-start | bytes 2162696 | tf_op jit(solution)/shard_map/ppermute | solution.py:242
  195.4 43.6 %collective-permute-start.26 = (bf16[2,320,448]{2,1,0:T(8,128)(2,1)}, bf16[2,320,448]{2,1,0:T(8,128)(2,1)}, u32[]{:S(2)}, u32[]{:S(2)}) collective-permute-start(bf16[2,320,448]{2,1,0:T(8,128)(2,1)} %dynamic-slice_bitcast_fusion.10), channel_id=1, source_target_pairs={{0,8},{8,0},{1,9},{9,1},{2,10},{10,2},{3,11},{11,3},{4,12},{12,4},... | collective-permute-start | bytes 1720328 | tf_op jit(solution)/shard_map/ppermute | solution.py:242
  196.0 45.6 %collective-permute-start.25 = (bf16[2,320,448]{2,1,0:T(8,128)(2,1)}, bf16[2,320,448]{2,1,0:T(8,128)(2,1)}, u32[]{:S(2)}, u32[]{:S(2)}) collective-permute-start(bf16[2,320,448]{2,1,0:T(8,128)(2,1)} %dynamic-slice_bitcast_fusion.11), channel_id=1, source_target_pairs={{0,16},{16,0},{1,17},{17,1},{2,18},{18,2},{3,19},{19,3},{4,20},{20... | collective-permute-start | bytes 1720328 | tf_op jit(solution)/shard_map/ppermute | solution.py:242
  199.5 38.7 %collective-permute-start.23 = (bf16[256,1408]{1,0:T(8,128)(2,1)}, bf16[256,1408]{1,0:T(8,128)(2,1)}, u32[]{:S(2)}, u32[]{:S(2)}) collective-permute-start(bf16[256,1408]{1,0:T(8,128)(2,1)} %pad_maximum_fusion.8.refs_4_), channel_id=1, source_target_pairs={{0,6},{2,0},{4,2},{6,4},{1,7},{3,1},{5,3},{7,5},{8,14},{10,8},{12,... | collective-permute-start | bytes 2162696 | tf_op jit(solution)/shard_map/ppermute | solution.py:242
  248.9 55.5 %collective-permute-start.35 = (bf16[320,448]{1,0:T(8,128)(2,1)}, bf16[320,448]{1,0:T(8,128)(2,1)}, u32[]{:S(2)}, u32[]{:S(2)}) collective-permute-start(bf16[320,448]{1,0:T(8,128)(2,1)} %dynamic-slice_bitcast_fusion.26), channel_id=1, source_target_pairs={{0,16},{16,0},{1,17},{17,1},{2,18},{18,2},{3,19},{19,3},{4,20},{20... | collective-permute-start | bytes 860168 | tf_op jit(solution)/shard_map/ppermute | solution.py:242
  251.4 53.6 %collective-permute-start.34 = (bf16[320,448]{1,0:T(8,128)(2,1)}, bf16[320,448]{1,0:T(8,128)(2,1)}, u32[]{:S(2)}, u32[]{:S(2)}) collective-permute-start(bf16[320,448]{1,0:T(8,128)(2,1)} %dynamic-slice_bitcast_fusion.27), channel_id=1, source_target_pairs={{0,8},{8,0},{1,9},{9,1},{2,10},{10,2},{3,11},{11,3},{4,12},{12,4},... | collective-permute-start | bytes 860168 | tf_op jit(solution)/shard_map/ppermute | solution.py:242
  257.6 49.6 %collective-permute-start.19 = (bf16[256,2688]{1,0:T(8,128)(2,1)}, bf16[256,2688]{1,0:T(8,128)(2,1)}, u32[]{:S(2)}, u32[]{:S(2)}) collective-permute-start(bf16[256,2688]{1,0:T(8,128)(2,1)} %fusion.34), channel_id=1, source_target_pairs={{0,1},{1,0},{2,3},{3,2},{4,5},{5,4},{6,7},{7,6},{8,9},{9,8},{10,11... | collective-permute-start | bytes 4128776 | tf_op jit(solution)/shard_map/ppermute | solution.py:242
  260.4 52.3 %collective-permute-start.21 = (bf16[256,1408]{1,0:T(8,128)(2,1)}, bf16[256,1408]{1,0:T(8,128)(2,1)}, u32[]{:S(2)}, u32[]{:S(2)}) collective-permute-start(bf16[256,1408]{1,0:T(8,128)(2,1)} %add_convert_fusion.2), channel_id=1, source_target_pairs={{0,4},{2,6},{4,0},{6,2},{1,5},{3,7},{5,1},{7,3},{8,12},{10,14},{12... | collective-permute-start | bytes 2162696 | tf_op jit(solution)/shard_map/ppermute | solution.py:242
  314.7 54.6 %collective-permute-start.37 = (bf16[256,1408]{1,0:T(8,128)(2,1)}, bf16[256,1408]{1,0:T(8,128)(2,1)}, u32[]{:S(2)}, u32[]{:S(2)}) collective-permute-start(bf16[256,1408]{1,0:T(8,128)(2,1)} %add_convert_fusion), channel_id=1, source_target_pairs={{0,2},{2,4},{4,6},{6,0},{1,3},{3,5},{5,7},{7,1},{8,10},{10,12},{12... | collective-permute-start | bytes 2162696 | tf_op jit(solution)/shard_map/ppermute | solution.py:242
  316.5 52.7 %collective-permute-start.36 = (bf16[256,1408]{1,0:T(8,128)(2,1)}, bf16[256,1408]{1,0:T(8,128)(2,1)}, u32[]{:S(2)}, u32[]{:S(2)}) collective-permute-start(bf16[256,1408]{1,0:T(8,128)(2,1)} %add_convert_fusion.1), channel_id=1, source_target_pairs={{0,6},{2,0},{4,2},{6,4},{1,7},{3,1},{5,3},{7,5},{8,14},{10,8},{12,... | collective-permute-start | bytes 2162696 | tf_op jit(solution)/shard_map/ppermute | solution.py:242
  340.5 27.4 %collective-permute-start.39 = (bf16[2,320,896]{2,1,0:T(8,128)(2,1)S(1)}, bf16[2,320,896]{2,1,0:T(8,128)(2,1)S(1)}, u32[]{:S(2)}, u32[]{:S(2)}) collective-permute-start(bf16[2,320,896]{2,1,0:T(8,128)(2,1)S(1)} %dynamic-slice_bitcast_fusion.4), channel_id=1, source_target_pairs={{0,8},{8,0},{1,9},{9,1},{2,10},{10,2},{3,11},{11,3},{4,12},{12,4},... | collective-permute-start | bytes 3440648 | tf_op jit(solution)/shard_map/ppermute | solution.py:242
  377.4 42.1 %collective-permute-start.40 = (bf16[256,1280]{1,0:T(8,128)(2,1)}, bf16[256,1280]{1,0:T(8,128)(2,1)}, u32[]{:S(2)}, u32[]{:S(2)}) collective-permute-start(bf16[256,1280]{1,0:T(8,128)(2,1)} %add_convert_fusion.5), channel_id=1, source_target_pairs={{0,4},{2,6},{4,0},{6,2},{1,5},{3,7},{5,1},{7,3},{8,12},{10,14},{12... | collective-permute-start | bytes 1966088 | tf_op jit(solution)/shard_map/ppermute | solution.py:242
  380.6 28.5 %collective-permute-start.43 = (bf16[2,320,896]{2,1,0:T(8,128)(2,1)}, bf16[2,320,896]{2,1,0:T(8,128)(2,1)}, u32[]{:S(2)}, u32[]{:S(2)}) collective-permute-start(bf16[2,320,896]{2,1,0:T(8,128)(2,1)} %dynamic-slice_bitcast_fusion.2), channel_id=1, source_target_pairs={{0,8},{8,0},{1,9},{9,1},{2,10},{10,2},{3,11},{11,3},{4,12},{12,4},... | collective-permute-start | bytes 3440648 | tf_op jit(solution)/shard_map/ppermute | solution.py:242
  385.0 28.7 %collective-permute-start.42 = (bf16[2,320,896]{2,1,0:T(8,128)(2,1)}, bf16[2,320,896]{2,1,0:T(8,128)(2,1)}, u32[]{:S(2)}, u32[]{:S(2)}) collective-permute-start(bf16[2,320,896]{2,1,0:T(8,128)(2,1)} %dynamic-slice_bitcast_fusion.3), channel_id=1, source_target_pairs={{0,16},{16,0},{1,17},{17,1},{2,18},{18,2},{3,19},{19,3},{4,20},{20... | collective-permute-start | bytes 3440648 | tf_op jit(solution)/shard_map/ppermute | solution.py:242
  398.1 38.3 %collective-permute-start.71 = (bf16[160,448]{1,0:T(8,128)(2,1)S(1)}, bf16[160,448]{1,0:T(8,128)(2,1)S(1)}, u32[]{:S(2)}, u32[]{:S(2)}) collective-permute-start(bf16[160,448]{1,0:T(8,128)(2,1)S(1)} %dynamic-slice_bitcast_fusion.31), channel_id=1, source_target_pairs={{0,4},{2,6},{4,0},{6,2},{1,5},{3,7},{5,1},{7,3},{8,12},{10,14},{12... | collective-permute-start | bytes 430088 | tf_op jit(solution)/shard_map/ppermute | solution.py:327
  400.3 33.5 %collective-permute-start.49 = (bf16[224,640]{1,0:T(8,128)(2,1)S(1)}, bf16[224,640]{1,0:T(8,128)(2,1)S(1)}, u32[]{:S(2)}, u32[]{:S(2)}) collective-permute-start(bf16[224,640]{1,0:T(8,128)(2,1)S(1)} %dynamic-slice_bitcast_fusion.28), channel_id=1, source_target_pairs={{0,8},{8,0},{1,9},{9,1},{2,10},{10,2},{3,11},{11,3},{4,12},{12,4},... | collective-permute-start | bytes 860168 | tf_op jit(solution)/shard_map/ppermute | solution.py:242
  439.4 49.2 %collective-permute-start.72 = (bf16[160,448]{1,0:T(8,128)(2,1)}, bf16[160,448]{1,0:T(8,128)(2,1)}, u32[]{:S(2)}, u32[]{:S(2)}) collective-permute-start(bf16[160,448]{1,0:T(8,128)(2,1)} %fusion.101), channel_id=1, source_target_pairs={{0,4},{2,6},{4,0},{6,2},{1,5},{3,7},{5,1},{7,3},{8,12},{10,14},{12... | collective-permute-start | bytes 430088 | tf_op jit(solution)/shard_map/ppermute | solution.py:327
  442.4 33.0 %collective-permute-start.56 = (bf16[2,320,640]{2,1,0:T(8,128)(2,1)}, bf16[2,320,640]{2,1,0:T(8,128)(2,1)}, u32[]{:S(2)}, u32[]{:S(2)}) collective-permute-start(bf16[2,320,640]{2,1,0:T(8,128)(2,1)} %dynamic-slice_bitcast_fusion.7), channel_id=1, source_target_pairs={{0,16},{16,0},{1,17},{17,1},{2,18},{18,2},{3,19},{19,3},{4,20},{20... | collective-permute-start | bytes 2457608 | tf_op jit(solution)/shard_map/ppermute | solution.py:242
  450.7 44.9 %collective-permute-start.51 = (bf16[256,1280]{1,0:T(8,128)(2,1)}, bf16[256,1280]{1,0:T(8,128)(2,1)S(1)}, u32[]{:S(2)}, u32[]{:S(2)}) collective-permute-start(bf16[256,1280]{1,0:T(8,128)(2,1)} %add_convert_fusion.3), channel_id=1, source_target_pairs={{0,2},{2,4},{4,6},{6,0},{1,3},{3,5},{5,7},{7,1},{8,10},{10,12},{12... | collective-permute-start | bytes 1966088 | tf_op jit(solution)/shard_map/ppermute | solution.py:242
  456.1 45.3 %collective-permute-start.57 = (bf16[2,320,768]{2,1,0:T(8,128)(2,1)}, bf16[2,320,768]{2,1,0:T(8,128)(2,1)}, u32[]{:S(2)}, u32[]{:S(2)}) collective-permute-start(bf16[2,320,768]{2,1,0:T(8,128)(2,1)} %dynamic-slice_bitcast_fusion.6), channel_id=1, source_target_pairs={{0,8},{8,0},{1,9},{9,1},{2,10},{10,2},{3,11},{11,3},{4,12},{12,4},... | collective-permute-start | bytes 2949128 | tf_op jit(solution)/shard_map/ppermute | solution.py:242
  537.5 37.2 %collective-permute-start.79 = (bf16[2,224,1280]{2,1,0:T(8,128)(2,1)}, bf16[2,224,1280]{2,1,0:T(8,128)(2,1)}, u32[]{:S(2)}, u32[]{:S(2)}) collective-permute-start(bf16[2,224,1280]{2,1,0:T(8,128)(2,1)} %dynamic-slice_bitcast_fusion), channel_id=1, source_target_pairs={{0,8},{8,0},{1,9},{9,1},{2,10},{10,2},{3,11},{11,3},{4,12},{12,4},... | collective-permute-start | bytes 3440648 | tf_op jit(solution)/shard_map/ppermute | solution.py:242
  539.1 38.5 %collective-permute-start.77 = (bf16[2,224,1280]{2,1,0:T(8,128)(2,1)}, bf16[2,224,1280]{2,1,0:T(8,128)(2,1)}, u32[]{:S(2)}, u32[]{:S(2)}) collective-permute-start(bf16[2,224,1280]{2,1,0:T(8,128)(2,1)} %dynamic-slice_bitcast_fusion.1), channel_id=1, source_target_pairs={{0,16},{16,0},{1,17},{17,1},{2,18},{18,2},{3,19},{19,3},{4,20},{20... | collective-permute-start | bytes 3440648 | tf_op jit(solution)/shard_map/ppermute | solution.py:242
  567.0 28.0 %collective-permute-start.69 = (bf16[864,640]{1,0:T(8,128)(2,1)S(1)}, bf16[864,640]{1,0:T(8,128)(2,1)S(1)}, u32[]{:S(2)}, u32[]{:S(2)}) collective-permute-start(bf16[864,640]{1,0:T(8,128)(2,1)S(1)} %bitcast.425), channel_id=1, source_target_pairs={{0,1},{1,0},{2,3},{3,2},{4,5},{5,4},{6,7},{7,6},{8,9},{9,8},{10,11... | collective-permute-start | bytes 3317768 | tf_op jit(solution)/shard_map/ppermute | solution.py:242
  (174 other events, 1607.3 us)
